TPU v7x, 32 devices: a whole 2x2x4 slice. The times are simulated.
32 devices in a mesh: grp: 4 (over y, x), tile: 8 (over z, core).
Axes of the slice: x: 2, y: 2, z: 4, core: 2. Of those that a mesh axis runs over, the one named last changes fastest.
Arguments:
- observed: bfloat16 [512, 32, 2048], P('tile', 'grp'), as said below
- visible: int32 [32, 2048], P('grp', 'tile'), may hold values from 0 to 65535
- params_start: float32 [8, 32, 2048], P(None, 'grp', 'tile'), may hold values from -1.5 to 1.5, as said below
- light_directions: float32 [3, 32], replicated, may hold values from -1 to 1
- view_dirs: float32 [3, 16], replicated, may hold values from -1 to 1
- gains_start: float32 [32], replicated, may hold values from 0.5 to 1.5
Outputs:
- params_out: float32 [8, 32, 2048], P(None, 'grp', 'tile')
- gains_out: float32 [32], replicated
Inputs may be any that keep to these rules, and one draw needn't show every extreme that they name: `observed`: luminance is positive. `params_start`: tilts within -0.3 to 0.3, diffuse 0.3 to 1.2, specular 0.1 to 0.8, sharpness logit -1.5 to 1.5, ambient -0.2 to 0.3, rim 0 to 0.5, retro -0.3 to 0.3.
All inputs are finite; a program needn't handle non-finite values.
Results may differ from a plain program's by a relative error of at most 0.0003.
Values may be sent and summed in bfloat16 or wider, within the bound.
No kernel may reach another device: no remote copies, remote signals or barrier semaphores. Data moves between devices by JAX's collectives and lax.ppermute only.
A program may use at most 64 MiB of HBM per device.

v0:
```python
import jax
import jax.numpy as jnp
from jax import lax
from jax.sharding import PartitionSpec as P

CAMS = 16
LIGHTS = 32
ITERS = 2


damping = 4.0
lift_z = 1.6


def padded_2(cells, sides, width):
    for axis, dim in sides:
        count = lax.axis_size(axis)
        ends = count - 1
        head = lax.slice_in_dim(cells, 0, width, axis=dim)
        tail = lax.slice_in_dim(cells, cells.shape[dim] - width, cells.shape[dim], axis=dim)
        cells = jnp.concatenate(
            [
                lax.ppermute(tail, axis, [(i, (i + 1) % count) for i in range(ends)]),
                cells,
                lax.ppermute(head, axis, [((i + 1) % count, i) for i in range(ends)]),
            ],
            axis=dim,
        )
    return cells


def unit_columns(raw):
    lifted = raw + jnp.array([0.0, 0.0, lift_z], jnp.float32)[:, None]
    return lifted / jnp.sqrt(jnp.sum(lifted * lifted, axis=0, keepdims=True))


def geometry(light_directions, view_dirs):
    lights = unit_columns(light_directions)
    views = unit_columns(view_dirs)
    raw_half = views.T[:, :, None] + lights[None]
    halves = raw_half / jnp.sqrt(jnp.sum(raw_half * raw_half, axis=1, keepdims=True))
    echoes = jnp.sum(views.T[:, :, None] * lights[None], axis=1)
    return (lights, halves, views.T, echoes)


def facing(dir_x, dir_y, dir_z, tilt_u, tilt_v, scale_q):
    facing_dot = (dir_x * tilt_u + dir_y * tilt_v + dir_z) * scale_q
    by_u = (dir_x - facing_dot * tilt_u * scale_q) * scale_q
    by_v = (dir_y - facing_dot * tilt_v * scale_q) * scale_q
    return (facing_dot, by_u, by_v)


def camera_terms(observed_c, weight_c, params, gains, lights, half_c, view_c, echo_c):
    tilt_u, tilt_v, diffuse, specular, sharp_raw, ambient, rim_gain, retro_gain = [
        params[i] for i in range(8)
    ]
    scale_q = 1.0 / jnp.sqrt(1.0 + tilt_u * tilt_u + tilt_v * tilt_v)
    light_dot, light_u, light_v = facing(
        lights[0][:, None], lights[1][:, None], lights[2][:, None], tilt_u, tilt_v, scale_q
    )
    half_dot, half_u, half_v = facing(
        half_c[0][:, None], half_c[1][:, None], half_c[2][:, None], tilt_u, tilt_v, scale_q
    )
    view_dot, view_u, view_v = facing(view_c[0], view_c[1], view_c[2], tilt_u, tilt_v, scale_q)
    sigma = jax.nn.sigmoid(sharp_raw)
    sharp = 1.0 + 20.0 * sigma
    lobe = jnp.exp(sharp * (half_dot - 1.0))
    back = 1.0 - view_dot
    rim_shape = back * back
    shaped = (
        diffuse * light_dot
        + specular * lobe
        + ambient
        + rim_gain * rim_shape
        + retro_gain * echo_c[:, None]
    )
    full = light_dot.shape
    jacob = [
        diffuse * light_u + specular * sharp * lobe * half_u - 2.0 * rim_gain * back * view_u,
        diffuse * light_v + specular * sharp * lobe * half_v - 2.0 * rim_gain * back * view_v,
        light_dot,
        lobe,
        specular * lobe * (half_dot - 1.0) * 20.0 * sigma * (1.0 - sigma),
        jnp.ones(full, jnp.float32),
        jnp.broadcast_to(rim_shape, full),
        jnp.broadcast_to(echo_c[:, None], full),
    ]
    column = gains[:, None]
    resid = observed_c.astype(jnp.float32) - column * shaped
    scaled = [column * piece for piece in jacob]
    surface_normal = []
    for i in range(8):
        for j in range(i, 8):
            surface_normal.append(weight_c * jnp.sum(scaled[i] * scaled[j], axis=0))
    right_side = [weight_c * jnp.sum(piece * resid, axis=0) for piece in scaled]
    lifted = jnp.sum(weight_c * shaped * resid, axis=1)
    energy = jnp.sum(weight_c * shaped * shaped, axis=1)
    return (jnp.stack(surface_normal), jnp.stack(right_side), lifted, energy)


def assemble(observed, weights, params, gains, lights, halves, views, echoes):
    texels = params.shape[1]

    def one_camera(carry, inputs):
        observed_c, weight_c, half_c, view_c, echo_c = inputs
        terms = camera_terms(observed_c, weight_c, params, gains, lights, half_c, view_c, echo_c)
        return (tuple((a + b for a, b in zip(carry, terms))), None)

    start = (
        jnp.zeros((36, texels), jnp.float32),
        jnp.zeros((8, texels), jnp.float32),
        jnp.zeros((LIGHTS,), jnp.float32),
        jnp.zeros((LIGHTS,), jnp.float32),
    )
    result, unused = lax.scan(one_camera, start, (observed, weights, halves, views, echoes))
    return result


def solve_eight(surface_normal, right_side):
    entries = {}
    where = 0
    for i in range(8):
        for j in range(i, 8):
            entries[i, j] = surface_normal[where]
            where += 1
    lower = {}
    for j in range(8):
        accum = entries[j, j] + damping
        for k in range(j):
            accum = accum - lower[j, k] * lower[j, k]
        root = jnp.sqrt(accum)
        lower[j, j] = root
        for i in range(j + 1, 8):
            accum = entries[j, i]
            for k in range(j):
                accum = accum - lower[i, k] * lower[j, k]
            lower[i, j] = accum / root
    forward = []
    for i in range(8):
        accum = right_side[i]
        for k in range(i):
            accum = accum - lower[i, k] * forward[k]
        forward.append(accum / lower[i, i])
    answer = [None] * 8
    for i in range(7, -1, -1):
        accum = forward[i]
        for k in range(i + 1, 8):
            accum = accum - lower[k, i] * answer[k]
        answer[i] = accum / lower[i, i]
    return jnp.stack(answer)


def smooth_tilts(tilt):
    rows = tilt.shape[1]
    cols = tilt.shape[2]
    padded = padded_2(tilt, (("grp", 1), ("tile", 2)), 1)
    boxed = jnp.zeros(tilt.shape, jnp.float32)
    for i in range(3):
        for j in range(3):
            boxed = boxed + padded[:, i : i + rows, j : j + cols]
    return 0.5 * tilt + boxed * (0.5 / 9.0)


def update_gains(gains, lifted, energy):
    totals = lax.psum(jnp.stack([lifted, energy]), ("grp", "tile"))
    return gains + totals[0] / (totals[1] + 1.0)


def on_device(observed, visible, params_start, light_directions, view_dirs, gains_start):
    lights, halves, views, echoes = geometry(light_directions, view_dirs)
    rows = visible.shape[0]
    cols = visible.shape[1]
    shifts = jnp.arange(CAMS, dtype=jnp.int32)
    weights = jnp.bitwise_and(jnp.right_shift(visible.reshape(1, -1), shifts[:, None]), 1).astype(
        jnp.float32
    )
    params = params_start.reshape(8, -1)
    gains = gains_start
    regrouped = lax.all_to_all(observed, "tile", split_axis=2, concat_axis=0, tiled=True)
    flat_obs = regrouped.reshape(CAMS, LIGHTS, rows * cols)
    first_terms = assemble(flat_obs, weights, params, gains, lights, halves, views, echoes)
    for iteration in range(ITERS):
        if iteration == 0:
            surface_normal, right_side, lifted, energy = first_terms
        else:
            surface_normal, right_side, lifted, energy = assemble(
                flat_obs, weights, params, gains, lights, halves, views, echoes
            )
        params = params + solve_eight(surface_normal, right_side)
        gains = update_gains(gains, lifted, energy)
        grid = params.reshape(8, rows, cols)
        params = jnp.concatenate([smooth_tilts(grid[:2]), grid[2:]], axis=0).reshape(8, -1)
    return (params.reshape(8, rows, cols), gains)


def solution(mesh):
    return jax.shard_map(
        on_device,
        mesh=mesh,
        in_specs=(P("tile", "grp", None), P("grp", "tile"), P(None, "grp", "tile"), P(), P(), P()),
        out_specs=(P(None, "grp", "tile"), P()),
        check_vma=False,
    )
```

profile of v0, /device:TPU:1, one launch (start us, length us, event | category | flops | bytes accessed | tf_op | source)
XLA Modules:
  0.0 603.4 jit_solution(8106772559715947173)
XLA Ops:
  0.6 6.7 %copy.16 = bf16[64,8,2048]{0,1,2:T(8,128)(2,1)} copy(bf16[64,8,2048]{2,1,0:T(8,128)(2,1)} %param.12) | data formatting | bytes 4194304 | tf_op args[0]
  7.3 7.6 %reshape.750 = bf16[8,2,65536]{2,1,0:T(2,128)(2,1)} reshape(bf16[2048,8,64]{2,1,0:T(8,128)(2,1)} %bitcast.458) | data formatting | bytes 4194304
  14.9 6.5 %all-to-all-start = ((bf16[8,2,65536]{2,1,0:T(2,128)(2,1)}), bf16[8,2,65536]{2,1,0:T(2,128)(2,1)S(1)}, u32[]{:S(2)}, u32[]{:S(2)}) async-start(bf16[8,2,65536]{2,1,0:T(2,128)(2,1)} %reshape.750), calls=%async_computation | async-start | bytes 4194304 | tf_op jit(solution)/shard_map/all_to_all | solution.py:179
  23.0 46.7 %all-to-all-done = bf16[8,2,65536]{2,1,0:T(2,128)(2,1)S(1)} async-done(((bf16[8,2,65536]{2,1,0:T(2,128)(2,1)}), bf16[8,2,65536]{2,1,0:T(2,128)(2,1)S(1)}, u32[]{:S(2)}, u32[]{:S(2)}) %all-to-all-start) | async-done | bytes 2097184 | tf_op jit(solution)/shard_map/all_to_all | solution.py:179
  69.6 5.0 reshape.751
  74.6 5.0 copy.17
  82.1 201.9 %while.40 = (s32[]{:T(128)}, f32[36,2048]{1,0:T(8,128)S(1)}, f32[8,2048]{1,0:T(8,128)S(1)}, f32[32]{0:T(128)S(1)}, f32[32]{0:T(128)S(1)}, /*index=5*/f32[16,2048...) while((s32[]{:T(128)}, f32[36,2048]{1,0:T(8,128)S(1)}, ...), condition=%wide.region_51.52_spmd.clone, body=%wide.region_5.51_spmd.clone.sunk | while | flops 14035169 | bytes 4423358 | solution.py:115
  83.4 2.4 multiply_multiply_fusion.36
  96.0 2.4 multiply_multiply_fusion.36
  108.6 2.4 multiply_multiply_fusion.36
  121.2 2.4 multiply_multiply_fusion.36
  133.8 2.4 multiply_multiply_fusion.36
  146.4 2.4 multiply_multiply_fusion.36
  159.1 2.4 multiply_multiply_fusion.36
  171.7 2.4 multiply_multiply_fusion.36
  184.3 2.4 multiply_multiply_fusion.36
  196.9 2.4 multiply_multiply_fusion.36
  209.5 2.4 multiply_multiply_fusion.36
  222.1 2.4 multiply_multiply_fusion.36
  234.8 2.4 multiply_multiply_fusion.36
  247.4 2.4 multiply_multiply_fusion.36
  260.0 2.4 multiply_multiply_fusion.36
  272.6 2.4 multiply_multiply_fusion.36
  285.7 3.1 collective-permute-start
  290.1 38.7 %psum.14 = f32[2,32]{1,0:T(2,128)S(1)} all-reduce(f32[2,32]{1,0:T(2,128)S(1)} %pad_maximum_fusion.10), channel_id=1, replica_groups=mesh['grp'=4,'tile'=8] {'grp','tile'}, use_global_device_ids=true, to_apply=%region_52.53 | all-reduce | flops 64 | bytes 512 | tf_op jit(solution)/shard_map/psum | solution.py:165
  329.6 5.9 collective-permute-start.2
  337.6 2.9 collective-permute-done.3
  340.8 203.1 %while.41 = (s32[]{:T(128)}, f32[36,2048]{1,0:T(8,128)S(1)}, f32[8,2048]{1,0:T(8,128)S(1)}, f32[32]{0:T(128)S(1)}, f32[32]{0:T(128)S(1)}, /*index=5*/f32[16,2048...) while((s32[]{:T(128)}, f32[36,2048]{1,0:T(8,128)S(1)}, ...), condition=%wide.region_100.101_spmd.clone, body=%wide.region_54.100_spmd.clone.sunk | while | flops 14035169 | bytes 4423358 | solution.py:115
  342.1 2.4 multiply_multiply_fusion.38
  354.8 2.4 multiply_multiply_fusion.38
  367.5 2.4 multiply_multiply_fusion.38
  380.2 2.4 multiply_multiply_fusion.38
  392.9 2.4 multiply_multiply_fusion.38
  405.6 2.4 multiply_multiply_fusion.38
  418.3 2.4 multiply_multiply_fusion.38
  431.0 2.4 multiply_multiply_fusion.38
  443.7 2.4 multiply_multiply_fusion.38
  456.4 2.4 multiply_multiply_fusion.38
  469.1 2.4 multiply_multiply_fusion.38
  481.7 2.4 multiply_multiply_fusion.38
  494.4 2.4 multiply_multiply_fusion.38
  519.8 2.4 multiply_multiply_fusion.38
  532.5 2.4 multiply_multiply_fusion.38
  543.9 38.4 %psum.15 = f32[2,32]{1,0:T(2,128)S(1)} all-reduce(f32[2,32]{1,0:T(2,128)S(1)} %pad_maximum_fusion.11), channel_id=1, replica_groups=mesh['grp'=4,'tile'=8] {'grp','tile'}, use_global_device_ids=true, to_apply=%region_101.102 | all-reduce | flops 64 | bytes 512 | tf_op jit(solution)/shard_map/psum | solution.py:165
  584.1 3.2 collective-permute-start.4
  589.1 2.5 collective-permute-done.5
  591.7 5.8 collective-permute-start.6
  599.5 3.1 collective-permute-done.7
  (827 shorter events, 340.7 us)
Async XLA Ops:
  14.9 6.6 %copy-start.3 = (f32[3,16]{1,0:T(4,128)S(1)}, f32[3,16]{1,0:T(4,128)}, u32[]{:S(2)}) copy-start(f32[3,16]{1,0:T(4,128)} %param.16) | copy-start | bytes 580
  14.9 6.6 %copy-start.5 = (f32[3]{0:T(128)S(1)}, f32[3]{0:T(128)}, u32[]{:S(2)}) copy-start(f32[3]{0:T(128)} %constant.128.clone) | copy-start | bytes 40
  14.9 6.9 %copy-start.4 = (f32[3,32]{1,0:T(4,128)S(1)}, f32[3,32]{1,0:T(4,128)}, u32[]{:S(2)}) copy-start(f32[3,32]{1,0:T(4,128)} %param.15) | copy-start | bytes 1156
  14.9 7.2 %copy-start.1 = (f32[8,8,256]{2,1,0:T(8,128)S(1)}, f32[8,8,256]{2,1,0:T(8,128)}, u32[]{:S(2)}) copy-start(f32[8,8,256]{2,1,0:T(8,128)} %param.14) | copy-start | bytes 196612
  14.9 7.3 %copy-start.2 = (s32[8,256]{1,0:T(8,128)S(1)}, s32[8,256]{1,0:T(8,128)}, u32[]{:S(2)}) copy-start(s32[8,256]{1,0:T(8,128)} %param.13) | copy-start | bytes 24580
  14.9 7.3 %copy-start = (f32[32]{0:T(128)S(1)}, f32[32]{0:T(128)}, u32[]{:S(2)}) copy-start(f32[32]{0:T(128)} %param.17) | copy-start | bytes 388
  14.9 54.7 %all-to-all-start = ((bf16[8,2,65536]{2,1,0:T(2,128)(2,1)}), bf16[8,2,65536]{2,1,0:T(2,128)(2,1)S(1)}, u32[]{:S(2)}, u32[]{:S(2)}) async-start(bf16[8,2,65536]{2,1,0:T(2,128)(2,1)} %reshape.750), calls=%async_computation | async-start | bytes 4194304 | tf_op jit(solution)/shard_map/all_to_all | solution.py:179
  285.7 43.8 %collective-permute-start = (f32[2,1,256]{2,1,0:T(1,128)S(1)}, f32[2,1,256]{2,1,0:T(1,128)S(1)}, u32[]{:S(2)}, u32[]{:S(2)}) collective-permute-start(f32[2,1,256]{2,1,0:T(1,128)S(1)} %get-tuple-element.1093), channel_id=1, source_target_pairs={{0,8},{8,16},{16,24},{1,9},{9,17},{17,25},{2,10},{10,18},{18,26},{... | collective-permute-start | bytes 6152 | tf_op jit(solution)/shard_map/ppermute | solution.py:23
  288.8 40.7 %collective-permute-start.1 = (f32[2,1,256]{2,1,0:T(1,128)S(1)}, f32[2,1,256]{2,1,0:T(1,128)S(1)}, u32[]{:S(2)}, u32[]{:S(2)}) collective-permute-start(f32[2,1,256]{2,1,0:T(1,128)S(1)} %get-tuple-element.1094), channel_id=1, source_target_pairs={{8,0},{16,8},{24,16},{9,1},{17,9},{25,17},{10,2},{18,10},{26,18},{... | collective-permute-start | bytes 6152 | tf_op jit(solution)/shard_map/ppermute | solution.py:25
  329.6 8.0 %collective-permute-start.2 = (f32[2,10,1]{2,1,0:T(8,128)S(1)}, f32[2,10,1]{2,1,0:T(8,128)S(1)}, u32[]{:S(2)}, u32[]{:S(2)}) collective-permute-start(f32[2,10,1]{2,1,0:T(8,128)S(1)} %get-tuple-element.1081), channel_id=1, source_target_pairs={{0,1},{1,2},{2,3},{3,4},{4,5},{5,6},{6,7},{8,9},{9,10},{10,11},{11... | collective-permute-start | bytes 248 | tf_op jit(solution)/shard_map/ppermute | solution.py:23
  335.5 5.1 collective-permute-start.3
  584.1 5.1 collective-permute-start.4
  587.2 4.3 collective-permute-start.5
  591.7 7.8 %collective-permute-start.6 = (f32[2,10,1]{2,1,0:T(8,128)S(1)}, f32[2,10,1]{2,1,0:T(8,128)S(1)}, u32[]{:S(2)}, u32[]{:S(2)}) collective-permute-start(f32[2,10,1]{2,1,0:T(8,128)S(1)} %get-tuple-element.1079), channel_id=1, source_target_pairs={{0,1},{1,2},{2,3},{3,4},{4,5},{5,6},{6,7},{8,9},{9,10},{10,11},{11... | collective-permute-start | bytes 248 | tf_op jit(solution)/shard_map/ppermute | solution.py:23
  597.5 5.1 collective-permute-start.7
where the time goes:
time: 608 us; the launch traced here: 603 us
  other arithmetic  366 us (60%)
  blocking collectives  77.1 us (13%)
  local copies, waits for them, and re-layouts  67.8 us (11%)
  waiting for transfers between devices  55.2 us (9%)
  starting transfers between devices  31.1 us (5%)
    mul x32, other arithmetic, camera_terms(): 2.0 * rim_gain * back * view_v  78.1 us
    psum x2, blocking collectives, update_gains(): totals = lax.psum(jnp.stack([lifted, energy]), ('grp', 'tile'))  77.1 us
    reduce_sum x98, other arithmetic, camera_terms(): surface_normal.append(weight_c * jnp.sum(scaled[i] * scaled[j], axis=0))  61.1 us
    mul x32, other arithmetic, camera_terms(): rim_shape = back * back  57.2 us
    all_to_all x1, waiting for transfers between devices, on_device(): lax.all_to_all(observed, 'tile', split_axis=2, concat_axis=0, tiled=True)  46.7 us
    reduce_sum x32, other arithmetic, camera_terms(): lifted = jnp.sum(weight_c * shaped * resid, axis=1)  46.1 us
    mul x32, other arithmetic, camera_terms(): right_side = [weight_c * jnp.sum(piece * resid, axis=0) for piece in scaled]  43.2 us
    reduce_sum x32, other arithmetic, camera_terms(): right_side = [weight_c * jnp.sum(piece * resid, axis=0) for piece in scaled]  41.6 us
  transfers between devices with their start and end apart: 9, of which 4 were waited for; matrix products, arithmetic and copies ran while one was open for 0% of the time, Pallas kernels for 0%

commit v1 on v0

v1 whole, which is shorter than its diff:
```python
import functools

import jax
import jax.numpy as jnp
from jax import lax
from jax.experimental import pallas as pl
from jax.experimental.pallas import tpu as pltpu
from jax.sharding import PartitionSpec as P

CAMS = 16
LIGHTS = 32
ITERS = 2

damping = 4.0
lift_z = 1.6
hidden = 1024.0
f32 = jnp.float32
bf16 = jnp.bfloat16
LANES = 128
VMEM_BYTES = 40 * 1024 * 1024
LINEAR = (2, 3, 5, 6, 7)
ENTRIES = [(i, j) for i in range(8) for j in range(i, 8)]


def unit_columns(raw):
    lifted = raw + jnp.array([0.0, 0.0, lift_z], f32)[:, None]
    return lifted / jnp.sqrt(jnp.sum(lifted * lifted, axis=0, keepdims=True))


def geometry(light_directions, view_dirs):
    lights = unit_columns(light_directions)
    views = unit_columns(view_dirs)
    raw_half = views[:, :, None] + lights[:, None, :]
    halves = raw_half / jnp.sqrt(jnp.sum(raw_half * raw_half, axis=0, keepdims=True))
    echoes = jnp.sum(views[:, :, None] * lights[:, None, :], axis=0)
    return lights, views, halves.reshape(3, -1), echoes.reshape(1, -1)


def thirds(x):
    first = lax.reduce_precision(x, 8, 7)
    rest = x - first
    second = lax.reduce_precision(rest, 8, 7)
    return first, second, rest - second


def split_value(x, count):
    pieces = []
    for _ in range(count - 1):
        head = x.astype(bf16).astype(f32)
        pieces.append(head)
        x = x - head
    pieces.append(x)
    return pieces


def split_pair(x):
    head = x.astype(bf16)
    return head, (x - head.astype(f32)).astype(bf16)


def dot(a, b):
    return jnp.dot(a, b, preferred_element_type=f32)


def total(terms):
    terms = list(terms)
    out = terms[0]
    for t in terms[1:]:
        out = out + t
    return out


def inner(a, b):
    return total(x * y for x, y in zip(a, b))


def texel_forms(p):
    tu, tv, diffuse, spec, raw, ambient, rim, retro = p
    q = 1.0 / jnp.sqrt(1.0 + tu * tu + tv * tv)
    nx, ny, nz = tu * q, tv * q, q
    side = -(nx * ny) * q
    by_u = ((1.0 - nx * nx) * q, side, -(nz * nx) * q)
    by_v = (side, (1.0 - ny * ny) * q, -(nz * ny) * q)
    sigma = 1.0 / (1.0 + jnp.exp(-raw))
    sharp = 1.0 + 20.0 * sigma
    slope = 20.0 * sigma * (1.0 - sigma)
    return (nx, ny, nz), by_u, by_v, sharp, slope


def seen(mask, c):
    return jnp.bitwise_and(jnp.right_shift(mask, c), 1).astype(f32)


def put_slab(ref, k, value):
    rows, cols = value.shape
    for h in range(cols // LANES):
        ref[h, k * rows : (k + 1) * rows, :] = value[:, h * LANES : (h + 1) * LANES]


def get_slab(ref, k, rows):
    return jnp.concatenate([ref[h, k * rows : (k + 1) * rows, :] for h in range(ref.shape[0])], axis=1)


def get_rows(ref, start, count, stride):
    return jnp.concatenate([ref[h, pl.ds(start, count, stride=stride), :] for h in range(ref.shape[0])], axis=1)


def put_rows(ref, start, stride, value):
    count, cols = value.shape
    for h in range(cols // LANES):
        ref[h, pl.ds(start, count, stride=stride), :] = value[:, h * LANES : (h + 1) * LANES]


def put_lobe_rows(slab, normal, sharp):
    base = [sharp * normal[0], sharp * normal[1], sharp * normal[2], -sharp]
    parts = [split_value(x, 3) for x in base]
    row = 0
    for which in (0, 1, 0, 2, 1, 0):
        for part in parts:
            slab(row, part[which])
            row += 1
    return row


def normal_kernel(
    cam_ref, par_ref, vis_ref, gain_ref, lobe_ref, mixed_ref, square_ref, out_ref,
    rows_ref, sums_ref, mixed_scr, square_scr,
):
    rows, cols = par_ref.shape[1], par_ref.shape[2]
    depth = lobe_ref.shape[1]
    chunk = 4 * LIGHTS
    chunks = CAMS // 4

    gain2 = gain_ref[...] * gain_ref[...]
    for src, dst in ((mixed_ref, mixed_scr), (square_ref, square_scr)):
        head, tail = split_pair(src[...] * gain2)
        count = src.shape[0]
        dst[0:count, :] = head
        dst[count : 2 * count, :] = tail

    def slab(k, value):
        put_slab(rows_ref, k, value)

    p = [par_ref[i] for i in range(8)]
    normal, _, _, sharp, _ = texel_forms(p)
    used = put_lobe_rows(slab, normal, sharp)
    mask = vis_ref[...]
    for c in range(CAMS):
        slab(used + c, (seen(mask, c) - 1.0) * hidden)
    for k in range(used + CAMS, depth):
        slab(k, jnp.zeros((rows, cols), f32))

    def one_row(r, carry):
        texel = get_rows(rows_ref, r, depth, rows).astype(bf16)
        mixed = jnp.zeros((16, cols), f32)
        square = jnp.zeros((16, cols), f32)
        for ch in range(chunks):
            at = slice(ch * chunk, (ch + 1) * chunk)
            lobe = jnp.exp(dot(lobe_ref[at, :], texel))
            head, tail = split_pair(lobe)
            both = dot(mixed_scr[:, at], head)
            got = both[0:32] + both[32:64] + dot(mixed_scr[0:32, at], tail)
            mixed = mixed + got[0:16]
            put_rows(sums_ref, (32 + 16 * ch) * rows + r, rows, got[16:32])
            head, tail = split_pair(lobe * lobe)
            both = dot(square_scr[:, at], head)
            square = square + both[0:16] + both[16:32] + dot(square_scr[0:16, at], tail)
        put_rows(sums_ref, r, rows, mixed)
        put_rows(sums_ref, 16 * rows + r, rows, square)
        return carry

    lax.fori_loop(0, rows, one_row, 0)

    def one_part(h, carry):
        at = pl.ds(pl.multiple_of(h * LANES, LANES), LANES)

        def sums(k):
            return sums_ref[h, k * rows : (k + 1) * rows, :]

        p = [par_ref[i, :, at] for i in range(8)]
        mask = vis_ref[:, at]
        normal, by_u, by_v, sharp, slope = texel_forms(p)
        diffuse, spec, rim = p[2], p[3], p[6]
        zero = jnp.zeros((rows, LANES), f32)
        gam = {i: zero for i in (0, 1, 5, 6)}
        own = {(i, j): zero for i in (0, 1, 5, 6) for j in (0, 1, 5, 6) if i <= j and j != 5 and i != 5}
        lit = {i: zero for i in (0, 1, 5, 6)}
        grid = {(i, k): zero for i in (0, 1, 5, 6) for k in range(4)}
        echo_sq = zero
        view_sum = [zero, zero, zero]
        for c in range(CAMS):
            w = seen(mask, c)
            v = [cam_ref[i, c] for i in range(3)]
            back = 1.0 - inner(v, normal)
            turn = (-2.0 * rim) * back
            shape = {0: turn * inner(v, by_u), 1: turn * inner(v, by_v), 6: back * back}
            weighted = {i: w * shape[i] for i in shape}
            weighted[5] = w
            for i in gam:
                gam[i] = gam[i] + weighted[i]
                lit[i] = lit[i] + weighted[i] * cam_ref[4, c]
            for i, j in own:
                own[i, j] = own[i, j] + weighted[i] * shape[j]
            echo_sq = echo_sq + w * cam_ref[3, c]
            view_sum = [s + w * x for s, x in zip(view_sum, v)]
            for k in range(4):
                peak = sums(32 + 4 * c + k)
                for i in (0, 1, 6):
                    grid[i, k] = grid[i, k] + shape[i] * peak
                grid[5, k] = grid[5, k] + peak
        own[5, 5] = gam[5]
        for i in (0, 1):
            own[i, 5] = gam[i]
        own[5, 6] = gam[6]

        def gram(i, j):
            return cam_ref[5, 4 * i + j]

        entries = {ij: None for ij in ENTRIES}

        def add(i, j, value):
            ij = (min(i, j), max(i, j))
            entries[ij] = value if entries[ij] is None else entries[ij] + value

        def cross(i, j, value):
            add(i, j, value + value if i == j else value)

        flat = {0: [diffuse * x for x in by_u], 1: [diffuse * x for x in by_v], 2: list(normal)}
        edge = spec * sharp
        tilt = spec * slope
        glow = {
            0: {1 + k: edge * by_u[k] for k in range(3)},
            1: {1 + k: edge * by_v[k] for k in range(3)},
            3: {0: None},
            4: {0: -tilt, 1: tilt * normal[0], 2: tilt * normal[1], 3: tilt * normal[2]},
        }

        def combine(coefs, values):
            return total(values[k] if x is None else x * values[k] for k, x in coefs.items())

        count = gam[5]
        spread = {i: [total(gram(r, k) * flat[i][k] for k in range(3)) for r in range(3)] for i in flat}
        reach = {i: total(gram(3, k) * flat[i][k] for k in range(3)) for i in flat}
        view_spread = [total(gram(r, k) * view_sum[k] for k in range(3)) for r in range(3)]
        for i in flat:
            for j in flat:
                if i <= j:
                    add(i, j, count * inner(flat[j], spread[i]))
            for j in gam:
                cross(i, j, reach[i] * gam[j])
            cross(i, 7, inner(flat[i], view_spread))
        for i, j in own:
            add(i, j, gram(3, 3) * own[i, j])
        for i in lit:
            cross(i, 7, lit[i])
        add(7, 7, echo_sq)
        for j in glow:
            for i in flat:
                cross(i, j, total(flat[i][x] * combine(glow[j], {k: sums(4 * k + x) for k in glow[j]}) for x in range(3)))
            for i in gam:
                cross(i, j, combine(glow[j], {k: grid[i, k] for k in glow[j]}))
            cross(j, 7, combine(glow[j], {k: sums(4 * k + 3) for k in glow[j]}))
        packed = {}
        where = 0
        for i in range(4):
            for j in range(i, 4):
                packed[i, j] = packed[j, i] = where
                where += 1
        for i in glow:
            for j in glow:
                if i <= j:
                    half = {k: combine(glow[j], {x: sums(16 + packed[k, x]) for x in glow[j]}) for k in glow[i]}
                    add(i, j, combine(glow[i], half))

        def entry(i, j):
            return entries[min(i, j), max(i, j)]

        for i in range(8):
            out_ref[36 + i, :, at] = total(entry(i, j) * p[j] for j in LINEAR)
        lower = {}
        for j in range(8):
            accum = entries[j, j] + damping
            for k in range(j):
                accum = accum - lower[j, k] * lower[j, k]
            inverse = lax.rsqrt(accum)
            lower[j, j] = inverse
            for i in range(j + 1, 8):
                accum = entries[j, i]
                for k in range(j):
                    accum = accum - lower[i, k] * lower[j, k]
                lower[i, j] = accum * inverse
        for where, (i, j) in enumerate(ENTRIES):
            out_ref[where, :, at] = lower[j, i]
        return carry

    lax.fori_loop(0, cols // LANES, one_part, 0)


def sample_kernel(
    place_ref, cam_ref, own_ref, got_ref, gain_ref, lobe_ref, shade_ref, plain_ref, peak_ref, *refs, parts
):
    par_refs, vis_refs = refs[:parts], refs[parts : 2 * parts]
    out_refs = refs[2 * parts : 3 * parts]
    light_ref = refs[3 * parts]
    par_scr, vis_scr, obs_scr, rows_ref, sums_ref, light_scr = refs[3 * parts + 1 :]
    step = pl.program_id(0)
    samples, rows, cols = own_ref.shape
    held = 2 * samples
    cams = held // LIGHTS
    for s in range(parts):

        @pl.when(step == s)
        def _():
            par_scr[...] = par_refs[s][0:8]
            vis_scr[...] = vis_refs[s][...]

    core = place_ref[parts]
    mine = pl.multiple_of(core * (samples * rows), rows)
    theirs = pl.multiple_of((1 - core) * (samples * rows), rows)
    for h in range(cols // LANES):
        lanes = slice(h * LANES, (h + 1) * LANES)
        for src, at in ((own_ref, mine), (got_ref, theirs)):
            obs_scr[h, pl.ds(at, samples * rows), :] = src[:, :, lanes].astype(f32).reshape(samples * rows, LANES)

    def slab(k, value):
        put_slab(rows_ref, k, value)

    p = [par_scr[i] for i in range(8)]
    mask = vis_scr[...]
    normal, by_u, by_v, sharp, slope = texel_forms(p)
    base = cam_ref[3, 0].astype(jnp.int32)
    used = put_lobe_rows(slab, normal, sharp)
    weights = [seen(mask, base + c) for c in range(cams)]
    for c in range(cams):
        slab(used + c, (weights[c] - 1.0) * hidden)
        slab(65 + c, weights[c])
    for k in range(used + cams, 32):
        slab(k, jnp.zeros((rows, cols), f32))
    shade = [p[2] * normal[0], p[2] * normal[1], p[2] * normal[2], p[5], p[7]]
    pieces = [split_value(x, 2) for x in shade]
    at = 32
    for which in (0, 1, 0):
        for piece in pieces:
            slab(at, piece[which])
            at += 1
    for c in range(cams):
        back = 1.0 - inner([cam_ref[i, c] for i in range(3)], normal)
        head, tail = split_value(p[6] * (back * back), 2)
        slab(at + c, head)
        slab(at + cams + c, tail)
    for k in range(at + 2 * cams, 64):
        slab(k, jnp.zeros((rows, cols), f32))
    slab(64, p[3])

    gains = gain_ref[...]
    plain = jnp.concatenate(split_value(plain_ref[...] * gains, 2), axis=0).astype(bf16)
    peak = jnp.concatenate(split_value(peak_ref[...] * gains, 2), axis=0).astype(bf16)
    count = plain_ref.shape[0]

    def fold(x):
        return total(x[:, k * LANES : (k + 1) * LANES] for k in range(cols // LANES))

    def one_row(r, carry):
        lift, energy = carry
        lobe = jnp.exp(dot(lobe_ref[...], get_rows(rows_ref, r, 32, rows).astype(bf16)))
        shade = dot(shade_ref[...], get_rows(rows_ref, 32 * rows + r, 32, rows).astype(bf16))
        misc = get_rows(rows_ref, 64 * rows + r, 8, rows)
        obs = get_rows(obs_scr, r, held, rows)
        for c in range(cams):
            part = slice(c * LIGHTS, (c + 1) * LIGHTS)
            full = shade[part] + misc[0:1] * lobe[part]
            kept = full * misc[1 + c : 2 + c]
            lift = lift + fold(kept * obs[part])
            energy = energy + fold(kept * full)
        head, tail = split_pair(obs * lobe)
        both = dot(plain, obs.astype(bf16))
        put_rows(sums_ref, r, rows, both[0:count] + both[count : 2 * count])
        both = dot(peak, head)
        put_rows(sums_ref, count * rows + r, rows, both[0:8] + both[8:16] + dot(peak[0:8], tail))
        return lift, energy

    zero = jnp.zeros((LIGHTS, LANES), f32)
    lift, energy = lax.fori_loop(0, rows, one_row, (zero, zero))

    @pl.when(step == 0)
    def _():
        light_scr[0:LIGHTS, :] = lift
        light_scr[LIGHTS : 2 * LIGHTS, :] = energy

    @pl.when(step != 0)
    def _():
        light_scr[0:LIGHTS, :] = light_scr[0:LIGHTS, :] + lift
        light_scr[LIGHTS : 2 * LIGHTS, :] = light_scr[LIGHTS : 2 * LIGHTS, :] + energy

    @pl.when(step == parts - 1)
    def _():
        light_ref[...] = lax.dot_general(
            jnp.ones((8, LANES), f32),
            light_scr[...],
            (((1,), (1,)), ((), ())),
            precision=lax.Precision.HIGHEST,
            preferred_element_type=f32,
        )

    def sums(k):
        return get_slab(sums_ref, k, rows)

    flat = [None, None, None]
    lone, rim_sum, echo_sum, turn_u, turn_v = None, None, None, None, None

    def grow(old, new):
        return new if old is None else old + new

    for c in range(cams):
        v = [cam_ref[i, c] for i in range(3)]
        w = weights[c]
        one = w * sums(4 * c)
        lit = [w * sums(4 * c + 1 + x) for x in range(3)]
        back = 1.0 - inner(v, normal)
        bent = back * one
        lone = grow(lone, one)
        rim_sum = grow(rim_sum, back * bent)
        turn_u = grow(turn_u, bent * inner(v, by_u))
        turn_v = grow(turn_v, bent * inner(v, by_v))
        echo_sum = grow(echo_sum, inner(v, lit))
        flat = [grow(f, x) for f, x in zip(flat, lit)]
    spot = sums(count)
    spots = [sums(count + 1 + x) for x in range(3)]
    edge = p[3] * sharp
    twice = -2.0 * p[6]
    right = [
        p[2] * inner(by_u, flat) + edge * inner(by_u, spots) + twice * turn_u,
        p[2] * inner(by_v, flat) + edge * inner(by_v, spots) + twice * turn_v,
        inner(normal, flat),
        spot,
        p[3] * slope * (inner(normal, spots) - spot),
        lone,
        rim_sum,
        echo_sum,
    ]
    for s in range(parts):

        @pl.when(step == s)
        def _():
            for i in range(8):
                out_refs[s][i] = right[i]


def solve_kernel(low_ref, par_ref, *refs):
    right_refs, out_ref = refs[:-1], refs[-1]
    lower = {}
    for where, (i, j) in enumerate(ENTRIES):
        lower[j, i] = low_ref[where]
    right = [total(ref[i] for ref in right_refs) - low_ref[36 + i] for i in range(8)]
    forward = []
    for i in range(8):
        accum = right[i]
        for k in range(i):
            accum = accum - lower[i, k] * forward[k]
        forward.append(accum * lower[i, i])
    answer = [None] * 8
    for i in range(7, -1, -1):
        accum = forward[i]
        for k in range(i + 1, 8):
            accum = accum - lower[k, i] * answer[k]
        answer[i] = accum * lower[i, i]
    for i in range(8):
        out_ref[i] = par_ref[i] + answer[i]


def smem():
    return pl.BlockSpec(memory_space=pltpu.SMEM)


def vmem():
    return pl.BlockSpec(memory_space=pltpu.VMEM)


def params_of():
    return pltpu.CompilerParams(vmem_limit_bytes=VMEM_BYTES)


def normal_call(cam_table, par, vis, gain_row, tables):
    _, rows, cols = par.shape
    depth = tables["lobe"].shape[1]
    return pl.pallas_call(
        normal_kernel,
        name="normal_factor",
        out_shape=jax.ShapeDtypeStruct((44, rows, cols), f32),
        in_specs=[smem()] + [vmem()] * 6,
        out_specs=vmem(),
        scratch_shapes=[
            pltpu.VMEM((cols // LANES, depth * rows, LANES), f32),
            pltpu.VMEM((cols // LANES, 96 * rows, LANES), f32),
            pltpu.VMEM((64, CAMS * LIGHTS), bf16),
            pltpu.VMEM((32, CAMS * LIGHTS), bf16),
        ],
        compiler_params=params_of(),
    )(cam_table, par, vis, gain_row, tables["lobe"], tables["mixed"], tables["square"])


def sample_call(place, cam_table, own, got, gain_row, tables, pars, vises):
    parts = len(pars)
    samples, rows, _ = own.shape
    cols = pars[0].shape[2]
    held = 2 * samples
    whole2 = lambda s, place: (0, 0)
    whole3 = lambda s, place: (0, 0, 0)

    def full(x):
        return pl.BlockSpec(x.shape, whole2 if x.ndim == 2 else whole3)

    outs = [jax.ShapeDtypeStruct((8, rows, cols), f32) for _ in range(parts)]
    outs.append(jax.ShapeDtypeStruct((8, 2 * LIGHTS), f32))
    small = [gain_row, tables["lobe_here"], tables["shade"], tables["plain"], tables["peak"]]
    return pl.pallas_call(
        functools.partial(sample_kernel, parts=parts),
        name="sample_sums",
        out_shape=outs,
        grid_spec=pltpu.PrefetchScalarGridSpec(
            num_scalar_prefetch=1,
            grid=(parts,),
            in_specs=[
                smem(),
                pl.BlockSpec((samples, rows, cols), lambda s, place: (0, 0, place[s])),
                pl.BlockSpec((samples, rows, cols), lambda s, place: (0, 0, place[s] // 2)),
            ]
            + [full(x) for x in small]
            + [full(x) for x in pars]
            + [full(x) for x in vises],
            out_specs=[full(x) for x in outs],
            scratch_shapes=[
                pltpu.VMEM((8, rows, cols), f32),
                pltpu.VMEM((rows, cols), jnp.int32),
                pltpu.VMEM((cols // LANES, held * rows, LANES), f32),
                pltpu.VMEM((cols // LANES, 72 * rows, LANES), f32),
                pltpu.VMEM((cols // LANES, 32 * rows, LANES), f32),
                pltpu.VMEM((2 * LIGHTS, LANES), f32),
            ],
        ),
        compiler_params=params_of(),
    )(place, cam_table, own, got, *small, *pars, *vises)


def solve_call(low, par, rights):
    return pl.pallas_call(
        solve_kernel,
        name="solve",
        out_shape=jax.ShapeDtypeStruct((8,) + par.shape[1:], f32),
        in_specs=[vmem()] * (2 + len(rights)),
        out_specs=vmem(),
        compiler_params=params_of(),
    )(low, par, *rights)


def shared_tables(lights, views, halves, echoes, first, held):
    samples = halves.shape[1]
    tiled = jnp.tile(lights, (1, CAMS))
    ones = jnp.ones((1, samples), f32)
    high = jnp.concatenate([ones, halves], axis=0)
    lobe = thirds(jnp.concatenate([halves, ones], axis=0))
    lobe = jnp.concatenate([lobe[k] for k in (0, 0, 1, 0, 1, 2)], axis=0)
    cam = jnp.arange(samples, dtype=jnp.int32)[None] // LIGHTS
    one_hot = (cam == jnp.arange(CAMS, dtype=jnp.int32)[:, None]).astype(f32)
    pad = jnp.zeros((8, samples), f32)
    mixed = [high[i : i + 1] * low for i in range(4) for low in (tiled[0:1], tiled[1:2], tiled[2:3], echoes)]
    quads = (cam % 4 == jnp.arange(4, dtype=jnp.int32)[:, None]).astype(f32)
    peaks = [quads[c : c + 1] * high for c in range(4)]
    square = [high[i : i + 1] * high[j : j + 1] for i in range(4) for j in range(i, 4)]

    def here(x):
        return lax.dynamic_slice_in_dim(x, first, held, axis=1)

    cams = held // LIGHTS
    local = one_hot[:cams, :held]
    shade = thirds(jnp.concatenate([tiled, ones, echoes], axis=0))
    shade = here(jnp.concatenate([shade[0], shade[0], shade[1]], axis=0))
    near = jnp.concatenate([ones, tiled], axis=0)[:, :held]
    return {
        "lobe": jnp.concatenate([lobe, one_hot, pad], axis=0).T.astype(bf16),
        "mixed": jnp.concatenate(mixed + peaks, axis=0),
        "square": jnp.concatenate(square + [jnp.zeros((6, samples), f32)], axis=0),
        "lobe_here": jnp.concatenate([here(lobe), local, jnp.zeros((8 - cams, held), f32)], axis=0).T.astype(bf16),
        "shade": jnp.concatenate([shade, local, local, jnp.zeros((17 - 2 * cams, held), f32)], axis=0).T.astype(bf16),
        "plain": (local[:, None, :] * near[None]).reshape(4 * cams, held),
        "peak": jnp.concatenate([here(high), jnp.zeros((4, held), f32)], axis=0),
    }


def camera_table(views, lights, gains):
    near = jnp.concatenate([lights, jnp.ones((1, LIGHTS), f32)], axis=0)
    gram = jnp.sum(near[:, None] * near[None] * (gains * gains), axis=-1)
    spread = jnp.sum(gram[:3, :3, None] * views[None], axis=1)
    echo_sq = jnp.sum(spread * views, axis=0, keepdims=True)
    lit = jnp.sum(gram[:3, 3:4] * views, axis=0, keepdims=True)
    return jnp.concatenate([views, echo_sq, lit, gram.reshape(1, 16)], axis=0)


def shifted(x, by, nz):
    return lax.ppermute(x, "tile", [(2 * z + c, 2 * ((z + by) % nz) + c) for z in range(nz) for c in range(2)])


def padded_2(cells, sides, width):
    for axis, dim in sides:
        count = lax.axis_size(axis)
        ends = count - 1
        head = lax.slice_in_dim(cells, 0, width, axis=dim)
        tail = lax.slice_in_dim(cells, cells.shape[dim] - width, cells.shape[dim], axis=dim)
        cells = jnp.concatenate(
            [
                lax.ppermute(tail, axis, [(i, i + 1) for i in range(ends)]),
                cells,
                lax.ppermute(head, axis, [(i + 1, i) for i in range(ends)]),
            ],
            axis=dim,
        )
    return cells


def smooth_tilts(tilt):
    rows = tilt.shape[1]
    cols = tilt.shape[2]
    padded = padded_2(tilt, (("grp", 1), ("tile", 2)), 1)
    boxed = jnp.zeros(tilt.shape, f32)
    for i in range(3):
        for j in range(3):
            boxed = boxed + padded[:, i : i + rows, j : j + cols]
    return 0.5 * tilt + boxed * (0.5 / 9.0)


def summed_everywhere(x):
    for axis in ("tile", "grp"):
        size = lax.axis_size(axis)
        bit = 1
        while bit < size:
            x = x + lax.ppermute(x, axis, [(i, i ^ bit) for i in range(size)])
            bit *= 2
    return x


def on_device(observed, visible, params_start, light_directions, view_dirs, gains_start):
    samples, rows, _ = observed.shape
    cols = visible.shape[1]
    tiles = lax.axis_size("tile")
    nz = tiles // 2
    tile = lax.axis_index("tile")
    chip, core = tile // 2, tile % 2
    held = 2 * samples
    cams = held // LIGHTS

    split = observed.reshape(samples, rows, nz, 2, cols)
    send = lax.dynamic_index_in_dim(split, 1 - core, axis=3, keepdims=False).reshape(samples, rows, nz * cols)
    got = lax.ppermute(send, "tile", [(i, i ^ 1) for i in range(tiles)])
    first = jnp.concatenate([params_start, visible.astype(f32)[None]], axis=0)
    blocks = [first] + [shifted(first, s, nz) for s in range(1, nz)]
    vises = [b[8].astype(jnp.int32) for b in blocks]
    place = jnp.stack([2 * ((chip - s) % nz) + core for s in range(nz)] + [core]).astype(jnp.int32)

    lights, views, halves, echoes = geometry(light_directions, view_dirs)
    tables = shared_tables(lights, views, halves, echoes, chip * held, held)
    near_views = lax.dynamic_slice_in_dim(views, chip * cams, cams, axis=1)
    near_table = jnp.concatenate([near_views, jnp.full((1, cams), chip * cams, jnp.int32).astype(f32)], axis=0)

    params = params_start
    gains = gains_start
    for iteration in range(ITERS):
        row = jnp.tile(gains[None], (1, CAMS))
        low = normal_call(camera_table(views, lights, gains), params, visible, row, tables)
        *rights, light = sample_call(
            place, near_table, observed, got, row[:, :held], tables, blocks, vises
        )
        moved = [rights[0]] + [shifted(rights[s], -s, nz) for s in range(1, nz)]
        params = solve_call(low, params, moved)
        sums = summed_everywhere(light[0].reshape(2, LIGHTS))
        gains = gains + (sums[0] - gains * sums[1]) / (sums[1] + 1.0)
        params = jnp.concatenate([smooth_tilts(params[:2]), params[2:]], axis=0)
        if iteration + 1 < ITERS:
            blocks = [params] + [shifted(params, s, nz) for s in range(1, nz)]
    return params, gains


def solution(mesh):
    return jax.shard_map(
        on_device,
        mesh=mesh,
        in_specs=(P("tile", "grp", None), P("grp", "tile"), P(None, "grp", "tile"), P(), P(), P()),
        out_specs=(P(None, "grp", "tile"), P()),
        check_vma=False,
    )
```

time: 608 us -> 174 us (0.29)
  other arithmetic: 366 us -> 14.9 us
  blocking collectives: 77.1 us -> 0 us
  Pallas kernels: 0 us -> 44.4 us
  waiting for transfers between devices: 55.2 us -> 16.6 us
  local copies, waits for them, and re-layouts: 67.8 us -> 36.5 us
  starting transfers between devices: 31.1 us -> 58.4 us
    mul x192 -> x5, other arithmetic: 207 us -> 4.56 us  [the longest x2 1.35 us: shared_tables(): high[i:i + 1] * high[j:j + 1]]
    reduce_sum x163 -> x4, other arithmetic: 149 us -> 2.45 us  [the longest x1 0.83 us: camera_table(): gram = jnp.sum(near[:, None] * near[None] * (gains * gains), axis=-1)]
    psum x2 -> x0, blocking collectives: 77.1 us -> none  [update_gains(): totals = lax.psum(jnp.stack([lifted, energy]), ('grp', 'tile'))]
    all_to_all x1 -> x0, waiting for transfers between devices: 46.7 us -> none  [on_device(): lax.all_to_all(observed, 'tile', split_axis=2, concat_axis=0, tiled=True)]
    pallas_call x0 -> x6, Pallas kernels: none -> 44.4 us  [the longest x2 26.5 us: sample_call(): pl.pallas_call(functools.partial(sample_kernel, parts=parts), name='sampl...]
    ppermute x8 -> x31, starting transfers between devices: 24.6 us -> 58.4 us  [the longest x4 23.9 us: padded_2(): lax.ppermute(tail, axis, [(i, i + 1) for i in range(ends)])]
    another operation x66 -> x16, local copies, waits for them, and re-layouts: 19.3 us -> 4.3 us  [the longest x4 2.7 us: on_device(): row = jnp.tile(gains[None], (1, CAMS))]
    slice x36 -> x19, local copies, waits for them, and re-layouts: 18.5 us -> 5.81 us  [the longest x2 1.42 us: camera_table(): lit = jnp.sum(gram[:3, 3:4] * views, axis=0, keepdims=True)]
  transfers between devices with their start and end apart: 9 -> 31, of which waited for: 4 -> 10; matrix products, arithmetic and copies ran while one was open for 0% -> 20% of each run, Pallas kernels for 0% -> 10%
where the time goes in v1:
time: 174 us; the launch traced here: 172 us
  starting transfers between devices  58.4 us (34%)
  Pallas kernels  44.4 us (26%)
  local copies, waits for them, and re-layouts  36.5 us (21%)
  waiting for transfers between devices  16.6 us (10%)
  other arithmetic  14.9 us (9%)
    pallas_call x2, Pallas kernels, sample_call(): pl.pallas_call(functools.partial(sample_kernel, parts=parts), name='sampl...  26.5 us
    ppermute x4, starting transfers between devices, padded_2(): lax.ppermute(tail, axis, [(i, i + 1) for i in range(ends)])  23.9 us
    pallas_call x2, Pallas kernels, normal_call(): pl.pallas_call(normal_kernel, name='normal_factor', out_shape=jax.ShapeDt...  16.8 us
    ppermute x12, starting transfers between devices, shifted(): lax.ppermute(x, 'tile', [(2 * z + c, 2 * ((z + by) % nz) + c) for z in ra...  14.8 us
    unnamed x108, local copies, waits for them, and re-layouts  13.4 us
    ppermute x10, starting transfers between devices, summed_everywhere(): x = x + lax.ppermute(x, axis, [(i, i ^ bit) for i in range(size)])  11.9 us
    ppermute x10, waiting for transfers between devices, summed_everywhere(): x = x + lax.ppermute(x, axis, [(i, i ^ bit) for i in range(size)])  8.91 us
    ppermute x4, starting transfers between devices, padded_2(): lax.ppermute(head, axis, [(i + 1, i) for i in range(ends)])  6.43 us
  transfers between devices with their start and end apart: 31, of which 10 were waited for; matrix products, arithmetic and copies ran while one was open for 20% of the time, Pallas kernels for 10%

profile of v1, /device:TPU:1, one launch (start us, length us, event | category | flops | bytes accessed | tf_op | source)
XLA Modules:
  0.0 172.1 jit_solution(1571075704962605049)
XLA Ops:
  0.7 0.8 convert_convert_fusion
  2.4 2.1 %collective-permute-start.1 = (f32[9,8,256]{2,1,0:T(8,128)S(1)}, f32[9,8,256]{2,1,0:T(8,128)S(1)}, u32[]{:S(2)}, u32[]{:S(2)}) collective-permute-start(f32[9,8,256]{2,1,0:T(8,128)S(1)} %pad_maximum_fusion.refs_0_), channel_id=1, source_target_pairs={{0,2},{1,3},{2,4},{3,5},{4,6},{5,7},{6,0},{7,1},{8,10},{9,11},{10,... | collective-permute-start | bytes 221192 | tf_op jit(solution)/shard_map/ppermute | solution.py:600
  4.5 2.3 %collective-permute-start.2 = (f32[9,8,256]{2,1,0:T(8,128)S(1)}, f32[9,8,256]{2,1,0:T(8,128)S(1)}, u32[]{:S(2)}, u32[]{:S(2)}) collective-permute-start(f32[9,8,256]{2,1,0:T(8,128)S(1)} %pad_maximum_fusion.refs_0_), channel_id=1, source_target_pairs={{0,4},{1,5},{2,6},{3,7},{4,0},{5,1},{6,2},{7,3},{8,12},{9,13},{10,... | collective-permute-start | bytes 221192 | tf_op jit(solution)/shard_map/ppermute | solution.py:600
  6.8 1.1 collective-permute-start.3
  7.9 2.3 %constant_dynamic-slice_fusion = bf16[64,8,4,1,256]{4,1,3,2,0:T(8,128)(2,1)} fusion(bf16[64,8,4,2,256]{4,1,3,2,0:T(8,128)(2,1)} %bitcast.67, s32[]{:T(128)S(6)} %select_n.92), kind=kLoop, calls=%fused_computation.108 | loop fusion | bytes 2097156 | tf_op jit(solution)/shard_map/jit(dynamic_index_in_dim)/dynamic_slice | solution.py:652
  10.2 1.5 collective-permute-start
  20.5 1.3 fusion.50
  24.7 1.3 pad_multiply_fusion
  28.1 0.9 copy-done.3
  29.0 0.9 copy-done.5
  31.1 12.8 %sample_sums.2 = (f32[8,8,256]{2,1,0:T(8,128)S(1)}, f32[8,8,256]{2,1,0:T(8,128)S(1)}, f32[8,8,256]{2,1,0:T(8,128)S(1)}, f32[8,8,256]{2,1,0:T(8,128)S(1)}, f32[8,64]{1,0:T(8,128)S(1)}) custom-call(s32[5]{0:T(128)S(1)} %copy-done.27, f32[4,4]{1,0:T(4,128)S(1)} %concatenate.103.cam_ref, bf16[64,8,2048]{2,1,0:T(8,128)(2,1)S(1)} %copy-done, ...), custom_call_target="tpu_custom_call" | custom-call | tf_op jit(solution)/shard_map/sample_sums/pallas_call | solution.py:516
  45.9 1.2 concatenate.102
  48.5 1.1 collective-permute-done.5
  50.4 2.5 %collective-permute-done.6 = f32[2,32]{1,0:T(2,128)S(1)} collective-permute-done((f32[2,32]{1,0:T(2,128)S(1)}, f32[2,32]{1,0:T(2,128)S(1)}, u32[]{:S(2)}, u32[]{:S(2)}) %collective-permute-start.6) | collective-permute-done | bytes 288 | tf_op jit(solution)/shard_map/ppermute | solution.py:636
  52.9 1.2 collective-permute-start.7
  54.2 3.0 %concatenate.117.mixed_ref = f32[32,512]{1,0:T(8,128)S(1)} concatenate(f32[1,512]{1,0:T(1,128)} %copy-done.46, f32[1,512]{1,0:T(1,128)} %copy-done.47, f32[1,512]{1,0:T(1,128)} %tile.40, f32[1,512]{1,0:T(1,128)} %copy-done.39, f32[1,512]{1,0:T(1,128)} %get-tuple-element.96, f32[1,512]{1,0:T(1,128)} %get-tuple-element.99, f32[1,512]{1,0:T(1,128)} %get-tuple-element.102, ...), dimensions={0} | concatenate | bytes 131072 | tf_op jit(solution)/shard_map/concatenate | solution.py:581
  57.8 1.2 collective-permute-start.8
  59.2 1.4 collective-permute-start.10
  60.7 1.2 fusion.41
  66.9 1.3 fusion.26
  69.5 8.4 %normal_factor.2.low_ref = f32[44,8,256]{2,1,0:T(8,128)S(1)} custom-call(f32[6,16]{1,0:T(8,128)S(1)} %get-tuple-element.89.cam_ref, f32[8,8,256]{2,1,0:T(8,128)S(1)} %copy-done.1, s32[8,256]{1,0:T(8,128)S(1)} %copy-done.14, f32[1,512]{1,0:T(1,128)S(1)} %copy-done.25, bf16[512,48]{1,0:T(8,128)(2,1)S(1)} %copy.27.lobe_ref, ...), custom_call_target="tpu_custom_call" | custom-call | tf_op jit(solution)/shard_map/normal_factor/pallas_call | solution.py:486
  78.8 1.0 solve.2
  79.8 1.3 collective-permute-start.13
  81.1 4.0 %collective-permute-start.12 = (f32[2,1,256]{2,1,0:T(1,128)S(1)}, f32[2,1,256]{2,1,0:T(1,128)S(1)}, u32[]{:S(2)}, u32[]{:S(2)}) collective-permute-start(f32[2,1,256]{2,1,0:T(1,128)S(1)} %get-tuple-element.36), channel_id=1, source_target_pairs={{0,8},{8,16},{16,24},{1,9},{9,17},{17,25},{2,10},{10,18},{18,26},{... | collective-permute-start | bytes 6152 | tf_op jit(solution)/shard_map/ppermute | solution.py:611
  85.9 8.3 %collective-permute-start.14 = (f32[2,10,1]{2,1,0:T(8,128)S(1)}, f32[2,10,1]{2,1,0:T(8,128)S(1)}, u32[]{:S(2)}, u32[]{:S(2)}) collective-permute-start(f32[2,10,1]{2,1,0:T(8,128)S(1)} %get-tuple-element.40), channel_id=1, source_target_pairs={{0,1},{1,2},{2,3},{3,4},{4,5},{5,6},{6,7},{8,9},{9,10},{10,11},{11... | collective-permute-start | bytes 248 | tf_op jit(solution)/shard_map/ppermute | solution.py:611
  94.3 1.9 %collective-permute-start.15 = (f32[2,10,1]{2,1,0:T(8,128)S(1)}, f32[2,10,1]{2,1,0:T(8,128)S(1)}, u32[]{:S(2)}, u32[]{:S(2)}) collective-permute-start(f32[2,10,1]{2,1,0:T(8,128)S(1)} %get-tuple-element.41), channel_id=1, source_target_pairs={{1,0},{2,1},{3,2},{4,3},{5,4},{6,5},{7,6},{9,8},{10,9},{11,10},{12... | collective-permute-start | bytes 248 | tf_op jit(solution)/shard_map/ppermute | solution.py:613
  96.2 3.1 %collective-permute-done.15 = f32[2,10,1]{2,1,0:T(8,128)S(1)} collective-permute-done((f32[2,10,1]{2,1,0:T(8,128)S(1)}, f32[2,10,1]{2,1,0:T(8,128)S(1)}, u32[]{:S(2)}, u32[]{:S(2)}) %collective-permute-start.15) | collective-permute-done | bytes 112 | tf_op jit(solution)/shard_map/ppermute | solution.py:613
  99.5 1.3 collective-permute-start.16
  100.9 1.1 collective-permute-start.17
  101.9 2.3 %collective-permute-start.18 = (f32[8,8,256]{2,1,0:T(8,128)S(1)}, f32[8,8,256]{2,1,0:T(8,128)}, u32[]{:S(2)}, u32[]{:S(2)}) collective-permute-start(f32[8,8,256]{2,1,0:T(8,128)S(1)} %pad_maximum_fusion.1.par_ref.refs_0_), channel_id=1, source_target_pairs={{0,6},{1,7},{2,0},{3,1},{4,2},{5,3},{6,4},{7,5},{8,14},{9,15},{10,... | collective-permute-start | bytes 196616 | tf_op jit(solution)/shard_map/ppermute | solution.py:600
  104.8 1.4 tile.42.gain_ref
  109.5 13.8 %sample_sums.3 = (f32[8,8,256]{2,1,0:T(8,128)S(1)}, f32[8,8,256]{2,1,0:T(8,128)}, f32[8,8,256]{2,1,0:T(8,128)}, f32[8,8,256]{2,1,0:T(8,128)}, f32[8,64]{1,0:T(8,128)S(1)}) custom-call(s32[5]{0:T(128)S(1)} %copy-done.28, f32[4,4]{1,0:T(4,128)S(1)} %copy-done.22, bf16[64,8,2048]{2,1,0:T(8,128)(2,1)S(1)} %copy-done, ...), custom_call_target="tpu_custom_call" | custom-call | tf_op jit(solution)/shard_map/sample_sums/pallas_call | solution.py:516
  123.9 2.7 %collective-permute-start.19 = (f32[8,8,256]{2,1,0:T(8,128)}, f32[8,8,256]{2,1,0:T(8,128)S(1)}, u32[]{:S(2)}, u32[]{:S(2)}) collective-permute-start(f32[8,8,256]{2,1,0:T(8,128)} %get-tuple-element.18), channel_id=1, source_target_pairs={{0,6},{1,7},{2,0},{3,1},{4,2},{5,3},{6,4},{7,5},{8,14},{9,15},{10,... | collective-permute-start | bytes 196616 | tf_op jit(solution)/shard_map/ppermute | solution.py:600
  126.9 0.9 collective-permute-start.26
  128.6 2.6 %collective-permute-start.27 = (f32[2,32]{1,0:T(2,128)S(1)}, f32[2,32]{1,0:T(2,128)S(1)}, u32[]{:S(2)}, u32[]{:S(2)}) collective-permute-start(f32[2,32]{1,0:T(2,128)S(1)} %add.263), channel_id=1, source_target_pairs={{0,2},{1,3},{2,0},{3,1},{4,6},{5,7},{6,4},{7,5},{8,10},{9,11},{10,... | collective-permute-start | bytes 776 | tf_op jit(solution)/shard_map/ppermute | solution.py:636
  131.2 1.4 collective-permute-done.27
  132.6 1.1 collective-permute-start.28
  133.7 2.2 %collective-permute-done.28 = f32[2,32]{1,0:T(2,128)S(1)} collective-permute-done((f32[2,32]{1,0:T(2,128)S(1)}, f32[2,32]{1,0:T(2,128)S(1)}, u32[]{:S(2)}, u32[]{:S(2)}) %collective-permute-start.28) | collective-permute-done | bytes 288 | tf_op jit(solution)/shard_map/ppermute | solution.py:636
  135.9 2.0 %collective-permute-start.29 = (f32[2,32]{1,0:T(2,128)S(1)}, f32[2,32]{1,0:T(2,128)S(1)}, u32[]{:S(2)}, u32[]{:S(2)}) collective-permute-start(f32[2,32]{1,0:T(2,128)S(1)} %add.265), channel_id=1, source_target_pairs={{0,8},{8,0},{16,24},{24,16},{1,9},{9,1},{17,25},{25,17},{2,10},{10... | collective-permute-start | bytes 776 | tf_op jit(solution)/shard_map/ppermute | solution.py:636
  137.9 1.0 collective-permute-done.29
  138.9 2.4 %collective-permute-start.30 = (f32[2,32]{1,0:T(2,128)S(1)}, f32[2,32]{1,0:T(2,128)S(1)}, u32[]{:S(2)}, u32[]{:S(2)}) collective-permute-start(f32[2,32]{1,0:T(2,128)S(1)} %add.266), channel_id=1, source_target_pairs={{0,16},{8,24},{16,0},{24,8},{1,17},{9,25},{17,1},{25,9},{2,18},{10... | collective-permute-start | bytes 776 | tf_op jit(solution)/shard_map/ppermute | solution.py:636
  142.7 8.4 %normal_factor.3.low_ref = f32[44,8,256]{2,1,0:T(8,128)S(1)} custom-call(f32[6,16]{1,0:T(8,128)S(1)} %copy-done.23, f32[8,8,256]{2,1,0:T(8,128)S(1)} %pad_maximum_fusion.1.par_ref.refs_0_, s32[8,256]{1,0:T(8,128)S(1)} %copy-done.14, f32[1,512]{1,0:T(1,128)S(1)} %copy-done.26, bf16[512,48]{1,0:T(8,128)(2,1)S(1)} %copy.27.lobe_ref, ...), custom_call_target="tpu_custom_call" | custom-call | tf_op jit(solution)/shard_map/normal_factor/pallas_call | solution.py:486
  152.1 1.3 collective-permute-start.23
  153.4 4.0 %collective-permute-start.22 = (f32[2,1,256]{2,1,0:T(1,128)S(1)}, f32[2,1,256]{2,1,0:T(1,128)S(1)}, u32[]{:S(2)}, u32[]{:S(2)}) collective-permute-start(f32[2,1,256]{2,1,0:T(1,128)S(1)} %get-tuple-element.34), channel_id=1, source_target_pairs={{0,8},{8,16},{16,24},{1,9},{9,17},{17,25},{2,10},{10,18},{18,26},{... | collective-permute-start | bytes 6152 | tf_op jit(solution)/shard_map/ppermute | solution.py:611
  157.3 1.2 fusion.36
  158.6 7.5 %collective-permute-start.24 = (f32[2,10,1]{2,1,0:T(8,128)S(1)}, f32[2,10,1]{2,1,0:T(8,128)S(1)}, u32[]{:S(2)}, u32[]{:S(2)}) collective-permute-start(f32[2,10,1]{2,1,0:T(8,128)S(1)} %get-tuple-element.38), channel_id=1, source_target_pairs={{0,1},{1,2},{2,3},{3,4},{4,5},{5,6},{6,7},{8,9},{9,10},{10,11},{11... | collective-permute-start | bytes 248 | tf_op jit(solution)/shard_map/ppermute | solution.py:611
  166.2 1.9 %collective-permute-start.25 = (f32[2,10,1]{2,1,0:T(8,128)S(1)}, f32[2,10,1]{2,1,0:T(8,128)S(1)}, u32[]{:S(2)}, u32[]{:S(2)}) collective-permute-start(f32[2,10,1]{2,1,0:T(8,128)S(1)} %get-tuple-element.39), channel_id=1, source_target_pairs={{1,0},{2,1},{3,2},{4,3},{5,4},{6,5},{7,6},{9,8},{10,9},{11,10},{12... | collective-permute-start | bytes 248 | tf_op jit(solution)/shard_map/ppermute | solution.py:613
  168.1 3.1 %collective-permute-done.25 = f32[2,10,1]{2,1,0:T(8,128)S(1)} collective-permute-done((f32[2,10,1]{2,1,0:T(8,128)S(1)}, f32[2,10,1]{2,1,0:T(8,128)S(1)}, u32[]{:S(2)}, u32[]{:S(2)}) %collective-permute-start.25) | collective-permute-done | bytes 112 | tf_op jit(solution)/shard_map/ppermute | solution.py:613
  (243 shorter events, 37.8 us)
Async XLA Ops:
  0.6 27.5 %copy-start = (bf16[64,8,2048]{2,1,0:T(8,128)(2,1)S(1)}, bf16[64,8,2048]{2,1,0:T(8,128)(2,1)}, u32[]{:S(2)}) copy-start(bf16[64,8,2048]{2,1,0:T(8,128)(2,1)} %own_ref.3) | copy-start | bytes 6291460
  2.4 24.4 %collective-permute-start.1 = (f32[9,8,256]{2,1,0:T(8,128)S(1)}, f32[9,8,256]{2,1,0:T(8,128)S(1)}, u32[]{:S(2)}, u32[]{:S(2)}) collective-permute-start(f32[9,8,256]{2,1,0:T(8,128)S(1)} %pad_maximum_fusion.refs_0_), channel_id=1, source_target_pairs={{0,2},{1,3},{2,4},{3,5},{4,6},{5,7},{6,0},{7,1},{8,10},{9,11},{10,... | collective-permute-start | bytes 221192 | tf_op jit(solution)/shard_map/ppermute | solution.py:600
  4.5 22.3 %collective-permute-start.2 = (f32[9,8,256]{2,1,0:T(8,128)S(1)}, f32[9,8,256]{2,1,0:T(8,128)S(1)}, u32[]{:S(2)}, u32[]{:S(2)}) collective-permute-start(f32[9,8,256]{2,1,0:T(8,128)S(1)} %pad_maximum_fusion.refs_0_), channel_id=1, source_target_pairs={{0,4},{1,5},{2,6},{3,7},{4,0},{5,1},{6,2},{7,3},{8,12},{9,13},{10,... | collective-permute-start | bytes 221192 | tf_op jit(solution)/shard_map/ppermute | solution.py:600
  6.8 20.7 %collective-permute-start.3 = (f32[9,8,256]{2,1,0:T(8,128)S(1)}, f32[9,8,256]{2,1,0:T(8,128)S(1)}, u32[]{:S(2)}, u32[]{:S(2)}) collective-permute-start(f32[9,8,256]{2,1,0:T(8,128)S(1)} %pad_maximum_fusion.refs_0_), channel_id=1, source_target_pairs={{0,6},{1,7},{2,0},{3,1},{4,2},{5,3},{6,4},{7,5},{8,14},{9,15},{10,... | collective-permute-start | bytes 221192 | tf_op jit(solution)/shard_map/ppermute | solution.py:600
  10.2 17.9 %collective-permute-start = (bf16[64,8,1024]{2,1,0:T(8,128)(2,1)}, bf16[64,8,1024]{2,1,0:T(8,128)(2,1)S(1)}, u32[]{:S(2)}, u32[]{:S(2)}) collective-permute-start(bf16[64,8,1024]{2,1,0:T(8,128)(2,1)} %bitcast.6), channel_id=1, source_target_pairs={{0,1},{1,0},{2,3},{3,2},{4,5},{5,4},{6,7},{7,6},{8,9},{9,8},{10,11... | collective-permute-start | bytes 3145736 | tf_op jit(solution)/shard_map/ppermute | solution.py:653
  19.6 28.9 %copy-start.6 = (f32[4,4,128]{2,1,0:T(4,128)}, f32[4,4,128]{2,1,0:T(4,128)S(1)}, u32[]{:S(2)}) copy-start(f32[4,4,128]{2,1,0:T(4,128)S(1)} %broadcast_multiply_fusion) | copy-start | bytes 24580
  24.7 29.4 %copy-start.21 = (f32[4,4]{1,0:T(4,128)}, f32[4,4]{1,0:T(4,128)S(1)}, u32[]{:S(2)}) copy-start(f32[4,4]{1,0:T(4,128)S(1)} %concatenate.103.cam_ref) | copy-start | bytes 196
  26.2 28.0 %copy-start.19 = (f32[8,128]{1,0:T(8,128)}, f32[8,128]{1,0:T(8,128)S(1)}, u32[]{:S(2)}) copy-start(f32[8,128]{1,0:T(8,128)S(1)} %concatenate.112.peak_ref) | copy-start | bytes 12292
  26.8 27.4 %copy-start.8 = (s32[8,256]{1,0:T(8,128)}, s32[8,256]{1,0:T(8,128)S(1)}, u32[]{:S(2)}) copy-start(s32[8,256]{1,0:T(8,128)S(1)} %fusion.21.refs_5_) | copy-start | bytes 24580
  27.4 26.7 %copy-start.10 = (s32[8,256]{1,0:T(8,128)}, s32[8,256]{1,0:T(8,128)S(1)}, u32[]{:S(2)}) copy-start(s32[8,256]{1,0:T(8,128)S(1)} %fusion.20.refs_6_) | copy-start | bytes 24580
  27.4 20.1 %copy-start.35 = (bf16[4,512]{1,0:T(4,128)(2,1)S(1)}, bf16[4,512]{1,0:T(4,128)(2,1)}, u32[]{:S(2)}) copy-start(bf16[4,512]{1,0:T(4,128)(2,1)} %get-tuple-element.53) | copy-start | bytes 12292
  27.4 20.1 %copy-start.36 = (bf16[4,512]{1,0:T(4,128)(2,1)S(1)}, bf16[4,512]{1,0:T(4,128)(2,1)}, u32[]{:S(2)}) copy-start(bf16[4,512]{1,0:T(4,128)(2,1)} %get-tuple-element.52) | copy-start | bytes 12292
  27.5 20.1 %copy-start.38 = (bf16[4,512]{1,0:T(4,128)(2,1)S(1)}, bf16[4,512]{1,0:T(4,128)(2,1)}, u32[]{:S(2)}) copy-start(bf16[4,512]{1,0:T(4,128)(2,1)} %copy-done.37) | copy-start | bytes 12292
  28.1 26.0 %copy-start.12 = (s32[8,256]{1,0:T(8,128)}, s32[8,256]{1,0:T(8,128)S(1)}, u32[]{:S(2)}) copy-start(s32[8,256]{1,0:T(8,128)S(1)} %fusion.19.refs_7_) | copy-start | bytes 24580
  28.1 21.5 %copy-start.42 = (f32[1,512]{1,0:T(1,128)S(1)}, f32[1,512]{1,0:T(1,128)}, u32[]{:S(2)}) copy-start(f32[1,512]{1,0:T(1,128)} %copy-done.40) | copy-start | bytes 6148
  31.1 37.1 %copy-start.1 = (f32[8,8,256]{2,1,0:T(8,128)S(1)}, f32[8,8,256]{2,1,0:T(8,128)}, u32[]{:S(2)}) copy-start(f32[8,8,256]{2,1,0:T(8,128)} %par_ref.3) | copy-start | bytes 196612
  45.9 1.3 collective-permute-start.4
  47.2 2.4 %collective-permute-start.5 = (f32[2,32]{1,0:T(2,128)S(1)}, f32[2,32]{1,0:T(2,128)S(1)}, u32[]{:S(2)}, u32[]{:S(2)}) collective-permute-start(f32[2,32]{1,0:T(2,128)S(1)} %add.237), channel_id=1, source_target_pairs={{0,2},{1,3},{2,0},{3,1},{4,6},{5,7},{6,4},{7,5},{8,10},{9,11},{10,... | collective-permute-start | bytes 776 | tf_op jit(solution)/shard_map/ppermute | solution.py:636
  49.6 58.0 %copy-start.7 = (f32[4,4,128]{2,1,0:T(4,128)S(1)}, f32[4,4,128]{2,1,0:T(4,128)}, u32[]{:S(2)}) copy-start(f32[4,4,128]{2,1,0:T(4,128)} %copy-done.6) | copy-start | bytes 24580
  49.6 3.3 %collective-permute-start.6 = (f32[2,32]{1,0:T(2,128)S(1)}, f32[2,32]{1,0:T(2,128)S(1)}, u32[]{:S(2)}, u32[]{:S(2)}) collective-permute-start(f32[2,32]{1,0:T(2,128)S(1)} %add.238), channel_id=1, source_target_pairs={{0,4},{1,5},{2,6},{3,7},{4,0},{5,1},{6,2},{7,3},{8,12},{9,13},{10,... | collective-permute-start | bytes 776 | tf_op jit(solution)/shard_map/ppermute | solution.py:636
  52.9 4.2 %collective-permute-start.7 = (f32[2,32]{1,0:T(2,128)S(1)}, f32[2,32]{1,0:T(2,128)}, u32[]{:S(2)}, u32[]{:S(2)}) collective-permute-start(f32[2,32]{1,0:T(2,128)S(1)} %add.239), channel_id=1, source_target_pairs={{0,8},{8,0},{16,24},{24,16},{1,9},{9,1},{17,25},{25,17},{2,10},{10... | collective-permute-start | bytes 776 | tf_op jit(solution)/shard_map/ppermute | solution.py:636
  54.2 53.4 %copy-start.9 = (s32[8,256]{1,0:T(8,128)S(1)}, s32[8,256]{1,0:T(8,128)}, u32[]{:S(2)}) copy-start(s32[8,256]{1,0:T(8,128)} %copy-done.8) | copy-start | bytes 24580
  54.2 53.4 %copy-start.11 = (s32[8,256]{1,0:T(8,128)S(1)}, s32[8,256]{1,0:T(8,128)}, u32[]{:S(2)}) copy-start(s32[8,256]{1,0:T(8,128)} %copy-done.10) | copy-start | bytes 24580
  54.2 53.4 %copy-start.13 = (s32[8,256]{1,0:T(8,128)S(1)}, s32[8,256]{1,0:T(8,128)}, u32[]{:S(2)}) copy-start(s32[8,256]{1,0:T(8,128)} %copy-done.12) | copy-start | bytes 24580
  57.8 2.8 %collective-permute-start.8 = (f32[2,32]{1,0:T(2,128)S(1)}, f32[2,32]{1,0:T(2,128)S(1)}, u32[]{:S(2)}, u32[]{:S(2)}) collective-permute-start(f32[2,32]{1,0:T(2,128)S(1)} %add.240), channel_id=1, source_target_pairs={{0,16},{8,24},{16,0},{24,8},{1,17},{9,25},{17,1},{25,9},{2,18},{10... | collective-permute-start | bytes 776 | tf_op jit(solution)/shard_map/ppermute | solution.py:636
  59.1 18.9 %collective-permute-start.9 = (f32[8,8,256]{2,1,0:T(8,128)}, f32[8,8,256]{2,1,0:T(8,128)}, u32[]{:S(2)}, u32[]{:S(2)}) collective-permute-start(f32[8,8,256]{2,1,0:T(8,128)} %copy-done.32), channel_id=1, source_target_pairs={{0,6},{1,7},{2,0},{3,1},{4,2},{5,3},{6,4},{7,5},{8,14},{9,15},{10,... | collective-permute-start | bytes 196616 | tf_op jit(solution)/shard_map/ppermute | solution.py:600
  59.2 18.7 %collective-permute-start.10 = (f32[8,8,256]{2,1,0:T(8,128)}, f32[8,8,256]{2,1,0:T(8,128)}, u32[]{:S(2)}, u32[]{:S(2)}) collective-permute-start(f32[8,8,256]{2,1,0:T(8,128)} %copy-done.31), channel_id=1, source_target_pairs={{0,4},{1,5},{2,6},{3,7},{4,0},{5,1},{6,2},{7,3},{8,12},{9,13},{10,... | collective-permute-start | bytes 196616 | tf_op jit(solution)/shard_map/ppermute | solution.py:600
  60.7 17.3 %collective-permute-start.11 = (f32[8,8,256]{2,1,0:T(8,128)}, f32[8,8,256]{2,1,0:T(8,128)}, u32[]{:S(2)}, u32[]{:S(2)}) collective-permute-start(f32[8,8,256]{2,1,0:T(8,128)} %copy-done.30), channel_id=1, source_target_pairs={{0,2},{1,3},{2,4},{3,5},{4,6},{5,7},{6,0},{7,1},{8,10},{9,11},{10,... | collective-permute-start | bytes 196616 | tf_op jit(solution)/shard_map/ppermute | solution.py:600
  65.4 38.9 %copy-start.52 = (f32[32]{0:T(128)S(1)}, f32[32]{0:T(128)}, u32[]{:S(2)}) copy-start(f32[32]{0:T(128)} %get-tuple-element.33) | copy-start | bytes 388
  79.8 5.3 %collective-permute-start.13 = (f32[2,1,256]{2,1,0:T(1,128)S(1)}, f32[2,1,256]{2,1,0:T(1,128)S(1)}, u32[]{:S(2)}, u32[]{:S(2)}) collective-permute-start(f32[2,1,256]{2,1,0:T(1,128)S(1)} %get-tuple-element.37), channel_id=1, source_target_pairs={{8,0},{16,8},{24,16},{9,1},{17,9},{25,17},{10,2},{18,10},{26,18},{... | collective-permute-start | bytes 6152 | tf_op jit(solution)/shard_map/ppermute | solution.py:613
  81.1 4.7 %collective-permute-start.12 = (f32[2,1,256]{2,1,0:T(1,128)S(1)}, f32[2,1,256]{2,1,0:T(1,128)S(1)}, u32[]{:S(2)}, u32[]{:S(2)}) collective-permute-start(f32[2,1,256]{2,1,0:T(1,128)S(1)} %get-tuple-element.36), channel_id=1, source_target_pairs={{0,8},{8,16},{16,24},{1,9},{9,17},{17,25},{2,10},{10,18},{18,26},{... | collective-permute-start | bytes 6152 | tf_op jit(solution)/shard_map/ppermute | solution.py:611
  85.9 10.3 %collective-permute-start.14 = (f32[2,10,1]{2,1,0:T(8,128)S(1)}, f32[2,10,1]{2,1,0:T(8,128)S(1)}, u32[]{:S(2)}, u32[]{:S(2)}) collective-permute-start(f32[2,10,1]{2,1,0:T(8,128)S(1)} %get-tuple-element.40), channel_id=1, source_target_pairs={{0,1},{1,2},{2,3},{3,4},{4,5},{5,6},{6,7},{8,9},{9,10},{10,11},{11... | collective-permute-start | bytes 248 | tf_op jit(solution)/shard_map/ppermute | solution.py:611
  94.3 5.1 %collective-permute-start.15 = (f32[2,10,1]{2,1,0:T(8,128)S(1)}, f32[2,10,1]{2,1,0:T(8,128)S(1)}, u32[]{:S(2)}, u32[]{:S(2)}) collective-permute-start(f32[2,10,1]{2,1,0:T(8,128)S(1)} %get-tuple-element.41), channel_id=1, source_target_pairs={{1,0},{2,1},{3,2},{4,3},{5,4},{6,5},{7,6},{9,8},{10,9},{11,10},{12... | collective-permute-start | bytes 248 | tf_op jit(solution)/shard_map/ppermute | solution.py:613
  99.5 7.3 %collective-permute-start.16 = (f32[8,8,256]{2,1,0:T(8,128)S(1)}, f32[8,8,256]{2,1,0:T(8,128)}, u32[]{:S(2)}, u32[]{:S(2)}) collective-permute-start(f32[8,8,256]{2,1,0:T(8,128)S(1)} %pad_maximum_fusion.1.par_ref.refs_0_), channel_id=1, source_target_pairs={{0,2},{1,3},{2,4},{3,5},{4,6},{5,7},{6,0},{7,1},{8,10},{9,11},{10,... | collective-permute-start | bytes 196616 | tf_op jit(solution)/shard_map/ppermute | solution.py:600
  100.9 6.7 %collective-permute-start.17 = (f32[8,8,256]{2,1,0:T(8,128)S(1)}, f32[8,8,256]{2,1,0:T(8,128)}, u32[]{:S(2)}, u32[]{:S(2)}) collective-permute-start(f32[8,8,256]{2,1,0:T(8,128)S(1)} %pad_maximum_fusion.1.par_ref.refs_0_), channel_id=1, source_target_pairs={{0,4},{1,5},{2,6},{3,7},{4,0},{5,1},{6,2},{7,3},{8,12},{9,13},{10,... | collective-permute-start | bytes 196616 | tf_op jit(solution)/shard_map/ppermute | solution.py:600
  101.9 5.6 %collective-permute-start.18 = (f32[8,8,256]{2,1,0:T(8,128)S(1)}, f32[8,8,256]{2,1,0:T(8,128)}, u32[]{:S(2)}, u32[]{:S(2)}) collective-permute-start(f32[8,8,256]{2,1,0:T(8,128)S(1)} %pad_maximum_fusion.1.par_ref.refs_0_), channel_id=1, source_target_pairs={{0,6},{1,7},{2,0},{3,1},{4,2},{5,3},{6,4},{7,5},{8,14},{9,15},{10,... | collective-permute-start | bytes 196616 | tf_op jit(solution)/shard_map/ppermute | solution.py:600
  123.9 27.2 %collective-permute-start.19 = (f32[8,8,256]{2,1,0:T(8,128)}, f32[8,8,256]{2,1,0:T(8,128)S(1)}, u32[]{:S(2)}, u32[]{:S(2)}) collective-permute-start(f32[8,8,256]{2,1,0:T(8,128)} %get-tuple-element.18), channel_id=1, source_target_pairs={{0,6},{1,7},{2,0},{3,1},{4,2},{5,3},{6,4},{7,5},{8,14},{9,15},{10,... | collective-permute-start | bytes 196616 | tf_op jit(solution)/shard_map/ppermute | solution.py:600
  126.6 24.5 %collective-permute-start.20 = (f32[8,8,256]{2,1,0:T(8,128)}, f32[8,8,256]{2,1,0:T(8,128)S(1)}, u32[]{:S(2)}, u32[]{:S(2)}) collective-permute-start(f32[8,8,256]{2,1,0:T(8,128)} %get-tuple-element.19), channel_id=1, source_target_pairs={{0,4},{1,5},{2,6},{3,7},{4,0},{5,1},{6,2},{7,3},{8,12},{9,13},{10,... | collective-permute-start | bytes 196616 | tf_op jit(solution)/shard_map/ppermute | solution.py:600
  126.8 24.3 %collective-permute-start.21 = (f32[8,8,256]{2,1,0:T(8,128)}, f32[8,8,256]{2,1,0:T(8,128)S(1)}, u32[]{:S(2)}, u32[]{:S(2)}) collective-permute-start(f32[8,8,256]{2,1,0:T(8,128)} %get-tuple-element.20), channel_id=1, source_target_pairs={{0,2},{1,3},{2,4},{3,5},{4,6},{5,7},{6,0},{7,1},{8,10},{9,11},{10,... | collective-permute-start | bytes 196616 | tf_op jit(solution)/shard_map/ppermute | solution.py:600
  126.9 1.7 collective-permute-start.26
  128.6 3.9 %collective-permute-start.27 = (f32[2,32]{1,0:T(2,128)S(1)}, f32[2,32]{1,0:T(2,128)S(1)}, u32[]{:S(2)}, u32[]{:S(2)}) collective-permute-start(f32[2,32]{1,0:T(2,128)S(1)} %add.263), channel_id=1, source_target_pairs={{0,2},{1,3},{2,0},{3,1},{4,6},{5,7},{6,4},{7,5},{8,10},{9,11},{10,... | collective-permute-start | bytes 776 | tf_op jit(solution)/shard_map/ppermute | solution.py:636
  132.6 3.3 %collective-permute-start.28 = (f32[2,32]{1,0:T(2,128)S(1)}, f32[2,32]{1,0:T(2,128)S(1)}, u32[]{:S(2)}, u32[]{:S(2)}) collective-permute-start(f32[2,32]{1,0:T(2,128)S(1)} %add.264), channel_id=1, source_target_pairs={{0,4},{1,5},{2,6},{3,7},{4,0},{5,1},{6,2},{7,3},{8,12},{9,13},{10,... | collective-permute-start | bytes 776 | tf_op jit(solution)/shard_map/ppermute | solution.py:636
  135.9 3.0 %collective-permute-start.29 = (f32[2,32]{1,0:T(2,128)S(1)}, f32[2,32]{1,0:T(2,128)S(1)}, u32[]{:S(2)}, u32[]{:S(2)}) collective-permute-start(f32[2,32]{1,0:T(2,128)S(1)} %add.265), channel_id=1, source_target_pairs={{0,8},{8,0},{16,24},{24,16},{1,9},{9,1},{17,25},{25,17},{2,10},{10... | collective-permute-start | bytes 776 | tf_op jit(solution)/shard_map/ppermute | solution.py:636
  138.9 12.2 %collective-permute-start.30 = (f32[2,32]{1,0:T(2,128)S(1)}, f32[2,32]{1,0:T(2,128)S(1)}, u32[]{:S(2)}, u32[]{:S(2)}) collective-permute-start(f32[2,32]{1,0:T(2,128)S(1)} %add.266), channel_id=1, source_target_pairs={{0,16},{8,24},{16,0},{24,8},{1,17},{9,25},{17,1},{25,9},{2,18},{10... | collective-permute-start | bytes 776 | tf_op jit(solution)/shard_map/ppermute | solution.py:636
  152.1 6.5 %collective-permute-start.23 = (f32[2,1,256]{2,1,0:T(1,128)S(1)}, f32[2,1,256]{2,1,0:T(1,128)S(1)}, u32[]{:S(2)}, u32[]{:S(2)}) collective-permute-start(f32[2,1,256]{2,1,0:T(1,128)S(1)} %get-tuple-element.35), channel_id=1, source_target_pairs={{8,0},{16,8},{24,16},{9,1},{17,9},{25,17},{10,2},{18,10},{26,18},{... | collective-permute-start | bytes 6152 | tf_op jit(solution)/shard_map/ppermute | solution.py:613
  153.4 5.2 %collective-permute-start.22 = (f32[2,1,256]{2,1,0:T(1,128)S(1)}, f32[2,1,256]{2,1,0:T(1,128)S(1)}, u32[]{:S(2)}, u32[]{:S(2)}) collective-permute-start(f32[2,1,256]{2,1,0:T(1,128)S(1)} %get-tuple-element.34), channel_id=1, source_target_pairs={{0,8},{8,16},{16,24},{1,9},{9,17},{17,25},{2,10},{10,18},{18,26},{... | collective-permute-start | bytes 6152 | tf_op jit(solution)/shard_map/ppermute | solution.py:611
  158.6 9.5 %collective-permute-start.24 = (f32[2,10,1]{2,1,0:T(8,128)S(1)}, f32[2,10,1]{2,1,0:T(8,128)S(1)}, u32[]{:S(2)}, u32[]{:S(2)}) collective-permute-start(f32[2,10,1]{2,1,0:T(8,128)S(1)} %get-tuple-element.38), channel_id=1, source_target_pairs={{0,1},{1,2},{2,3},{3,4},{4,5},{5,6},{6,7},{8,9},{9,10},{10,11},{11... | collective-permute-start | bytes 248 | tf_op jit(solution)/shard_map/ppermute | solution.py:611
  166.2 5.1 %collective-permute-start.25 = (f32[2,10,1]{2,1,0:T(8,128)S(1)}, f32[2,10,1]{2,1,0:T(8,128)S(1)}, u32[]{:S(2)}, u32[]{:S(2)}) collective-permute-start(f32[2,10,1]{2,1,0:T(8,128)S(1)} %get-tuple-element.39), channel_id=1, source_target_pairs={{1,0},{2,1},{3,2},{4,3},{5,4},{6,5},{7,6},{9,8},{10,9},{11,10},{12... | collective-permute-start | bytes 248 | tf_op jit(solution)/shard_map/ppermute | solution.py:613
  (37 other events, 168.1 us)

commit v2 on v1

--- a/solution.py
+++ b/solution.py
@@ -17,30 +17,9 @@
 f32 = jnp.float32
 bf16 = jnp.bfloat16
 LANES = 128
-VMEM_BYTES = 40 * 1024 * 1024
+VMEM_BYTES = 16 * 1024 * 1024
 LINEAR = (2, 3, 5, 6, 7)
 ENTRIES = [(i, j) for i in range(8) for j in range(i, 8)]
-
-
-def unit_columns(raw):
-    lifted = raw + jnp.array([0.0, 0.0, lift_z], f32)[:, None]
-    return lifted / jnp.sqrt(jnp.sum(lifted * lifted, axis=0, keepdims=True))
-
-
-def geometry(light_directions, view_dirs):
-    lights = unit_columns(light_directions)
-    views = unit_columns(view_dirs)
-    raw_half = views[:, :, None] + lights[:, None, :]
-    halves = raw_half / jnp.sqrt(jnp.sum(raw_half * raw_half, axis=0, keepdims=True))
-    echoes = jnp.sum(views[:, :, None] * lights[:, None, :], axis=0)
-    return lights, views, halves.reshape(3, -1), echoes.reshape(1, -1)
-
-
-def thirds(x):
-    first = lax.reduce_precision(x, 8, 7)
-    rest = x - first
-    second = lax.reduce_precision(rest, 8, 7)
-    return first, second, rest - second
 
 
 def split_value(x, count):
@@ -123,15 +102,29 @@
 
 
 def normal_kernel(
-    cam_ref, par_ref, vis_ref, gain_ref, lobe_ref, mixed_ref, square_ref, out_ref,
-    rows_ref, sums_ref, mixed_scr, square_scr,
+    par_ref, vis_ref, gain_ref, near_ref, cams_ref, lobe_ref, mixed_ref, square_ref, out_ref,
+    rows_ref, sums_ref, mixed_scr, square_scr, cam_scr, gram_scr,
 ):
     rows, cols = par_ref.shape[1], par_ref.shape[2]
     depth = lobe_ref.shape[1]
     chunk = 4 * LIGHTS
     chunks = CAMS // 4
 
+    near, views = near_ref[...], cams_ref[...]
     gain2 = gain_ref[...] * gain_ref[...]
+    grams = [jnp.sum(near * near[i : i + 1] * gain2, axis=1, keepdims=True) for i in range(4)]
+    for i in range(4):
+        gram_scr[8 * i : 8 * i + 8, :] = jnp.broadcast_to(grams[i], (8, LANES))
+    spread = [total(grams[i][k : k + 1] * views[k : k + 1] for k in range(3)) for i in range(4)]
+    echo_sq = total(spread[k] * views[k : k + 1] for k in range(3))
+    row = iota(views.shape, 0)
+    full = jnp.where(row == 3, echo_sq, jnp.where(row == 4, spread[3], views))
+    for c in range(CAMS):
+        cam_scr[8 * c : 8 * c + 8, :] = jnp.broadcast_to(full[:, c : c + 1], (8, LANES))
+
+    across = CAMS * LIGHTS
+    at_light = pick(iota((LIGHTS, across), 1) % LIGHTS == iota((LIGHTS, across), 0))
+    gain2 = exact(jnp.broadcast_to(gain2, (8, LIGHTS)), at_light, ((1,), (0,)))[0:1]
     for src, dst in ((mixed_ref, mixed_scr), (square_ref, square_scr)):
         head, tail = split_pair(src[...] * gain2)
         count = src.shape[0]
@@ -169,10 +162,13 @@
         put_rows(sums_ref, 16 * rows + r, rows, square)
         return carry
 
-    lax.fori_loop(0, rows, one_row, 0)
+    lax.fori_loop(0, rows, one_row, 0, unroll=4)
 
     def one_part(h, carry):
         at = pl.ds(pl.multiple_of(h * LANES, LANES), LANES)
+
+        def cam(c, i):
+            return cam_scr[8 * c + i : 8 * c + i + 1, :]
 
         def sums(k):
             return sums_ref[h, k * rows : (k + 1) * rows, :]
@@ -190,7 +186,7 @@
         view_sum = [zero, zero, zero]
         for c in range(CAMS):
             w = seen(mask, c)
-            v = [cam_ref[i, c] for i in range(3)]
+            v = [cam(c, i) for i in range(3)]
             back = 1.0 - inner(v, normal)
             turn = (-2.0 * rim) * back
             shape = {0: turn * inner(v, by_u), 1: turn * inner(v, by_v), 6: back * back}
@@ -198,10 +194,10 @@
             weighted[5] = w
             for i in gam:
                 gam[i] = gam[i] + weighted[i]
-                lit[i] = lit[i] + weighted[i] * cam_ref[4, c]
+                lit[i] = lit[i] + weighted[i] * cam(c, 4)
             for i, j in own:
                 own[i, j] = own[i, j] + weighted[i] * shape[j]
-            echo_sq = echo_sq + w * cam_ref[3, c]
+            echo_sq = echo_sq + w * cam(c, 3)
             view_sum = [s + w * x for s, x in zip(view_sum, v)]
             for k in range(4):
                 peak = sums(32 + 4 * c + k)
@@ -214,7 +210,7 @@
         own[5, 6] = gam[6]
 
         def gram(i, j):
-            return cam_ref[5, 4 * i + j]
+            return gram_scr[8 * i + j : 8 * i + j + 1, :]
 
         entries = {ij: None for ij in ENTRIES}
 
@@ -297,7 +293,7 @@
 
 
 def sample_kernel(
-    place_ref, cam_ref, own_ref, got_ref, gain_ref, lobe_ref, shade_ref, plain_ref, peak_ref, *refs, parts
+    tile_ref, own_ref, got_ref, gain_ref, lobe_ref, shade_ref, plain_ref, peak_ref, slab_ref, *refs, parts
 ):
     par_refs, vis_refs = refs[:parts], refs[parts : 2 * parts]
     out_refs = refs[2 * parts : 3 * parts]
@@ -312,9 +308,9 @@
         @pl.when(step == s)
         def _():
             par_scr[...] = par_refs[s][0:8]
-            vis_scr[...] = vis_refs[s][...]
-
-    core = place_ref[parts]
+            vis_scr[...] = vis_refs[s][8].astype(jnp.int32)
+
+    core = tile_ref[0] % 2
     mine = pl.multiple_of(core * (samples * rows), rows)
     theirs = pl.multiple_of((1 - core) * (samples * rows), rows)
     for h in range(cols // LANES):
@@ -328,7 +324,11 @@
     p = [par_scr[i] for i in range(8)]
     mask = vis_scr[...]
     normal, by_u, by_v, sharp, slope = texel_forms(p)
-    base = cam_ref[3, 0].astype(jnp.int32)
+    base = (tile_ref[0] // 2) * cams
+
+    def cam(c, i):
+        return slab_ref[8 * c + i : 8 * c + i + 1, :][:, 0:1]
+
     used = put_lobe_rows(slab, normal, sharp)
     weights = [seen(mask, base + c) for c in range(cams)]
     for c in range(cams):
@@ -344,7 +344,7 @@
             slab(at, piece[which])
             at += 1
     for c in range(cams):
-        back = 1.0 - inner([cam_ref[i, c] for i in range(3)], normal)
+        back = 1.0 - inner([cam(c, i) for i in range(3)], normal)
         head, tail = split_value(p[6] * (back * back), 2)
         slab(at + c, head)
         slab(at + cams + c, tail)
@@ -352,7 +352,8 @@
         slab(k, jnp.zeros((rows, cols), f32))
     slab(64, p[3])
 
-    gains = gain_ref[...]
+    at_light = pick(iota((LIGHTS, held), 1) % LIGHTS == iota((LIGHTS, held), 0))
+    gains = exact(jnp.broadcast_to(gain_ref[...], (8, LIGHTS)), at_light, ((1,), (0,)))[0:1]
     plain = jnp.concatenate(split_value(plain_ref[...] * gains, 2), axis=0).astype(bf16)
     peak = jnp.concatenate(split_value(peak_ref[...] * gains, 2), axis=0).astype(bf16)
     count = plain_ref.shape[0]
@@ -380,7 +381,7 @@
         return lift, energy
 
     zero = jnp.zeros((LIGHTS, LANES), f32)
-    lift, energy = lax.fori_loop(0, rows, one_row, (zero, zero))
+    lift, energy = lax.fori_loop(0, rows, one_row, (zero, zero), unroll=4)
 
     @pl.when(step == 0)
     def _():
@@ -394,13 +395,9 @@
 
     @pl.when(step == parts - 1)
     def _():
-        light_ref[...] = lax.dot_general(
-            jnp.ones((8, LANES), f32),
-            light_scr[...],
-            (((1,), (1,)), ((), ())),
-            precision=lax.Precision.HIGHEST,
-            preferred_element_type=f32,
-        )
+        for k in range(2):
+            part = light_scr[k * LIGHTS : (k + 1) * LIGHTS, :]
+            light_ref[k : k + 1, :] = exact(jnp.ones((8, LANES), f32), part, ((1,), (1,)))[0:1]
 
     def sums(k):
         return get_slab(sums_ref, k, rows)
@@ -412,7 +409,7 @@
         return new if old is None else old + new
 
     for c in range(cams):
-        v = [cam_ref[i, c] for i in range(3)]
+        v = [cam(c, i) for i in range(3)]
         w = weights[c]
         one = w * sums(4 * c)
         lit = [w * sums(4 * c + 1 + x) for x in range(3)]
@@ -480,39 +477,44 @@
     return pltpu.CompilerParams(vmem_limit_bytes=VMEM_BYTES)
 
 
-def normal_call(cam_table, par, vis, gain_row, tables):
+def normal_call(par, vis, gains, tables):
     _, rows, cols = par.shape
-    depth = tables["lobe"].shape[1]
+    parts = cols // LANES
+    small = [tables[n] for n in ("near", "cams", "lobe", "mixed", "square")]
     return pl.pallas_call(
         normal_kernel,
         name="normal_factor",
         out_shape=jax.ShapeDtypeStruct((44, rows, cols), f32),
-        in_specs=[smem()] + [vmem()] * 6,
+        in_specs=[vmem()] * 8,
         out_specs=vmem(),
         scratch_shapes=[
-            pltpu.VMEM((cols // LANES, depth * rows, LANES), f32),
-            pltpu.VMEM((cols // LANES, 96 * rows, LANES), f32),
+            pltpu.VMEM((parts, 48 * rows, LANES), f32),
+            pltpu.VMEM((parts, 96 * rows, LANES), f32),
             pltpu.VMEM((64, CAMS * LIGHTS), bf16),
             pltpu.VMEM((32, CAMS * LIGHTS), bf16),
+            pltpu.VMEM((8 * CAMS, LANES), f32),
+            pltpu.VMEM((32, LANES), f32),
         ],
         compiler_params=params_of(),
-    )(cam_table, par, vis, gain_row, tables["lobe"], tables["mixed"], tables["square"])
-
-
-def sample_call(place, cam_table, own, got, gain_row, tables, pars, vises):
+    )(par, vis, gains, *small)
+
+
+def sample_call(tile, own, got, gains, tables, pars, vises):
     parts = len(pars)
     samples, rows, _ = own.shape
     cols = pars[0].shape[2]
     held = 2 * samples
-    whole2 = lambda s, place: (0, 0)
-    whole3 = lambda s, place: (0, 0, 0)
 
     def full(x):
-        return pl.BlockSpec(x.shape, whole2 if x.ndim == 2 else whole3)
+        zeros = (0,) * len(x.shape)
+        return pl.BlockSpec(x.shape, lambda s, tile: zeros)
+
+    def chip(s, tile):
+        return lax.rem(tile[0] // 2 + (parts - s), parts)
 
     outs = [jax.ShapeDtypeStruct((8, rows, cols), f32) for _ in range(parts)]
-    outs.append(jax.ShapeDtypeStruct((8, 2 * LIGHTS), f32))
-    small = [gain_row, tables["lobe_here"], tables["shade"], tables["plain"], tables["peak"]]
+    outs.append(jax.ShapeDtypeStruct((2, LIGHTS), f32))
+    small = [gains] + [tables[n] for n in ("here", "shade", "plain", "peak", "slab")]
     return pl.pallas_call(
         functools.partial(sample_kernel, parts=parts),
         name="sample_sums",
@@ -521,9 +523,8 @@
             num_scalar_prefetch=1,
             grid=(parts,),
             in_specs=[
-                smem(),
-                pl.BlockSpec((samples, rows, cols), lambda s, place: (0, 0, place[s])),
-                pl.BlockSpec((samples, rows, cols), lambda s, place: (0, 0, place[s] // 2)),
+                pl.BlockSpec((samples, rows, cols), lambda s, tile: (0, 0, 2 * chip(s, tile) + lax.rem(tile[0], 2))),
+                pl.BlockSpec((samples, rows, cols), lambda s, tile: (0, 0, chip(s, tile))),
             ]
             + [full(x) for x in small]
             + [full(x) for x in pars]
@@ -539,7 +540,7 @@
             ],
         ),
         compiler_params=params_of(),
-    )(place, cam_table, own, got, *small, *pars, *vises)
+    )(tile, own, got, *small, *pars, *vises)
 
 
 def solve_call(low, par, rights):
@@ -553,64 +554,168 @@
     )(low, par, *rights)
 
 
-def shared_tables(lights, views, halves, echoes, first, held):
-    samples = halves.shape[1]
-    tiled = jnp.tile(lights, (1, CAMS))
-    ones = jnp.ones((1, samples), f32)
-    high = jnp.concatenate([ones, halves], axis=0)
-    lobe = thirds(jnp.concatenate([halves, ones], axis=0))
-    lobe = jnp.concatenate([lobe[k] for k in (0, 0, 1, 0, 1, 2)], axis=0)
-    cam = jnp.arange(samples, dtype=jnp.int32)[None] // LIGHTS
-    one_hot = (cam == jnp.arange(CAMS, dtype=jnp.int32)[:, None]).astype(f32)
-    pad = jnp.zeros((8, samples), f32)
-    mixed = [high[i : i + 1] * low for i in range(4) for low in (tiled[0:1], tiled[1:2], tiled[2:3], echoes)]
-    quads = (cam % 4 == jnp.arange(4, dtype=jnp.int32)[:, None]).astype(f32)
-    peaks = [quads[c : c + 1] * high for c in range(4)]
-    square = [high[i : i + 1] * high[j : j + 1] for i in range(4) for j in range(i, 4)]
-
-    def here(x):
-        return lax.dynamic_slice_in_dim(x, first, held, axis=1)
-
+def exact(a, b, sides):
+    return lax.dot_general(
+        a, b, (sides, ((), ())), precision=lax.Precision.HIGHEST, preferred_element_type=f32
+    )
+
+
+def iota(shape, axis):
+    return lax.broadcasted_iota(jnp.int32, shape, axis)
+
+
+def pick(test):
+    return jnp.where(test, 1.0, 0.0).astype(f32)
+
+
+def setup_kernel(
+    tile_ref, light_ref, view_ref,
+    near_ref, cams_ref, lobe_ref, mixed_ref, square_ref,
+    here_ref, shade_ref, plain_ref, peak_ref, slab_ref, light_scr, view_scr,
+):
+    samples = lobe_ref.shape[0]
+    held = here_ref.shape[0]
     cams = held // LIGHTS
-    local = one_hot[:cams, :held]
-    shade = thirds(jnp.concatenate([tiled, ones, echoes], axis=0))
-    shade = here(jnp.concatenate([shade[0], shade[0], shade[1]], axis=0))
-    near = jnp.concatenate([ones, tiled], axis=0)[:, :held]
-    return {
-        "lobe": jnp.concatenate([lobe, one_hot, pad], axis=0).T.astype(bf16),
-        "mixed": jnp.concatenate(mixed + peaks, axis=0),
-        "square": jnp.concatenate(square + [jnp.zeros((6, samples), f32)], axis=0),
-        "lobe_here": jnp.concatenate([here(lobe), local, jnp.zeros((8 - cams, held), f32)], axis=0).T.astype(bf16),
-        "shade": jnp.concatenate([shade, local, local, jnp.zeros((17 - 2 * cams, held), f32)], axis=0).T.astype(bf16),
-        "plain": (local[:, None, :] * near[None]).reshape(4 * cams, held),
-        "peak": jnp.concatenate([here(high), jnp.zeros((4, held), f32)], axis=0),
-    }
-
-
-def camera_table(views, lights, gains):
-    near = jnp.concatenate([lights, jnp.ones((1, LIGHTS), f32)], axis=0)
-    gram = jnp.sum(near[:, None] * near[None] * (gains * gains), axis=-1)
-    spread = jnp.sum(gram[:3, :3, None] * views[None], axis=1)
-    echo_sq = jnp.sum(spread * views, axis=0, keepdims=True)
-    lit = jnp.sum(gram[:3, 3:4] * views, axis=0, keepdims=True)
-    return jnp.concatenate([views, echo_sq, lit, gram.reshape(1, 16)], axis=0)
+    first = (tile_ref[0] // 2) * cams
+
+    def unit(raw_ref, scr):
+        scr[...] = jnp.zeros(scr.shape, f32)
+        scr[0:3, :] = raw_ref[...]
+        scr[2:3, :] = scr[2:3, :] + lift_z
+        lifted = scr[...]
+        return lifted / jnp.sqrt(jnp.sum(lifted * lifted, axis=0, keepdims=True))
+
+    lights = unit(light_ref, light_scr)
+    views = unit(view_ref, view_scr)
+    near = jnp.where(iota(lights.shape, 0) == 3, 1.0, lights)
+    near_ref[...] = near
+    cams_ref[...] = views
+
+    def across(count, start):
+        at_light = pick(iota((LIGHTS, count), 1) % LIGHTS == iota((LIGHTS, count), 0))
+        at_view = pick(iota((CAMS, count), 1) // LIGHTS + start == iota((CAMS, count), 0))
+        wide = exact(near, at_light, ((1,), (0,)))
+        view = exact(views, at_view, ((1,), (0,)))
+        row = iota((8, count), 0)
+        raw = jnp.where(row < 3, wide + view, 0.0)
+        half = raw / jnp.sqrt(jnp.sum(raw * raw, axis=0, keepdims=True))
+        echo = jnp.sum(wide * view, axis=0, keepdims=True)
+        return wide, half, echo
+
+    def down(count, start):
+        at_light = pick(iota((count, LIGHTS), 0) % LIGHTS == iota((count, LIGHTS), 1))
+        at_view = pick(iota((count, CAMS), 0) // LIGHTS + start == iota((count, CAMS), 1))
+        tall = exact(at_light, near, ((1,), (1,)))
+        view = exact(at_view, views, ((1,), (1,)))
+        lane = iota((count, 8), 1)
+        raw = jnp.where(lane < 3, tall + view, 0.0)
+        half = raw / jnp.sqrt(jnp.sum(raw * raw, axis=1, keepdims=True))
+        half = jnp.where(lane == 3, 1.0, half)
+        echo = jnp.sum(tall * view, axis=1, keepdims=True)
+        return half, jnp.where(lane == 4, echo, tall)
+
+    def spread(values, width, depth, order):
+        lane = iota((8, depth), 1)
+        out = None
+        for which in range(max(order) + 1):
+            head = values.astype(bf16)
+            values = values - head.astype(f32)
+            group = None
+            for g, k in enumerate(order):
+                if k == which:
+                    hit = lane // width == g
+                    group = hit if group is None else jnp.logical_or(group, hit)
+            place = pick(jnp.logical_and(group, lane % width == iota((8, depth), 0)))
+            place = jnp.where(iota((8, depth), 0) < width, place, 0.0).astype(bf16)
+            got = dot(head, place)
+            out = got if out is None else out + got
+        return out
+
+    wide, half, echo = across(samples, 0)
+    high = [jnp.ones((1, samples), f32)] + [half[k : k + 1] for k in range(3)]
+    low = [wide[k : k + 1] for k in range(3)] + [echo]
+    which = iota((1, samples), 1) // LIGHTS % 4
+    for i in range(4):
+        for j in range(4):
+            mixed_ref[4 * i + j : 4 * i + j + 1, :] = high[i] * low[j]
+            mixed_ref[16 + 4 * i + j : 17 + 4 * i + j, :] = jnp.where(which == i, high[j], 0.0)
+    at = 0
+    square_ref[8:16, :] = jnp.zeros((8, samples), f32)
+    for i in range(4):
+        for j in range(i, 4):
+            square_ref[at : at + 1, :] = high[i] * high[j]
+            at += 1
+
+    depth = lobe_ref.shape[1]
+    half, _ = down(samples, 0)
+    hot = pick(iota((samples, depth), 0) // LIGHTS + 24 == iota((samples, depth), 1))
+    lobe_ref[...] = (spread(half, 4, depth, (0, 0, 1, 0, 1, 2)) + hot).astype(bf16)
+
+    half, tall = down(held, first)
+    cam = iota((held, 32), 0) // LIGHTS
+    lane = iota((held, 32), 1)
+    hot = pick(cam + 24 == lane)
+    here_ref[...] = (spread(half, 4, 32, (0, 0, 1, 0, 1, 2)) + hot).astype(bf16)
+    hot = pick(cam + 15 == lane) + pick(cam + (15 + cams) == lane)
+    shade_ref[...] = (spread(tall, 5, 32, (0, 0, 1)) + hot).astype(bf16)
+
+    wide, half, _ = across(held, first)
+    peak_ref[...] = jnp.zeros(peak_ref.shape, f32)
+    peak_ref[0:1, :] = jnp.ones((1, held), f32)
+    plain_ref[...] = jnp.zeros(plain_ref.shape, f32)
+    for k in range(3):
+        peak_ref[k + 1 : k + 2, :] = half[k : k + 1]
+    which = iota((1, held), 1) // LIGHTS
+    for c in range(cams):
+        plain_ref[4 * c : 4 * c + 1, :] = pick(which == c)
+        for k in range(3):
+            plain_ref[4 * c + 1 + k : 4 * c + 2 + k, :] = jnp.where(which == c, wide[k : k + 1], 0.0)
+        mine = jnp.sum(jnp.where(iota(views.shape, 1) == first + c, views, 0.0), axis=1, keepdims=True)
+        slab_ref[8 * c : 8 * c + 8, :] = jnp.broadcast_to(mine, (8, LANES))
+
+
+TABLES = ("near", "cams", "lobe", "mixed", "square", "here", "shade", "plain", "peak", "slab")
+
+
+def setup_call(tile, light_directions, view_dirs, held):
+    samples = CAMS * LIGHTS
+    cams = held // LIGHTS
+    count = max(8, 4 * cams)
+    shapes = [
+        ((8, LIGHTS), f32), ((8, CAMS), f32), ((samples, 48), bf16), ((32, samples), f32),
+        ((16, samples), f32), ((held, 32), bf16), ((held, 32), bf16), ((count, held), f32),
+        ((8, held), f32), ((8 * cams, LANES), f32),
+    ]
+    outs = pl.pallas_call(
+        setup_kernel,
+        name="tables",
+        out_shape=[jax.ShapeDtypeStruct(a, b) for a, b in shapes],
+        in_specs=[smem(), vmem(), vmem()],
+        out_specs=[vmem()] * len(shapes),
+        scratch_shapes=[pltpu.VMEM((8, LIGHTS), f32), pltpu.VMEM((8, CAMS), f32)],
+        compiler_params=params_of(),
+    )(tile, light_directions, view_dirs)
+    return dict(zip(TABLES, outs))
 
 
 def shifted(x, by, nz):
     return lax.ppermute(x, "tile", [(2 * z + c, 2 * ((z + by) % nz) + c) for z in range(nz) for c in range(2)])
 
 
-def padded_2(cells, sides, width):
-    for axis, dim in sides:
+def padded_2(cells, sides):
+    for axis, dim, width in sides:
         count = lax.axis_size(axis)
         ends = count - 1
+        size = cells.shape[dim]
         head = lax.slice_in_dim(cells, 0, width, axis=dim)
-        tail = lax.slice_in_dim(cells, cells.shape[dim] - width, cells.shape[dim], axis=dim)
+        tail = lax.slice_in_dim(cells, size - width, size, axis=dim)
+        before = lax.ppermute(tail, axis, [(i, i + 1) for i in range(ends)])
+        after = lax.ppermute(head, axis, [(i + 1, i) for i in range(ends)])
         cells = jnp.concatenate(
             [
-                lax.ppermute(tail, axis, [(i, i + 1) for i in range(ends)]),
+                lax.slice_in_dim(before, width - 1, width, axis=dim),
                 cells,
-                lax.ppermute(head, axis, [(i + 1, i) for i in range(ends)]),
+                lax.slice_in_dim(after, 0, 1, axis=dim),
             ],
             axis=dim,
         )
@@ -620,7 +725,7 @@
 def smooth_tilts(tilt):
     rows = tilt.shape[1]
     cols = tilt.shape[2]
-    padded = padded_2(tilt, (("grp", 1), ("tile", 2)), 1)
+    padded = padded_2(tilt, (("grp", 1, 1), ("tile", 2, LANES)))
     boxed = jnp.zeros(tilt.shape, f32)
     for i in range(3):
         for j in range(3):
@@ -644,39 +749,31 @@
     tiles = lax.axis_size("tile")
     nz = tiles // 2
     tile = lax.axis_index("tile")
-    chip, core = tile // 2, tile % 2
+    core = tile % 2
     held = 2 * samples
-    cams = held // LIGHTS
 
     split = observed.reshape(samples, rows, nz, 2, cols)
     send = lax.dynamic_index_in_dim(split, 1 - core, axis=3, keepdims=False).reshape(samples, rows, nz * cols)
     got = lax.ppermute(send, "tile", [(i, i ^ 1) for i in range(tiles)])
     first = jnp.concatenate([params_start, visible.astype(f32)[None]], axis=0)
     blocks = [first] + [shifted(first, s, nz) for s in range(1, nz)]
-    vises = [b[8].astype(jnp.int32) for b in blocks]
-    place = jnp.stack([2 * ((chip - s) % nz) + core for s in range(nz)] + [core]).astype(jnp.int32)
-
-    lights, views, halves, echoes = geometry(light_directions, view_dirs)
-    tables = shared_tables(lights, views, halves, echoes, chip * held, held)
-    near_views = lax.dynamic_slice_in_dim(views, chip * cams, cams, axis=1)
-    near_table = jnp.concatenate([near_views, jnp.full((1, cams), chip * cams, jnp.int32).astype(f32)], axis=0)
+    vises = blocks
+    here = tile.astype(jnp.int32).reshape(1)
+    tables = setup_call(here, light_directions, view_dirs, held)
 
     params = params_start
-    gains = gains_start
+    gains = gains_start.reshape(1, LIGHTS)
     for iteration in range(ITERS):
-        row = jnp.tile(gains[None], (1, CAMS))
-        low = normal_call(camera_table(views, lights, gains), params, visible, row, tables)
-        *rights, light = sample_call(
-            place, near_table, observed, got, row[:, :held], tables, blocks, vises
-        )
+        low = normal_call(params, visible, gains, tables)
+        *rights, light = sample_call(here, observed, got, gains, tables, blocks, vises)
         moved = [rights[0]] + [shifted(rights[s], -s, nz) for s in range(1, nz)]
         params = solve_call(low, params, moved)
-        sums = summed_everywhere(light[0].reshape(2, LIGHTS))
-        gains = gains + (sums[0] - gains * sums[1]) / (sums[1] + 1.0)
+        sums = summed_everywhere(light)
+        gains = gains + (sums[0:1] - gains * sums[1:2]) / (sums[1:2] + 1.0)
         params = jnp.concatenate([smooth_tilts(params[:2]), params[2:]], axis=0)
         if iteration + 1 < ITERS:
             blocks = [params] + [shifted(params, s, nz) for s in range(1, nz)]
-    return params, gains
+    return params, gains.reshape(LIGHTS)
 
 
 def solution(mesh):

time: 174 us -> 128 us (0.74)
  local copies, waits for them, and re-layouts: 36.5 us -> 1.65 us
  other arithmetic: 14.9 us -> 2.43 us
  Pallas kernels: 44.4 us -> 34.8 us
  waiting for transfers between devices: 16.6 us -> 24.2 us
  starting transfers between devices: 58.4 us -> 63.4 us
    unnamed x108 -> x12, local copies, waits for them, and re-layouts: 13.4 us -> 0.03 us
    pallas_call x2, Pallas kernels: 26.5 us -> 18.5 us  [sample_call(): pl.pallas_call(functools.partial(sample_kernel, parts=parts), name='sampl...]
    ppermute x10, starting transfers between devices: 11.9 us -> 19.8 us  [summed_everywhere(): x = x + lax.ppermute(x, axis, [(i, i ^ bit) for i in range(size)])]
    concatenate x9 -> x0, local copies, waits for them, and re-layouts: 7.73 us -> none  [the longest x1 2.97 us: shared_tables(): jnp.concatenate(mixed + peaks, axis=0)]
    slice x19 -> x6, local copies, waits for them, and re-layouts: 5.96 us -> 0.17 us  [the longest x2 0.14 us: padded_2(): lax.slice_in_dim(before, width - 1, width, axis=dim)]
    ppermute x12, waiting for transfers between devices: 0.77 us -> 5.41 us  [shifted(): lax.ppermute(x, 'tile', [(2 * z + c, 2 * ((z + by) % nz) + c) for z in ra...]
    mul x5 -> x0, other arithmetic: 4.56 us -> none  [the longest x2 1.35 us: shared_tables(): high[i:i + 1] * high[j:j + 1]]
    ppermute x10, waiting for transfers between devices: 8.91 us -> 13.2 us  [summed_everywhere(): x = x + lax.ppermute(x, axis, [(i, i ^ bit) for i in range(size)])]
  transfers between devices with their start and end apart: 31 -> 31, of which waited for: 10 -> 15; matrix products, arithmetic and copies ran while one was open for 20% -> 1% of each run, Pallas kernels for 10% -> 13%
where the time goes in v2:
time: 128 us; the launch traced here: 127 us
  starting transfers between devices  63.4 us (50%)
  Pallas kernels  34.8 us (27%)
  waiting for transfers between devices  24.2 us (19%)
  other arithmetic  2.43 us (2%)
  local copies, waits for them, and re-layouts  1.65 us (1%)
    ppermute x4, starting transfers between devices, padded_2(): before = lax.ppermute(tail, axis, [(i, i + 1) for i in range(ends)])  21.4 us
    ppermute x10, starting transfers between devices, summed_everywhere(): x = x + lax.ppermute(x, axis, [(i, i ^ bit) for i in range(size)])  19.8 us
    pallas_call x2, Pallas kernels, sample_call(): pl.pallas_call(functools.partial(sample_kernel, parts=parts), name='sampl...  18.5 us
    ppermute x12, starting transfers between devices, shifted(): lax.ppermute(x, 'tile', [(2 * z + c, 2 * ((z + by) % nz) + c) for z in ra...  15.7 us
    pallas_call x2, Pallas kernels, normal_call(): pl.pallas_call(normal_kernel, name='normal_factor', out_shape=jax.ShapeDt...  14.3 us
    ppermute x10, waiting for transfers between devices, summed_everywhere(): x = x + lax.ppermute(x, axis, [(i, i ^ bit) for i in range(size)])  13.2 us
    ppermute x4, starting transfers between devices, padded_2(): after = lax.ppermute(head, axis, [(i + 1, i) for i in range(ends)])  6.43 us
    ppermute x4, waiting for transfers between devices, padded_2(): after = lax.ppermute(head, axis, [(i + 1, i) for i in range(ends)])  5.54 us
  transfers between devices with their start and end apart: 31, of which 15 were waited for; matrix products, arithmetic and copies ran while one was open for 1% of the time, Pallas kernels for 13%

profile of v2, /device:TPU:1, one launch (start us, length us, event | category | flops | bytes accessed | tf_op | source)
XLA Modules:
  0.0 127.5 jit_solution(300832684052288190)
XLA Ops:
  0.7 1.4 %constant_dynamic-slice_fusion = bf16[64,8,4,1,256]{4,1,3,2,0:T(8,128)(2,1)S(1)} fusion(bf16[64,8,4,2,256]{4,1,3,2,0:T(8,128)(2,1)} %bitcast.13, s32[]{:T(128)S(6)} %select_n.12), kind=kLoop, calls=%fused_computation.36 | loop fusion | bytes 2097156 | tf_op jit(solution)/shard_map/jit(dynamic_index_in_dim)/dynamic_slice | solution.py:756
  2.3 0.8 pad_maximum_fusion.refs_0_.refs_4_
  3.1 2.7 %collective-permute-start.1 = (f32[9,8,256]{2,1,0:T(8,128)S(1)}, f32[9,8,256]{2,1,0:T(8,128)S(1)}, u32[]{:S(2)}, u32[]{:S(2)}) collective-permute-start(f32[9,8,256]{2,1,0:T(8,128)S(1)} %pad_maximum_fusion.refs_0_.refs_4_), channel_id=1, source_target_pairs={{0,2},{1,3},{2,4},{3,5},{4,6},{5,7},{6,0},{7,1},{8,10},{9,11},{10,... | collective-permute-start | bytes 221192 | tf_op jit(solution)/shard_map/ppermute | solution.py:702
  5.9 2.3 %collective-permute-start.2 = (f32[9,8,256]{2,1,0:T(8,128)S(1)}, f32[9,8,256]{2,1,0:T(8,128)S(1)}, u32[]{:S(2)}, u32[]{:S(2)}) collective-permute-start(f32[9,8,256]{2,1,0:T(8,128)S(1)} %pad_maximum_fusion.refs_0_.refs_4_), channel_id=1, source_target_pairs={{0,4},{1,5},{2,6},{3,7},{4,0},{5,1},{6,2},{7,3},{8,12},{9,13},{10,... | collective-permute-start | bytes 221192 | tf_op jit(solution)/shard_map/ppermute | solution.py:702
  8.2 1.1 collective-permute-start.3
  9.2 1.8 %tables.1 = (f32[8,32]{1,0:T(8,128)S(1)}, f32[8,16]{1,0:T(8,128)S(1)}, bf16[512,48]{1,0:T(8,128)(2,1)S(1)}, f32[32,512]{1,0:T(8,128)S(1)}, f32[16,512]{1,0:T(8,1...) custom-call(s32[1]{0:T(128)} %bitcast.1.tile_ref, ...), custom_call_target="tpu_custom_call" | custom-call | tf_op jit(solution)/shard_map/tables/pallas_call | solution.py:689
  11.1 2.7 %collective-permute-done.2.refs_2_.refs_6_ = f32[9,8,256]{2,1,0:T(8,128)S(1)} collective-permute-done((f32[9,8,256]{2,1,0:T(8,128)S(1)}, f32[9,8,256]{2,1,0:T(8,128)S(1)}, u32[]{:S(2)}, u32[]{:S(2)}) %collective-permute-start.2) | collective-permute-done | bytes 73760 | tf_op jit(solution)/shard_map/ppermute | solution.py:702
  13.8 9.3 %sample_sums.2 = (f32[8,8,256]{2,1,0:T(8,128)S(1)}, f32[8,8,256]{2,1,0:T(8,128)S(1)}, f32[8,8,256]{2,1,0:T(8,128)S(1)}, f32[8,8,256]{2,1,0:T(8,128)S(1)}, f32[2,32]{1,0:T(2,128)S(1)}) custom-call(s32[1]{0:T(128)} %bitcast.1.tile_ref, bf16[64,8,2048]{2,1,0:T(8,128)(2,1)S(1)} %copy-done, bf16[64,8,1024]{2,1,0:T(8,128)(2,1)S(1)} %collective-permute-done.got_ref, ...), custom_call_target="tpu_custom_call" | custom-call | tf_op jit(solution)/shard_map/sample_sums/pallas_call | solution.py:518
  23.1 2.6 %collective-permute-start.4 = (f32[8,8,256]{2,1,0:T(8,128)S(1)}, f32[8,8,256]{2,1,0:T(8,128)S(1)}, u32[]{:S(2)}, u32[]{:S(2)}) collective-permute-start(f32[8,8,256]{2,1,0:T(8,128)S(1)} %get-tuple-element.33), channel_id=1, source_target_pairs={{0,6},{1,7},{2,0},{3,1},{4,2},{5,3},{6,4},{7,5},{8,14},{9,15},{10,... | collective-permute-start | bytes 196616 | tf_op jit(solution)/shard_map/ppermute | solution.py:702
  26.2 7.1 %normal_factor.2.low_ref = f32[44,8,256]{2,1,0:T(8,128)S(1)} custom-call(f32[8,8,256]{2,1,0:T(8,128)S(1)} %copy-done.1, s32[8,256]{1,0:T(8,128)S(1)} %copy-done.2, f32[1,32]{1,0:T(1,128)S(1)} %bitcast.15, f32[8,32]{1,0:T(8,128)S(1)} %get-tuple-element.22.near_ref, f32[8,16]{1,0:T(8,128)S(1)} %get-tuple-element.23.cams_ref, ...), custom_call_target="tpu_custom_call" | custom-call | tf_op jit(solution)/shard_map/normal_factor/pallas_call | solution.py:484
  33.5 3.2 %collective-permute-start.7 = (f32[2,1,256]{2,1,0:T(1,128)S(1)}, f32[2,1,256]{2,1,0:T(1,128)S(1)}, u32[]{:S(2)}, u32[]{:S(2)}) collective-permute-start(f32[2,1,256]{2,1,0:T(1,128)S(1)} %get-tuple-element.44), channel_id=1, source_target_pairs={{0,8},{8,16},{16,24},{1,9},{9,17},{17,25},{2,10},{10,18},{18,26},{... | collective-permute-start | bytes 6152 | tf_op jit(solution)/shard_map/ppermute | solution.py:712
  36.6 1.3 %collective-permute-start.8 = (f32[2,1,256]{2,1,0:T(1,128)S(1)}, f32[2,1,256]{2,1,0:T(1,128)S(1)}, u32[]{:S(2)}, u32[]{:S(2)}) collective-permute-start(f32[2,1,256]{2,1,0:T(1,128)S(1)} %get-tuple-element.45), channel_id=1, source_target_pairs={{8,0},{16,8},{24,16},{9,1},{17,9},{25,17},{10,2},{18,10},{26,18},{... | collective-permute-start | bytes 6152 | tf_op jit(solution)/shard_map/ppermute | solution.py:713
  38.0 3.0 %collective-permute-done.8 = f32[2,1,256]{2,1,0:T(1,128)S(1)} collective-permute-done((f32[2,1,256]{2,1,0:T(1,128)S(1)}, f32[2,1,256]{2,1,0:T(1,128)S(1)}, u32[]{:S(2)}, u32[]{:S(2)}) %collective-permute-start.8) | collective-permute-done | bytes 2080 | tf_op jit(solution)/shard_map/ppermute | solution.py:713
  41.0 7.0 %collective-permute-start.9 = (f32[2,10,128]{2,1,0:T(8,128)S(1)}, f32[2,10,128]{2,1,0:T(8,128)S(1)}, u32[]{:S(2)}, u32[]{:S(2)}) collective-permute-start(f32[2,10,128]{2,1,0:T(8,128)S(1)} %get-tuple-element.48), channel_id=1, source_target_pairs={{0,1},{1,2},{2,3},{3,4},{4,5},{5,6},{6,7},{8,9},{9,10},{10,11},{11... | collective-permute-start | bytes 30728 | tf_op jit(solution)/shard_map/ppermute | solution.py:712
  48.0 1.9 %collective-permute-start.10 = (f32[2,10,128]{2,1,0:T(8,128)S(1)}, f32[2,10,128]{2,1,0:T(8,128)S(1)}, u32[]{:S(2)}, u32[]{:S(2)}) collective-permute-start(f32[2,10,128]{2,1,0:T(8,128)S(1)} %get-tuple-element.49), channel_id=1, source_target_pairs={{1,0},{2,1},{3,2},{4,3},{5,4},{6,5},{7,6},{9,8},{10,9},{11,10},{12... | collective-permute-start | bytes 30728 | tf_op jit(solution)/shard_map/ppermute | solution.py:713
  50.0 1.1 collective-permute-done.11
  51.2 1.5 %collective-permute-start.12 = (f32[2,32]{1,0:T(2,128)S(1)}, f32[2,32]{1,0:T(2,128)S(1)}, u32[]{:S(2)}, u32[]{:S(2)}) collective-permute-start(f32[2,32]{1,0:T(2,128)S(1)} %add.116), channel_id=1, source_target_pairs={{0,2},{1,3},{2,0},{3,1},{4,6},{5,7},{6,4},{7,5},{8,10},{9,11},{10,... | collective-permute-start | bytes 776 | tf_op jit(solution)/shard_map/ppermute | solution.py:741
  52.7 1.0 collective-permute-done.12
  53.7 1.0 collective-permute-start.13
  54.7 2.3 %collective-permute-done.13 = f32[2,32]{1,0:T(2,128)S(1)} collective-permute-done((f32[2,32]{1,0:T(2,128)S(1)}, f32[2,32]{1,0:T(2,128)S(1)}, u32[]{:S(2)}, u32[]{:S(2)}) %collective-permute-start.13) | collective-permute-done | bytes 288 | tf_op jit(solution)/shard_map/ppermute | solution.py:741
  57.0 2.1 %collective-permute-start.14 = (f32[2,32]{1,0:T(2,128)S(1)}, f32[2,32]{1,0:T(2,128)S(1)}, u32[]{:S(2)}, u32[]{:S(2)}) collective-permute-start(f32[2,32]{1,0:T(2,128)S(1)} %add.118), channel_id=1, source_target_pairs={{0,8},{8,0},{16,24},{24,16},{1,9},{9,1},{17,25},{25,17},{2,10},{10... | collective-permute-start | bytes 776 | tf_op jit(solution)/shard_map/ppermute | solution.py:741
  59.1 1.0 collective-permute-done.14
  60.1 0.6 collective-permute-start.15
  60.6 1.8 %collective-permute-done.15 = f32[2,32]{1,0:T(2,128)S(1)} collective-permute-done((f32[2,32]{1,0:T(2,128)S(1)}, f32[2,32]{1,0:T(2,128)S(1)}, u32[]{:S(2)}, u32[]{:S(2)}) %collective-permute-start.15) | collective-permute-done | bytes 288 | tf_op jit(solution)/shard_map/ppermute | solution.py:741
  62.8 1.5 %collective-permute-start.16 = (f32[8,8,256]{2,1,0:T(8,128)S(1)}, f32[8,8,256]{2,1,0:T(8,128)S(1)}, u32[]{:S(2)}, u32[]{:S(2)}) collective-permute-start(f32[8,8,256]{2,1,0:T(8,128)S(1)} %pad_maximum_fusion.1.par_ref.refs_0_), channel_id=1, source_target_pairs={{0,2},{1,3},{2,4},{3,5},{4,6},{5,7},{6,0},{7,1},{8,10},{9,11},{10,... | collective-permute-start | bytes 196616 | tf_op jit(solution)/shard_map/ppermute | solution.py:702
  64.3 1.0 collective-permute-start.17
  65.3 1.1 collective-permute-start.18
  66.5 1.3 %collective-permute-done.16.refs_1_ = f32[8,8,256]{2,1,0:T(8,128)S(1)} collective-permute-done((f32[8,8,256]{2,1,0:T(8,128)S(1)}, f32[8,8,256]{2,1,0:T(8,128)S(1)}, u32[]{:S(2)}, u32[]{:S(2)}) %collective-permute-start.16) | collective-permute-done | bytes 65568 | tf_op jit(solution)/shard_map/ppermute | solution.py:702
  67.8 1.4 %collective-permute-done.17.refs_2_ = f32[8,8,256]{2,1,0:T(8,128)S(1)} collective-permute-done((f32[8,8,256]{2,1,0:T(8,128)S(1)}, f32[8,8,256]{2,1,0:T(8,128)S(1)}, u32[]{:S(2)}, u32[]{:S(2)}) %collective-permute-start.17) | collective-permute-done | bytes 65568 | tf_op jit(solution)/shard_map/ppermute | solution.py:702
  69.2 9.2 %sample_sums.3 = (f32[8,8,256]{2,1,0:T(8,128)S(1)}, f32[8,8,256]{2,1,0:T(8,128)S(1)}, f32[8,8,256]{2,1,0:T(8,128)S(1)}, f32[8,8,256]{2,1,0:T(8,128)S(1)}, f32[2,32]{1,0:T(2,128)S(1)}) custom-call(s32[1]{0:T(128)} %bitcast.1.tile_ref, bf16[64,8,2048]{2,1,0:T(8,128)(2,1)S(1)} %copy-done, bf16[64,8,1024]{2,1,0:T(8,128)(2,1)S(1)} %collective-permute-done.got_ref, ...), custom_call_target="tpu_custom_call" | custom-call | tf_op jit(solution)/shard_map/sample_sums/pallas_call | solution.py:518
  78.4 2.4 %collective-permute-start.19 = (f32[8,8,256]{2,1,0:T(8,128)S(1)}, f32[8,8,256]{2,1,0:T(8,128)S(1)}, u32[]{:S(2)}, u32[]{:S(2)}) collective-permute-start(f32[8,8,256]{2,1,0:T(8,128)S(1)} %get-tuple-element.38), channel_id=1, source_target_pairs={{0,6},{1,7},{2,0},{3,1},{4,2},{5,3},{6,4},{7,5},{8,14},{9,15},{10,... | collective-permute-start | bytes 196616 | tf_op jit(solution)/shard_map/ppermute | solution.py:702
  81.2 7.1 %normal_factor.3.low_ref = f32[44,8,256]{2,1,0:T(8,128)S(1)} custom-call(f32[8,8,256]{2,1,0:T(8,128)S(1)} %pad_maximum_fusion.1.par_ref.refs_0_, s32[8,256]{1,0:T(8,128)S(1)} %copy-done.2, f32[1,32]{1,0:T(1,128)S(1)} %divide_add_fusion.gain_ref, f32[8,32]{1,0:T(8,128)S(1)} %get-tuple-element.22.near_ref, f32[8,16]{1,0:T(8,128)S(1)} %get-tuple-element.23.cams_ref, ...), custom_call_target="tpu_custom_call" | custom-call | tf_op jit(solution)/shard_map/normal_factor/pallas_call | solution.py:484
  88.4 3.4 %collective-permute-start.22 = (f32[2,1,256]{2,1,0:T(1,128)S(1)}, f32[2,1,256]{2,1,0:T(1,128)S(1)}, u32[]{:S(2)}, u32[]{:S(2)}) collective-permute-start(f32[2,1,256]{2,1,0:T(1,128)S(1)} %get-tuple-element.42), channel_id=1, source_target_pairs={{0,8},{8,16},{16,24},{1,9},{9,17},{17,25},{2,10},{10,18},{18,26},{... | collective-permute-start | bytes 6152 | tf_op jit(solution)/shard_map/ppermute | solution.py:712
  91.8 1.3 %collective-permute-start.23 = (f32[2,1,256]{2,1,0:T(1,128)S(1)}, f32[2,1,256]{2,1,0:T(1,128)S(1)}, u32[]{:S(2)}, u32[]{:S(2)}) collective-permute-start(f32[2,1,256]{2,1,0:T(1,128)S(1)} %get-tuple-element.43), channel_id=1, source_target_pairs={{8,0},{16,8},{24,16},{9,1},{17,9},{25,17},{10,2},{18,10},{26,18},{... | collective-permute-start | bytes 6152 | tf_op jit(solution)/shard_map/ppermute | solution.py:713
  93.1 7.2 %collective-permute-start.26 = (f32[2,32]{1,0:T(2,128)S(1)}, f32[2,32]{1,0:T(2,128)S(1)}, u32[]{:S(2)}, u32[]{:S(2)}) collective-permute-start(f32[2,32]{1,0:T(2,128)S(1)} %get-tuple-element.41), channel_id=1, source_target_pairs={{0,1},{1,0},{2,3},{3,2},{4,5},{5,4},{6,7},{7,6},{8,9},{9,8},{10,11... | collective-permute-start | bytes 776 | tf_op jit(solution)/shard_map/ppermute | solution.py:741
  100.3 0.8 collective-permute-done.26
  101.1 2.5 %collective-permute-start.27 = (f32[2,32]{1,0:T(2,128)S(1)}, f32[2,32]{1,0:T(2,128)S(1)}, u32[]{:S(2)}, u32[]{:S(2)}) collective-permute-start(f32[2,32]{1,0:T(2,128)S(1)} %add.132), channel_id=1, source_target_pairs={{0,2},{1,3},{2,0},{3,1},{4,6},{5,7},{6,4},{7,5},{8,10},{9,11},{10,... | collective-permute-start | bytes 776 | tf_op jit(solution)/shard_map/ppermute | solution.py:741
  103.6 1.0 collective-permute-done.27
  104.6 0.9 collective-permute-start.28
  105.5 2.4 %collective-permute-done.28 = f32[2,32]{1,0:T(2,128)S(1)} collective-permute-done((f32[2,32]{1,0:T(2,128)S(1)}, f32[2,32]{1,0:T(2,128)S(1)}, u32[]{:S(2)}, u32[]{:S(2)}) %collective-permute-start.28) | collective-permute-done | bytes 288 | tf_op jit(solution)/shard_map/ppermute | solution.py:741
  107.9 2.4 %collective-permute-start.29 = (f32[2,32]{1,0:T(2,128)S(1)}, f32[2,32]{1,0:T(2,128)S(1)}, u32[]{:S(2)}, u32[]{:S(2)}) collective-permute-start(f32[2,32]{1,0:T(2,128)S(1)} %add.134), channel_id=1, source_target_pairs={{0,8},{8,0},{16,24},{24,16},{1,9},{9,1},{17,25},{25,17},{2,10},{10... | collective-permute-start | bytes 776 | tf_op jit(solution)/shard_map/ppermute | solution.py:741
  110.3 1.0 collective-permute-done.29
  111.2 1.5 %collective-permute-start.30 = (f32[2,32]{1,0:T(2,128)S(1)}, f32[2,32]{1,0:T(2,128)S(1)}, u32[]{:S(2)}, u32[]{:S(2)}) collective-permute-start(f32[2,32]{1,0:T(2,128)S(1)} %add.135), channel_id=1, source_target_pairs={{0,16},{8,24},{16,0},{24,8},{1,17},{9,25},{17,1},{25,9},{2,18},{10... | collective-permute-start | bytes 776 | tf_op jit(solution)/shard_map/ppermute | solution.py:741
  112.7 1.0 collective-permute-done.30
  113.7 7.9 %collective-permute-start.24 = (f32[2,10,128]{2,1,0:T(8,128)S(1)}, f32[2,10,128]{2,1,0:T(8,128)S(1)}, u32[]{:S(2)}, u32[]{:S(2)}) collective-permute-start(f32[2,10,128]{2,1,0:T(8,128)S(1)} %get-tuple-element.46), channel_id=1, source_target_pairs={{0,1},{1,2},{2,3},{3,4},{4,5},{5,6},{6,7},{8,9},{9,10},{10,11},{11... | collective-permute-start | bytes 30728 | tf_op jit(solution)/shard_map/ppermute | solution.py:712
  121.6 1.9 %collective-permute-start.25 = (f32[2,10,128]{2,1,0:T(8,128)S(1)}, f32[2,10,128]{2,1,0:T(8,128)S(1)}, u32[]{:S(2)}, u32[]{:S(2)}) collective-permute-start(f32[2,10,128]{2,1,0:T(8,128)S(1)} %get-tuple-element.47), channel_id=1, source_target_pairs={{1,0},{2,1},{3,2},{4,3},{5,4},{6,5},{7,6},{9,8},{10,9},{11,10},{12... | collective-permute-start | bytes 30728 | tf_op jit(solution)/shard_map/ppermute | solution.py:713
  124.1 2.5 %collective-permute-done.25 = f32[2,10,128]{2,1,0:T(8,128)S(1)} collective-permute-done((f32[2,10,128]{2,1,0:T(8,128)S(1)}, f32[2,10,128]{2,1,0:T(8,128)S(1)}, u32[]{:S(2)}, u32[]{:S(2)}) %collective-permute-start.25) | collective-permute-done | bytes 10272 | tf_op jit(solution)/shard_map/ppermute | solution.py:713
  126.9 0.6 pad_maximum_fusion.2
  (66 shorter events, 2.4 us)
Async XLA Ops:
  0.6 13.2 %copy-start = (bf16[64,8,2048]{2,1,0:T(8,128)(2,1)S(1)}, bf16[64,8,2048]{2,1,0:T(8,128)(2,1)}, u32[]{:S(2)}) copy-start(bf16[64,8,2048]{2,1,0:T(8,128)(2,1)} %own_ref.3) | copy-start | bytes 6291460
  0.6 1.6 %copy-start.2 = (s32[8,256]{1,0:T(8,128)S(1)}, s32[8,256]{1,0:T(8,128)}, u32[]{:S(2)}) copy-start(s32[8,256]{1,0:T(8,128)} %vis_ref.3) | copy-start | bytes 24580
  0.7 8.6 %copy-start.5 = (f32[3,16]{1,0:T(4,128)S(1)}, f32[3,16]{1,0:T(4,128)}, u32[]{:S(2)}) copy-start(f32[3,16]{1,0:T(4,128)} %view_ref.1) | copy-start | bytes 580
  0.7 8.6 %copy-start.4 = (f32[3,32]{1,0:T(4,128)S(1)}, f32[3,32]{1,0:T(4,128)}, u32[]{:S(2)}) copy-start(f32[3,32]{1,0:T(4,128)} %light_ref.1) | copy-start | bytes 1156
  0.7 13.1 %copy-start.3 = (f32[32]{0:T(128)S(1)}, f32[32]{0:T(128)}, u32[]{:S(2)}) copy-start(f32[32]{0:T(128)} %param.11) | copy-start | bytes 388
  2.1 24.1 %copy-start.1 = (f32[8,8,256]{2,1,0:T(8,128)S(1)}, f32[8,8,256]{2,1,0:T(8,128)}, u32[]{:S(2)}) copy-start(f32[8,8,256]{2,1,0:T(8,128)} %par_ref.3) | copy-start | bytes 196612
  2.1 11.7 %collective-permute-start = (bf16[64,8,1024]{2,1,0:T(8,128)(2,1)S(1)}, bf16[64,8,1024]{2,1,0:T(8,128)(2,1)S(1)}, u32[]{:S(2)}, u32[]{:S(2)}) collective-permute-start(bf16[64,8,1024]{2,1,0:T(8,128)(2,1)S(1)} %bitcast.16), channel_id=1, source_target_pairs={{0,1},{1,0},{2,3},{3,2},{4,5},{5,4},{6,7},{7,6},{8,9},{9,8},{10,11... | collective-permute-start | bytes 3145736 | tf_op jit(solution)/shard_map/ppermute | solution.py:757
  3.1 8.0 %collective-permute-start.1 = (f32[9,8,256]{2,1,0:T(8,128)S(1)}, f32[9,8,256]{2,1,0:T(8,128)S(1)}, u32[]{:S(2)}, u32[]{:S(2)}) collective-permute-start(f32[9,8,256]{2,1,0:T(8,128)S(1)} %pad_maximum_fusion.refs_0_.refs_4_), channel_id=1, source_target_pairs={{0,2},{1,3},{2,4},{3,5},{4,6},{5,7},{6,0},{7,1},{8,10},{9,11},{10,... | collective-permute-start | bytes 221192 | tf_op jit(solution)/shard_map/ppermute | solution.py:702
  5.9 7.9 %collective-permute-start.2 = (f32[9,8,256]{2,1,0:T(8,128)S(1)}, f32[9,8,256]{2,1,0:T(8,128)S(1)}, u32[]{:S(2)}, u32[]{:S(2)}) collective-permute-start(f32[9,8,256]{2,1,0:T(8,128)S(1)} %pad_maximum_fusion.refs_0_.refs_4_), channel_id=1, source_target_pairs={{0,4},{1,5},{2,6},{3,7},{4,0},{5,1},{6,2},{7,3},{8,12},{9,13},{10,... | collective-permute-start | bytes 221192 | tf_op jit(solution)/shard_map/ppermute | solution.py:702
  8.2 5.6 %collective-permute-start.3 = (f32[9,8,256]{2,1,0:T(8,128)S(1)}, f32[9,8,256]{2,1,0:T(8,128)S(1)}, u32[]{:S(2)}, u32[]{:S(2)}) collective-permute-start(f32[9,8,256]{2,1,0:T(8,128)S(1)} %pad_maximum_fusion.refs_0_.refs_4_), channel_id=1, source_target_pairs={{0,6},{1,7},{2,0},{3,1},{4,2},{5,3},{6,4},{7,5},{8,14},{9,15},{10,... | collective-permute-start | bytes 221192 | tf_op jit(solution)/shard_map/ppermute | solution.py:702
  23.1 10.2 %collective-permute-start.4 = (f32[8,8,256]{2,1,0:T(8,128)S(1)}, f32[8,8,256]{2,1,0:T(8,128)S(1)}, u32[]{:S(2)}, u32[]{:S(2)}) collective-permute-start(f32[8,8,256]{2,1,0:T(8,128)S(1)} %get-tuple-element.33), channel_id=1, source_target_pairs={{0,6},{1,7},{2,0},{3,1},{4,2},{5,3},{6,4},{7,5},{8,14},{9,15},{10,... | collective-permute-start | bytes 196616 | tf_op jit(solution)/shard_map/ppermute | solution.py:702
  25.7 7.6 %collective-permute-start.5 = (f32[8,8,256]{2,1,0:T(8,128)S(1)}, f32[8,8,256]{2,1,0:T(8,128)S(1)}, u32[]{:S(2)}, u32[]{:S(2)}) collective-permute-start(f32[8,8,256]{2,1,0:T(8,128)S(1)} %get-tuple-element.34), channel_id=1, source_target_pairs={{0,4},{1,5},{2,6},{3,7},{4,0},{5,1},{6,2},{7,3},{8,12},{9,13},{10,... | collective-permute-start | bytes 196616 | tf_op jit(solution)/shard_map/ppermute | solution.py:702
  26.2 7.2 %collective-permute-start.6 = (f32[8,8,256]{2,1,0:T(8,128)S(1)}, f32[8,8,256]{2,1,0:T(8,128)S(1)}, u32[]{:S(2)}, u32[]{:S(2)}) collective-permute-start(f32[8,8,256]{2,1,0:T(8,128)S(1)} %get-tuple-element.35), channel_id=1, source_target_pairs={{0,2},{1,3},{2,4},{3,5},{4,6},{5,7},{6,0},{7,1},{8,10},{9,11},{10,... | collective-permute-start | bytes 196616 | tf_op jit(solution)/shard_map/ppermute | solution.py:702
  33.5 4.5 %collective-permute-start.7 = (f32[2,1,256]{2,1,0:T(1,128)S(1)}, f32[2,1,256]{2,1,0:T(1,128)S(1)}, u32[]{:S(2)}, u32[]{:S(2)}) collective-permute-start(f32[2,1,256]{2,1,0:T(1,128)S(1)} %get-tuple-element.44), channel_id=1, source_target_pairs={{0,8},{8,16},{16,24},{1,9},{9,17},{17,25},{2,10},{10,18},{18,26},{... | collective-permute-start | bytes 6152 | tf_op jit(solution)/shard_map/ppermute | solution.py:712
  36.6 4.3 %collective-permute-start.8 = (f32[2,1,256]{2,1,0:T(1,128)S(1)}, f32[2,1,256]{2,1,0:T(1,128)S(1)}, u32[]{:S(2)}, u32[]{:S(2)}) collective-permute-start(f32[2,1,256]{2,1,0:T(1,128)S(1)} %get-tuple-element.45), channel_id=1, source_target_pairs={{8,0},{16,8},{24,16},{9,1},{17,9},{25,17},{10,2},{18,10},{26,18},{... | collective-permute-start | bytes 6152 | tf_op jit(solution)/shard_map/ppermute | solution.py:713
  41.0 21.5 %collective-permute-start.9 = (f32[2,10,128]{2,1,0:T(8,128)S(1)}, f32[2,10,128]{2,1,0:T(8,128)S(1)}, u32[]{:S(2)}, u32[]{:S(2)}) collective-permute-start(f32[2,10,128]{2,1,0:T(8,128)S(1)} %get-tuple-element.48), channel_id=1, source_target_pairs={{0,1},{1,2},{2,3},{3,4},{4,5},{5,6},{6,7},{8,9},{9,10},{10,11},{11... | collective-permute-start | bytes 30728 | tf_op jit(solution)/shard_map/ppermute | solution.py:712
  48.0 14.5 %collective-permute-start.10 = (f32[2,10,128]{2,1,0:T(8,128)S(1)}, f32[2,10,128]{2,1,0:T(8,128)S(1)}, u32[]{:S(2)}, u32[]{:S(2)}) collective-permute-start(f32[2,10,128]{2,1,0:T(8,128)S(1)} %get-tuple-element.49), channel_id=1, source_target_pairs={{1,0},{2,1},{3,2},{4,3},{5,4},{6,5},{7,6},{9,8},{10,9},{11,10},{12... | collective-permute-start | bytes 30728 | tf_op jit(solution)/shard_map/ppermute | solution.py:713
  50.0 1.2 collective-permute-start.11
  51.2 2.5 %collective-permute-start.12 = (f32[2,32]{1,0:T(2,128)S(1)}, f32[2,32]{1,0:T(2,128)S(1)}, u32[]{:S(2)}, u32[]{:S(2)}) collective-permute-start(f32[2,32]{1,0:T(2,128)S(1)} %add.116), channel_id=1, source_target_pairs={{0,2},{1,3},{2,0},{3,1},{4,6},{5,7},{6,4},{7,5},{8,10},{9,11},{10,... | collective-permute-start | bytes 776 | tf_op jit(solution)/shard_map/ppermute | solution.py:741
  53.7 3.3 %collective-permute-start.13 = (f32[2,32]{1,0:T(2,128)S(1)}, f32[2,32]{1,0:T(2,128)S(1)}, u32[]{:S(2)}, u32[]{:S(2)}) collective-permute-start(f32[2,32]{1,0:T(2,128)S(1)} %add.117), channel_id=1, source_target_pairs={{0,4},{1,5},{2,6},{3,7},{4,0},{5,1},{6,2},{7,3},{8,12},{9,13},{10,... | collective-permute-start | bytes 776 | tf_op jit(solution)/shard_map/ppermute | solution.py:741
  57.0 3.1 %collective-permute-start.14 = (f32[2,32]{1,0:T(2,128)S(1)}, f32[2,32]{1,0:T(2,128)S(1)}, u32[]{:S(2)}, u32[]{:S(2)}) collective-permute-start(f32[2,32]{1,0:T(2,128)S(1)} %add.118), channel_id=1, source_target_pairs={{0,8},{8,0},{16,24},{24,16},{1,9},{9,1},{17,25},{25,17},{2,10},{10... | collective-permute-start | bytes 776 | tf_op jit(solution)/shard_map/ppermute | solution.py:741
  60.1 2.4 %collective-permute-start.15 = (f32[2,32]{1,0:T(2,128)S(1)}, f32[2,32]{1,0:T(2,128)S(1)}, u32[]{:S(2)}, u32[]{:S(2)}) collective-permute-start(f32[2,32]{1,0:T(2,128)S(1)} %add.119), channel_id=1, source_target_pairs={{0,16},{8,24},{16,0},{24,8},{1,17},{9,25},{17,1},{25,9},{2,18},{10... | collective-permute-start | bytes 776 | tf_op jit(solution)/shard_map/ppermute | solution.py:741
  62.8 5.0 %collective-permute-start.16 = (f32[8,8,256]{2,1,0:T(8,128)S(1)}, f32[8,8,256]{2,1,0:T(8,128)S(1)}, u32[]{:S(2)}, u32[]{:S(2)}) collective-permute-start(f32[8,8,256]{2,1,0:T(8,128)S(1)} %pad_maximum_fusion.1.par_ref.refs_0_), channel_id=1, source_target_pairs={{0,2},{1,3},{2,4},{3,5},{4,6},{5,7},{6,0},{7,1},{8,10},{9,11},{10,... | collective-permute-start | bytes 196616 | tf_op jit(solution)/shard_map/ppermute | solution.py:702
  64.3 4.9 %collective-permute-start.17 = (f32[8,8,256]{2,1,0:T(8,128)S(1)}, f32[8,8,256]{2,1,0:T(8,128)S(1)}, u32[]{:S(2)}, u32[]{:S(2)}) collective-permute-start(f32[8,8,256]{2,1,0:T(8,128)S(1)} %pad_maximum_fusion.1.par_ref.refs_0_), channel_id=1, source_target_pairs={{0,4},{1,5},{2,6},{3,7},{4,0},{5,1},{6,2},{7,3},{8,12},{9,13},{10,... | collective-permute-start | bytes 196616 | tf_op jit(solution)/shard_map/ppermute | solution.py:702
  65.3 3.8 %collective-permute-start.18 = (f32[8,8,256]{2,1,0:T(8,128)S(1)}, f32[8,8,256]{2,1,0:T(8,128)S(1)}, u32[]{:S(2)}, u32[]{:S(2)}) collective-permute-start(f32[8,8,256]{2,1,0:T(8,128)S(1)} %pad_maximum_fusion.1.par_ref.refs_0_), channel_id=1, source_target_pairs={{0,6},{1,7},{2,0},{3,1},{4,2},{5,3},{6,4},{7,5},{8,14},{9,15},{10,... | collective-permute-start | bytes 196616 | tf_op jit(solution)/shard_map/ppermute | solution.py:702
  78.4 9.9 %collective-permute-start.19 = (f32[8,8,256]{2,1,0:T(8,128)S(1)}, f32[8,8,256]{2,1,0:T(8,128)S(1)}, u32[]{:S(2)}, u32[]{:S(2)}) collective-permute-start(f32[8,8,256]{2,1,0:T(8,128)S(1)} %get-tuple-element.38), channel_id=1, source_target_pairs={{0,6},{1,7},{2,0},{3,1},{4,2},{5,3},{6,4},{7,5},{8,14},{9,15},{10,... | collective-permute-start | bytes 196616 | tf_op jit(solution)/shard_map/ppermute | solution.py:702
  80.8 7.5 %collective-permute-start.20 = (f32[8,8,256]{2,1,0:T(8,128)S(1)}, f32[8,8,256]{2,1,0:T(8,128)S(1)}, u32[]{:S(2)}, u32[]{:S(2)}) collective-permute-start(f32[8,8,256]{2,1,0:T(8,128)S(1)} %get-tuple-element.39), channel_id=1, source_target_pairs={{0,4},{1,5},{2,6},{3,7},{4,0},{5,1},{6,2},{7,3},{8,12},{9,13},{10,... | collective-permute-start | bytes 196616 | tf_op jit(solution)/shard_map/ppermute | solution.py:702
  80.8 7.5 %collective-permute-start.21 = (f32[8,8,256]{2,1,0:T(8,128)S(1)}, f32[8,8,256]{2,1,0:T(8,128)S(1)}, u32[]{:S(2)}, u32[]{:S(2)}) collective-permute-start(f32[8,8,256]{2,1,0:T(8,128)S(1)} %get-tuple-element.40), channel_id=1, source_target_pairs={{0,2},{1,3},{2,4},{3,5},{4,6},{5,7},{6,0},{7,1},{8,10},{9,11},{10,... | collective-permute-start | bytes 196616 | tf_op jit(solution)/shard_map/ppermute | solution.py:702
  88.4 25.2 %collective-permute-start.22 = (f32[2,1,256]{2,1,0:T(1,128)S(1)}, f32[2,1,256]{2,1,0:T(1,128)S(1)}, u32[]{:S(2)}, u32[]{:S(2)}) collective-permute-start(f32[2,1,256]{2,1,0:T(1,128)S(1)} %get-tuple-element.42), channel_id=1, source_target_pairs={{0,8},{8,16},{16,24},{1,9},{9,17},{17,25},{2,10},{10,18},{18,26},{... | collective-permute-start | bytes 6152 | tf_op jit(solution)/shard_map/ppermute | solution.py:712
  91.8 21.9 %collective-permute-start.23 = (f32[2,1,256]{2,1,0:T(1,128)S(1)}, f32[2,1,256]{2,1,0:T(1,128)S(1)}, u32[]{:S(2)}, u32[]{:S(2)}) collective-permute-start(f32[2,1,256]{2,1,0:T(1,128)S(1)} %get-tuple-element.43), channel_id=1, source_target_pairs={{8,0},{16,8},{24,16},{9,1},{17,9},{25,17},{10,2},{18,10},{26,18},{... | collective-permute-start | bytes 6152 | tf_op jit(solution)/shard_map/ppermute | solution.py:713
  93.1 8.0 %collective-permute-start.26 = (f32[2,32]{1,0:T(2,128)S(1)}, f32[2,32]{1,0:T(2,128)S(1)}, u32[]{:S(2)}, u32[]{:S(2)}) collective-permute-start(f32[2,32]{1,0:T(2,128)S(1)} %get-tuple-element.41), channel_id=1, source_target_pairs={{0,1},{1,0},{2,3},{3,2},{4,5},{5,4},{6,7},{7,6},{8,9},{9,8},{10,11... | collective-permute-start | bytes 776 | tf_op jit(solution)/shard_map/ppermute | solution.py:741
  101.1 3.5 %collective-permute-start.27 = (f32[2,32]{1,0:T(2,128)S(1)}, f32[2,32]{1,0:T(2,128)S(1)}, u32[]{:S(2)}, u32[]{:S(2)}) collective-permute-start(f32[2,32]{1,0:T(2,128)S(1)} %add.132), channel_id=1, source_target_pairs={{0,2},{1,3},{2,0},{3,1},{4,6},{5,7},{6,4},{7,5},{8,10},{9,11},{10,... | collective-permute-start | bytes 776 | tf_op jit(solution)/shard_map/ppermute | solution.py:741
  104.6 3.3 %collective-permute-start.28 = (f32[2,32]{1,0:T(2,128)S(1)}, f32[2,32]{1,0:T(2,128)S(1)}, u32[]{:S(2)}, u32[]{:S(2)}) collective-permute-start(f32[2,32]{1,0:T(2,128)S(1)} %add.133), channel_id=1, source_target_pairs={{0,4},{1,5},{2,6},{3,7},{4,0},{5,1},{6,2},{7,3},{8,12},{9,13},{10,... | collective-permute-start | bytes 776 | tf_op jit(solution)/shard_map/ppermute | solution.py:741
  107.9 3.3 %collective-permute-start.29 = (f32[2,32]{1,0:T(2,128)S(1)}, f32[2,32]{1,0:T(2,128)S(1)}, u32[]{:S(2)}, u32[]{:S(2)}) collective-permute-start(f32[2,32]{1,0:T(2,128)S(1)} %add.134), channel_id=1, source_target_pairs={{0,8},{8,0},{16,24},{24,16},{1,9},{9,1},{17,25},{25,17},{2,10},{10... | collective-permute-start | bytes 776 | tf_op jit(solution)/shard_map/ppermute | solution.py:741
  111.2 2.4 %collective-permute-start.30 = (f32[2,32]{1,0:T(2,128)S(1)}, f32[2,32]{1,0:T(2,128)S(1)}, u32[]{:S(2)}, u32[]{:S(2)}) collective-permute-start(f32[2,32]{1,0:T(2,128)S(1)} %add.135), channel_id=1, source_target_pairs={{0,16},{8,24},{16,0},{24,8},{1,17},{9,25},{17,1},{25,9},{2,18},{10... | collective-permute-start | bytes 776 | tf_op jit(solution)/shard_map/ppermute | solution.py:741
  113.7 10.4 %collective-permute-start.24 = (f32[2,10,128]{2,1,0:T(8,128)S(1)}, f32[2,10,128]{2,1,0:T(8,128)S(1)}, u32[]{:S(2)}, u32[]{:S(2)}) collective-permute-start(f32[2,10,128]{2,1,0:T(8,128)S(1)} %get-tuple-element.46), channel_id=1, source_target_pairs={{0,1},{1,2},{2,3},{3,4},{4,5},{5,6},{6,7},{8,9},{9,10},{10,11},{11... | collective-permute-start | bytes 30728 | tf_op jit(solution)/shard_map/ppermute | solution.py:712
  121.6 5.1 %collective-permute-start.25 = (f32[2,10,128]{2,1,0:T(8,128)S(1)}, f32[2,10,128]{2,1,0:T(8,128)S(1)}, u32[]{:S(2)}, u32[]{:S(2)}) collective-permute-start(f32[2,10,128]{2,1,0:T(8,128)S(1)} %get-tuple-element.47), channel_id=1, source_target_pairs={{1,0},{2,1},{3,2},{4,3},{5,4},{6,5},{7,6},{9,8},{10,9},{11,10},{12... | collective-permute-start | bytes 30728 | tf_op jit(solution)/shard_map/ppermute | solution.py:713

commit v3 on v2

--- a/solution.py
+++ b/solution.py
@@ -20,6 +20,21 @@
 VMEM_BYTES = 16 * 1024 * 1024
 LINEAR = (2, 3, 5, 6, 7)
 ENTRIES = [(i, j) for i in range(8) for j in range(i, 8)]
+
+
+PLACE = 4096
+
+
+def tile_of(ref):
+    return lax.rem(ref[0], PLACE)
+
+
+def row_is_odd(ref):
+    return lax.rem(ref[0] // PLACE, 2) == 1
+
+
+def column_is_odd(ref):
+    return lax.rem(ref[0], 2) == 1
 
 
 def split_value(x, count):
@@ -297,8 +312,7 @@
 ):
     par_refs, vis_refs = refs[:parts], refs[parts : 2 * parts]
     out_refs = refs[2 * parts : 3 * parts]
-    light_ref = refs[3 * parts]
-    par_scr, vis_scr, obs_scr, rows_ref, sums_ref, light_scr = refs[3 * parts + 1 :]
+    par_scr, vis_scr, obs_scr, rows_ref, sums_ref, light_scr = refs[3 * parts :]
     step = pl.program_id(0)
     samples, rows, cols = own_ref.shape
     held = 2 * samples
@@ -310,7 +324,7 @@
             par_scr[...] = par_refs[s][0:8]
             vis_scr[...] = vis_refs[s][8].astype(jnp.int32)
 
-    core = tile_ref[0] % 2
+    core = tile_of(tile_ref) % 2
     mine = pl.multiple_of(core * (samples * rows), rows)
     theirs = pl.multiple_of((1 - core) * (samples * rows), rows)
     for h in range(cols // LANES):
@@ -324,7 +338,7 @@
     p = [par_scr[i] for i in range(8)]
     mask = vis_scr[...]
     normal, by_u, by_v, sharp, slope = texel_forms(p)
-    base = (tile_ref[0] // 2) * cams
+    base = (tile_of(tile_ref) // 2) * cams
 
     def cam(c, i):
         return slab_ref[8 * c + i : 8 * c + i + 1, :][:, 0:1]
@@ -395,9 +409,12 @@
 
     @pl.when(step == parts - 1)
     def _():
+        out_refs[parts - 1][8] = jnp.zeros((rows, cols), f32)
         for k in range(2):
             part = light_scr[k * LIGHTS : (k + 1) * LIGHTS, :]
-            light_ref[k : k + 1, :] = exact(jnp.ones((8, LANES), f32), part, ((1,), (1,)))[0:1]
+            line = exact(jnp.ones((8, LANES), f32), part, ((1,), (1,)))[0:1]
+            for ref in out_refs:
+                ref[8, k : k + 1, 0:LIGHTS] = line
 
     def sums(k):
         return get_slab(sums_ref, k, rows)
@@ -441,10 +458,19 @@
         def _():
             for i in range(8):
                 out_refs[s][i] = right[i]
-
-
-def solve_kernel(low_ref, par_ref, *refs):
-    right_refs, out_ref = refs[:-1], refs[-1]
+            if s < parts - 1:
+                out_refs[s][8] = jnp.zeros((rows, cols), f32)
+
+
+def ring_total(terms):
+    while len(terms) > 1:
+        half = len(terms) // 2
+        terms = [terms[k] + terms[k + half] for k in range(half)]
+    return terms[0]
+
+
+def solve_kernel(tile_ref, low_ref, par_ref, *refs):
+    right_refs, (out_ref, first_ref, second_ref) = refs[:-3], refs[-3:]
     lower = {}
     for where, (i, j) in enumerate(ENTRIES):
         lower[j, i] = low_ref[where]
@@ -461,8 +487,56 @@
         for k in range(i + 1, 8):
             accum = accum - lower[k, i] * answer[k]
         answer[i] = accum * lower[i, i]
+    rows = par_ref.shape[1]
+    odd = row_is_odd(tile_ref)
+    first_ref[...] = jnp.zeros(first_ref.shape, f32)
+    second_ref[...] = jnp.zeros(second_ref.shape, f32)
     for i in range(8):
-        out_ref[i] = par_ref[i] + answer[i]
+        fresh = par_ref[i] + answer[i]
+        out_ref[i] = fresh
+        if i < 2:
+            top, bottom = fresh[0:1], fresh[rows - 1 : rows]
+            first_ref[i : i + 1, :] = jnp.where(odd, top, bottom)
+            second_ref[i : i + 1, :] = jnp.where(odd, bottom, top)
+    first_ref[2:4, 0:LANES] = ring_total([ref[8, 0:2, 0:LANES] for ref in right_refs])
+
+
+def rows_kernel(tile_ref, par_ref, sent_ref, first_ref, second_ref, tall_ref, near_ref, far_ref, scr):
+    rows, cols = par_ref.shape[1:]
+    odd, side = row_is_odd(tile_ref), column_is_odd(tile_ref)
+    near_ref[...] = jnp.zeros(near_ref.shape, f32)
+    far_ref[...] = jnp.zeros(far_ref.shape, f32)
+    for k in range(2):
+        one, two = first_ref[k : k + 1, :], second_ref[k : k + 1, :]
+        scr[7:8, :] = jnp.where(odd, one, two)
+        scr[8 : 8 + rows, :] = par_ref[k]
+        scr[8 + rows : 9 + rows, :] = jnp.where(odd, two, one)
+        tall = scr[7 : 7 + rows, :] + scr[8 : 8 + rows, :] + scr[9 : 9 + rows, :]
+        tall_ref[k] = tall
+        left, right = tall[:, 0:LANES], tall[:, cols - LANES : cols]
+        near_ref[k * rows : (k + 1) * rows, :] = jnp.where(side, left, right)
+        far_ref[k * rows : (k + 1) * rows, :] = jnp.where(side, right, left)
+    near_ref[2 * rows : 2 * rows + 2, :] = sent_ref[2:4, 0:LANES] + first_ref[2:4, 0:LANES]
+
+
+def smooth_kernel(tile_ref, par_ref, tall_ref, sent_ref, near_ref, far_ref, out_ref, light_ref):
+    rows, cols = par_ref.shape[1:]
+    side = column_is_odd(tile_ref)
+    lane = iota((rows, cols), 1)
+    for k in range(2):
+        at = slice(k * rows, (k + 1) * rows)
+        tall = tall_ref[k]
+        near_first, near_last = near_ref[at, 0:1], near_ref[at, LANES - 1 : LANES]
+        far_first, far_last = far_ref[at, 0:1], far_ref[at, LANES - 1 : LANES]
+        before = jnp.where(side, near_last, far_last)
+        after = jnp.where(side, far_first, near_first)
+        left = jnp.where(lane == 0, before, pltpu.roll(tall, 1, 1))
+        right = jnp.where(lane == cols - 1, after, pltpu.roll(tall, cols - 1, 1))
+        out_ref[k] = 0.5 * par_ref[k] + (tall + left + right) * (0.5 / 9.0)
+    for k in range(2, 8):
+        out_ref[k] = par_ref[k]
+    light_ref[...] = jnp.zeros(light_ref.shape, f32)
+    light_ref[0:2, :] = sent_ref[2 * rows : 2 * rows + 2, :] + near_ref[2 * rows : 2 * rows + 2, :]
 
 
 def smem():
@@ -510,10 +584,9 @@
         return pl.BlockSpec(x.shape, lambda s, tile: zeros)
 
     def chip(s, tile):
-        return lax.rem(tile[0] // 2 + (parts - s), parts)
-
-    outs = [jax.ShapeDtypeStruct((8, rows, cols), f32) for _ in range(parts)]
-    outs.append(jax.ShapeDtypeStruct((2, LIGHTS), f32))
+        return lax.rem(tile_of(tile) // 2 + (parts - s), parts)
+
+    outs = [jax.ShapeDtypeStruct((9, rows, cols), f32) for _ in range(parts)]
     small = [gains] + [tables[n] for n in ("here", "shade", "plain", "peak", "slab")]
     return pl.pallas_call(
         functools.partial(sample_kernel, parts=parts),
@@ -543,15 +616,48 @@
     )(tile, own, got, *small, *pars, *vises)
 
 
-def solve_call(low, par, rights):
+def plain_call(kernel, name, shapes, scratch, tile, *args):
     return pl.pallas_call(
-        solve_kernel,
-        name="solve",
-        out_shape=jax.ShapeDtypeStruct((8,) + par.shape[1:], f32),
-        in_specs=[vmem()] * (2 + len(rights)),
-        out_specs=vmem(),
+        kernel,
+        name=name,
+        out_shape=[jax.ShapeDtypeStruct(shape, f32) for shape in shapes],
+        in_specs=[smem()] + [vmem()] * len(args),
+        out_specs=[vmem()] * len(shapes),
+        scratch_shapes=[pltpu.VMEM(shape, f32) for shape in scratch],
         compiler_params=params_of(),
-    )(low, par, *rights)
+    )(tile, *args)
+
+
+def pairs(count, start):
+    out = []
+    for i in range(start, count - 1, 2):
+        out += [(i, i + 1), (i + 1, i)]
+    return out
+
+
+def settle(tile, low, params, moved):
+    _, rows, cols = params.shape
+    grps, tiles = lax.axis_size("grp"), lax.axis_size("tile")
+    strip = (8, cols)
+    params, sent, other = plain_call(
+        solve_kernel, "solve", [params.shape, strip, strip], [], tile, low, params, *moved
+    )
+    first = lax.ppermute(sent, "grp", pairs(grps, 0))
+    second = lax.ppermute(other, "grp", pairs(grps, 1))
+    patch = (2 * rows + 8, LANES)
+    tall, sent, other = plain_call(
+        rows_kernel, "rows", [(2, rows, cols), patch, patch], [(24, cols)], tile, params, sent, first, second
+    )
+    near = lax.ppermute(sent, "tile", pairs(tiles, 0))
+    far = lax.ppermute(other, "tile", pairs(tiles, 1))
+    params, light = plain_call(
+        smooth_kernel, "smooth", [params.shape, (8, LANES)], [], tile, params, tall, sent, near, far
+    )
+    bit = 2
+    while bit < grps:
+        light = light + lax.ppermute(light, "grp", [(i, i ^ bit) for i in range(grps)])
+        bit *= 2
+    return params, light[0:1, 0:LIGHTS], light[1:2, 0:LIGHTS]
 
 
 def exact(a, b, sides):
@@ -576,7 +682,7 @@
     samples = lobe_ref.shape[0]
     held = here_ref.shape[0]
     cams = held // LIGHTS
-    first = (tile_ref[0] // 2) * cams
+    first = (tile_of(tile_ref) // 2) * cams
 
     def unit(raw_ref, scr):
         scr[...] = jnp.zeros(scr.shape, f32)
@@ -702,47 +808,6 @@
     return lax.ppermute(x, "tile", [(2 * z + c, 2 * ((z + by) % nz) + c) for z in range(nz) for c in range(2)])
 
 
-def padded_2(cells, sides):
-    for axis, dim, width in sides:
-        count = lax.axis_size(axis)
-        ends = count - 1
-        size = cells.shape[dim]
-        head = lax.slice_in_dim(cells, 0, width, axis=dim)
-        tail = lax.slice_in_dim(cells, size - width, size, axis=dim)
-        before = lax.ppermute(tail, axis, [(i, i + 1) for i in range(ends)])
-        after = lax.ppermute(head, axis, [(i + 1, i) for i in range(ends)])
-        cells = jnp.concatenate(
-            [
-                lax.slice_in_dim(before, width - 1, width, axis=dim),
-                cells,
-                lax.slice_in_dim(after, 0, 1, axis=dim),
-            ],
-            axis=dim,
-        )
-    return cells
-
-
-def smooth_tilts(tilt):
-    rows = tilt.shape[1]
-    cols = tilt.shape[2]
-    padded = padded_2(tilt, (("grp", 1, 1), ("tile", 2, LANES)))
-    boxed = jnp.zeros(tilt.shape, f32)
-    for i in range(3):
-        for j in range(3):
-            boxed = boxed + padded[:, i : i + rows, j : j + cols]
-    return 0.5 * tilt + boxed * (0.5 / 9.0)
-
-
-def summed_everywhere(x):
-    for axis in ("tile", "grp"):
-        size = lax.axis_size(axis)
-        bit = 1
-        while bit < size:
-            x = x + lax.ppermute(x, axis, [(i, i ^ bit) for i in range(size)])
-            bit *= 2
-    return x
-
-
 def on_device(observed, visible, params_start, light_directions, view_dirs, gains_start):
     samples, rows, _ = observed.shape
     cols = visible.shape[1]
@@ -758,19 +823,17 @@
     first = jnp.concatenate([params_start, visible.astype(f32)[None]], axis=0)
     blocks = [first] + [shifted(first, s, nz) for s in range(1, nz)]
     vises = blocks
-    here = tile.astype(jnp.int32).reshape(1)
+    here = (tile + PLACE * lax.axis_index("grp")).astype(jnp.int32).reshape(1)
     tables = setup_call(here, light_directions, view_dirs, held)
 
     params = params_start
     gains = gains_start.reshape(1, LIGHTS)
     for iteration in range(ITERS):
         low = normal_call(params, visible, gains, tables)
-        *rights, light = sample_call(here, observed, got, gains, tables, blocks, vises)
+        rights = sample_call(here, observed, got, gains, tables, blocks, vises)
         moved = [rights[0]] + [shifted(rights[s], -s, nz) for s in range(1, nz)]
-        params = solve_call(low, params, moved)
-        sums = summed_everywhere(light)
-        gains = gains + (sums[0:1] - gains * sums[1:2]) / (sums[1:2] + 1.0)
-        params = jnp.concatenate([smooth_tilts(params[:2]), params[2:]], axis=0)
+        params, lifted, energy = settle(here, low, params, moved)
+        gains = gains + (lifted - gains * energy) / (energy + 1.0)
         if iteration + 1 < ITERS:
             blocks = [params] + [shifted(params, s, nz) for s in range(1, nz)]
     return params, gains.reshape(LIGHTS)

time: 128 us -> 96.5 us (0.75)
  starting transfers between devices: 63.4 us -> 42.3 us
  waiting for transfers between devices: 24.2 us -> 12.1 us
    ppermute x18 -> x10, starting transfers between devices: 47.6 us -> 26.3 us  [the longest x2 11 us: settle(): far = lax.ppermute(other, 'tile', pairs(tiles, 1))]
    ppermute x18 -> x10, waiting for transfers between devices: 18.8 us -> 6.09 us  [the longest x2 2.64 us: settle(): far = lax.ppermute(other, 'tile', pairs(tiles, 1))]
  transfers between devices with their start and end apart: 31 -> 23, of which waited for: 15 -> 9; matrix products, arithmetic and copies ran while one was open for 1% -> 1% of each run, Pallas kernels for 13% -> 17%
where the time goes in v3:
time: 96.5 us; the launch traced here: 94.8 us
  starting transfers between devices  42.3 us (44%)
  Pallas kernels  35.7 us (37%)
  waiting for transfers between devices  12.1 us (13%)
  local copies, waits for them, and re-layouts  2.43 us (3%)
  other arithmetic  1.4 us (1%)
    pallas_call x2, Pallas kernels, sample_call(): pl.pallas_call(functools.partial(sample_kernel, parts=parts), name='sampl...  18.6 us
    ppermute x12, starting transfers between devices, shifted(): lax.ppermute(x, 'tile', [(2 * z + c, 2 * ((z + by) % nz) + c) for z in ra...  16 us
    pallas_call x2, Pallas kernels, normal_call(): pl.pallas_call(normal_kernel, name='normal_factor', out_shape=jax.ShapeDt...  14.3 us
    ppermute x2, starting transfers between devices, settle(): far = lax.ppermute(other, 'tile', pairs(tiles, 1))  11 us
    ppermute x2, starting transfers between devices, settle(): lax.ppermute(light, 'grp', [(i, i ^ bit) for i in range(grps)])  9.12 us
    ppermute x12, waiting for transfers between devices, shifted(): lax.ppermute(x, 'tile', [(2 * z + c, 2 * ((z + by) % nz) + c) for z in ra...  5.97 us
    ppermute x2, starting transfers between devices, settle(): near = lax.ppermute(sent, 'tile', pairs(tiles, 0))  3.47 us
    ppermute x2, waiting for transfers between devices, settle(): far = lax.ppermute(other, 'tile', pairs(tiles, 1))  2.64 us
  transfers between devices with their start and end apart: 23, of which 9 were waited for; matrix products, arithmetic and copies ran while one was open for 1% of the time, Pallas kernels for 17%

profile of v3, /device:TPU:1, one launch (start us, length us, event | category | flops | bytes accessed | tf_op | source)
XLA Modules:
  0.0 94.8 jit_solution(9679057936443844299)
XLA Ops:
  0.7 2.4 %constant_dynamic-slice_fusion = bf16[64,8,4,1,256]{4,1,3,2,0:T(8,128)(2,1)} fusion(bf16[64,8,4,2,256]{4,1,3,2,0:T(8,128)(2,1)} %bitcast.11, s32[]{:T(128)S(6)} %select_n.12), kind=kLoop, calls=%fused_computation.4 | loop fusion | bytes 2097156 | tf_op jit(solution)/shard_map/jit(dynamic_index_in_dim)/dynamic_slice | solution.py:821
  3.1 0.1 collective-permute-start
  3.2 0.9 pad_maximum_fusion.refs_0_.refs_4_
  4.0 2.7 %collective-permute-start.1 = (f32[9,8,256]{2,1,0:T(8,128)S(1)}, f32[9,8,256]{2,1,0:T(8,128)S(1)}, u32[]{:S(2)}, u32[]{:S(2)}) collective-permute-start(f32[9,8,256]{2,1,0:T(8,128)S(1)} %pad_maximum_fusion.refs_0_.refs_4_), channel_id=1, source_target_pairs={{0,2},{1,3},{2,4},{3,5},{4,6},{5,7},{6,0},{7,1},{8,10},{9,11},{10,... | collective-permute-start | bytes 221192 | tf_op jit(solution)/shard_map/ppermute | solution.py:808
  6.8 2.3 %collective-permute-start.2 = (f32[9,8,256]{2,1,0:T(8,128)S(1)}, f32[9,8,256]{2,1,0:T(8,128)S(1)}, u32[]{:S(2)}, u32[]{:S(2)}) collective-permute-start(f32[9,8,256]{2,1,0:T(8,128)S(1)} %pad_maximum_fusion.refs_0_.refs_4_), channel_id=1, source_target_pairs={{0,4},{1,5},{2,6},{3,7},{4,0},{5,1},{6,2},{7,3},{8,12},{9,13},{10,... | collective-permute-start | bytes 221192 | tf_op jit(solution)/shard_map/ppermute | solution.py:808
  9.1 1.1 %collective-permute-start.3 = (f32[9,8,256]{2,1,0:T(8,128)S(1)}, f32[9,8,256]{2,1,0:T(8,128)S(1)}, u32[]{:S(2)}, u32[]{:S(2)}) collective-permute-start(f32[9,8,256]{2,1,0:T(8,128)S(1)} %pad_maximum_fusion.refs_0_.refs_4_), channel_id=1, source_target_pairs={{0,6},{1,7},{2,0},{3,1},{4,2},{5,3},{6,4},{7,5},{8,14},{9,15},{10,... | collective-permute-start | bytes 221192 | tf_op jit(solution)/shard_map/ppermute | solution.py:808
  10.1 1.8 %tables.1 = (f32[8,32]{1,0:T(8,128)S(1)}, f32[8,16]{1,0:T(8,128)S(1)}, bf16[512,48]{1,0:T(8,128)(2,1)S(1)}, f32[32,512]{1,0:T(8,128)S(1)}, f32[16,512]{1,0:T(8,1...) custom-call(s32[1]{0:T(128)} %bitcast.tile_ref, ...), custom_call_target="tpu_custom_call" | custom-call | tf_op jit(solution)/shard_map/tables/pallas_call | solution.py:795
  12.0 2.7 %collective-permute-done.2.refs_2_.refs_6_ = f32[9,8,256]{2,1,0:T(8,128)S(1)} collective-permute-done((f32[9,8,256]{2,1,0:T(8,128)S(1)}, f32[9,8,256]{2,1,0:T(8,128)S(1)}, u32[]{:S(2)}, u32[]{:S(2)}) %collective-permute-start.2) | collective-permute-done | bytes 73760 | tf_op jit(solution)/shard_map/ppermute | solution.py:808
  14.7 0.0 collective-permute-done.3.refs_3_.refs_7_
  14.7 0.0 collective-permute-done.got_ref
  14.7 9.3 %sample_sums.2 = (f32[9,8,256]{2,1,0:T(8,128)S(1)}, f32[9,8,256]{2,1,0:T(8,128)S(1)}, f32[9,8,256]{2,1,0:T(8,128)S(1)}, f32[9,8,256]{2,1,0:T(8,128)S(1)}) custom-call(s32[1]{0:T(128)} %bitcast.tile_ref, bf16[64,8,2048]{2,1,0:T(8,128)(2,1)S(1)} %copy-done, bf16[64,8,1024]{2,1,0:T(8,128)(2,1)S(1)} %collective-permute-done.got_ref, f32[1,32]{1,0:T(1,128)S(1)} %bitcast.12, ...), custom_call_target="tpu_custom_call" | custom-call | tf_op jit(solution)/shard_map/sample_sums/pallas_call | solution.py:591
  24.0 2.6 %collective-permute-start.4 = (f32[9,8,256]{2,1,0:T(8,128)S(1)}, f32[9,8,256]{2,1,0:T(8,128)S(1)}, u32[]{:S(2)}, u32[]{:S(2)}) collective-permute-start(f32[9,8,256]{2,1,0:T(8,128)S(1)} %get-tuple-element.47), channel_id=1, source_target_pairs={{0,6},{1,7},{2,0},{3,1},{4,2},{5,3},{6,4},{7,5},{8,14},{9,15},{10,... | collective-permute-start | bytes 221192 | tf_op jit(solution)/shard_map/ppermute | solution.py:808
  26.6 0.5 collective-permute-start.5
  27.2 7.1 %normal_factor.2.low_ref = f32[44,8,256]{2,1,0:T(8,128)S(1)} custom-call(f32[8,8,256]{2,1,0:T(8,128)S(1)} %copy-done.1, s32[8,256]{1,0:T(8,128)S(1)} %copy-done.2, f32[1,32]{1,0:T(1,128)S(1)} %bitcast.13, f32[8,32]{1,0:T(8,128)S(1)} %get-tuple-element.36.near_ref, f32[8,16]{1,0:T(8,128)S(1)} %get-tuple-element.37.cams_ref, ...), custom_call_target="tpu_custom_call" | custom-call | tf_op jit(solution)/shard_map/normal_factor/pallas_call | solution.py:558
  34.3 0.0 collective-permute-done.4.refs_1_
  34.3 0.1 collective-permute-done.5.refs_2_
  34.4 0.1 solve.2
  34.6 1.3 %collective-permute-start.7 = (f32[8,256]{1,0:T(8,128)S(1)}, f32[8,256]{1,0:T(8,128)S(1)}, u32[]{:S(2)}, u32[]{:S(2)}) collective-permute-start(f32[8,256]{1,0:T(8,128)S(1)} %get-tuple-element.51.sent_ref), channel_id=1, source_target_pairs={{0,8},{8,0},{16,24},{24,16},{1,9},{9,1},{17,25},{25,17},{2,10},{10... | collective-permute-start | bytes 24584 | tf_op jit(solution)/shard_map/ppermute | solution.py:645
  35.8 0.6 collective-permute-start.8
  36.5 0.6 collective-permute-done.7.first_ref
  37.1 0.0 collective-permute-done.8.second_ref
  37.2 6.6 %collective-permute-start.10 = (f32[24,128]{1,0:T(8,128)S(1)}, f32[24,128]{1,0:T(8,128)S(1)}, u32[]{:S(2)}, u32[]{:S(2)}) collective-permute-start(f32[24,128]{1,0:T(8,128)S(1)} %get-tuple-element.55), channel_id=1, source_target_pairs={{1,2},{2,1},{3,4},{4,3},{5,6},{6,5},{9,10},{10,9},{11,12},{12,11},... | collective-permute-start | bytes 36872 | tf_op jit(solution)/shard_map/ppermute | solution.py:652
  43.8 0.1 collective-permute-start.9
  43.9 1.3 %collective-permute-done.10.far_ref = f32[24,128]{1,0:T(8,128)S(1)} collective-permute-done((f32[24,128]{1,0:T(8,128)S(1)}, f32[24,128]{1,0:T(8,128)S(1)}, u32[]{:S(2)}, u32[]{:S(2)}) %collective-permute-start.10) | collective-permute-done | bytes 12320 | tf_op jit(solution)/shard_map/ppermute | solution.py:652
  45.2 0.1 smooth.2
  45.3 5.6 %collective-permute-start.11 = (f32[8,128]{1,0:T(8,128)S(1)}, f32[8,128]{1,0:T(8,128)S(1)}, u32[]{:S(2)}, u32[]{:S(2)}) collective-permute-start(f32[8,128]{1,0:T(8,128)S(1)} %get-tuple-element.57), channel_id=1, source_target_pairs={{0,16},{8,24},{16,0},{24,8},{1,17},{9,25},{17,1},{25,9},{2,18},{10... | collective-permute-start | bytes 12296 | tf_op jit(solution)/shard_map/ppermute | solution.py:658
  50.8 0.0 collective-permute-start.12
  50.9 1.0 %collective-permute-start.13 = (f32[8,8,256]{2,1,0:T(8,128)S(1)}, f32[8,8,256]{2,1,0:T(8,128)S(1)}, u32[]{:S(2)}, u32[]{:S(2)}) collective-permute-start(f32[8,8,256]{2,1,0:T(8,128)S(1)} %get-tuple-element.56.par_ref.refs_0_), channel_id=1, source_target_pairs={{0,4},{1,5},{2,6},{3,7},{4,0},{5,1},{6,2},{7,3},{8,12},{9,13},{10,... | collective-permute-start | bytes 196616 | tf_op jit(solution)/shard_map/ppermute | solution.py:808
  51.9 2.4 %collective-permute-start.14 = (f32[8,8,256]{2,1,0:T(8,128)S(1)}, f32[8,8,256]{2,1,0:T(8,128)S(1)}, u32[]{:S(2)}, u32[]{:S(2)}) collective-permute-start(f32[8,8,256]{2,1,0:T(8,128)S(1)} %get-tuple-element.56.par_ref.refs_0_), channel_id=1, source_target_pairs={{0,6},{1,7},{2,0},{3,1},{4,2},{5,3},{6,4},{7,5},{8,14},{9,15},{10,... | collective-permute-start | bytes 196616 | tf_op jit(solution)/shard_map/ppermute | solution.py:808
  54.3 1.6 %collective-permute-done.12.refs_1_ = f32[8,8,256]{2,1,0:T(8,128)S(1)} collective-permute-done((f32[8,8,256]{2,1,0:T(8,128)S(1)}, f32[8,8,256]{2,1,0:T(8,128)S(1)}, u32[]{:S(2)}, u32[]{:S(2)}) %collective-permute-start.12) | collective-permute-done | bytes 65568 | tf_op jit(solution)/shard_map/ppermute | solution.py:808
  55.8 0.0 collective-permute-done.13.refs_2_
  55.8 1.6 %collective-permute-done.14.refs_3_ = f32[8,8,256]{2,1,0:T(8,128)S(1)} collective-permute-done((f32[8,8,256]{2,1,0:T(8,128)S(1)}, f32[8,8,256]{2,1,0:T(8,128)S(1)}, u32[]{:S(2)}, u32[]{:S(2)}) %collective-permute-start.14) | collective-permute-done | bytes 65568 | tf_op jit(solution)/shard_map/ppermute | solution.py:808
  57.4 9.3 %sample_sums.3 = (f32[9,8,256]{2,1,0:T(8,128)S(1)}, f32[9,8,256]{2,1,0:T(8,128)S(1)}, f32[9,8,256]{2,1,0:T(8,128)S(1)}, f32[9,8,256]{2,1,0:T(8,128)S(1)}) custom-call(s32[1]{0:T(128)} %bitcast.tile_ref, bf16[64,8,2048]{2,1,0:T(8,128)(2,1)S(1)} %copy-done, bf16[64,8,1024]{2,1,0:T(8,128)(2,1)S(1)} %collective-permute-done.got_ref, ...), custom_call_target="tpu_custom_call" | custom-call | tf_op jit(solution)/shard_map/sample_sums/pallas_call | solution.py:591
  66.6 2.2 %collective-permute-start.15 = (f32[9,8,256]{2,1,0:T(8,128)S(1)}, f32[9,8,256]{2,1,0:T(8,128)S(1)}, u32[]{:S(2)}, u32[]{:S(2)}) collective-permute-start(f32[9,8,256]{2,1,0:T(8,128)S(1)} %get-tuple-element.59), channel_id=1, source_target_pairs={{0,6},{1,7},{2,0},{3,1},{4,2},{5,3},{6,4},{7,5},{8,14},{9,15},{10,... | collective-permute-start | bytes 221192 | tf_op jit(solution)/shard_map/ppermute | solution.py:808
  68.8 1.2 %collective-permute-start.16 = (f32[9,8,256]{2,1,0:T(8,128)S(1)}, f32[9,8,256]{2,1,0:T(8,128)S(1)}, u32[]{:S(2)}, u32[]{:S(2)}) collective-permute-start(f32[9,8,256]{2,1,0:T(8,128)S(1)} %get-tuple-element.60), channel_id=1, source_target_pairs={{0,4},{1,5},{2,6},{3,7},{4,0},{5,1},{6,2},{7,3},{8,12},{9,13},{10,... | collective-permute-start | bytes 221192 | tf_op jit(solution)/shard_map/ppermute | solution.py:808
  70.0 7.1 %normal_factor.3.low_ref = f32[44,8,256]{2,1,0:T(8,128)S(1)} custom-call(f32[8,8,256]{2,1,0:T(8,128)S(1)} %get-tuple-element.56.par_ref.refs_0_, s32[8,256]{1,0:T(8,128)S(1)} %copy-done.2, f32[1,32]{1,0:T(1,128)S(1)} %divide_add_fusion.gain_ref, f32[8,32]{1,0:T(8,128)S(1)} %get-tuple-element.36.near_ref, f32[8,16]{1,0:T(8,128)S(1)} %get-tuple-element.37.cams_ref, ...), custom_call_target="tpu_custom_call" | custom-call | tf_op jit(solution)/shard_map/normal_factor/pallas_call | solution.py:558
  77.1 0.0 collective-permute-done.15.refs_1_
  77.2 0.1 solve.3
  77.3 0.1 collective-permute-start.18
  77.4 0.7 collective-permute-start.19
  78.0 1.8 %collective-permute-done.18.first_ref = f32[8,256]{1,0:T(8,128)S(1)} collective-permute-done((f32[8,256]{1,0:T(8,128)S(1)}, f32[8,256]{1,0:T(8,128)S(1)}, u32[]{:S(2)}, u32[]{:S(2)}) %collective-permute-start.18) | collective-permute-done | bytes 8224 | tf_op jit(solution)/shard_map/ppermute | solution.py:645
  79.9 3.4 %collective-permute-start.20 = (f32[24,128]{1,0:T(8,128)S(1)}, f32[24,128]{1,0:T(8,128)S(1)}, u32[]{:S(2)}, u32[]{:S(2)}) collective-permute-start(f32[24,128]{1,0:T(8,128)S(1)} %get-tuple-element.66.sent_ref), channel_id=1, source_target_pairs={{0,1},{1,0},{2,3},{3,2},{4,5},{5,4},{6,7},{7,6},{8,9},{9,8},{10,11... | collective-permute-start | bytes 36872 | tf_op jit(solution)/shard_map/ppermute | solution.py:651
  83.3 4.4 %collective-permute-start.21 = (f32[24,128]{1,0:T(8,128)S(1)}, f32[24,128]{1,0:T(8,128)S(1)}, u32[]{:S(2)}, u32[]{:S(2)}) collective-permute-start(f32[24,128]{1,0:T(8,128)S(1)} %get-tuple-element.67), channel_id=1, source_target_pairs={{1,2},{2,1},{3,4},{4,3},{5,6},{6,5},{9,10},{10,9},{11,12},{12,11},... | collective-permute-start | bytes 36872 | tf_op jit(solution)/shard_map/ppermute | solution.py:652
  87.7 1.4 %collective-permute-done.21.far_ref = f32[24,128]{1,0:T(8,128)S(1)} collective-permute-done((f32[24,128]{1,0:T(8,128)S(1)}, f32[24,128]{1,0:T(8,128)S(1)}, u32[]{:S(2)}, u32[]{:S(2)}) %collective-permute-start.21) | collective-permute-done | bytes 12320 | tf_op jit(solution)/shard_map/ppermute | solution.py:652
  89.0 0.7 smooth.3
  89.8 3.5 %collective-permute-start.22 = (f32[8,128]{1,0:T(8,128)S(1)}, f32[8,128]{1,0:T(8,128)S(1)}, u32[]{:S(2)}, u32[]{:S(2)}) collective-permute-start(f32[8,128]{1,0:T(8,128)S(1)} %get-tuple-element.69), channel_id=1, source_target_pairs={{0,16},{8,24},{16,0},{24,8},{1,17},{9,25},{17,1},{25,9},{2,18},{10... | collective-permute-start | bytes 12296 | tf_op jit(solution)/shard_map/ppermute | solution.py:658
  93.3 1.0 %collective-permute-done.22 = f32[8,128]{1,0:T(8,128)S(1)} collective-permute-done((f32[8,128]{1,0:T(8,128)S(1)}, f32[8,128]{1,0:T(8,128)S(1)}, u32[]{:S(2)}, u32[]{:S(2)}) %collective-permute-start.22) | collective-permute-done | bytes 4128 | tf_op jit(solution)/shard_map/ppermute | solution.py:658
  94.3 0.5 add_bitcast_fusion
  (28 shorter events, 0.1 us)
Async XLA Ops:
  0.6 14.1 %copy-start = (bf16[64,8,2048]{2,1,0:T(8,128)(2,1)S(1)}, bf16[64,8,2048]{2,1,0:T(8,128)(2,1)}, u32[]{:S(2)}) copy-start(bf16[64,8,2048]{2,1,0:T(8,128)(2,1)} %own_ref.3) | copy-start | bytes 6291460
  0.6 2.5 %copy-start.2 = (s32[8,256]{1,0:T(8,128)S(1)}, s32[8,256]{1,0:T(8,128)}, u32[]{:S(2)}) copy-start(s32[8,256]{1,0:T(8,128)} %vis_ref.3) | copy-start | bytes 24580
  0.7 9.5 %copy-start.5 = (f32[3,16]{1,0:T(4,128)S(1)}, f32[3,16]{1,0:T(4,128)}, u32[]{:S(2)}) copy-start(f32[3,16]{1,0:T(4,128)} %view_ref.1) | copy-start | bytes 580
  0.7 9.5 %copy-start.4 = (f32[3,32]{1,0:T(4,128)S(1)}, f32[3,32]{1,0:T(4,128)}, u32[]{:S(2)}) copy-start(f32[3,32]{1,0:T(4,128)} %light_ref.1) | copy-start | bytes 1156
  0.7 14.0 %copy-start.3 = (f32[32]{0:T(128)S(1)}, f32[32]{0:T(128)}, u32[]{:S(2)}) copy-start(f32[32]{0:T(128)} %param.11) | copy-start | bytes 388
  3.1 24.0 %copy-start.1 = (f32[8,8,256]{2,1,0:T(8,128)S(1)}, f32[8,8,256]{2,1,0:T(8,128)}, u32[]{:S(2)}) copy-start(f32[8,8,256]{2,1,0:T(8,128)} %par_ref.3) | copy-start | bytes 196612
  3.1 11.6 %collective-permute-start = (bf16[64,8,1024]{2,1,0:T(8,128)(2,1)}, bf16[64,8,1024]{2,1,0:T(8,128)(2,1)S(1)}, u32[]{:S(2)}, u32[]{:S(2)}) collective-permute-start(bf16[64,8,1024]{2,1,0:T(8,128)(2,1)} %bitcast.3), channel_id=1, source_target_pairs={{0,1},{1,0},{2,3},{3,2},{4,5},{5,4},{6,7},{7,6},{8,9},{9,8},{10,11... | collective-permute-start | bytes 3145736 | tf_op jit(solution)/shard_map/ppermute | solution.py:822
  4.0 8.0 %collective-permute-start.1 = (f32[9,8,256]{2,1,0:T(8,128)S(1)}, f32[9,8,256]{2,1,0:T(8,128)S(1)}, u32[]{:S(2)}, u32[]{:S(2)}) collective-permute-start(f32[9,8,256]{2,1,0:T(8,128)S(1)} %pad_maximum_fusion.refs_0_.refs_4_), channel_id=1, source_target_pairs={{0,2},{1,3},{2,4},{3,5},{4,6},{5,7},{6,0},{7,1},{8,10},{9,11},{10,... | collective-permute-start | bytes 221192 | tf_op jit(solution)/shard_map/ppermute | solution.py:808
  6.8 7.9 %collective-permute-start.2 = (f32[9,8,256]{2,1,0:T(8,128)S(1)}, f32[9,8,256]{2,1,0:T(8,128)S(1)}, u32[]{:S(2)}, u32[]{:S(2)}) collective-permute-start(f32[9,8,256]{2,1,0:T(8,128)S(1)} %pad_maximum_fusion.refs_0_.refs_4_), channel_id=1, source_target_pairs={{0,4},{1,5},{2,6},{3,7},{4,0},{5,1},{6,2},{7,3},{8,12},{9,13},{10,... | collective-permute-start | bytes 221192 | tf_op jit(solution)/shard_map/ppermute | solution.py:808
  9.1 5.6 %collective-permute-start.3 = (f32[9,8,256]{2,1,0:T(8,128)S(1)}, f32[9,8,256]{2,1,0:T(8,128)S(1)}, u32[]{:S(2)}, u32[]{:S(2)}) collective-permute-start(f32[9,8,256]{2,1,0:T(8,128)S(1)} %pad_maximum_fusion.refs_0_.refs_4_), channel_id=1, source_target_pairs={{0,6},{1,7},{2,0},{3,1},{4,2},{5,3},{6,4},{7,5},{8,14},{9,15},{10,... | collective-permute-start | bytes 221192 | tf_op jit(solution)/shard_map/ppermute | solution.py:808
  24.0 10.3 %collective-permute-start.4 = (f32[9,8,256]{2,1,0:T(8,128)S(1)}, f32[9,8,256]{2,1,0:T(8,128)S(1)}, u32[]{:S(2)}, u32[]{:S(2)}) collective-permute-start(f32[9,8,256]{2,1,0:T(8,128)S(1)} %get-tuple-element.47), channel_id=1, source_target_pairs={{0,6},{1,7},{2,0},{3,1},{4,2},{5,3},{6,4},{7,5},{8,14},{9,15},{10,... | collective-permute-start | bytes 221192 | tf_op jit(solution)/shard_map/ppermute | solution.py:808
  26.6 7.8 %collective-permute-start.5 = (f32[9,8,256]{2,1,0:T(8,128)S(1)}, f32[9,8,256]{2,1,0:T(8,128)S(1)}, u32[]{:S(2)}, u32[]{:S(2)}) collective-permute-start(f32[9,8,256]{2,1,0:T(8,128)S(1)} %get-tuple-element.48), channel_id=1, source_target_pairs={{0,4},{1,5},{2,6},{3,7},{4,0},{5,1},{6,2},{7,3},{8,12},{9,13},{10,... | collective-permute-start | bytes 221192 | tf_op jit(solution)/shard_map/ppermute | solution.py:808
  27.1 7.3 %collective-permute-start.6 = (f32[9,8,256]{2,1,0:T(8,128)S(1)}, f32[9,8,256]{2,1,0:T(8,128)S(1)}, u32[]{:S(2)}, u32[]{:S(2)}) collective-permute-start(f32[9,8,256]{2,1,0:T(8,128)S(1)} %get-tuple-element.49), channel_id=1, source_target_pairs={{0,2},{1,3},{2,4},{3,5},{4,6},{5,7},{6,0},{7,1},{8,10},{9,11},{10,... | collective-permute-start | bytes 221192 | tf_op jit(solution)/shard_map/ppermute | solution.py:808
  34.6 2.6 %collective-permute-start.7 = (f32[8,256]{1,0:T(8,128)S(1)}, f32[8,256]{1,0:T(8,128)S(1)}, u32[]{:S(2)}, u32[]{:S(2)}) collective-permute-start(f32[8,256]{1,0:T(8,128)S(1)} %get-tuple-element.51.sent_ref), channel_id=1, source_target_pairs={{0,8},{8,0},{16,24},{24,16},{1,9},{9,1},{17,25},{25,17},{2,10},{10... | collective-permute-start | bytes 24584 | tf_op jit(solution)/shard_map/ppermute | solution.py:645
  35.8 1.3 %collective-permute-start.8 = (f32[8,256]{1,0:T(8,128)S(1)}, f32[8,256]{1,0:T(8,128)S(1)}, u32[]{:S(2)}, u32[]{:S(2)}) collective-permute-start(f32[8,256]{1,0:T(8,128)S(1)} %get-tuple-element.52), channel_id=1, source_target_pairs={{8,16},{16,8},{9,17},{17,9},{10,18},{18,10},{11,19},{19,11},{12,20... | collective-permute-start | bytes 24584 | tf_op jit(solution)/shard_map/ppermute | solution.py:646
  37.2 8.0 %collective-permute-start.10 = (f32[24,128]{1,0:T(8,128)S(1)}, f32[24,128]{1,0:T(8,128)S(1)}, u32[]{:S(2)}, u32[]{:S(2)}) collective-permute-start(f32[24,128]{1,0:T(8,128)S(1)} %get-tuple-element.55), channel_id=1, source_target_pairs={{1,2},{2,1},{3,4},{4,3},{5,6},{6,5},{9,10},{10,9},{11,12},{12,11},... | collective-permute-start | bytes 36872 | tf_op jit(solution)/shard_map/ppermute | solution.py:652
  43.8 1.4 %collective-permute-start.9 = (f32[24,128]{1,0:T(8,128)S(1)}, f32[24,128]{1,0:T(8,128)S(1)}, u32[]{:S(2)}, u32[]{:S(2)}) collective-permute-start(f32[24,128]{1,0:T(8,128)S(1)} %get-tuple-element.54.sent_ref), channel_id=1, source_target_pairs={{0,1},{1,0},{2,3},{3,2},{4,5},{5,4},{6,7},{7,6},{8,9},{9,8},{10,11... | collective-permute-start | bytes 36872 | tf_op jit(solution)/shard_map/ppermute | solution.py:651
  45.3 9.0 %collective-permute-start.11 = (f32[8,128]{1,0:T(8,128)S(1)}, f32[8,128]{1,0:T(8,128)S(1)}, u32[]{:S(2)}, u32[]{:S(2)}) collective-permute-start(f32[8,128]{1,0:T(8,128)S(1)} %get-tuple-element.57), channel_id=1, source_target_pairs={{0,16},{8,24},{16,0},{24,8},{1,17},{9,25},{17,1},{25,9},{2,18},{10... | collective-permute-start | bytes 12296 | tf_op jit(solution)/shard_map/ppermute | solution.py:658
  50.8 5.0 %collective-permute-start.12 = (f32[8,8,256]{2,1,0:T(8,128)S(1)}, f32[8,8,256]{2,1,0:T(8,128)S(1)}, u32[]{:S(2)}, u32[]{:S(2)}) collective-permute-start(f32[8,8,256]{2,1,0:T(8,128)S(1)} %get-tuple-element.56.par_ref.refs_0_), channel_id=1, source_target_pairs={{0,2},{1,3},{2,4},{3,5},{4,6},{5,7},{6,0},{7,1},{8,10},{9,11},{10,... | collective-permute-start | bytes 196616 | tf_op jit(solution)/shard_map/ppermute | solution.py:808
  50.9 5.0 %collective-permute-start.13 = (f32[8,8,256]{2,1,0:T(8,128)S(1)}, f32[8,8,256]{2,1,0:T(8,128)S(1)}, u32[]{:S(2)}, u32[]{:S(2)}) collective-permute-start(f32[8,8,256]{2,1,0:T(8,128)S(1)} %get-tuple-element.56.par_ref.refs_0_), channel_id=1, source_target_pairs={{0,4},{1,5},{2,6},{3,7},{4,0},{5,1},{6,2},{7,3},{8,12},{9,13},{10,... | collective-permute-start | bytes 196616 | tf_op jit(solution)/shard_map/ppermute | solution.py:808
  51.9 5.5 %collective-permute-start.14 = (f32[8,8,256]{2,1,0:T(8,128)S(1)}, f32[8,8,256]{2,1,0:T(8,128)S(1)}, u32[]{:S(2)}, u32[]{:S(2)}) collective-permute-start(f32[8,8,256]{2,1,0:T(8,128)S(1)} %get-tuple-element.56.par_ref.refs_0_), channel_id=1, source_target_pairs={{0,6},{1,7},{2,0},{3,1},{4,2},{5,3},{6,4},{7,5},{8,14},{9,15},{10,... | collective-permute-start | bytes 196616 | tf_op jit(solution)/shard_map/ppermute | solution.py:808
  66.6 10.5 %collective-permute-start.15 = (f32[9,8,256]{2,1,0:T(8,128)S(1)}, f32[9,8,256]{2,1,0:T(8,128)S(1)}, u32[]{:S(2)}, u32[]{:S(2)}) collective-permute-start(f32[9,8,256]{2,1,0:T(8,128)S(1)} %get-tuple-element.59), channel_id=1, source_target_pairs={{0,6},{1,7},{2,0},{3,1},{4,2},{5,3},{6,4},{7,5},{8,14},{9,15},{10,... | collective-permute-start | bytes 221192 | tf_op jit(solution)/shard_map/ppermute | solution.py:808
  68.8 8.3 %collective-permute-start.16 = (f32[9,8,256]{2,1,0:T(8,128)S(1)}, f32[9,8,256]{2,1,0:T(8,128)S(1)}, u32[]{:S(2)}, u32[]{:S(2)}) collective-permute-start(f32[9,8,256]{2,1,0:T(8,128)S(1)} %get-tuple-element.60), channel_id=1, source_target_pairs={{0,4},{1,5},{2,6},{3,7},{4,0},{5,1},{6,2},{7,3},{8,12},{9,13},{10,... | collective-permute-start | bytes 221192 | tf_op jit(solution)/shard_map/ppermute | solution.py:808
  70.0 7.2 %collective-permute-start.17 = (f32[9,8,256]{2,1,0:T(8,128)S(1)}, f32[9,8,256]{2,1,0:T(8,128)S(1)}, u32[]{:S(2)}, u32[]{:S(2)}) collective-permute-start(f32[9,8,256]{2,1,0:T(8,128)S(1)} %get-tuple-element.61), channel_id=1, source_target_pairs={{0,2},{1,3},{2,4},{3,5},{4,6},{5,7},{6,0},{7,1},{8,10},{9,11},{10,... | collective-permute-start | bytes 221192 | tf_op jit(solution)/shard_map/ppermute | solution.py:808
  77.3 2.6 %collective-permute-start.18 = (f32[8,256]{1,0:T(8,128)S(1)}, f32[8,256]{1,0:T(8,128)S(1)}, u32[]{:S(2)}, u32[]{:S(2)}) collective-permute-start(f32[8,256]{1,0:T(8,128)S(1)} %get-tuple-element.63.sent_ref), channel_id=1, source_target_pairs={{0,8},{8,0},{16,24},{24,16},{1,9},{9,1},{17,25},{25,17},{2,10},{10... | collective-permute-start | bytes 24584 | tf_op jit(solution)/shard_map/ppermute | solution.py:645
  77.4 2.5 %collective-permute-start.19 = (f32[8,256]{1,0:T(8,128)S(1)}, f32[8,256]{1,0:T(8,128)S(1)}, u32[]{:S(2)}, u32[]{:S(2)}) collective-permute-start(f32[8,256]{1,0:T(8,128)S(1)} %get-tuple-element.64), channel_id=1, source_target_pairs={{8,16},{16,8},{9,17},{17,9},{10,18},{18,10},{11,19},{19,11},{12,20... | collective-permute-start | bytes 24584 | tf_op jit(solution)/shard_map/ppermute | solution.py:646
  79.9 7.8 %collective-permute-start.20 = (f32[24,128]{1,0:T(8,128)S(1)}, f32[24,128]{1,0:T(8,128)S(1)}, u32[]{:S(2)}, u32[]{:S(2)}) collective-permute-start(f32[24,128]{1,0:T(8,128)S(1)} %get-tuple-element.66.sent_ref), channel_id=1, source_target_pairs={{0,1},{1,0},{2,3},{3,2},{4,5},{5,4},{6,7},{7,6},{8,9},{9,8},{10,11... | collective-permute-start | bytes 36872 | tf_op jit(solution)/shard_map/ppermute | solution.py:651
  83.3 5.7 %collective-permute-start.21 = (f32[24,128]{1,0:T(8,128)S(1)}, f32[24,128]{1,0:T(8,128)S(1)}, u32[]{:S(2)}, u32[]{:S(2)}) collective-permute-start(f32[24,128]{1,0:T(8,128)S(1)} %get-tuple-element.67), channel_id=1, source_target_pairs={{1,2},{2,1},{3,4},{4,3},{5,6},{6,5},{9,10},{10,9},{11,12},{12,11},... | collective-permute-start | bytes 36872 | tf_op jit(solution)/shard_map/ppermute | solution.py:652
  89.8 4.5 %collective-permute-start.22 = (f32[8,128]{1,0:T(8,128)S(1)}, f32[8,128]{1,0:T(8,128)S(1)}, u32[]{:S(2)}, u32[]{:S(2)}) collective-permute-start(f32[8,128]{1,0:T(8,128)S(1)} %get-tuple-element.69), channel_id=1, source_target_pairs={{0,16},{8,24},{16,0},{24,8},{1,17},{9,25},{17,1},{25,9},{2,18},{10... | collective-permute-start | bytes 12296 | tf_op jit(solution)/shard_map/ppermute | solution.py:658

commit v4 on v3

--- a/solution.py
+++ b/solution.py
@@ -470,7 +470,7 @@
 
 
 def solve_kernel(tile_ref, low_ref, par_ref, *refs):
-    right_refs, (out_ref, first_ref, second_ref) = refs[:-3], refs[-3:]
+    right_refs, (out_ref, sent_ref) = refs[:-2], refs[-2:]
     lower = {}
     for where, (i, j) in enumerate(ENTRIES):
         lower[j, i] = low_ref[where]
@@ -488,38 +488,44 @@
             accum = accum - lower[k, i] * answer[k]
         answer[i] = accum * lower[i, i]
     rows = par_ref.shape[1]
-    odd = row_is_odd(tile_ref)
-    first_ref[...] = jnp.zeros(first_ref.shape, f32)
-    second_ref[...] = jnp.zeros(second_ref.shape, f32)
+    sent_ref[...] = jnp.zeros(sent_ref.shape, f32)
     for i in range(8):
         fresh = par_ref[i] + answer[i]
         out_ref[i] = fresh
         if i < 2:
-            top, bottom = fresh[0:1], fresh[rows - 1 : rows]
-            first_ref[i : i + 1, :] = jnp.where(odd, top, bottom)
-            second_ref[i : i + 1, :] = jnp.where(odd, bottom, top)
-    first_ref[2:4, 0:LANES] = ring_total([ref[8, 0:2, 0:LANES] for ref in right_refs])
-
-
-def rows_kernel(tile_ref, par_ref, sent_ref, first_ref, second_ref, tall_ref, near_ref, far_ref, scr):
+            sent_ref[i : i + 1, :] = fresh[0:1]
+            sent_ref[2 + i : 3 + i, :] = fresh[rows - 1 : rows]
+    sent_ref[4:6, 0:LANES] = ring_total([ref[8, 0:2, 0:LANES] for ref in right_refs])
+
+
+def relay_kernel(tile_ref, sent_ref, first_ref, out_ref):
+    odd = row_is_odd(tile_ref)
+    out_ref[...] = sent_ref[...] + first_ref[...]
+    out_ref[0:2, :] = jnp.where(odd, first_ref[0:2, :], first_ref[2:4, :])
+
+
+def rows_kernel(tile_ref, par_ref, first_ref, edge_ref, *refs, last):
+    light_refs, (tall_ref, near_ref, far_ref, scr) = refs[:-4], refs[-4:]
     rows, cols = par_ref.shape[1:]
+    place = tile_ref[0] // PLACE
     odd, side = row_is_odd(tile_ref), column_is_odd(tile_ref)
+    outer = jnp.where(jnp.logical_or(place == 0, place == last), 0.0, 1.0)
     near_ref[...] = jnp.zeros(near_ref.shape, f32)
     far_ref[...] = jnp.zeros(far_ref.shape, f32)
     for k in range(2):
-        one, two = first_ref[k : k + 1, :], second_ref[k : k + 1, :]
-        scr[7:8, :] = jnp.where(odd, one, two)
+        other = outer * edge_ref[k : k + 1, :]
+        scr[7:8, :] = jnp.where(odd, first_ref[2 + k : 3 + k, :], other)
         scr[8 : 8 + rows, :] = par_ref[k]
-        scr[8 + rows : 9 + rows, :] = jnp.where(odd, two, one)
+        scr[8 + rows : 9 + rows, :] = jnp.where(odd, other, first_ref[k : k + 1, :])
         tall = scr[7 : 7 + rows, :] + scr[8 : 8 + rows, :] + scr[9 : 9 + rows, :]
         tall_ref[k] = tall
         left, right = tall[:, 0:LANES], tall[:, cols - LANES : cols]
         near_ref[k * rows : (k + 1) * rows, :] = jnp.where(side, left, right)
         far_ref[k * rows : (k + 1) * rows, :] = jnp.where(side, right, left)
-    near_ref[2 * rows : 2 * rows + 2, :] = sent_ref[2:4, 0:LANES] + first_ref[2:4, 0:LANES]
-
-
-def smooth_kernel(tile_ref, par_ref, tall_ref, sent_ref, near_ref, far_ref, out_ref, light_ref):
+    near_ref[2 * rows : 2 * rows + 2, :] = total(ref[4:6, 0:LANES] for ref in light_refs)
+
+
+def smooth_kernel(tile_ref, par_ref, tall_ref, sent_ref, near_ref, far_ref, gain_ref, out_ref, gain_out_ref):
     rows, cols = par_ref.shape[1:]
     side = column_is_odd(tile_ref)
     lane = iota((rows, cols), 1)
@@ -535,8 +541,9 @@
         out_ref[k] = 0.5 * par_ref[k] + (tall + left + right) * (0.5 / 9.0)
     for k in range(2, 8):
         out_ref[k] = par_ref[k]
-    light_ref[...] = jnp.zeros(light_ref.shape, f32)
-    light_ref[0:2, :] = sent_ref[2 * rows : 2 * rows + 2, :] + near_ref[2 * rows : 2 * rows + 2, :]
+    light = sent_ref[2 * rows : 2 * rows + 2, 0:LIGHTS] + near_ref[2 * rows : 2 * rows + 2, 0:LIGHTS]
+    gains = gain_ref[...]
+    gain_out_ref[...] = gains + (light[0:1] - gains * light[1:2]) / (light[1:2] + 1.0)
 
 
 def smem():
@@ -616,6 +623,43 @@
     )(tile, own, got, *small, *pars, *vises)
 
 
+def pack_kernel(tile_ref, seen_ref, par_ref, vis_ref, send_ref, first_ref, sems):
+    parts = sems.shape[0]
+    width = send_ref.shape[2] // parts
+    copies = []
+    for z in range(parts):
+        start = pl.multiple_of((2 * z + 1 - lax.rem(tile_ref[0], 2)) * width, LANES)
+        copies.append(
+            pltpu.make_async_copy(
+                seen_ref.at[:, :, pl.ds(start, width)],
+                send_ref.at[:, :, z * width : (z + 1) * width],
+                sems.at[z],
+            )
+        )
+        copies[z].start()
+    first_ref[0:8] = par_ref[...]
+    first_ref[8] = vis_ref[...].astype(f32)
+    for copy in copies:
+        copy.wait()
+
+
+def pack_call(tile, observed, params, visible, parts):
+    far = pl.BlockSpec(memory_space=pltpu.MemorySpace.HBM)
+    samples, rows, width = observed.shape
+    return pl.pallas_call(
+        pack_kernel,
+        name="pack",
+        out_shape=[
+            jax.ShapeDtypeStruct((samples, rows, width // 2), observed.dtype),
+            jax.ShapeDtypeStruct((9,) + params.shape[1:], f32),
+        ],
+        in_specs=[smem(), far, vmem(), vmem()],
+        out_specs=[far, vmem()],
+        scratch_shapes=[pltpu.SemaphoreType.DMA((parts,))],
+        compiler_params=params_of(),
+    )(tile, observed, params, visible)
+
+
 def plain_call(kernel, name, shapes, scratch, tile, *args):
     return pl.pallas_call(
         kernel,
@@ -635,29 +679,36 @@
     return out
 
 
-def settle(tile, low, params, moved):
+def settle(tile, low, params, moved, gains):
     _, rows, cols = params.shape
     grps, tiles = lax.axis_size("grp"), lax.axis_size("tile")
     strip = (8, cols)
-    params, sent, other = plain_call(
-        solve_kernel, "solve", [params.shape, strip, strip], [], tile, low, params, *moved
-    )
+    params, sent = plain_call(solve_kernel, "solve", [params.shape, strip], [], tile, low, params, *moved)
     first = lax.ppermute(sent, "grp", pairs(grps, 0))
-    second = lax.ppermute(other, "grp", pairs(grps, 1))
+    if grps == 4:
+        (relay,) = plain_call(relay_kernel, "relay", [strip], [], tile, sent, first)
+        edge = lax.ppermute(relay, "grp", [(i, i ^ 2) for i in range(grps)])
+        lights = [relay, edge]
+    else:
+        second = lax.ppermute(sent, "grp", pairs(grps, 1))
+        odd = lax.axis_index("grp") % 2 == 1
+        edge = jnp.where(odd, second, jnp.roll(second, -2, axis=0))
+        light = sent + first
+        bit = 2
+        while bit < grps:
+            light = light + lax.ppermute(light, "grp", [(i, i ^ bit) for i in range(grps)])
+            bit *= 2
+        lights = [light]
     patch = (2 * rows + 8, LANES)
     tall, sent, other = plain_call(
-        rows_kernel, "rows", [(2, rows, cols), patch, patch], [(24, cols)], tile, params, sent, first, second
+        functools.partial(rows_kernel, last=grps - 1), "rows", [(2, rows, cols), patch, patch], [(24, cols)],
+        tile, params, first, edge, *lights,
     )
+    far = lax.ppermute(other, "tile", pairs(tiles, 1))
     near = lax.ppermute(sent, "tile", pairs(tiles, 0))
-    far = lax.ppermute(other, "tile", pairs(tiles, 1))
-    params, light = plain_call(
-        smooth_kernel, "smooth", [params.shape, (8, LANES)], [], tile, params, tall, sent, near, far
+    return plain_call(
+        smooth_kernel, "smooth", [params.shape, gains.shape], [], tile, params, tall, sent, near, far, gains
     )
-    bit = 2
-    while bit < grps:
-        light = light + lax.ppermute(light, "grp", [(i, i ^ bit) for i in range(grps)])
-        bit *= 2
-    return params, light[0:1, 0:LIGHTS], light[1:2, 0:LIGHTS]
 
 
 def exact(a, b, sides):
@@ -809,21 +860,17 @@
 
 
 def on_device(observed, visible, params_start, light_directions, view_dirs, gains_start):
-    samples, rows, _ = observed.shape
-    cols = visible.shape[1]
+    samples = observed.shape[0]
     tiles = lax.axis_size("tile")
     nz = tiles // 2
     tile = lax.axis_index("tile")
-    core = tile % 2
     held = 2 * samples
 
-    split = observed.reshape(samples, rows, nz, 2, cols)
-    send = lax.dynamic_index_in_dim(split, 1 - core, axis=3, keepdims=False).reshape(samples, rows, nz * cols)
+    here = (tile + PLACE * lax.axis_index("grp")).astype(jnp.int32).reshape(1)
+    send, first = pack_call(here, observed, params_start, visible, nz)
     got = lax.ppermute(send, "tile", [(i, i ^ 1) for i in range(tiles)])
-    first = jnp.concatenate([params_start, visible.astype(f32)[None]], axis=0)
     blocks = [first] + [shifted(first, s, nz) for s in range(1, nz)]
     vises = blocks
-    here = (tile + PLACE * lax.axis_index("grp")).astype(jnp.int32).reshape(1)
     tables = setup_call(here, light_directions, view_dirs, held)
 
     params = params_start
@@ -832,8 +879,7 @@
         low = normal_call(params, visible, gains, tables)
         rights = sample_call(here, observed, got, gains, tables, blocks, vises)
         moved = [rights[0]] + [shifted(rights[s], -s, nz) for s in range(1, nz)]
-        params, lifted, energy = settle(here, low, params, moved)
-        gains = gains + (lifted - gains * energy) / (energy + 1.0)
+        params, gains = settle(here, low, params, moved, gains)
         if iteration + 1 < ITERS:
             blocks = [params] + [shifted(params, s, nz) for s in range(1, nz)]
     return params, gains.reshape(LIGHTS)

time: 96.5 us -> 91.7 us (0.950); the launches traced: 94.8 us -> 91.4 us
  starting transfers between devices: 42.3 us -> 37.5 us
  waiting for transfers between devices: 12.1 us -> 13.9 us
  other arithmetic: 1.4 us -> 0 us
    ppermute x4 -> x2, starting transfers between devices: 10.4 us -> 2.48 us  [settle(): edge = lax.ppermute(relay, 'grp', [(i, i ^ 2) for i in range(grps)])]
    unnamed x12 -> x18, local copies, waits for them, and re-layouts: 0.02 us -> 3.16 us
    dynamic_slice x1 -> x0, local copies, waits for them, and re-layouts: 2.41 us -> none  [on_device(): lax.dynamic_index_in_dim(split, 1 - core, axis=3, keepdims=False)]
    ppermute x4 -> x2, waiting for transfers between devices: 1 us -> 2.58 us  [settle(): edge = lax.ppermute(relay, 'grp', [(i, i ^ 2) for i in range(grps)])]
    ppermute x2, starting transfers between devices: 1.35 us -> 2.54 us  [settle(): first = lax.ppermute(sent, 'grp', pairs(grps, 0))]
    ppermute x2, starting transfers between devices: 11 us -> 12.1 us  [settle(): far = lax.ppermute(other, 'tile', pairs(tiles, 1))]
  transfers between devices with their start and end apart: 23 -> 21, of which waited for: 9 -> 10; matrix products, arithmetic and copies ran while one was open for 1% -> 0% of each run, Pallas kernels for 17% -> 18%
where the time goes in v4:
time: 91.7 us; the launch traced here: 91.4 us
  starting transfers between devices  37.5 us (41%)
  Pallas kernels  36 us (39%)
  waiting for transfers between devices  13.9 us (15%)
  local copies, waits for them, and re-layouts  3.16 us (3%)
    pallas_call x2, Pallas kernels, sample_call(): pl.pallas_call(functools.partial(sample_kernel, parts=parts), name='sampl...  18.6 us
    ppermute x12, starting transfers between devices, shifted(): lax.ppermute(x, 'tile', [(2 * z + c, 2 * ((z + by) % nz) + c) for z in ra...  16.1 us
    pallas_call x2, Pallas kernels, normal_call(): pl.pallas_call(normal_kernel, name='normal_factor', out_shape=jax.ShapeDt...  14.3 us
    ppermute x2, starting transfers between devices, settle(): far = lax.ppermute(other, 'tile', pairs(tiles, 1))  12.1 us
    ppermute x12, waiting for transfers between devices, shifted(): lax.ppermute(x, 'tile', [(2 * z + c, 2 * ((z + by) % nz) + c) for z in ra...  6.12 us
    ppermute x2, starting transfers between devices, settle(): near = lax.ppermute(sent, 'tile', pairs(tiles, 0))  4.19 us
    unnamed x18, local copies, waits for them, and re-layouts  3.16 us
    ppermute x2, waiting for transfers between devices, settle(): far = lax.ppermute(other, 'tile', pairs(tiles, 1))  2.64 us
  transfers between devices with their start and end apart: 21, of which 10 were waited for; matrix products, arithmetic and copies ran while one was open for 0% of the time, Pallas kernels for 18%

profile of v4, /device:TPU:1, one launch (start us, length us, event | category | flops | bytes accessed | tf_op | source)
XLA Modules:
  0.0 91.4 jit_solution(1565552004818291527)
XLA Ops:
  0.7 1.6 %copy-done = bf16[64,8,2048]{2,1,0:T(8,128)(2,1)S(1)} copy-done((bf16[64,8,2048]{2,1,0:T(8,128)(2,1)S(1)}, bf16[64,8,2048]{2,1,0:T(8,128)(2,1)}, u32[]{:S(2)}) %copy-start) | copy-done | bytes 2097176
  2.3 0.8 copy-done.2
  3.1 0.7 copy-done.4
  3.8 0.2 pack.1
  4.0 0.0 copy-start.3
  4.0 0.0 copy-start.5
  4.1 0.1 collective-permute-start
  4.2 2.7 %collective-permute-start.1 = (f32[9,8,256]{2,1,0:T(8,128)S(1)}, f32[9,8,256]{2,1,0:T(8,128)S(1)}, u32[]{:S(2)}, u32[]{:S(2)}) collective-permute-start(f32[9,8,256]{2,1,0:T(8,128)S(1)} %get-tuple-element.47.refs_0_.refs_4_), channel_id=1, source_target_pairs={{0,2},{1,3},{2,4},{3,5},{4,6},{5,7},{6,0},{7,1},{8,10},{9,11},{10,... | collective-permute-start | bytes 221192 | tf_op jit(solution)/shard_map/ppermute | solution.py:859
  6.9 2.3 %collective-permute-start.2 = (f32[9,8,256]{2,1,0:T(8,128)S(1)}, f32[9,8,256]{2,1,0:T(8,128)S(1)}, u32[]{:S(2)}, u32[]{:S(2)}) collective-permute-start(f32[9,8,256]{2,1,0:T(8,128)S(1)} %get-tuple-element.47.refs_0_.refs_4_), channel_id=1, source_target_pairs={{0,4},{1,5},{2,6},{3,7},{4,0},{5,1},{6,2},{7,3},{8,12},{9,13},{10,... | collective-permute-start | bytes 221192 | tf_op jit(solution)/shard_map/ppermute | solution.py:859
  9.2 1.1 %collective-permute-start.3 = (f32[9,8,256]{2,1,0:T(8,128)S(1)}, f32[9,8,256]{2,1,0:T(8,128)S(1)}, u32[]{:S(2)}, u32[]{:S(2)}) collective-permute-start(f32[9,8,256]{2,1,0:T(8,128)S(1)} %get-tuple-element.47.refs_0_.refs_4_), channel_id=1, source_target_pairs={{0,6},{1,7},{2,0},{3,1},{4,2},{5,3},{6,4},{7,5},{8,14},{9,15},{10,... | collective-permute-start | bytes 221192 | tf_op jit(solution)/shard_map/ppermute | solution.py:859
  10.3 1.8 %tables.1 = (f32[8,32]{1,0:T(8,128)S(1)}, f32[8,16]{1,0:T(8,128)S(1)}, bf16[512,48]{1,0:T(8,128)(2,1)S(1)}, f32[32,512]{1,0:T(8,128)S(1)}, f32[16,512]{1,0:T(8,1...) custom-call(s32[1]{0:T(128)} %bitcast.tile_ref, ...), custom_call_target="tpu_custom_call" | custom-call | tf_op jit(solution)/shard_map/tables/pallas_call | solution.py:846
  12.1 2.7 %collective-permute-done.2.refs_2_.refs_6_ = f32[9,8,256]{2,1,0:T(8,128)S(1)} collective-permute-done((f32[9,8,256]{2,1,0:T(8,128)S(1)}, f32[9,8,256]{2,1,0:T(8,128)S(1)}, u32[]{:S(2)}, u32[]{:S(2)}) %collective-permute-start.2) | collective-permute-done | bytes 73760 | tf_op jit(solution)/shard_map/ppermute | solution.py:859
  14.9 0.0 collective-permute-done.3.refs_3_.refs_7_
  14.9 0.0 collective-permute-done.got_ref
  14.9 9.3 %sample_sums.2 = (f32[9,8,256]{2,1,0:T(8,128)S(1)}, f32[9,8,256]{2,1,0:T(8,128)S(1)}, f32[9,8,256]{2,1,0:T(8,128)S(1)}, f32[9,8,256]{2,1,0:T(8,128)S(1)}) custom-call(s32[1]{0:T(128)} %bitcast.tile_ref, bf16[64,8,2048]{2,1,0:T(8,128)(2,1)S(1)} %copy-done.1, bf16[64,8,1024]{2,1,0:T(8,128)(2,1)S(1)} %collective-permute-done.got_ref, f32[1,32]{1,0:T(1,128)S(1)} %bitcast.3, ...), custom_call_target="tpu_custom_call" | custom-call | tf_op jit(solution)/shard_map/sample_sums/pallas_call | solution.py:598
  24.2 2.6 %collective-permute-start.4 = (f32[9,8,256]{2,1,0:T(8,128)S(1)}, f32[9,8,256]{2,1,0:T(8,128)S(1)}, u32[]{:S(2)}, u32[]{:S(2)}) collective-permute-start(f32[9,8,256]{2,1,0:T(8,128)S(1)} %get-tuple-element.49), channel_id=1, source_target_pairs={{0,6},{1,7},{2,0},{3,1},{4,2},{5,3},{6,4},{7,5},{8,14},{9,15},{10,... | collective-permute-start | bytes 221192 | tf_op jit(solution)/shard_map/ppermute | solution.py:859
  26.8 0.5 collective-permute-start.5
  27.3 0.0 collective-permute-start.6
  27.3 7.1 %normal_factor.2.low_ref = f32[44,8,256]{2,1,0:T(8,128)S(1)} custom-call(f32[8,8,256]{2,1,0:T(8,128)S(1)} %copy-done.3, s32[8,256]{1,0:T(8,128)S(1)} %copy-done.5, f32[1,32]{1,0:T(1,128)S(1)} %bitcast.4, f32[8,32]{1,0:T(8,128)S(1)} %get-tuple-element.36.near_ref, f32[8,16]{1,0:T(8,128)S(1)} %get-tuple-element.37.cams_ref, ...), custom_call_target="tpu_custom_call" | custom-call | tf_op jit(solution)/shard_map/normal_factor/pallas_call | solution.py:565
  34.5 0.1 collective-permute-done.5.refs_2_
  34.6 0.1 solve.2
  34.7 1.3 %collective-permute-start.7 = (f32[8,256]{1,0:T(8,128)S(1)}, f32[8,256]{1,0:T(8,128)S(1)}, u32[]{:S(2)}, u32[]{:S(2)}) collective-permute-start(f32[8,256]{1,0:T(8,128)S(1)} %get-tuple-element.53.sent_ref), channel_id=1, source_target_pairs={{0,8},{8,0},{16,24},{24,16},{1,9},{9,1},{17,25},{25,17},{2,10},{10... | collective-permute-start | bytes 24584 | tf_op jit(solution)/shard_map/ppermute | solution.py:687
  36.0 1.3 %collective-permute-done.7.first_ref = f32[8,256]{1,0:T(8,128)S(1)} collective-permute-done((f32[8,256]{1,0:T(8,128)S(1)}, f32[8,256]{1,0:T(8,128)S(1)}, u32[]{:S(2)}, u32[]{:S(2)}) %collective-permute-start.7) | collective-permute-done | bytes 8224 | tf_op jit(solution)/shard_map/ppermute | solution.py:687
  37.3 1.2 %collective-permute-start.8 = (f32[8,256]{1,0:T(8,128)S(1)}, f32[8,256]{1,0:T(8,128)S(1)}, u32[]{:S(2)}, u32[]{:S(2)}) collective-permute-start(f32[8,256]{1,0:T(8,128)S(1)} %relay.2.refs_0_), channel_id=1, source_target_pairs={{0,16},{8,24},{16,0},{24,8},{1,17},{9,25},{17,1},{25,9},{2,18},{10... | collective-permute-start | bytes 24584 | tf_op jit(solution)/shard_map/ppermute | solution.py:690
  38.5 1.3 %collective-permute-done.8.edge_ref.refs_1_ = f32[8,256]{1,0:T(8,128)S(1)} collective-permute-done((f32[8,256]{1,0:T(8,128)S(1)}, f32[8,256]{1,0:T(8,128)S(1)}, u32[]{:S(2)}, u32[]{:S(2)}) %collective-permute-start.8) | collective-permute-done | bytes 8224 | tf_op jit(solution)/shard_map/ppermute | solution.py:690
  39.8 7.8 %collective-permute-start.10 = (f32[24,128]{1,0:T(8,128)S(1)}, f32[24,128]{1,0:T(8,128)S(1)}, u32[]{:S(2)}, u32[]{:S(2)}) collective-permute-start(f32[24,128]{1,0:T(8,128)S(1)} %get-tuple-element.56), channel_id=1, source_target_pairs={{1,2},{2,1},{3,4},{4,3},{5,6},{6,5},{9,10},{10,9},{11,12},{12,11},... | collective-permute-start | bytes 36872 | tf_op jit(solution)/shard_map/ppermute | solution.py:707
  47.6 0.1 collective-permute-start.9
  47.7 1.3 %collective-permute-done.10.far_ref = f32[24,128]{1,0:T(8,128)S(1)} collective-permute-done((f32[24,128]{1,0:T(8,128)S(1)}, f32[24,128]{1,0:T(8,128)S(1)}, u32[]{:S(2)}, u32[]{:S(2)}) %collective-permute-start.10) | collective-permute-done | bytes 12320 | tf_op jit(solution)/shard_map/ppermute | solution.py:707
  49.0 0.1 smooth.2
  49.1 0.1 collective-permute-start.11
  49.2 1.1 %collective-permute-start.12 = (f32[8,8,256]{2,1,0:T(8,128)S(1)}, f32[8,8,256]{2,1,0:T(8,128)S(1)}, u32[]{:S(2)}, u32[]{:S(2)}) collective-permute-start(f32[8,8,256]{2,1,0:T(8,128)S(1)} %get-tuple-element.57.par_ref.refs_0_), channel_id=1, source_target_pairs={{0,4},{1,5},{2,6},{3,7},{4,0},{5,1},{6,2},{7,3},{8,12},{9,13},{10,... | collective-permute-start | bytes 196616 | tf_op jit(solution)/shard_map/ppermute | solution.py:859
  50.2 2.3 %collective-permute-start.13 = (f32[8,8,256]{2,1,0:T(8,128)S(1)}, f32[8,8,256]{2,1,0:T(8,128)S(1)}, u32[]{:S(2)}, u32[]{:S(2)}) collective-permute-start(f32[8,8,256]{2,1,0:T(8,128)S(1)} %get-tuple-element.57.par_ref.refs_0_), channel_id=1, source_target_pairs={{0,6},{1,7},{2,0},{3,1},{4,2},{5,3},{6,4},{7,5},{8,14},{9,15},{10,... | collective-permute-start | bytes 196616 | tf_op jit(solution)/shard_map/ppermute | solution.py:859
  52.5 2.1 %collective-permute-done.11.refs_1_ = f32[8,8,256]{2,1,0:T(8,128)S(1)} collective-permute-done((f32[8,8,256]{2,1,0:T(8,128)S(1)}, f32[8,8,256]{2,1,0:T(8,128)S(1)}, u32[]{:S(2)}, u32[]{:S(2)}) %collective-permute-start.11) | collective-permute-done | bytes 65568 | tf_op jit(solution)/shard_map/ppermute | solution.py:859
  54.6 1.2 %collective-permute-done.13.refs_3_ = f32[8,8,256]{2,1,0:T(8,128)S(1)} collective-permute-done((f32[8,8,256]{2,1,0:T(8,128)S(1)}, f32[8,8,256]{2,1,0:T(8,128)S(1)}, u32[]{:S(2)}, u32[]{:S(2)}) %collective-permute-start.13) | collective-permute-done | bytes 65568 | tf_op jit(solution)/shard_map/ppermute | solution.py:859
  55.8 9.3 %sample_sums.3 = (f32[9,8,256]{2,1,0:T(8,128)S(1)}, f32[9,8,256]{2,1,0:T(8,128)S(1)}, f32[9,8,256]{2,1,0:T(8,128)S(1)}, f32[9,8,256]{2,1,0:T(8,128)S(1)}) custom-call(s32[1]{0:T(128)} %bitcast.tile_ref, bf16[64,8,2048]{2,1,0:T(8,128)(2,1)S(1)} %copy-done.1, bf16[64,8,1024]{2,1,0:T(8,128)(2,1)S(1)} %collective-permute-done.got_ref, ...), custom_call_target="tpu_custom_call" | custom-call | tf_op jit(solution)/shard_map/sample_sums/pallas_call | solution.py:598
  65.0 2.3 %collective-permute-start.14 = (f32[9,8,256]{2,1,0:T(8,128)S(1)}, f32[9,8,256]{2,1,0:T(8,128)S(1)}, u32[]{:S(2)}, u32[]{:S(2)}) collective-permute-start(f32[9,8,256]{2,1,0:T(8,128)S(1)} %get-tuple-element.60), channel_id=1, source_target_pairs={{0,6},{1,7},{2,0},{3,1},{4,2},{5,3},{6,4},{7,5},{8,14},{9,15},{10,... | collective-permute-start | bytes 221192 | tf_op jit(solution)/shard_map/ppermute | solution.py:859
  67.3 1.0 %collective-permute-start.15 = (f32[9,8,256]{2,1,0:T(8,128)S(1)}, f32[9,8,256]{2,1,0:T(8,128)S(1)}, u32[]{:S(2)}, u32[]{:S(2)}) collective-permute-start(f32[9,8,256]{2,1,0:T(8,128)S(1)} %get-tuple-element.61), channel_id=1, source_target_pairs={{0,4},{1,5},{2,6},{3,7},{4,0},{5,1},{6,2},{7,3},{8,12},{9,13},{10,... | collective-permute-start | bytes 221192 | tf_op jit(solution)/shard_map/ppermute | solution.py:859
  68.3 0.2 collective-permute-start.16
  68.5 7.1 %normal_factor.3.low_ref = f32[44,8,256]{2,1,0:T(8,128)S(1)} custom-call(f32[8,8,256]{2,1,0:T(8,128)S(1)} %get-tuple-element.57.par_ref.refs_0_, s32[8,256]{1,0:T(8,128)S(1)} %copy-done.5, f32[1,32]{1,0:T(1,128)S(1)} %get-tuple-element.58.gain_ref, f32[8,32]{1,0:T(8,128)S(1)} %get-tuple-element.36.near_ref, f32[8,16]{1,0:T(8,128)S(1)} %get-tuple-element.37.cams_ref, ...), custom_call_target="tpu_custom_call" | custom-call | tf_op jit(solution)/shard_map/normal_factor/pallas_call | solution.py:565
  75.7 0.1 solve.3
  75.8 1.3 %collective-permute-start.17 = (f32[8,256]{1,0:T(8,128)S(1)}, f32[8,256]{1,0:T(8,128)S(1)}, u32[]{:S(2)}, u32[]{:S(2)}) collective-permute-start(f32[8,256]{1,0:T(8,128)S(1)} %get-tuple-element.64.sent_ref), channel_id=1, source_target_pairs={{0,8},{8,0},{16,24},{24,16},{1,9},{9,1},{17,25},{25,17},{2,10},{10... | collective-permute-start | bytes 24584 | tf_op jit(solution)/shard_map/ppermute | solution.py:687
  77.0 1.3 %collective-permute-done.17.first_ref = f32[8,256]{1,0:T(8,128)S(1)} collective-permute-done((f32[8,256]{1,0:T(8,128)S(1)}, f32[8,256]{1,0:T(8,128)S(1)}, u32[]{:S(2)}, u32[]{:S(2)}) %collective-permute-start.17) | collective-permute-done | bytes 8224 | tf_op jit(solution)/shard_map/ppermute | solution.py:687
  78.3 1.2 %collective-permute-start.18 = (f32[8,256]{1,0:T(8,128)S(1)}, f32[8,256]{1,0:T(8,128)S(1)}, u32[]{:S(2)}, u32[]{:S(2)}) collective-permute-start(f32[8,256]{1,0:T(8,128)S(1)} %relay.3.refs_0_), channel_id=1, source_target_pairs={{0,16},{8,24},{16,0},{24,8},{1,17},{9,25},{17,1},{25,9},{2,18},{10... | collective-permute-start | bytes 24584 | tf_op jit(solution)/shard_map/ppermute | solution.py:690
  79.6 1.3 %collective-permute-done.18.edge_ref.refs_1_ = f32[8,256]{1,0:T(8,128)S(1)} collective-permute-done((f32[8,256]{1,0:T(8,128)S(1)}, f32[8,256]{1,0:T(8,128)S(1)}, u32[]{:S(2)}, u32[]{:S(2)}) %collective-permute-start.18) | collective-permute-done | bytes 8224 | tf_op jit(solution)/shard_map/ppermute | solution.py:690
  80.9 4.1 %collective-permute-start.19 = (f32[24,128]{1,0:T(8,128)S(1)}, f32[24,128]{1,0:T(8,128)S(1)}, u32[]{:S(2)}, u32[]{:S(2)}) collective-permute-start(f32[24,128]{1,0:T(8,128)S(1)} %get-tuple-element.66.sent_ref), channel_id=1, source_target_pairs={{0,1},{1,0},{2,3},{3,2},{4,5},{5,4},{6,7},{7,6},{8,9},{9,8},{10,11... | collective-permute-start | bytes 36872 | tf_op jit(solution)/shard_map/ppermute | solution.py:708
  85.0 4.3 %collective-permute-start.20 = (f32[24,128]{1,0:T(8,128)S(1)}, f32[24,128]{1,0:T(8,128)S(1)}, u32[]{:S(2)}, u32[]{:S(2)}) collective-permute-start(f32[24,128]{1,0:T(8,128)S(1)} %get-tuple-element.67), channel_id=1, source_target_pairs={{1,2},{2,1},{3,4},{4,3},{5,6},{6,5},{9,10},{10,9},{11,12},{12,11},... | collective-permute-start | bytes 36872 | tf_op jit(solution)/shard_map/ppermute | solution.py:707
  89.4 1.4 %collective-permute-done.20.far_ref = f32[24,128]{1,0:T(8,128)S(1)} collective-permute-done((f32[24,128]{1,0:T(8,128)S(1)}, f32[24,128]{1,0:T(8,128)S(1)}, u32[]{:S(2)}, u32[]{:S(2)}) %collective-permute-start.20) | collective-permute-done | bytes 12320 | tf_op jit(solution)/shard_map/ppermute | solution.py:707
  90.7 0.7 smooth.3
  (26 shorter events, 0.1 us)
Async XLA Ops:
  0.6 9.7 %copy-start.8 = (f32[3,16]{1,0:T(4,128)S(1)}, f32[3,16]{1,0:T(4,128)}, u32[]{:S(2)}) copy-start(f32[3,16]{1,0:T(4,128)} %view_ref.1) | copy-start | bytes 580
  0.6 9.7 %copy-start.7 = (f32[3,32]{1,0:T(4,128)S(1)}, f32[3,32]{1,0:T(4,128)}, u32[]{:S(2)}) copy-start(f32[3,32]{1,0:T(4,128)} %light_ref.1) | copy-start | bytes 1156
  0.7 14.2 %copy-start.6 = (f32[32]{0:T(128)S(1)}, f32[32]{0:T(128)}, u32[]{:S(2)}) copy-start(f32[32]{0:T(128)} %param.11) | copy-start | bytes 388
  0.7 1.6 %copy-start = (bf16[64,8,2048]{2,1,0:T(8,128)(2,1)S(1)}, bf16[64,8,2048]{2,1,0:T(8,128)(2,1)}, u32[]{:S(2)}) copy-start(bf16[64,8,2048]{2,1,0:T(8,128)(2,1)} %own_ref.3) | copy-start | bytes 6291460
  2.3 0.8 copy-start.2
  3.1 0.7 copy-start.4
  3.8 11.1 %copy-start.1 = (bf16[64,8,2048]{2,1,0:T(8,128)(2,1)S(1)}, bf16[64,8,2048]{2,1,0:T(8,128)(2,1)}, u32[]{:S(2)}) copy-start(bf16[64,8,2048]{2,1,0:T(8,128)(2,1)} %own_ref.3) | copy-start | bytes 6291460
  4.0 23.3 %copy-start.3 = (f32[8,8,256]{2,1,0:T(8,128)S(1)}, f32[8,8,256]{2,1,0:T(8,128)}, u32[]{:S(2)}) copy-start(f32[8,8,256]{2,1,0:T(8,128)} %par_ref.5) | copy-start | bytes 196612
  4.0 23.3 %copy-start.5 = (s32[8,256]{1,0:T(8,128)S(1)}, s32[8,256]{1,0:T(8,128)}, u32[]{:S(2)}) copy-start(s32[8,256]{1,0:T(8,128)} %vis_ref.5) | copy-start | bytes 24580
  4.1 10.8 %collective-permute-start = (bf16[64,8,1024]{2,1,0:T(8,128)(2,1)S(1)}, bf16[64,8,1024]{2,1,0:T(8,128)(2,1)S(1)}, u32[]{:S(2)}, u32[]{:S(2)}) collective-permute-start(bf16[64,8,1024]{2,1,0:T(8,128)(2,1)S(1)} %get-tuple-element.41), channel_id=1, source_target_pairs={{0,1},{1,0},{2,3},{3,2},{4,5},{5,4},{6,7},{7,6},{8,9},{9,8},{10,11... | collective-permute-start | bytes 3145736 | tf_op jit(solution)/shard_map/ppermute | solution.py:871
  4.2 8.0 %collective-permute-start.1 = (f32[9,8,256]{2,1,0:T(8,128)S(1)}, f32[9,8,256]{2,1,0:T(8,128)S(1)}, u32[]{:S(2)}, u32[]{:S(2)}) collective-permute-start(f32[9,8,256]{2,1,0:T(8,128)S(1)} %get-tuple-element.47.refs_0_.refs_4_), channel_id=1, source_target_pairs={{0,2},{1,3},{2,4},{3,5},{4,6},{5,7},{6,0},{7,1},{8,10},{9,11},{10,... | collective-permute-start | bytes 221192 | tf_op jit(solution)/shard_map/ppermute | solution.py:859
  6.9 7.9 %collective-permute-start.2 = (f32[9,8,256]{2,1,0:T(8,128)S(1)}, f32[9,8,256]{2,1,0:T(8,128)S(1)}, u32[]{:S(2)}, u32[]{:S(2)}) collective-permute-start(f32[9,8,256]{2,1,0:T(8,128)S(1)} %get-tuple-element.47.refs_0_.refs_4_), channel_id=1, source_target_pairs={{0,4},{1,5},{2,6},{3,7},{4,0},{5,1},{6,2},{7,3},{8,12},{9,13},{10,... | collective-permute-start | bytes 221192 | tf_op jit(solution)/shard_map/ppermute | solution.py:859
  9.2 5.6 %collective-permute-start.3 = (f32[9,8,256]{2,1,0:T(8,128)S(1)}, f32[9,8,256]{2,1,0:T(8,128)S(1)}, u32[]{:S(2)}, u32[]{:S(2)}) collective-permute-start(f32[9,8,256]{2,1,0:T(8,128)S(1)} %get-tuple-element.47.refs_0_.refs_4_), channel_id=1, source_target_pairs={{0,6},{1,7},{2,0},{3,1},{4,2},{5,3},{6,4},{7,5},{8,14},{9,15},{10,... | collective-permute-start | bytes 221192 | tf_op jit(solution)/shard_map/ppermute | solution.py:859
  24.2 10.3 %collective-permute-start.4 = (f32[9,8,256]{2,1,0:T(8,128)S(1)}, f32[9,8,256]{2,1,0:T(8,128)S(1)}, u32[]{:S(2)}, u32[]{:S(2)}) collective-permute-start(f32[9,8,256]{2,1,0:T(8,128)S(1)} %get-tuple-element.49), channel_id=1, source_target_pairs={{0,6},{1,7},{2,0},{3,1},{4,2},{5,3},{6,4},{7,5},{8,14},{9,15},{10,... | collective-permute-start | bytes 221192 | tf_op jit(solution)/shard_map/ppermute | solution.py:859
  26.8 7.8 %collective-permute-start.5 = (f32[9,8,256]{2,1,0:T(8,128)S(1)}, f32[9,8,256]{2,1,0:T(8,128)S(1)}, u32[]{:S(2)}, u32[]{:S(2)}) collective-permute-start(f32[9,8,256]{2,1,0:T(8,128)S(1)} %get-tuple-element.50), channel_id=1, source_target_pairs={{0,4},{1,5},{2,6},{3,7},{4,0},{5,1},{6,2},{7,3},{8,12},{9,13},{10,... | collective-permute-start | bytes 221192 | tf_op jit(solution)/shard_map/ppermute | solution.py:859
  27.3 7.3 %collective-permute-start.6 = (f32[9,8,256]{2,1,0:T(8,128)S(1)}, f32[9,8,256]{2,1,0:T(8,128)S(1)}, u32[]{:S(2)}, u32[]{:S(2)}) collective-permute-start(f32[9,8,256]{2,1,0:T(8,128)S(1)} %get-tuple-element.51), channel_id=1, source_target_pairs={{0,2},{1,3},{2,4},{3,5},{4,6},{5,7},{6,0},{7,1},{8,10},{9,11},{10,... | collective-permute-start | bytes 221192 | tf_op jit(solution)/shard_map/ppermute | solution.py:859
  34.7 2.6 %collective-permute-start.7 = (f32[8,256]{1,0:T(8,128)S(1)}, f32[8,256]{1,0:T(8,128)S(1)}, u32[]{:S(2)}, u32[]{:S(2)}) collective-permute-start(f32[8,256]{1,0:T(8,128)S(1)} %get-tuple-element.53.sent_ref), channel_id=1, source_target_pairs={{0,8},{8,0},{16,24},{24,16},{1,9},{9,1},{17,25},{25,17},{2,10},{10... | collective-permute-start | bytes 24584 | tf_op jit(solution)/shard_map/ppermute | solution.py:687
  37.3 2.5 %collective-permute-start.8 = (f32[8,256]{1,0:T(8,128)S(1)}, f32[8,256]{1,0:T(8,128)S(1)}, u32[]{:S(2)}, u32[]{:S(2)}) collective-permute-start(f32[8,256]{1,0:T(8,128)S(1)} %relay.2.refs_0_), channel_id=1, source_target_pairs={{0,16},{8,24},{16,0},{24,8},{1,17},{9,25},{17,1},{25,9},{2,18},{10... | collective-permute-start | bytes 24584 | tf_op jit(solution)/shard_map/ppermute | solution.py:690
  39.8 9.2 %collective-permute-start.10 = (f32[24,128]{1,0:T(8,128)S(1)}, f32[24,128]{1,0:T(8,128)S(1)}, u32[]{:S(2)}, u32[]{:S(2)}) collective-permute-start(f32[24,128]{1,0:T(8,128)S(1)} %get-tuple-element.56), channel_id=1, source_target_pairs={{1,2},{2,1},{3,4},{4,3},{5,6},{6,5},{9,10},{10,9},{11,12},{12,11},... | collective-permute-start | bytes 36872 | tf_op jit(solution)/shard_map/ppermute | solution.py:707
  47.6 1.4 %collective-permute-start.9 = (f32[24,128]{1,0:T(8,128)S(1)}, f32[24,128]{1,0:T(8,128)S(1)}, u32[]{:S(2)}, u32[]{:S(2)}) collective-permute-start(f32[24,128]{1,0:T(8,128)S(1)} %get-tuple-element.55.sent_ref), channel_id=1, source_target_pairs={{0,1},{1,0},{2,3},{3,2},{4,5},{5,4},{6,7},{7,6},{8,9},{9,8},{10,11... | collective-permute-start | bytes 36872 | tf_op jit(solution)/shard_map/ppermute | solution.py:708
  49.1 5.5 %collective-permute-start.11 = (f32[8,8,256]{2,1,0:T(8,128)S(1)}, f32[8,8,256]{2,1,0:T(8,128)S(1)}, u32[]{:S(2)}, u32[]{:S(2)}) collective-permute-start(f32[8,8,256]{2,1,0:T(8,128)S(1)} %get-tuple-element.57.par_ref.refs_0_), channel_id=1, source_target_pairs={{0,2},{1,3},{2,4},{3,5},{4,6},{5,7},{6,0},{7,1},{8,10},{9,11},{10,... | collective-permute-start | bytes 196616 | tf_op jit(solution)/shard_map/ppermute | solution.py:859
  49.2 5.5 %collective-permute-start.12 = (f32[8,8,256]{2,1,0:T(8,128)S(1)}, f32[8,8,256]{2,1,0:T(8,128)S(1)}, u32[]{:S(2)}, u32[]{:S(2)}) collective-permute-start(f32[8,8,256]{2,1,0:T(8,128)S(1)} %get-tuple-element.57.par_ref.refs_0_), channel_id=1, source_target_pairs={{0,4},{1,5},{2,6},{3,7},{4,0},{5,1},{6,2},{7,3},{8,12},{9,13},{10,... | collective-permute-start | bytes 196616 | tf_op jit(solution)/shard_map/ppermute | solution.py:859
  50.2 5.5 %collective-permute-start.13 = (f32[8,8,256]{2,1,0:T(8,128)S(1)}, f32[8,8,256]{2,1,0:T(8,128)S(1)}, u32[]{:S(2)}, u32[]{:S(2)}) collective-permute-start(f32[8,8,256]{2,1,0:T(8,128)S(1)} %get-tuple-element.57.par_ref.refs_0_), channel_id=1, source_target_pairs={{0,6},{1,7},{2,0},{3,1},{4,2},{5,3},{6,4},{7,5},{8,14},{9,15},{10,... | collective-permute-start | bytes 196616 | tf_op jit(solution)/shard_map/ppermute | solution.py:859
  65.0 10.6 %collective-permute-start.14 = (f32[9,8,256]{2,1,0:T(8,128)S(1)}, f32[9,8,256]{2,1,0:T(8,128)S(1)}, u32[]{:S(2)}, u32[]{:S(2)}) collective-permute-start(f32[9,8,256]{2,1,0:T(8,128)S(1)} %get-tuple-element.60), channel_id=1, source_target_pairs={{0,6},{1,7},{2,0},{3,1},{4,2},{5,3},{6,4},{7,5},{8,14},{9,15},{10,... | collective-permute-start | bytes 221192 | tf_op jit(solution)/shard_map/ppermute | solution.py:859
  67.3 8.3 %collective-permute-start.15 = (f32[9,8,256]{2,1,0:T(8,128)S(1)}, f32[9,8,256]{2,1,0:T(8,128)S(1)}, u32[]{:S(2)}, u32[]{:S(2)}) collective-permute-start(f32[9,8,256]{2,1,0:T(8,128)S(1)} %get-tuple-element.61), channel_id=1, source_target_pairs={{0,4},{1,5},{2,6},{3,7},{4,0},{5,1},{6,2},{7,3},{8,12},{9,13},{10,... | collective-permute-start | bytes 221192 | tf_op jit(solution)/shard_map/ppermute | solution.py:859
  68.3 7.3 %collective-permute-start.16 = (f32[9,8,256]{2,1,0:T(8,128)S(1)}, f32[9,8,256]{2,1,0:T(8,128)S(1)}, u32[]{:S(2)}, u32[]{:S(2)}) collective-permute-start(f32[9,8,256]{2,1,0:T(8,128)S(1)} %get-tuple-element.62), channel_id=1, source_target_pairs={{0,2},{1,3},{2,4},{3,5},{4,6},{5,7},{6,0},{7,1},{8,10},{9,11},{10,... | collective-permute-start | bytes 221192 | tf_op jit(solution)/shard_map/ppermute | solution.py:859
  75.8 2.6 %collective-permute-start.17 = (f32[8,256]{1,0:T(8,128)S(1)}, f32[8,256]{1,0:T(8,128)S(1)}, u32[]{:S(2)}, u32[]{:S(2)}) collective-permute-start(f32[8,256]{1,0:T(8,128)S(1)} %get-tuple-element.64.sent_ref), channel_id=1, source_target_pairs={{0,8},{8,0},{16,24},{24,16},{1,9},{9,1},{17,25},{25,17},{2,10},{10... | collective-permute-start | bytes 24584 | tf_op jit(solution)/shard_map/ppermute | solution.py:687
  78.3 2.6 %collective-permute-start.18 = (f32[8,256]{1,0:T(8,128)S(1)}, f32[8,256]{1,0:T(8,128)S(1)}, u32[]{:S(2)}, u32[]{:S(2)}) collective-permute-start(f32[8,256]{1,0:T(8,128)S(1)} %relay.3.refs_0_), channel_id=1, source_target_pairs={{0,16},{8,24},{16,0},{24,8},{1,17},{9,25},{17,1},{25,9},{2,18},{10... | collective-permute-start | bytes 24584 | tf_op jit(solution)/shard_map/ppermute | solution.py:690
  80.9 8.4 %collective-permute-start.19 = (f32[24,128]{1,0:T(8,128)S(1)}, f32[24,128]{1,0:T(8,128)S(1)}, u32[]{:S(2)}, u32[]{:S(2)}) collective-permute-start(f32[24,128]{1,0:T(8,128)S(1)} %get-tuple-element.66.sent_ref), channel_id=1, source_target_pairs={{0,1},{1,0},{2,3},{3,2},{4,5},{5,4},{6,7},{7,6},{8,9},{9,8},{10,11... | collective-permute-start | bytes 36872 | tf_op jit(solution)/shard_map/ppermute | solution.py:708
  85.0 5.7 %collective-permute-start.20 = (f32[24,128]{1,0:T(8,128)S(1)}, f32[24,128]{1,0:T(8,128)S(1)}, u32[]{:S(2)}, u32[]{:S(2)}) collective-permute-start(f32[24,128]{1,0:T(8,128)S(1)} %get-tuple-element.67), channel_id=1, source_target_pairs={{1,2},{2,1},{3,4},{4,3},{5,6},{6,5},{9,10},{10,9},{11,12},{12,11},... | collective-permute-start | bytes 36872 | tf_op jit(solution)/shard_map/ppermute | solution.py:707

commit v5 on v4

--- a/solution.py
+++ b/solution.py
@@ -105,6 +105,16 @@
         ref[h, pl.ds(start, count, stride=stride), :] = value[:, h * LANES : (h + 1) * LANES]
 
 
+def gain_columns(gains):
+    same = pick(iota((LIGHTS, LIGHTS), 0) == iota((LIGHTS, LIGHTS), 1))
+    tall = exact(same, jnp.broadcast_to(gains, (8, LIGHTS)), ((1,), (1,)))
+    return jnp.broadcast_to(tall[:, 0:1], (LIGHTS, LANES))
+
+
+def eights(x):
+    return total(x[i : i + 8] for i in range(0, x.shape[0], 8))
+
+
 def put_lobe_rows(slab, normal, sharp):
     base = [sharp * normal[0], sharp * normal[1], sharp * normal[2], -sharp]
     parts = [split_value(x, 3) for x in base]
@@ -117,8 +127,8 @@
 
 
 def normal_kernel(
-    par_ref, vis_ref, gain_ref, near_ref, cams_ref, lobe_ref, mixed_ref, square_ref, out_ref,
-    rows_ref, sums_ref, mixed_scr, square_scr, cam_scr, gram_scr,
+    par_ref, vis_ref, gain_ref, near_ref, cams_ref, lobe_ref, mixed_ref, tall_ref, out_ref,
+    rows_ref, sums_ref, mixed_scr, gain_scr, cam_scr, gram_scr, lobe_scr,
 ):
     rows, cols = par_ref.shape[1], par_ref.shape[2]
     depth = lobe_ref.shape[1]
@@ -137,14 +147,21 @@
     for c in range(CAMS):
         cam_scr[8 * c : 8 * c + 8, :] = jnp.broadcast_to(full[:, c : c + 1], (8, LANES))
 
+    gain_scr[...] = gain_columns(gain2)
     across = CAMS * LIGHTS
     at_light = pick(iota((LIGHTS, across), 1) % LIGHTS == iota((LIGHTS, across), 0))
     gain2 = exact(jnp.broadcast_to(gain2, (8, LIGHTS)), at_light, ((1,), (0,)))[0:1]
-    for src, dst in ((mixed_ref, mixed_scr), (square_ref, square_scr)):
+    for src, dst in ((mixed_ref, mixed_scr),):
         head, tail = split_pair(src[...] * gain2)
         count = src.shape[0]
-        dst[0:count, :] = head
-        dst[count : 2 * count, :] = tail
+        for ch in range(chunks):
+            part = slice(ch * chunk, (ch + 1) * chunk)
+            first = slice(2 * ch * chunk, (2 * ch + 1) * chunk)
+            second = slice((2 * ch + 1) * chunk, (2 * ch + 2) * chunk)
+            dst[0:count, first] = head[:, part]
+            dst[0:count, second] = head[:, part]
+            dst[count : 2 * count, first] = tail[:, part]
+            dst[count : 2 * count, second] = jnp.zeros((count, chunk), bf16)
 
     def slab(k, value):
         put_slab(rows_ref, k, value)
@@ -158,26 +175,41 @@
     for k in range(used + CAMS, depth):
         slab(k, jnp.zeros((rows, cols), f32))
 
-    def one_row(r, carry):
+    quads = [(i, j) for i in range(4) for j in range(i, 4)]
+
+    def one_row(r):
         texel = get_rows(rows_ref, r, depth, rows).astype(bf16)
         mixed = jnp.zeros((16, cols), f32)
-        square = jnp.zeros((16, cols), f32)
+        bent = {(h, ij): None for h in range(cols // LANES) for ij in quads}
         for ch in range(chunks):
-            at = slice(ch * chunk, (ch + 1) * chunk)
-            lobe = jnp.exp(dot(lobe_ref[at, :], texel))
-            head, tail = split_pair(lobe)
-            both = dot(mixed_scr[:, at], head)
-            got = both[0:32] + both[32:64] + dot(mixed_scr[0:32, at], tail)
+            for c in range(4):
+                part = slice(ch * chunk + c * LIGHTS, ch * chunk + (c + 1) * LIGHTS)
+                lobe = jnp.exp(dot(lobe_ref[part, :], texel))
+                head, tail = split_pair(lobe)
+                lobe_scr[r, ch, c * LIGHTS : (c + 1) * LIGHTS, :] = head
+                lobe_scr[r, ch, chunk + c * LIGHTS : chunk + (c + 1) * LIGHTS, :] = tail
+                tall = [None] + [tall_ref[k, part, :] for k in range(3)]
+                for h in range(cols // LANES):
+                    lobe_h = lobe[:, h * LANES : (h + 1) * LANES]
+                    single = [lobe_h * lobe_h * gain_scr[...]]
+                    single += [single[0] * tall[k] for k in (1, 2, 3)]
+                    for i, j in quads:
+                        value = eights(single[j] if i == 0 else single[i] * tall[j])
+                        old = bent[h, (i, j)]
+                        bent[h, (i, j)] = value if old is None else old + value
+            at = slice(2 * ch * chunk, (2 * ch + 2) * chunk)
+            both = dot(mixed_scr[:, at], lobe_scr[r, ch])
+            got = both[0:32] + both[32:64]
             mixed = mixed + got[0:16]
             put_rows(sums_ref, (32 + 16 * ch) * rows + r, rows, got[16:32])
-            head, tail = split_pair(lobe * lobe)
-            both = dot(square_scr[:, at], head)
-            square = square + both[0:16] + both[16:32] + dot(square_scr[0:16, at], tail)
         put_rows(sums_ref, r, rows, mixed)
-        put_rows(sums_ref, 16 * rows + r, rows, square)
-        return carry
-
-    lax.fori_loop(0, rows, one_row, 0, unroll=4)
+        for h in range(cols // LANES):
+            for k, ij in enumerate(quads):
+                line = (16 + k) * rows + r
+                sums_ref[h, line : line + 1, :] = jnp.sum(bent[h, ij], axis=0, keepdims=True)
+
+    for r in range(rows):
+        one_row(r)
 
     def one_part(h, carry):
         at = pl.ds(pl.multiple_of(h * LANES, LANES), LANES)
@@ -308,11 +340,11 @@
 
 
 def sample_kernel(
-    tile_ref, own_ref, got_ref, gain_ref, lobe_ref, shade_ref, plain_ref, peak_ref, slab_ref, *refs, parts
+    tile_ref, own_ref, got_ref, gain_ref, lobe_ref, shade_ref, plain_ref, tall_ref, slab_ref, *refs, parts
 ):
     par_refs, vis_refs = refs[:parts], refs[parts : 2 * parts]
     out_refs = refs[2 * parts : 3 * parts]
-    par_scr, vis_scr, obs_scr, rows_ref, sums_ref, light_scr = refs[3 * parts :]
+    par_scr, vis_scr, obs_scr, rows_ref, sums_ref, light_scr, gain_scr, plain_scr, flat_scr = refs[3 * parts :]
     step = pl.program_id(0)
     samples, rows, cols = own_ref.shape
     held = 2 * samples
@@ -366,36 +398,48 @@
         slab(k, jnp.zeros((rows, cols), f32))
     slab(64, p[3])
 
-    at_light = pick(iota((LIGHTS, held), 1) % LIGHTS == iota((LIGHTS, held), 0))
-    gains = exact(jnp.broadcast_to(gain_ref[...], (8, LIGHTS)), at_light, ((1,), (0,)))[0:1]
-    plain = jnp.concatenate(split_value(plain_ref[...] * gains, 2), axis=0).astype(bf16)
-    peak = jnp.concatenate(split_value(peak_ref[...] * gains, 2), axis=0).astype(bf16)
+    @pl.when(step == 0)
+    def _():
+        at_light = pick(iota((LIGHTS, held), 1) % LIGHTS == iota((LIGHTS, held), 0))
+        gains = exact(jnp.broadcast_to(gain_ref[...], (8, LIGHTS)), at_light, ((1,), (0,)))[0:1]
+        plain_scr[...] = jnp.concatenate(split_value(plain_ref[...] * gains, 2), axis=0).astype(bf16)
+        gain_scr[...] = gain_columns(gain_ref[...])
+
     count = plain_ref.shape[0]
 
     def fold(x):
         return total(x[:, k * LANES : (k + 1) * LANES] for k in range(cols // LANES))
 
-    def one_row(r, carry):
-        lift, energy = carry
-        lobe = jnp.exp(dot(lobe_ref[...], get_rows(rows_ref, r, 32, rows).astype(bf16)))
-        shade = dot(shade_ref[...], get_rows(rows_ref, 32 * rows + r, 32, rows).astype(bf16))
+    def one_row(r, lift, energy):
+        texel = get_rows(rows_ref, r, 32, rows).astype(bf16)
+        tint = get_rows(rows_ref, 32 * rows + r, 32, rows).astype(bf16)
         misc = get_rows(rows_ref, 64 * rows + r, 8, rows)
-        obs = get_rows(obs_scr, r, held, rows)
+        peak = {}
         for c in range(cams):
             part = slice(c * LIGHTS, (c + 1) * LIGHTS)
-            full = shade[part] + misc[0:1] * lobe[part]
+            lobe = jnp.exp(dot(lobe_ref[part, :], texel))
+            full = dot(shade_ref[part, :], tint) + misc[0:1] * lobe
+            obs = get_rows(obs_scr, c * LIGHTS * rows + r, LIGHTS, rows)
             kept = full * misc[1 + c : 2 + c]
-            lift = lift + fold(kept * obs[part])
+            lift = lift + fold(kept * obs)
             energy = energy + fold(kept * full)
-        head, tail = split_pair(obs * lobe)
-        both = dot(plain, obs.astype(bf16))
+            flat_scr[r, part, :] = obs.astype(bf16)
+            lit = obs * lobe
+            for h in range(cols // LANES):
+                base = lit[:, h * LANES : (h + 1) * LANES] * gain_scr[...]
+                for k in range(4):
+                    value = eights(base if k == 0 else base * tall_ref[k - 1, part, :])
+                    peak[h, k] = value if c == 0 else peak[h, k] + value
+        both = dot(plain_scr[...], flat_scr[r])
         put_rows(sums_ref, r, rows, both[0:count] + both[count : 2 * count])
-        both = dot(peak, head)
-        put_rows(sums_ref, count * rows + r, rows, both[0:8] + both[8:16] + dot(peak[0:8], tail))
+        for h, k in peak:
+            line = (count + k) * rows + r
+            sums_ref[h, line : line + 1, :] = jnp.sum(peak[h, k], axis=0, keepdims=True)
         return lift, energy
 
-    zero = jnp.zeros((LIGHTS, LANES), f32)
-    lift, energy = lax.fori_loop(0, rows, one_row, (zero, zero), unroll=4)
+    lift = energy = jnp.zeros((LIGHTS, LANES), f32)
+    for r in range(rows):
+        lift, energy = one_row(r, lift, energy)
 
     @pl.when(step == 0)
     def _():
@@ -561,7 +605,7 @@
 def normal_call(par, vis, gains, tables):
     _, rows, cols = par.shape
     parts = cols // LANES
-    small = [tables[n] for n in ("near", "cams", "lobe", "mixed", "square")]
+    small = [tables[n] for n in ("near", "cams", "lobe", "mixed", "tall")]
     return pl.pallas_call(
         normal_kernel,
         name="normal_factor",
@@ -571,10 +615,11 @@
         scratch_shapes=[
             pltpu.VMEM((parts, 48 * rows, LANES), f32),
             pltpu.VMEM((parts, 96 * rows, LANES), f32),
-            pltpu.VMEM((64, CAMS * LIGHTS), bf16),
-            pltpu.VMEM((32, CAMS * LIGHTS), bf16),
+            pltpu.VMEM((64, 2 * CAMS * LIGHTS), bf16),
+            pltpu.VMEM((LIGHTS, LANES), f32),
             pltpu.VMEM((8 * CAMS, LANES), f32),
             pltpu.VMEM((32, LANES), f32),
+            pltpu.VMEM((rows, 4, 8 * LIGHTS, cols), bf16),
         ],
         compiler_params=params_of(),
     )(par, vis, gains, *small)
@@ -594,7 +639,7 @@
         return lax.rem(tile_of(tile) // 2 + (parts - s), parts)
 
     outs = [jax.ShapeDtypeStruct((9, rows, cols), f32) for _ in range(parts)]
-    small = [gains] + [tables[n] for n in ("here", "shade", "plain", "peak", "slab")]
+    small = [gains] + [tables[n] for n in ("here", "shade", "plain", "near_tall", "slab")]
     return pl.pallas_call(
         functools.partial(sample_kernel, parts=parts),
         name="sample_sums",
@@ -617,6 +662,9 @@
                 pltpu.VMEM((cols // LANES, 72 * rows, LANES), f32),
                 pltpu.VMEM((cols // LANES, 32 * rows, LANES), f32),
                 pltpu.VMEM((2 * LIGHTS, LANES), f32),
+                pltpu.VMEM((LIGHTS, LANES), f32),
+                pltpu.VMEM((2 * tables["plain"].shape[0], held), bf16),
+                pltpu.VMEM((rows, held, cols), bf16),
             ],
         ),
         compiler_params=params_of(),
@@ -727,8 +775,8 @@
 
 def setup_kernel(
     tile_ref, light_ref, view_ref,
-    near_ref, cams_ref, lobe_ref, mixed_ref, square_ref,
-    here_ref, shade_ref, plain_ref, peak_ref, slab_ref, light_scr, view_scr,
+    near_ref, cams_ref, lobe_ref, mixed_ref,
+    here_ref, shade_ref, plain_ref, tall_ref, near_tall_ref, slab_ref, light_scr, view_scr,
 ):
     samples = lobe_ref.shape[0]
     held = here_ref.shape[0]
@@ -748,9 +796,9 @@
     near_ref[...] = near
     cams_ref[...] = views
 
-    def across(count, start):
+    def across(count, start, period):
         at_light = pick(iota((LIGHTS, count), 1) % LIGHTS == iota((LIGHTS, count), 0))
-        at_view = pick(iota((CAMS, count), 1) // LIGHTS + start == iota((CAMS, count), 0))
+        at_view = pick(iota((CAMS, count), 1) // LIGHTS % period + start == iota((CAMS, count), 0))
         wide = exact(near, at_light, ((1,), (0,)))
         view = exact(views, at_view, ((1,), (0,)))
         row = iota((8, count), 0)
@@ -788,7 +836,7 @@
             out = got if out is None else out + got
         return out
 
-    wide, half, echo = across(samples, 0)
+    wide, half, echo = across(samples, 0, CAMS)
     high = [jnp.ones((1, samples), f32)] + [half[k : k + 1] for k in range(3)]
     low = [wide[k : k + 1] for k in range(3)] + [echo]
     which = iota((1, samples), 1) // LIGHTS % 4
@@ -796,19 +844,16 @@
         for j in range(4):
             mixed_ref[4 * i + j : 4 * i + j + 1, :] = high[i] * low[j]
             mixed_ref[16 + 4 * i + j : 17 + 4 * i + j, :] = jnp.where(which == i, high[j], 0.0)
-    at = 0
-    square_ref[8:16, :] = jnp.zeros((8, samples), f32)
-    for i in range(4):
-        for j in range(i, 4):
-            square_ref[at : at + 1, :] = high[i] * high[j]
-            at += 1
-
     depth = lobe_ref.shape[1]
     half, _ = down(samples, 0)
+    for k in range(3):
+        tall_ref[k] = jnp.broadcast_to(half[:, k : k + 1], (samples, LANES))
     hot = pick(iota((samples, depth), 0) // LIGHTS + 24 == iota((samples, depth), 1))
     lobe_ref[...] = (spread(half, 4, depth, (0, 0, 1, 0, 1, 2)) + hot).astype(bf16)
 
     half, tall = down(held, first)
+    for k in range(3):
+        near_tall_ref[k] = jnp.broadcast_to(half[:, k : k + 1], (held, LANES))
     cam = iota((held, 32), 0) // LIGHTS
     lane = iota((held, 32), 1)
     hot = pick(cam + 24 == lane)
@@ -816,12 +861,8 @@
     hot = pick(cam + 15 == lane) + pick(cam + (15 + cams) == lane)
     shade_ref[...] = (spread(tall, 5, 32, (0, 0, 1)) + hot).astype(bf16)
 
-    wide, half, _ = across(held, first)
-    peak_ref[...] = jnp.zeros(peak_ref.shape, f32)
-    peak_ref[0:1, :] = jnp.ones((1, held), f32)
+    wide, _, _ = across(held, first, cams)
     plain_ref[...] = jnp.zeros(plain_ref.shape, f32)
-    for k in range(3):
-        peak_ref[k + 1 : k + 2, :] = half[k : k + 1]
     which = iota((1, held), 1) // LIGHTS
     for c in range(cams):
         plain_ref[4 * c : 4 * c + 1, :] = pick(which == c)
@@ -831,7 +872,7 @@
         slab_ref[8 * c : 8 * c + 8, :] = jnp.broadcast_to(mine, (8, LANES))
 
 
-TABLES = ("near", "cams", "lobe", "mixed", "square", "here", "shade", "plain", "peak", "slab")
+TABLES = ("near", "cams", "lobe", "mixed", "here", "shade", "plain", "tall", "near_tall", "slab")
 
 
 def setup_call(tile, light_directions, view_dirs, held):
@@ -840,8 +881,8 @@
     count = max(8, 4 * cams)
     shapes = [
         ((8, LIGHTS), f32), ((8, CAMS), f32), ((samples, 48), bf16), ((32, samples), f32),
-        ((16, samples), f32), ((held, 32), bf16), ((held, 32), bf16), ((count, held), f32),
-        ((8, held), f32), ((8 * cams, LANES), f32),
+        ((held, 32), bf16), ((held, 32), bf16), ((count, held), f32),
+        ((3, samples, LANES), f32), ((3, held, LANES), f32), ((8 * cams, LANES), f32),
     ]
     outs = pl.pallas_call(
         setup_kernel,

time: 91.7 us -> 81.9 us (0.89)
  Pallas kernels: 36 us -> 26.7 us
  starting transfers between devices: 37.5 us -> 32.6 us
  waiting for transfers between devices: 13.9 us -> 18.3 us
    pallas_call x2, Pallas kernels: 18.6 us -> 13.2 us  [sample_call(): pl.pallas_call(functools.partial(sample_kernel, parts=parts), name='sampl...]
    ppermute x12, waiting for transfers between devices: 6.12 us -> 10.5 us  [shifted(): lax.ppermute(x, 'tile', [(2 * z + c, 2 * ((z + by) % nz) + c) for z in ra...]
    ppermute x2, starting transfers between devices: 4.19 us -> 0.14 us  [settle(): near = lax.ppermute(sent, 'tile', pairs(tiles, 0))]
    ppermute x12, starting transfers between devices: 16.1 us -> 12.2 us  [shifted(): lax.ppermute(x, 'tile', [(2 * z + c, 2 * ((z + by) % nz) + c) for z in ra...]
    pallas_call x2, Pallas kernels: 14.3 us -> 10.3 us  [normal_call(): pl.pallas_call(normal_kernel, name='normal_factor', out_shape=jax.ShapeDt...]
    ppermute x2, starting transfers between devices: 12.1 us -> 15.2 us  [settle(): far = lax.ppermute(other, 'tile', pairs(tiles, 1))]
  transfers between devices with their start and end apart: 21 -> 21, of which waited for: 10 -> 11; matrix products, arithmetic and copies ran while one was open for 0% -> 0% of each run, Pallas kernels for 18% -> 15%
where the time goes in v5:
time: 81.9 us; the launch traced here: 81.6 us
  starting transfers between devices  32.6 us (40%)
  Pallas kernels  26.7 us (33%)
  waiting for transfers between devices  18.3 us (22%)
  local copies, waits for them, and re-layouts  3.16 us (4%)
  between operations  0.85 us (1%)
    ppermute x2, starting transfers between devices, settle(): far = lax.ppermute(other, 'tile', pairs(tiles, 1))  15.2 us
    pallas_call x2, Pallas kernels, sample_call(): pl.pallas_call(functools.partial(sample_kernel, parts=parts), name='sampl...  13.2 us
    ppermute x12, starting transfers between devices, shifted(): lax.ppermute(x, 'tile', [(2 * z + c, 2 * ((z + by) % nz) + c) for z in ra...  12.2 us
    ppermute x12, waiting for transfers between devices, shifted(): lax.ppermute(x, 'tile', [(2 * z + c, 2 * ((z + by) % nz) + c) for z in ra...  10.5 us
    pallas_call x2, Pallas kernels, normal_call(): pl.pallas_call(normal_kernel, name='normal_factor', out_shape=jax.ShapeDt...  10.3 us
    unnamed x18, local copies, waits for them, and re-layouts  3.16 us
    ppermute x2, waiting for transfers between devices, settle(): first = lax.ppermute(sent, 'grp', pairs(grps, 0))  2.62 us
    ppermute x2, waiting for transfers between devices, settle(): far = lax.ppermute(other, 'tile', pairs(tiles, 1))  2.57 us
  transfers between devices with their start and end apart: 21, of which 11 were waited for; matrix products, arithmetic and copies ran while one was open for 0% of the time, Pallas kernels for 15%

profile of v5, /device:TPU:1, one launch (start us, length us, event | category | flops | bytes accessed | tf_op | source)
XLA Modules:
  0.0 81.6 jit_solution(10506970210111867716)
XLA Ops:
  0.7 1.6 %copy-done = bf16[64,8,2048]{2,1,0:T(8,128)(2,1)S(1)} copy-done((bf16[64,8,2048]{2,1,0:T(8,128)(2,1)S(1)}, bf16[64,8,2048]{2,1,0:T(8,128)(2,1)}, u32[]{:S(2)}) %copy-start) | copy-done | bytes 2097176
  2.3 0.8 %copy-done.2 = f32[8,8,256]{2,1,0:T(8,128)S(1)} copy-done((f32[8,8,256]{2,1,0:T(8,128)S(1)}, f32[8,8,256]{2,1,0:T(8,128)}, u32[]{:S(2)}) %copy-start.2) | copy-done | bytes 65560
  3.1 0.7 copy-done.4
  3.8 0.2 pack.1
  4.0 0.0 copy-start.3
  4.0 0.0 copy-start.5
  4.1 0.1 collective-permute-start
  4.2 4.8 %collective-permute-start.3 = (f32[9,8,256]{2,1,0:T(8,128)S(1)}, f32[9,8,256]{2,1,0:T(8,128)S(1)}, u32[]{:S(2)}, u32[]{:S(2)}) collective-permute-start(f32[9,8,256]{2,1,0:T(8,128)S(1)} %get-tuple-element.47.refs_0_.refs_4_), channel_id=1, source_target_pairs={{0,6},{1,7},{2,0},{3,1},{4,2},{5,3},{6,4},{7,5},{8,14},{9,15},{10,... | collective-permute-start | bytes 221192 | tf_op jit(solution)/shard_map/ppermute | solution.py:900
  9.0 0.5 collective-permute-start.1
  9.4 1.9 %tables.1 = (f32[8,32]{1,0:T(8,128)S(1)}, f32[8,16]{1,0:T(8,128)S(1)}, bf16[512,48]{1,0:T(8,128)(2,1)S(1)}, f32[32,512]{1,0:T(8,128)S(1)}, bf16[128,32]{1,0:T(8,...) custom-call(s32[1]{0:T(128)} %bitcast.tile_ref, ...), custom_call_target="tpu_custom_call" | custom-call | tf_op jit(solution)/shard_map/tables/pallas_call | solution.py:887
  11.3 5.3 %collective-permute-done.2.refs_2_.refs_6_ = f32[9,8,256]{2,1,0:T(8,128)S(1)} collective-permute-done((f32[9,8,256]{2,1,0:T(8,128)S(1)}, f32[9,8,256]{2,1,0:T(8,128)S(1)}, u32[]{:S(2)}, u32[]{:S(2)}) %collective-permute-start.2) | collective-permute-done | bytes 73760 | tf_op jit(solution)/shard_map/ppermute | solution.py:900
  16.6 6.6 %sample_sums.2 = (f32[9,8,256]{2,1,0:T(8,128)S(1)}, f32[9,8,256]{2,1,0:T(8,128)S(1)}, f32[9,8,256]{2,1,0:T(8,128)S(1)}, f32[9,8,256]{2,1,0:T(8,128)S(1)}) custom-call(s32[1]{0:T(128)} %bitcast.tile_ref, bf16[64,8,2048]{2,1,0:T(8,128)(2,1)S(1)} %copy-done.1, bf16[64,8,1024]{2,1,0:T(8,128)(2,1)S(1)} %collective-permute-done.got_ref, f32[1,32]{1,0:T(1,128)S(1)} %bitcast.3, ...), custom_call_target="tpu_custom_call" | custom-call | tf_op jit(solution)/shard_map/sample_sums/pallas_call | solution.py:643
  23.3 0.2 collective-permute-start.4
  23.4 0.7 collective-permute-start.5
  24.2 1.4 %collective-permute-start.6 = (f32[9,8,256]{2,1,0:T(8,128)S(1)}, f32[9,8,256]{2,1,0:T(8,128)S(1)}, u32[]{:S(2)}, u32[]{:S(2)}) collective-permute-start(f32[9,8,256]{2,1,0:T(8,128)S(1)} %get-tuple-element.51), channel_id=1, source_target_pairs={{0,2},{1,3},{2,4},{3,5},{4,6},{5,7},{6,0},{7,1},{8,10},{9,11},{10,... | collective-permute-start | bytes 221192 | tf_op jit(solution)/shard_map/ppermute | solution.py:900
  25.6 5.2 %normal_factor.2.low_ref = f32[44,8,256]{2,1,0:T(8,128)S(1)} custom-call(f32[8,8,256]{2,1,0:T(8,128)S(1)} %copy-done.3, s32[8,256]{1,0:T(8,128)S(1)} %copy-done.5, f32[1,32]{1,0:T(1,128)S(1)} %bitcast.4, f32[8,32]{1,0:T(8,128)S(1)} %get-tuple-element.36.near_ref, f32[8,16]{1,0:T(8,128)S(1)} %get-tuple-element.37.cams_ref, ...), custom_call_target="tpu_custom_call" | custom-call | tf_op jit(solution)/shard_map/normal_factor/pallas_call | solution.py:609
  30.7 0.0 collective-permute-done.4.refs_1_
  30.7 0.0 collective-permute-done.5.refs_2_
  30.8 0.2 collective-permute-done.6.refs_3_
  31.0 0.1 solve.2
  31.1 1.2 %collective-permute-start.7 = (f32[8,256]{1,0:T(8,128)S(1)}, f32[8,256]{1,0:T(8,128)S(1)}, u32[]{:S(2)}, u32[]{:S(2)}) collective-permute-start(f32[8,256]{1,0:T(8,128)S(1)} %get-tuple-element.53.sent_ref), channel_id=1, source_target_pairs={{0,8},{8,0},{16,24},{24,16},{1,9},{9,1},{17,25},{25,17},{2,10},{10... | collective-permute-start | bytes 24584 | tf_op jit(solution)/shard_map/ppermute | solution.py:735
  32.3 1.3 %collective-permute-done.7.first_ref = f32[8,256]{1,0:T(8,128)S(1)} collective-permute-done((f32[8,256]{1,0:T(8,128)S(1)}, f32[8,256]{1,0:T(8,128)S(1)}, u32[]{:S(2)}, u32[]{:S(2)}) %collective-permute-start.7) | collective-permute-done | bytes 8224 | tf_op jit(solution)/shard_map/ppermute | solution.py:735
  33.6 1.2 %collective-permute-start.8 = (f32[8,256]{1,0:T(8,128)S(1)}, f32[8,256]{1,0:T(8,128)S(1)}, u32[]{:S(2)}, u32[]{:S(2)}) collective-permute-start(f32[8,256]{1,0:T(8,128)S(1)} %relay.2.refs_0_), channel_id=1, source_target_pairs={{0,16},{8,24},{16,0},{24,8},{1,17},{9,25},{17,1},{25,9},{2,18},{10... | collective-permute-start | bytes 24584 | tf_op jit(solution)/shard_map/ppermute | solution.py:738
  34.9 1.3 %collective-permute-done.8.edge_ref.refs_1_ = f32[8,256]{1,0:T(8,128)S(1)} collective-permute-done((f32[8,256]{1,0:T(8,128)S(1)}, f32[8,256]{1,0:T(8,128)S(1)}, u32[]{:S(2)}, u32[]{:S(2)}) %collective-permute-start.8) | collective-permute-done | bytes 8224 | tf_op jit(solution)/shard_map/ppermute | solution.py:738
  36.2 7.2 %collective-permute-start.10 = (f32[24,128]{1,0:T(8,128)S(1)}, f32[24,128]{1,0:T(8,128)S(1)}, u32[]{:S(2)}, u32[]{:S(2)}) collective-permute-start(f32[24,128]{1,0:T(8,128)S(1)} %get-tuple-element.56), channel_id=1, source_target_pairs={{1,2},{2,1},{3,4},{4,3},{5,6},{6,5},{9,10},{10,9},{11,12},{12,11},... | collective-permute-start | bytes 36872 | tf_op jit(solution)/shard_map/ppermute | solution.py:755
  43.3 0.1 collective-permute-start.9
  43.4 1.3 %collective-permute-done.10.far_ref = f32[24,128]{1,0:T(8,128)S(1)} collective-permute-done((f32[24,128]{1,0:T(8,128)S(1)}, f32[24,128]{1,0:T(8,128)S(1)}, u32[]{:S(2)}, u32[]{:S(2)}) %collective-permute-start.10) | collective-permute-done | bytes 12320 | tf_op jit(solution)/shard_map/ppermute | solution.py:755
  44.7 0.1 smooth.2
  44.8 0.1 collective-permute-start.13
  44.9 1.2 %collective-permute-start.12 = (f32[8,8,256]{2,1,0:T(8,128)S(1)}, f32[8,8,256]{2,1,0:T(8,128)S(1)}, u32[]{:S(2)}, u32[]{:S(2)}) collective-permute-start(f32[8,8,256]{2,1,0:T(8,128)S(1)} %get-tuple-element.57.par_ref.refs_0_), channel_id=1, source_target_pairs={{0,4},{1,5},{2,6},{3,7},{4,0},{5,1},{6,2},{7,3},{8,12},{9,13},{10,... | collective-permute-start | bytes 196616 | tf_op jit(solution)/shard_map/ppermute | solution.py:900
  46.0 0.9 %collective-permute-start.11 = (f32[8,8,256]{2,1,0:T(8,128)S(1)}, f32[8,8,256]{2,1,0:T(8,128)S(1)}, u32[]{:S(2)}, u32[]{:S(2)}) collective-permute-start(f32[8,8,256]{2,1,0:T(8,128)S(1)} %get-tuple-element.57.par_ref.refs_0_), channel_id=1, source_target_pairs={{0,2},{1,3},{2,4},{3,5},{4,6},{5,7},{6,0},{7,1},{8,10},{9,11},{10,... | collective-permute-start | bytes 196616 | tf_op jit(solution)/shard_map/ppermute | solution.py:900
  46.9 1.5 %collective-permute-done.13.refs_3_ = f32[8,8,256]{2,1,0:T(8,128)S(1)} collective-permute-done((f32[8,8,256]{2,1,0:T(8,128)S(1)}, f32[8,8,256]{2,1,0:T(8,128)S(1)}, u32[]{:S(2)}, u32[]{:S(2)}) %collective-permute-start.13) | collective-permute-done | bytes 65568 | tf_op jit(solution)/shard_map/ppermute | solution.py:900
  48.5 0.6 collective-permute-done.12.refs_2_
  49.1 2.9 %collective-permute-done.11.refs_1_ = f32[8,8,256]{2,1,0:T(8,128)S(1)} collective-permute-done((f32[8,8,256]{2,1,0:T(8,128)S(1)}, f32[8,8,256]{2,1,0:T(8,128)S(1)}, u32[]{:S(2)}, u32[]{:S(2)}) %collective-permute-start.11) | collective-permute-done | bytes 65568 | tf_op jit(solution)/shard_map/ppermute | solution.py:900
  51.9 6.6 %sample_sums.3 = (f32[9,8,256]{2,1,0:T(8,128)S(1)}, f32[9,8,256]{2,1,0:T(8,128)S(1)}, f32[9,8,256]{2,1,0:T(8,128)S(1)}, f32[9,8,256]{2,1,0:T(8,128)S(1)}) custom-call(s32[1]{0:T(128)} %bitcast.tile_ref, bf16[64,8,2048]{2,1,0:T(8,128)(2,1)S(1)} %copy-done.1, bf16[64,8,1024]{2,1,0:T(8,128)(2,1)S(1)} %collective-permute-done.got_ref, ...), custom_call_target="tpu_custom_call" | custom-call | tf_op jit(solution)/shard_map/sample_sums/pallas_call | solution.py:643
  58.5 0.9 %collective-permute-start.14 = (f32[9,8,256]{2,1,0:T(8,128)S(1)}, f32[9,8,256]{2,1,0:T(8,128)S(1)}, u32[]{:S(2)}, u32[]{:S(2)}) collective-permute-start(f32[9,8,256]{2,1,0:T(8,128)S(1)} %get-tuple-element.60), channel_id=1, source_target_pairs={{0,6},{1,7},{2,0},{3,1},{4,2},{5,3},{6,4},{7,5},{8,14},{9,15},{10,... | collective-permute-start | bytes 221192 | tf_op jit(solution)/shard_map/ppermute | solution.py:900
  59.4 0.2 collective-permute-start.15
  59.6 1.4 %collective-permute-start.16 = (f32[9,8,256]{2,1,0:T(8,128)S(1)}, f32[9,8,256]{2,1,0:T(8,128)S(1)}, u32[]{:S(2)}, u32[]{:S(2)}) collective-permute-start(f32[9,8,256]{2,1,0:T(8,128)S(1)} %get-tuple-element.62), channel_id=1, source_target_pairs={{0,2},{1,3},{2,4},{3,5},{4,6},{5,7},{6,0},{7,1},{8,10},{9,11},{10,... | collective-permute-start | bytes 221192 | tf_op jit(solution)/shard_map/ppermute | solution.py:900
  61.0 5.2 %normal_factor.3.low_ref = f32[44,8,256]{2,1,0:T(8,128)S(1)} custom-call(f32[8,8,256]{2,1,0:T(8,128)S(1)} %get-tuple-element.57.par_ref.refs_0_, s32[8,256]{1,0:T(8,128)S(1)} %copy-done.5, f32[1,32]{1,0:T(1,128)S(1)} %get-tuple-element.58.gain_ref, f32[8,32]{1,0:T(8,128)S(1)} %get-tuple-element.36.near_ref, f32[8,16]{1,0:T(8,128)S(1)} %get-tuple-element.37.cams_ref, ...), custom_call_target="tpu_custom_call" | custom-call | tf_op jit(solution)/shard_map/normal_factor/pallas_call | solution.py:609
  66.2 0.1 solve.3
  66.3 1.3 %collective-permute-start.17 = (f32[8,256]{1,0:T(8,128)S(1)}, f32[8,256]{1,0:T(8,128)S(1)}, u32[]{:S(2)}, u32[]{:S(2)}) collective-permute-start(f32[8,256]{1,0:T(8,128)S(1)} %get-tuple-element.64.sent_ref), channel_id=1, source_target_pairs={{0,8},{8,0},{16,24},{24,16},{1,9},{9,1},{17,25},{25,17},{2,10},{10... | collective-permute-start | bytes 24584 | tf_op jit(solution)/shard_map/ppermute | solution.py:735
  67.6 1.3 %collective-permute-done.17.first_ref = f32[8,256]{1,0:T(8,128)S(1)} collective-permute-done((f32[8,256]{1,0:T(8,128)S(1)}, f32[8,256]{1,0:T(8,128)S(1)}, u32[]{:S(2)}, u32[]{:S(2)}) %collective-permute-start.17) | collective-permute-done | bytes 8224 | tf_op jit(solution)/shard_map/ppermute | solution.py:735
  68.9 1.2 %collective-permute-start.18 = (f32[8,256]{1,0:T(8,128)S(1)}, f32[8,256]{1,0:T(8,128)S(1)}, u32[]{:S(2)}, u32[]{:S(2)}) collective-permute-start(f32[8,256]{1,0:T(8,128)S(1)} %relay.3.refs_0_), channel_id=1, source_target_pairs={{0,16},{8,24},{16,0},{24,8},{1,17},{9,25},{17,1},{25,9},{2,18},{10... | collective-permute-start | bytes 24584 | tf_op jit(solution)/shard_map/ppermute | solution.py:738
  70.1 1.3 %collective-permute-done.18.edge_ref.refs_1_ = f32[8,256]{1,0:T(8,128)S(1)} collective-permute-done((f32[8,256]{1,0:T(8,128)S(1)}, f32[8,256]{1,0:T(8,128)S(1)}, u32[]{:S(2)}, u32[]{:S(2)}) %collective-permute-start.18) | collective-permute-done | bytes 8224 | tf_op jit(solution)/shard_map/ppermute | solution.py:738
  71.4 8.1 %collective-permute-start.20 = (f32[24,128]{1,0:T(8,128)S(1)}, f32[24,128]{1,0:T(8,128)S(1)}, u32[]{:S(2)}, u32[]{:S(2)}) collective-permute-start(f32[24,128]{1,0:T(8,128)S(1)} %get-tuple-element.67), channel_id=1, source_target_pairs={{1,2},{2,1},{3,4},{4,3},{5,6},{6,5},{9,10},{10,9},{11,12},{12,11},... | collective-permute-start | bytes 36872 | tf_op jit(solution)/shard_map/ppermute | solution.py:755
  79.5 0.1 collective-permute-start.19
  79.6 1.3 %collective-permute-done.20.far_ref = f32[24,128]{1,0:T(8,128)S(1)} collective-permute-done((f32[24,128]{1,0:T(8,128)S(1)}, f32[24,128]{1,0:T(8,128)S(1)}, u32[]{:S(2)}, u32[]{:S(2)}) %collective-permute-start.20) | collective-permute-done | bytes 12320 | tf_op jit(solution)/shard_map/ppermute | solution.py:755
  80.9 0.7 smooth.3
  (26 shorter events, 0.1 us)
Async XLA Ops:
  0.6 8.8 %copy-start.8 = (f32[3,16]{1,0:T(4,128)S(1)}, f32[3,16]{1,0:T(4,128)}, u32[]{:S(2)}) copy-start(f32[3,16]{1,0:T(4,128)} %view_ref.1) | copy-start | bytes 580
  0.6 8.8 %copy-start.7 = (f32[3,32]{1,0:T(4,128)S(1)}, f32[3,32]{1,0:T(4,128)}, u32[]{:S(2)}) copy-start(f32[3,32]{1,0:T(4,128)} %light_ref.1) | copy-start | bytes 1156
  0.7 16.0 %copy-start.6 = (f32[32]{0:T(128)S(1)}, f32[32]{0:T(128)}, u32[]{:S(2)}) copy-start(f32[32]{0:T(128)} %param.11) | copy-start | bytes 388
  0.7 1.6 %copy-start = (bf16[64,8,2048]{2,1,0:T(8,128)(2,1)S(1)}, bf16[64,8,2048]{2,1,0:T(8,128)(2,1)}, u32[]{:S(2)}) copy-start(bf16[64,8,2048]{2,1,0:T(8,128)(2,1)} %own_ref.3) | copy-start | bytes 6291460
  2.3 0.8 %copy-start.2 = (f32[8,8,256]{2,1,0:T(8,128)S(1)}, f32[8,8,256]{2,1,0:T(8,128)}, u32[]{:S(2)}) copy-start(f32[8,8,256]{2,1,0:T(8,128)} %par_ref.5) | copy-start | bytes 196612
  3.1 0.7 copy-start.4
  3.8 12.8 %copy-start.1 = (bf16[64,8,2048]{2,1,0:T(8,128)(2,1)S(1)}, bf16[64,8,2048]{2,1,0:T(8,128)(2,1)}, u32[]{:S(2)}) copy-start(bf16[64,8,2048]{2,1,0:T(8,128)(2,1)} %own_ref.3) | copy-start | bytes 6291460
  4.0 21.5 %copy-start.3 = (f32[8,8,256]{2,1,0:T(8,128)S(1)}, f32[8,8,256]{2,1,0:T(8,128)}, u32[]{:S(2)}) copy-start(f32[8,8,256]{2,1,0:T(8,128)} %par_ref.5) | copy-start | bytes 196612
  4.0 21.5 %copy-start.5 = (s32[8,256]{1,0:T(8,128)S(1)}, s32[8,256]{1,0:T(8,128)}, u32[]{:S(2)}) copy-start(s32[8,256]{1,0:T(8,128)} %vis_ref.5) | copy-start | bytes 24580
  4.1 12.6 %collective-permute-start = (bf16[64,8,1024]{2,1,0:T(8,128)(2,1)S(1)}, bf16[64,8,1024]{2,1,0:T(8,128)(2,1)S(1)}, u32[]{:S(2)}, u32[]{:S(2)}) collective-permute-start(bf16[64,8,1024]{2,1,0:T(8,128)(2,1)S(1)} %get-tuple-element.41), channel_id=1, source_target_pairs={{0,1},{1,0},{2,3},{3,2},{4,5},{5,4},{6,7},{7,6},{8,9},{9,8},{10,11... | collective-permute-start | bytes 3145736 | tf_op jit(solution)/shard_map/ppermute | solution.py:912
  4.2 7.1 %collective-permute-start.3 = (f32[9,8,256]{2,1,0:T(8,128)S(1)}, f32[9,8,256]{2,1,0:T(8,128)S(1)}, u32[]{:S(2)}, u32[]{:S(2)}) collective-permute-start(f32[9,8,256]{2,1,0:T(8,128)S(1)} %get-tuple-element.47.refs_0_.refs_4_), channel_id=1, source_target_pairs={{0,6},{1,7},{2,0},{3,1},{4,2},{5,3},{6,4},{7,5},{8,14},{9,15},{10,... | collective-permute-start | bytes 221192 | tf_op jit(solution)/shard_map/ppermute | solution.py:900
  9.0 7.7 %collective-permute-start.2 = (f32[9,8,256]{2,1,0:T(8,128)S(1)}, f32[9,8,256]{2,1,0:T(8,128)S(1)}, u32[]{:S(2)}, u32[]{:S(2)}) collective-permute-start(f32[9,8,256]{2,1,0:T(8,128)S(1)} %get-tuple-element.47.refs_0_.refs_4_), channel_id=1, source_target_pairs={{0,4},{1,5},{2,6},{3,7},{4,0},{5,1},{6,2},{7,3},{8,12},{9,13},{10,... | collective-permute-start | bytes 221192 | tf_op jit(solution)/shard_map/ppermute | solution.py:900
  9.0 7.7 %collective-permute-start.1 = (f32[9,8,256]{2,1,0:T(8,128)S(1)}, f32[9,8,256]{2,1,0:T(8,128)S(1)}, u32[]{:S(2)}, u32[]{:S(2)}) collective-permute-start(f32[9,8,256]{2,1,0:T(8,128)S(1)} %get-tuple-element.47.refs_0_.refs_4_), channel_id=1, source_target_pairs={{0,2},{1,3},{2,4},{3,5},{4,6},{5,7},{6,0},{7,1},{8,10},{9,11},{10,... | collective-permute-start | bytes 221192 | tf_op jit(solution)/shard_map/ppermute | solution.py:900
  23.3 7.5 %collective-permute-start.4 = (f32[9,8,256]{2,1,0:T(8,128)S(1)}, f32[9,8,256]{2,1,0:T(8,128)S(1)}, u32[]{:S(2)}, u32[]{:S(2)}) collective-permute-start(f32[9,8,256]{2,1,0:T(8,128)S(1)} %get-tuple-element.49), channel_id=1, source_target_pairs={{0,6},{1,7},{2,0},{3,1},{4,2},{5,3},{6,4},{7,5},{8,14},{9,15},{10,... | collective-permute-start | bytes 221192 | tf_op jit(solution)/shard_map/ppermute | solution.py:900
  23.4 7.3 %collective-permute-start.5 = (f32[9,8,256]{2,1,0:T(8,128)S(1)}, f32[9,8,256]{2,1,0:T(8,128)S(1)}, u32[]{:S(2)}, u32[]{:S(2)}) collective-permute-start(f32[9,8,256]{2,1,0:T(8,128)S(1)} %get-tuple-element.50), channel_id=1, source_target_pairs={{0,4},{1,5},{2,6},{3,7},{4,0},{5,1},{6,2},{7,3},{8,12},{9,13},{10,... | collective-permute-start | bytes 221192 | tf_op jit(solution)/shard_map/ppermute | solution.py:900
  24.2 6.8 %collective-permute-start.6 = (f32[9,8,256]{2,1,0:T(8,128)S(1)}, f32[9,8,256]{2,1,0:T(8,128)S(1)}, u32[]{:S(2)}, u32[]{:S(2)}) collective-permute-start(f32[9,8,256]{2,1,0:T(8,128)S(1)} %get-tuple-element.51), channel_id=1, source_target_pairs={{0,2},{1,3},{2,4},{3,5},{4,6},{5,7},{6,0},{7,1},{8,10},{9,11},{10,... | collective-permute-start | bytes 221192 | tf_op jit(solution)/shard_map/ppermute | solution.py:900
  31.1 2.6 %collective-permute-start.7 = (f32[8,256]{1,0:T(8,128)S(1)}, f32[8,256]{1,0:T(8,128)S(1)}, u32[]{:S(2)}, u32[]{:S(2)}) collective-permute-start(f32[8,256]{1,0:T(8,128)S(1)} %get-tuple-element.53.sent_ref), channel_id=1, source_target_pairs={{0,8},{8,0},{16,24},{24,16},{1,9},{9,1},{17,25},{25,17},{2,10},{10... | collective-permute-start | bytes 24584 | tf_op jit(solution)/shard_map/ppermute | solution.py:735
  33.6 2.5 %collective-permute-start.8 = (f32[8,256]{1,0:T(8,128)S(1)}, f32[8,256]{1,0:T(8,128)S(1)}, u32[]{:S(2)}, u32[]{:S(2)}) collective-permute-start(f32[8,256]{1,0:T(8,128)S(1)} %relay.2.refs_0_), channel_id=1, source_target_pairs={{0,16},{8,24},{16,0},{24,8},{1,17},{9,25},{17,1},{25,9},{2,18},{10... | collective-permute-start | bytes 24584 | tf_op jit(solution)/shard_map/ppermute | solution.py:738
  36.2 8.5 %collective-permute-start.10 = (f32[24,128]{1,0:T(8,128)S(1)}, f32[24,128]{1,0:T(8,128)S(1)}, u32[]{:S(2)}, u32[]{:S(2)}) collective-permute-start(f32[24,128]{1,0:T(8,128)S(1)} %get-tuple-element.56), channel_id=1, source_target_pairs={{1,2},{2,1},{3,4},{4,3},{5,6},{6,5},{9,10},{10,9},{11,12},{12,11},... | collective-permute-start | bytes 36872 | tf_op jit(solution)/shard_map/ppermute | solution.py:755
  43.3 1.4 %collective-permute-start.9 = (f32[24,128]{1,0:T(8,128)S(1)}, f32[24,128]{1,0:T(8,128)S(1)}, u32[]{:S(2)}, u32[]{:S(2)}) collective-permute-start(f32[24,128]{1,0:T(8,128)S(1)} %get-tuple-element.55.sent_ref), channel_id=1, source_target_pairs={{0,1},{1,0},{2,3},{3,2},{4,5},{5,4},{6,7},{7,6},{8,9},{9,8},{10,11... | collective-permute-start | bytes 36872 | tf_op jit(solution)/shard_map/ppermute | solution.py:756
  44.8 3.7 %collective-permute-start.13 = (f32[8,8,256]{2,1,0:T(8,128)S(1)}, f32[8,8,256]{2,1,0:T(8,128)S(1)}, u32[]{:S(2)}, u32[]{:S(2)}) collective-permute-start(f32[8,8,256]{2,1,0:T(8,128)S(1)} %get-tuple-element.57.par_ref.refs_0_), channel_id=1, source_target_pairs={{0,6},{1,7},{2,0},{3,1},{4,2},{5,3},{6,4},{7,5},{8,14},{9,15},{10,... | collective-permute-start | bytes 196616 | tf_op jit(solution)/shard_map/ppermute | solution.py:900
  44.9 4.2 %collective-permute-start.12 = (f32[8,8,256]{2,1,0:T(8,128)S(1)}, f32[8,8,256]{2,1,0:T(8,128)S(1)}, u32[]{:S(2)}, u32[]{:S(2)}) collective-permute-start(f32[8,8,256]{2,1,0:T(8,128)S(1)} %get-tuple-element.57.par_ref.refs_0_), channel_id=1, source_target_pairs={{0,4},{1,5},{2,6},{3,7},{4,0},{5,1},{6,2},{7,3},{8,12},{9,13},{10,... | collective-permute-start | bytes 196616 | tf_op jit(solution)/shard_map/ppermute | solution.py:900
  46.0 5.9 %collective-permute-start.11 = (f32[8,8,256]{2,1,0:T(8,128)S(1)}, f32[8,8,256]{2,1,0:T(8,128)S(1)}, u32[]{:S(2)}, u32[]{:S(2)}) collective-permute-start(f32[8,8,256]{2,1,0:T(8,128)S(1)} %get-tuple-element.57.par_ref.refs_0_), channel_id=1, source_target_pairs={{0,2},{1,3},{2,4},{3,5},{4,6},{5,7},{6,0},{7,1},{8,10},{9,11},{10,... | collective-permute-start | bytes 196616 | tf_op jit(solution)/shard_map/ppermute | solution.py:900
  58.5 7.7 %collective-permute-start.14 = (f32[9,8,256]{2,1,0:T(8,128)S(1)}, f32[9,8,256]{2,1,0:T(8,128)S(1)}, u32[]{:S(2)}, u32[]{:S(2)}) collective-permute-start(f32[9,8,256]{2,1,0:T(8,128)S(1)} %get-tuple-element.60), channel_id=1, source_target_pairs={{0,6},{1,7},{2,0},{3,1},{4,2},{5,3},{6,4},{7,5},{8,14},{9,15},{10,... | collective-permute-start | bytes 221192 | tf_op jit(solution)/shard_map/ppermute | solution.py:900
  59.4 6.8 %collective-permute-start.15 = (f32[9,8,256]{2,1,0:T(8,128)S(1)}, f32[9,8,256]{2,1,0:T(8,128)S(1)}, u32[]{:S(2)}, u32[]{:S(2)}) collective-permute-start(f32[9,8,256]{2,1,0:T(8,128)S(1)} %get-tuple-element.61), channel_id=1, source_target_pairs={{0,4},{1,5},{2,6},{3,7},{4,0},{5,1},{6,2},{7,3},{8,12},{9,13},{10,... | collective-permute-start | bytes 221192 | tf_op jit(solution)/shard_map/ppermute | solution.py:900
  59.6 6.6 %collective-permute-start.16 = (f32[9,8,256]{2,1,0:T(8,128)S(1)}, f32[9,8,256]{2,1,0:T(8,128)S(1)}, u32[]{:S(2)}, u32[]{:S(2)}) collective-permute-start(f32[9,8,256]{2,1,0:T(8,128)S(1)} %get-tuple-element.62), channel_id=1, source_target_pairs={{0,2},{1,3},{2,4},{3,5},{4,6},{5,7},{6,0},{7,1},{8,10},{9,11},{10,... | collective-permute-start | bytes 221192 | tf_op jit(solution)/shard_map/ppermute | solution.py:900
  66.3 2.6 %collective-permute-start.17 = (f32[8,256]{1,0:T(8,128)S(1)}, f32[8,256]{1,0:T(8,128)S(1)}, u32[]{:S(2)}, u32[]{:S(2)}) collective-permute-start(f32[8,256]{1,0:T(8,128)S(1)} %get-tuple-element.64.sent_ref), channel_id=1, source_target_pairs={{0,8},{8,0},{16,24},{24,16},{1,9},{9,1},{17,25},{25,17},{2,10},{10... | collective-permute-start | bytes 24584 | tf_op jit(solution)/shard_map/ppermute | solution.py:735
  68.9 2.5 %collective-permute-start.18 = (f32[8,256]{1,0:T(8,128)S(1)}, f32[8,256]{1,0:T(8,128)S(1)}, u32[]{:S(2)}, u32[]{:S(2)}) collective-permute-start(f32[8,256]{1,0:T(8,128)S(1)} %relay.3.refs_0_), channel_id=1, source_target_pairs={{0,16},{8,24},{16,0},{24,8},{1,17},{9,25},{17,1},{25,9},{2,18},{10... | collective-permute-start | bytes 24584 | tf_op jit(solution)/shard_map/ppermute | solution.py:738
  71.4 9.4 %collective-permute-start.20 = (f32[24,128]{1,0:T(8,128)S(1)}, f32[24,128]{1,0:T(8,128)S(1)}, u32[]{:S(2)}, u32[]{:S(2)}) collective-permute-start(f32[24,128]{1,0:T(8,128)S(1)} %get-tuple-element.67), channel_id=1, source_target_pairs={{1,2},{2,1},{3,4},{4,3},{5,6},{6,5},{9,10},{10,9},{11,12},{12,11},... | collective-permute-start | bytes 36872 | tf_op jit(solution)/shard_map/ppermute | solution.py:755
  79.5 1.4 %collective-permute-start.19 = (f32[24,128]{1,0:T(8,128)S(1)}, f32[24,128]{1,0:T(8,128)S(1)}, u32[]{:S(2)}, u32[]{:S(2)}) collective-permute-start(f32[24,128]{1,0:T(8,128)S(1)} %get-tuple-element.66.sent_ref), channel_id=1, source_target_pairs={{0,1},{1,0},{2,3},{3,2},{4,5},{5,4},{6,7},{7,6},{8,9},{9,8},{10,11... | collective-permute-start | bytes 36872 | tf_op jit(solution)/shard_map/ppermute | solution.py:756

commit v6 on v5

--- a/solution.py
+++ b/solution.py
@@ -340,11 +340,13 @@
 
 
 def sample_kernel(
-    tile_ref, own_ref, got_ref, gain_ref, lobe_ref, shade_ref, plain_ref, tall_ref, slab_ref, *refs, parts
+    tile_ref, own_ref, got_ref, gain_ref, lobe_ref, shade_ref, plain_ref, tall_ref, slab_ref, *refs, parts, mend
 ):
     par_refs, vis_refs = refs[:parts], refs[parts : 2 * parts]
     out_refs = refs[2 * parts : 3 * parts]
-    par_scr, vis_scr, obs_scr, rows_ref, sums_ref, light_scr, gain_scr, plain_scr, flat_scr = refs[3 * parts :]
+    extra = 1 if mend else 0
+    own_out_refs = refs[3 * parts : 3 * parts + extra]
+    par_scr, vis_scr, obs_scr, rows_ref, sums_ref, light_scr, gain_scr, plain_scr, flat_scr = refs[3 * parts + extra :]
     step = pl.program_id(0)
     samples, rows, cols = own_ref.shape
     held = 2 * samples
@@ -354,6 +356,18 @@
         @pl.when(step == s)
         def _():
             par_scr[...] = par_refs[s][0:8]
+            if mend:
+                side = column_is_odd(tile_ref)
+                chip = lax.rem(tile_of(tile_ref) // 2 + (parts - s), parts)
+                inside = jnp.where(side, chip, parts - 1 - chip) < parts - 1
+                lane = iota((rows, cols), 1)
+                hit = jnp.logical_and(lane == jnp.where(side, cols - 1, 0), inside)
+                lower, upper = par_refs[(s + 1) % parts], par_refs[(s - 1) % parts]
+                for k in range(2):
+                    end = jnp.where(side, upper[8, :, k : k + 1], lower[8, :, k : k + 1])
+                    par_scr[k] = par_refs[s][k] + jnp.where(hit, end, 0.0)
+                if s == 0:
+                    own_out_refs[0][...] = par_scr[...]
             vis_scr[...] = vis_refs[s][8].astype(jnp.int32)
 
     core = tile_of(tile_ref) % 2
@@ -549,13 +563,13 @@
 
 
 def rows_kernel(tile_ref, par_ref, first_ref, edge_ref, *refs, last):
-    light_refs, (tall_ref, near_ref, far_ref, scr) = refs[:-4], refs[-4:]
+    light_refs, (tall_ref, near_ref, scr) = refs[:-3], refs[-3:]
     rows, cols = par_ref.shape[1:]
     place = tile_ref[0] // PLACE
-    odd, side = row_is_odd(tile_ref), column_is_odd(tile_ref)
+    odd = row_is_odd(tile_ref)
     outer = jnp.where(jnp.logical_or(place == 0, place == last), 0.0, 1.0)
     near_ref[...] = jnp.zeros(near_ref.shape, f32)
-    far_ref[...] = jnp.zeros(far_ref.shape, f32)
+    lane = iota((rows, LANES), 1)
     for k in range(2):
         other = outer * edge_ref[k : k + 1, :]
         scr[7:8, :] = jnp.where(odd, first_ref[2 + k : 3 + k, :], other)
@@ -563,28 +577,34 @@
         scr[8 + rows : 9 + rows, :] = jnp.where(odd, other, first_ref[k : k + 1, :])
         tall = scr[7 : 7 + rows, :] + scr[8 : 8 + rows, :] + scr[9 : 9 + rows, :]
         tall_ref[k] = tall
-        left, right = tall[:, 0:LANES], tall[:, cols - LANES : cols]
-        near_ref[k * rows : (k + 1) * rows, :] = jnp.where(side, left, right)
-        far_ref[k * rows : (k + 1) * rows, :] = jnp.where(side, right, left)
+        ends = jnp.where(lane == 0, tall[:, 0:1], jnp.where(lane == 1, tall[:, cols - 1 : cols], 0.0))
+        near_ref[k * rows : (k + 1) * rows, :] = ends
     near_ref[2 * rows : 2 * rows + 2, :] = total(ref[4:6, 0:LANES] for ref in light_refs)
 
 
-def smooth_kernel(tile_ref, par_ref, tall_ref, sent_ref, near_ref, far_ref, gain_ref, out_ref, gain_out_ref):
+def smooth_kernel(tile_ref, par_ref, tall_ref, gain_ref, sent_ref, near_ref, *refs):
+    far_refs, (out_ref, gain_out_ref) = refs[:-2], refs[-2:]
     rows, cols = par_ref.shape[1:]
     side = column_is_odd(tile_ref)
     lane = iota((rows, cols), 1)
+    spill = jnp.zeros((rows, cols), f32)
     for k in range(2):
         at = slice(k * rows, (k + 1) * rows)
         tall = tall_ref[k]
-        near_first, near_last = near_ref[at, 0:1], near_ref[at, LANES - 1 : LANES]
-        far_first, far_last = far_ref[at, 0:1], far_ref[at, LANES - 1 : LANES]
-        before = jnp.where(side, near_last, far_last)
-        after = jnp.where(side, far_first, near_first)
+        near_left, near_right = near_ref[at, 0:1], near_ref[at, 1:2]
+        far_left = far_right = jnp.zeros((rows, 1), f32)
+        if far_refs:
+            far_left, far_right = far_refs[0][at, 0:1], far_refs[0][at, 1:2]
+        before = jnp.where(side, near_right, far_right)
+        after = jnp.where(side, far_left, near_left)
         left = jnp.where(lane == 0, before, pltpu.roll(tall, 1, 1))
         right = jnp.where(lane == cols - 1, after, pltpu.roll(tall, cols - 1, 1))
         out_ref[k] = 0.5 * par_ref[k] + (tall + left + right) * (0.5 / 9.0)
+        spill = jnp.where(lane == k, jnp.where(side, near_left, near_right) * (0.5 / 9.0), spill)
     for k in range(2, 8):
         out_ref[k] = par_ref[k]
+    if not far_refs:
+        out_ref[8] = spill
     light = sent_ref[2 * rows : 2 * rows + 2, 0:LIGHTS] + near_ref[2 * rows : 2 * rows + 2, 0:LIGHTS]
     gains = gain_ref[...]
     gain_out_ref[...] = gains + (light[0:1] - gains * light[1:2]) / (light[1:2] + 1.0)
@@ -625,7 +645,7 @@
     )(par, vis, gains, *small)
 
 
-def sample_call(tile, own, got, gains, tables, pars, vises):
+def sample_call(tile, own, got, gains, tables, pars, vises, mend):
     parts = len(pars)
     samples, rows, _ = own.shape
     cols = pars[0].shape[2]
@@ -639,9 +659,11 @@
         return lax.rem(tile_of(tile) // 2 + (parts - s), parts)
 
     outs = [jax.ShapeDtypeStruct((9, rows, cols), f32) for _ in range(parts)]
+    if mend:
+        outs.append(jax.ShapeDtypeStruct((8, rows, cols), f32))
     small = [gains] + [tables[n] for n in ("here", "shade", "plain", "near_tall", "slab")]
     return pl.pallas_call(
-        functools.partial(sample_kernel, parts=parts),
+        functools.partial(sample_kernel, parts=parts, mend=mend),
         name="sample_sums",
         out_shape=outs,
         grid_spec=pltpu.PrefetchScalarGridSpec(
@@ -727,7 +749,7 @@
     return out
 
 
-def settle(tile, low, params, moved, gains):
+def settle(tile, low, params, moved, gains, closed):
     _, rows, cols = params.shape
     grps, tiles = lax.axis_size("grp"), lax.axis_size("tile")
     strip = (8, cols)
@@ -748,14 +770,15 @@
             bit *= 2
         lights = [light]
     patch = (2 * rows + 8, LANES)
-    tall, sent, other = plain_call(
-        functools.partial(rows_kernel, last=grps - 1), "rows", [(2, rows, cols), patch, patch], [(24, cols)],
+    tall, sent = plain_call(
+        functools.partial(rows_kernel, last=grps - 1), "rows", [(2, rows, cols), patch], [(24, cols)],
         tile, params, first, edge, *lights,
     )
-    far = lax.ppermute(other, "tile", pairs(tiles, 1))
+    ends = [lax.ppermute(sent, "tile", pairs(tiles, 1))] if closed else []
     near = lax.ppermute(sent, "tile", pairs(tiles, 0))
+    slabs = 8 if closed else 9
     return plain_call(
-        smooth_kernel, "smooth", [params.shape, gains.shape], [], tile, params, tall, sent, near, far, gains
+        smooth_kernel, "smooth", [(slabs, rows, cols), gains.shape], [], tile, params, tall, gains, sent, near, *ends
     )
 
 
@@ -917,11 +940,14 @@
     params = params_start
     gains = gains_start.reshape(1, LIGHTS)
     for iteration in range(ITERS):
+        rights = sample_call(here, observed, got, gains, tables, blocks, vises, iteration > 0)
+        if iteration > 0:
+            *rights, params = rights
         low = normal_call(params, visible, gains, tables)
-        rights = sample_call(here, observed, got, gains, tables, blocks, vises)
         moved = [rights[0]] + [shifted(rights[s], -s, nz) for s in range(1, nz)]
-        params, gains = settle(here, low, params, moved, gains)
-        if iteration + 1 < ITERS:
+        closed = iteration + 1 == ITERS
+        params, gains = settle(here, low, params, moved, gains, closed)
+        if not closed:
             blocks = [params] + [shifted(params, s, nz) for s in range(1, nz)]
     return params, gains.reshape(LIGHTS)
 

time: 81.9 us -> 79.8 us (0.974)
  starting transfers between devices: 32.6 us -> 28.2 us
  waiting for transfers between devices: 18.3 us -> 20.4 us
    ppermute x2 -> x1, starting transfers between devices: 15.2 us -> 6.36 us  [settle(): ends = [lax.ppermute(sent, 'tile', pairs(tiles, 1))] if closed else []]
    ppermute x2, starting transfers between devices: 0.14 us -> 4.67 us  [settle(): near = lax.ppermute(sent, 'tile', pairs(tiles, 0))]
    ppermute x12, waiting for transfers between devices: 10.5 us -> 13.1 us  [shifted(): lax.ppermute(x, 'tile', [(2 * z + c, 2 * ((z + by) % nz) + c) for z in ra...]
    ppermute x2 -> x1, waiting for transfers between devices: 2.57 us -> 1.29 us  [settle(): ends = [lax.ppermute(sent, 'tile', pairs(tiles, 1))] if closed else []]
    ppermute x2, waiting for transfers between devices: 0.01 us -> 0.84 us  [settle(): near = lax.ppermute(sent, 'tile', pairs(tiles, 0))]
    unnamed x18 -> x16, local copies, waits for them, and re-layouts: 3.16 us -> 3.15 us
  transfers between devices with their start and end apart: 21 -> 20, of which waited for: 11 -> 11; matrix products, arithmetic and copies ran while one was open for 0% -> 0% of each run, Pallas kernels for 15% -> 15%
where the time goes in v6:
time: 79.8 us; the launch traced here: 79.5 us
  starting transfers between devices  28.2 us (35%)
  Pallas kernels  27 us (34%)
  waiting for transfers between devices  20.4 us (26%)
  local copies, waits for them, and re-layouts  3.15 us (4%)
  between operations  0.8 us (1%)
    pallas_call x2, Pallas kernels, sample_call(): pl.pallas_call(functools.partial(sample_kernel, parts=parts, mend=mend),...  13.2 us
    ppermute x12, waiting for transfers between devices, shifted(): lax.ppermute(x, 'tile', [(2 * z + c, 2 * ((z + by) % nz) + c) for z in ra...  13.1 us
    ppermute x12, starting transfers between devices, shifted(): lax.ppermute(x, 'tile', [(2 * z + c, 2 * ((z + by) % nz) + c) for z in ra...  12 us
    pallas_call x2, Pallas kernels, normal_call(): pl.pallas_call(normal_kernel, name='normal_factor', out_shape=jax.ShapeDt...  10.4 us
    ppermute x1, starting transfers between devices, settle(): ends = [lax.ppermute(sent, 'tile', pairs(tiles, 1))] if closed else []  6.36 us
    ppermute x2, starting transfers between devices, settle(): near = lax.ppermute(sent, 'tile', pairs(tiles, 0))  4.67 us
    unnamed x16, local copies, waits for them, and re-layouts  3.15 us
    ppermute x2, waiting for transfers between devices, settle(): first = lax.ppermute(sent, 'grp', pairs(grps, 0))  2.59 us
  transfers between devices with their start and end apart: 20, of which 11 were waited for; matrix products, arithmetic and copies ran while one was open for 0% of the time, Pallas kernels for 15%

profile of v6, /device:TPU:1, one launch (start us, length us, event | category | flops | bytes accessed | tf_op | source)
XLA Modules:
  0.0 79.5 jit_solution(4058468622955834485)
XLA Ops:
  0.7 1.6 %copy-done = bf16[64,8,2048]{2,1,0:T(8,128)(2,1)S(1)} copy-done((bf16[64,8,2048]{2,1,0:T(8,128)(2,1)S(1)}, bf16[64,8,2048]{2,1,0:T(8,128)(2,1)}, u32[]{:S(2)}) %copy-start) | copy-done | bytes 2097176
  2.3 0.8 %copy-done.2 = f32[8,8,256]{2,1,0:T(8,128)S(1)} copy-done((f32[8,8,256]{2,1,0:T(8,128)S(1)}, f32[8,8,256]{2,1,0:T(8,128)}, u32[]{:S(2)}) %copy-start.2) | copy-done | bytes 65560
  3.1 0.7 copy-done.3
  3.8 0.2 pack.1
  4.0 0.0 copy-start.4
  4.0 0.1 collective-permute-start
  4.2 4.8 %collective-permute-start.3 = (f32[9,8,256]{2,1,0:T(8,128)S(1)}, f32[9,8,256]{2,1,0:T(8,128)S(1)}, u32[]{:S(2)}, u32[]{:S(2)}) collective-permute-start(f32[9,8,256]{2,1,0:T(8,128)S(1)} %get-tuple-element.46.refs_0_.refs_4_), channel_id=1, source_target_pairs={{0,6},{1,7},{2,0},{3,1},{4,2},{5,3},{6,4},{7,5},{8,14},{9,15},{10,... | collective-permute-start | bytes 221192 | tf_op jit(solution)/shard_map/ppermute | solution.py:923
  8.9 0.0 collective-permute-start.2
  8.9 0.5 collective-permute-start.1
  9.4 1.9 %tables.1 = (f32[8,32]{1,0:T(8,128)S(1)}, f32[8,16]{1,0:T(8,128)S(1)}, bf16[512,48]{1,0:T(8,128)(2,1)S(1)}, f32[32,512]{1,0:T(8,128)S(1)}, bf16[128,32]{1,0:T(8,...) custom-call(s32[1]{0:T(128)} %bitcast.tile_ref, ...), custom_call_target="tpu_custom_call" | custom-call | tf_op jit(solution)/shard_map/tables/pallas_call | solution.py:910
  11.3 5.3 %collective-permute-done.2.refs_2_.refs_6_ = f32[9,8,256]{2,1,0:T(8,128)S(1)} collective-permute-done((f32[9,8,256]{2,1,0:T(8,128)S(1)}, f32[9,8,256]{2,1,0:T(8,128)S(1)}, u32[]{:S(2)}, u32[]{:S(2)}) %collective-permute-start.2) | collective-permute-done | bytes 73760 | tf_op jit(solution)/shard_map/ppermute | solution.py:923
  16.6 0.0 collective-permute-done.1.refs_1_.refs_5_
  16.6 6.5 %sample_sums.2 = (f32[9,8,256]{2,1,0:T(8,128)S(1)}, f32[9,8,256]{2,1,0:T(8,128)S(1)}, f32[9,8,256]{2,1,0:T(8,128)S(1)}, f32[9,8,256]{2,1,0:T(8,128)S(1)}) custom-call(s32[1]{0:T(128)} %bitcast.tile_ref, bf16[64,8,2048]{2,1,0:T(8,128)(2,1)S(1)} %copy-done.1, bf16[64,8,1024]{2,1,0:T(8,128)(2,1)S(1)} %collective-permute-done.got_ref, f32[1,32]{1,0:T(1,128)S(1)} %bitcast.3, ...), custom_call_target="tpu_custom_call" | custom-call | tf_op jit(solution)/shard_map/sample_sums/pallas_call | solution.py:665
  23.1 0.2 collective-permute-start.4
  23.3 0.7 collective-permute-start.5
  24.0 1.4 %collective-permute-start.6 = (f32[9,8,256]{2,1,0:T(8,128)S(1)}, f32[9,8,256]{2,1,0:T(8,128)S(1)}, u32[]{:S(2)}, u32[]{:S(2)}) collective-permute-start(f32[9,8,256]{2,1,0:T(8,128)S(1)} %get-tuple-element.50), channel_id=1, source_target_pairs={{0,2},{1,3},{2,4},{3,5},{4,6},{5,7},{6,0},{7,1},{8,10},{9,11},{10,... | collective-permute-start | bytes 221192 | tf_op jit(solution)/shard_map/ppermute | solution.py:923
  25.4 5.2 %normal_factor.2.low_ref = f32[44,8,256]{2,1,0:T(8,128)S(1)} custom-call(f32[8,8,256]{2,1,0:T(8,128)S(1)} %copy-done.2, s32[8,256]{1,0:T(8,128)S(1)} %copy-done.4, f32[1,32]{1,0:T(1,128)S(1)} %bitcast.4, f32[8,32]{1,0:T(8,128)S(1)} %get-tuple-element.36.near_ref, f32[8,16]{1,0:T(8,128)S(1)} %get-tuple-element.37.cams_ref, ...), custom_call_target="tpu_custom_call" | custom-call | tf_op jit(solution)/shard_map/normal_factor/pallas_call | solution.py:629
  30.7 0.2 collective-permute-done.6.refs_3_
  30.8 0.1 solve.2
  30.9 1.3 %collective-permute-start.7 = (f32[8,256]{1,0:T(8,128)S(1)}, f32[8,256]{1,0:T(8,128)S(1)}, u32[]{:S(2)}, u32[]{:S(2)}) collective-permute-start(f32[8,256]{1,0:T(8,128)S(1)} %get-tuple-element.52.sent_ref), channel_id=1, source_target_pairs={{0,8},{8,0},{16,24},{24,16},{1,9},{9,1},{17,25},{25,17},{2,10},{10... | collective-permute-start | bytes 24584 | tf_op jit(solution)/shard_map/ppermute | solution.py:757
  32.2 1.3 %collective-permute-done.7.first_ref = f32[8,256]{1,0:T(8,128)S(1)} collective-permute-done((f32[8,256]{1,0:T(8,128)S(1)}, f32[8,256]{1,0:T(8,128)S(1)}, u32[]{:S(2)}, u32[]{:S(2)}) %collective-permute-start.7) | collective-permute-done | bytes 8224 | tf_op jit(solution)/shard_map/ppermute | solution.py:757
  33.5 1.2 %collective-permute-start.8 = (f32[8,256]{1,0:T(8,128)S(1)}, f32[8,256]{1,0:T(8,128)S(1)}, u32[]{:S(2)}, u32[]{:S(2)}) collective-permute-start(f32[8,256]{1,0:T(8,128)S(1)} %relay.2.refs_0_), channel_id=1, source_target_pairs={{0,16},{8,24},{16,0},{24,8},{1,17},{9,25},{17,1},{25,9},{2,18},{10... | collective-permute-start | bytes 24584 | tf_op jit(solution)/shard_map/ppermute | solution.py:760
  34.7 1.3 %collective-permute-done.8.edge_ref.refs_1_ = f32[8,256]{1,0:T(8,128)S(1)} collective-permute-done((f32[8,256]{1,0:T(8,128)S(1)}, f32[8,256]{1,0:T(8,128)S(1)}, u32[]{:S(2)}, u32[]{:S(2)}) %collective-permute-start.8) | collective-permute-done | bytes 8224 | tf_op jit(solution)/shard_map/ppermute | solution.py:760
  36.0 0.1 rows.2
  36.1 4.6 %collective-permute-start.9 = (f32[24,128]{1,0:T(8,128)S(1)}, f32[24,128]{1,0:T(8,128)S(1)}, u32[]{:S(2)}, u32[]{:S(2)}) collective-permute-start(f32[24,128]{1,0:T(8,128)S(1)} %get-tuple-element.54.sent_ref), channel_id=1, source_target_pairs={{0,1},{1,0},{2,3},{3,2},{4,5},{5,4},{6,7},{7,6},{8,9},{9,8},{10,11... | collective-permute-start | bytes 36872 | tf_op jit(solution)/shard_map/ppermute | solution.py:778
  40.7 0.8 %collective-permute-done.9.near_ref = f32[24,128]{1,0:T(8,128)S(1)} collective-permute-done((f32[24,128]{1,0:T(8,128)S(1)}, f32[24,128]{1,0:T(8,128)S(1)}, u32[]{:S(2)}, u32[]{:S(2)}) %collective-permute-start.9) | collective-permute-done | bytes 12320 | tf_op jit(solution)/shard_map/ppermute | solution.py:778
  41.5 0.1 smooth.2
  41.7 1.2 %collective-permute-start.12 = (f32[9,8,256]{2,1,0:T(8,128)S(1)}, f32[9,8,256]{2,1,0:T(8,128)S(1)}, u32[]{:S(2)}, u32[]{:S(2)}) collective-permute-start(f32[9,8,256]{2,1,0:T(8,128)S(1)} %get-tuple-element.56.refs_0_), channel_id=1, source_target_pairs={{0,6},{1,7},{2,0},{3,1},{4,2},{5,3},{6,4},{7,5},{8,14},{9,15},{10,... | collective-permute-start | bytes 221192 | tf_op jit(solution)/shard_map/ppermute | solution.py:923
  42.8 0.8 %collective-permute-start.11 = (f32[9,8,256]{2,1,0:T(8,128)S(1)}, f32[9,8,256]{2,1,0:T(8,128)S(1)}, u32[]{:S(2)}, u32[]{:S(2)}) collective-permute-start(f32[9,8,256]{2,1,0:T(8,128)S(1)} %get-tuple-element.56.refs_0_), channel_id=1, source_target_pairs={{0,4},{1,5},{2,6},{3,7},{4,0},{5,1},{6,2},{7,3},{8,12},{9,13},{10,... | collective-permute-start | bytes 221192 | tf_op jit(solution)/shard_map/ppermute | solution.py:923
  43.7 0.0 collective-permute-start.10
  43.7 1.2 %collective-permute-done.12.refs_3_ = f32[9,8,256]{2,1,0:T(8,128)S(1)} collective-permute-done((f32[9,8,256]{2,1,0:T(8,128)S(1)}, f32[9,8,256]{2,1,0:T(8,128)S(1)}, u32[]{:S(2)}, u32[]{:S(2)}) %collective-permute-start.12) | collective-permute-done | bytes 73760 | tf_op jit(solution)/shard_map/ppermute | solution.py:923
  44.9 6.1 %collective-permute-done.11.refs_2_ = f32[9,8,256]{2,1,0:T(8,128)S(1)} collective-permute-done((f32[9,8,256]{2,1,0:T(8,128)S(1)}, f32[9,8,256]{2,1,0:T(8,128)S(1)}, u32[]{:S(2)}, u32[]{:S(2)}) %collective-permute-start.11) | collective-permute-done | bytes 73760 | tf_op jit(solution)/shard_map/ppermute | solution.py:923
  51.0 6.7 %sample_sums.3 = (f32[9,8,256]{2,1,0:T(8,128)S(1)}, f32[9,8,256]{2,1,0:T(8,128)S(1)}, f32[9,8,256]{2,1,0:T(8,128)S(1)}, f32[9,8,256]{2,1,0:T(8,128)S(1)}, f32[8,8,256]{2,1,0:T(8,128)S(1)}) custom-call(s32[1]{0:T(128)} %bitcast.tile_ref, bf16[64,8,2048]{2,1,0:T(8,128)(2,1)S(1)} %copy-done.1, bf16[64,8,1024]{2,1,0:T(8,128)(2,1)S(1)} %collective-permute-done.got_ref, ...), custom_call_target="tpu_custom_call" | custom-call | tf_op jit(solution)/shard_map/sample_sums/pallas_call | solution.py:665
  57.7 0.3 collective-permute-start.13
  58.1 0.8 collective-permute-start.14
  58.9 1.4 %collective-permute-start.15 = (f32[9,8,256]{2,1,0:T(8,128)S(1)}, f32[9,8,256]{2,1,0:T(8,128)S(1)}, u32[]{:S(2)}, u32[]{:S(2)}) collective-permute-start(f32[9,8,256]{2,1,0:T(8,128)S(1)} %get-tuple-element.61), channel_id=1, source_target_pairs={{0,2},{1,3},{2,4},{3,5},{4,6},{5,7},{6,0},{7,1},{8,10},{9,11},{10,... | collective-permute-start | bytes 221192 | tf_op jit(solution)/shard_map/ppermute | solution.py:923
  60.2 5.2 %normal_factor.3.low_ref = f32[44,8,256]{2,1,0:T(8,128)S(1)} custom-call(f32[8,8,256]{2,1,0:T(8,128)S(1)} %get-tuple-element.57.par_ref, s32[8,256]{1,0:T(8,128)S(1)} %copy-done.4, f32[1,32]{1,0:T(1,128)S(1)} %get-tuple-element.55.gain_ref, f32[8,32]{1,0:T(8,128)S(1)} %get-tuple-element.36.near_ref, f32[8,16]{1,0:T(8,128)S(1)} %get-tuple-element.37.cams_ref, ...), custom_call_target="tpu_custom_call" | custom-call | tf_op jit(solution)/shard_map/normal_factor/pallas_call | solution.py:629
  65.5 0.3 collective-permute-done.15.refs_3_
  65.8 0.1 solve.3
  65.9 1.3 %collective-permute-start.16 = (f32[8,256]{1,0:T(8,128)S(1)}, f32[8,256]{1,0:T(8,128)S(1)}, u32[]{:S(2)}, u32[]{:S(2)}) collective-permute-start(f32[8,256]{1,0:T(8,128)S(1)} %get-tuple-element.63.sent_ref), channel_id=1, source_target_pairs={{0,8},{8,0},{16,24},{24,16},{1,9},{9,1},{17,25},{25,17},{2,10},{10... | collective-permute-start | bytes 24584 | tf_op jit(solution)/shard_map/ppermute | solution.py:757
  67.2 1.3 %collective-permute-done.16.first_ref = f32[8,256]{1,0:T(8,128)S(1)} collective-permute-done((f32[8,256]{1,0:T(8,128)S(1)}, f32[8,256]{1,0:T(8,128)S(1)}, u32[]{:S(2)}, u32[]{:S(2)}) %collective-permute-start.16) | collective-permute-done | bytes 8224 | tf_op jit(solution)/shard_map/ppermute | solution.py:757
  68.5 1.2 %collective-permute-start.17 = (f32[8,256]{1,0:T(8,128)S(1)}, f32[8,256]{1,0:T(8,128)S(1)}, u32[]{:S(2)}, u32[]{:S(2)}) collective-permute-start(f32[8,256]{1,0:T(8,128)S(1)} %relay.3.refs_0_), channel_id=1, source_target_pairs={{0,16},{8,24},{16,0},{24,8},{1,17},{9,25},{17,1},{25,9},{2,18},{10... | collective-permute-start | bytes 24584 | tf_op jit(solution)/shard_map/ppermute | solution.py:760
  69.7 1.3 %collective-permute-done.17.edge_ref.refs_1_ = f32[8,256]{1,0:T(8,128)S(1)} collective-permute-done((f32[8,256]{1,0:T(8,128)S(1)}, f32[8,256]{1,0:T(8,128)S(1)}, u32[]{:S(2)}, u32[]{:S(2)}) %collective-permute-start.17) | collective-permute-done | bytes 8224 | tf_op jit(solution)/shard_map/ppermute | solution.py:760
  71.0 0.1 rows.3
  71.1 6.4 %collective-permute-start.19 = (f32[24,128]{1,0:T(8,128)S(1)}, f32[24,128]{1,0:T(8,128)S(1)}, u32[]{:S(2)}, u32[]{:S(2)}) collective-permute-start(f32[24,128]{1,0:T(8,128)S(1)} %get-tuple-element.65.sent_ref), channel_id=1, source_target_pairs={{1,2},{2,1},{3,4},{4,3},{5,6},{6,5},{9,10},{10,9},{11,12},{12,11},... | collective-permute-start | bytes 36872 | tf_op jit(solution)/shard_map/ppermute | solution.py:777
  77.4 0.1 collective-permute-start.18
  77.5 1.3 %collective-permute-done.19.refs_0_ = f32[24,128]{1,0:T(8,128)S(1)} collective-permute-done((f32[24,128]{1,0:T(8,128)S(1)}, f32[24,128]{1,0:T(8,128)S(1)}, u32[]{:S(2)}, u32[]{:S(2)}) %collective-permute-start.19) | collective-permute-done | bytes 12320 | tf_op jit(solution)/shard_map/ppermute | solution.py:777
  78.8 0.7 smooth.3
  (22 shorter events, 0.1 us)
Async XLA Ops:
  0.6 8.8 %copy-start.7 = (f32[3,16]{1,0:T(4,128)S(1)}, f32[3,16]{1,0:T(4,128)}, u32[]{:S(2)}) copy-start(f32[3,16]{1,0:T(4,128)} %view_ref.1) | copy-start | bytes 580
  0.6 8.8 %copy-start.6 = (f32[3,32]{1,0:T(4,128)S(1)}, f32[3,32]{1,0:T(4,128)}, u32[]{:S(2)}) copy-start(f32[3,32]{1,0:T(4,128)} %light_ref.1) | copy-start | bytes 1156
  0.7 16.0 %copy-start.5 = (f32[32]{0:T(128)S(1)}, f32[32]{0:T(128)}, u32[]{:S(2)}) copy-start(f32[32]{0:T(128)} %param.11) | copy-start | bytes 388
  0.7 1.6 %copy-start = (bf16[64,8,2048]{2,1,0:T(8,128)(2,1)S(1)}, bf16[64,8,2048]{2,1,0:T(8,128)(2,1)}, u32[]{:S(2)}) copy-start(bf16[64,8,2048]{2,1,0:T(8,128)(2,1)} %own_ref.3) | copy-start | bytes 6291460
  2.3 0.8 %copy-start.2 = (f32[8,8,256]{2,1,0:T(8,128)S(1)}, f32[8,8,256]{2,1,0:T(8,128)}, u32[]{:S(2)}) copy-start(f32[8,8,256]{2,1,0:T(8,128)} %par_ref.5) | copy-start | bytes 196612
  3.1 0.7 copy-start.3
  3.8 12.8 %copy-start.1 = (bf16[64,8,2048]{2,1,0:T(8,128)(2,1)S(1)}, bf16[64,8,2048]{2,1,0:T(8,128)(2,1)}, u32[]{:S(2)}) copy-start(bf16[64,8,2048]{2,1,0:T(8,128)(2,1)} %own_ref.3) | copy-start | bytes 6291460
  4.0 21.4 %copy-start.4 = (s32[8,256]{1,0:T(8,128)S(1)}, s32[8,256]{1,0:T(8,128)}, u32[]{:S(2)}) copy-start(s32[8,256]{1,0:T(8,128)} %vis_ref.5) | copy-start | bytes 24580
  4.0 12.6 %collective-permute-start = (bf16[64,8,1024]{2,1,0:T(8,128)(2,1)S(1)}, bf16[64,8,1024]{2,1,0:T(8,128)(2,1)S(1)}, u32[]{:S(2)}, u32[]{:S(2)}) collective-permute-start(bf16[64,8,1024]{2,1,0:T(8,128)(2,1)S(1)} %get-tuple-element.35), channel_id=1, source_target_pairs={{0,1},{1,0},{2,3},{3,2},{4,5},{5,4},{6,7},{7,6},{8,9},{9,8},{10,11... | collective-permute-start | bytes 3145736 | tf_op jit(solution)/shard_map/ppermute | solution.py:935
  4.2 7.1 %collective-permute-start.3 = (f32[9,8,256]{2,1,0:T(8,128)S(1)}, f32[9,8,256]{2,1,0:T(8,128)S(1)}, u32[]{:S(2)}, u32[]{:S(2)}) collective-permute-start(f32[9,8,256]{2,1,0:T(8,128)S(1)} %get-tuple-element.46.refs_0_.refs_4_), channel_id=1, source_target_pairs={{0,6},{1,7},{2,0},{3,1},{4,2},{5,3},{6,4},{7,5},{8,14},{9,15},{10,... | collective-permute-start | bytes 221192 | tf_op jit(solution)/shard_map/ppermute | solution.py:923
  8.9 7.7 %collective-permute-start.2 = (f32[9,8,256]{2,1,0:T(8,128)S(1)}, f32[9,8,256]{2,1,0:T(8,128)S(1)}, u32[]{:S(2)}, u32[]{:S(2)}) collective-permute-start(f32[9,8,256]{2,1,0:T(8,128)S(1)} %get-tuple-element.46.refs_0_.refs_4_), channel_id=1, source_target_pairs={{0,4},{1,5},{2,6},{3,7},{4,0},{5,1},{6,2},{7,3},{8,12},{9,13},{10,... | collective-permute-start | bytes 221192 | tf_op jit(solution)/shard_map/ppermute | solution.py:923
  8.9 7.7 %collective-permute-start.1 = (f32[9,8,256]{2,1,0:T(8,128)S(1)}, f32[9,8,256]{2,1,0:T(8,128)S(1)}, u32[]{:S(2)}, u32[]{:S(2)}) collective-permute-start(f32[9,8,256]{2,1,0:T(8,128)S(1)} %get-tuple-element.46.refs_0_.refs_4_), channel_id=1, source_target_pairs={{0,2},{1,3},{2,4},{3,5},{4,6},{5,7},{6,0},{7,1},{8,10},{9,11},{10,... | collective-permute-start | bytes 221192 | tf_op jit(solution)/shard_map/ppermute | solution.py:923
  23.1 7.5 %collective-permute-start.4 = (f32[9,8,256]{2,1,0:T(8,128)S(1)}, f32[9,8,256]{2,1,0:T(8,128)S(1)}, u32[]{:S(2)}, u32[]{:S(2)}) collective-permute-start(f32[9,8,256]{2,1,0:T(8,128)S(1)} %get-tuple-element.48), channel_id=1, source_target_pairs={{0,6},{1,7},{2,0},{3,1},{4,2},{5,3},{6,4},{7,5},{8,14},{9,15},{10,... | collective-permute-start | bytes 221192 | tf_op jit(solution)/shard_map/ppermute | solution.py:923
  23.3 7.3 %collective-permute-start.5 = (f32[9,8,256]{2,1,0:T(8,128)S(1)}, f32[9,8,256]{2,1,0:T(8,128)S(1)}, u32[]{:S(2)}, u32[]{:S(2)}) collective-permute-start(f32[9,8,256]{2,1,0:T(8,128)S(1)} %get-tuple-element.49), channel_id=1, source_target_pairs={{0,4},{1,5},{2,6},{3,7},{4,0},{5,1},{6,2},{7,3},{8,12},{9,13},{10,... | collective-permute-start | bytes 221192 | tf_op jit(solution)/shard_map/ppermute | solution.py:923
  24.0 6.8 %collective-permute-start.6 = (f32[9,8,256]{2,1,0:T(8,128)S(1)}, f32[9,8,256]{2,1,0:T(8,128)S(1)}, u32[]{:S(2)}, u32[]{:S(2)}) collective-permute-start(f32[9,8,256]{2,1,0:T(8,128)S(1)} %get-tuple-element.50), channel_id=1, source_target_pairs={{0,2},{1,3},{2,4},{3,5},{4,6},{5,7},{6,0},{7,1},{8,10},{9,11},{10,... | collective-permute-start | bytes 221192 | tf_op jit(solution)/shard_map/ppermute | solution.py:923
  30.9 2.6 %collective-permute-start.7 = (f32[8,256]{1,0:T(8,128)S(1)}, f32[8,256]{1,0:T(8,128)S(1)}, u32[]{:S(2)}, u32[]{:S(2)}) collective-permute-start(f32[8,256]{1,0:T(8,128)S(1)} %get-tuple-element.52.sent_ref), channel_id=1, source_target_pairs={{0,8},{8,0},{16,24},{24,16},{1,9},{9,1},{17,25},{25,17},{2,10},{10... | collective-permute-start | bytes 24584 | tf_op jit(solution)/shard_map/ppermute | solution.py:757
  33.5 2.5 %collective-permute-start.8 = (f32[8,256]{1,0:T(8,128)S(1)}, f32[8,256]{1,0:T(8,128)S(1)}, u32[]{:S(2)}, u32[]{:S(2)}) collective-permute-start(f32[8,256]{1,0:T(8,128)S(1)} %relay.2.refs_0_), channel_id=1, source_target_pairs={{0,16},{8,24},{16,0},{24,8},{1,17},{9,25},{17,1},{25,9},{2,18},{10... | collective-permute-start | bytes 24584 | tf_op jit(solution)/shard_map/ppermute | solution.py:760
  36.1 5.4 %collective-permute-start.9 = (f32[24,128]{1,0:T(8,128)S(1)}, f32[24,128]{1,0:T(8,128)S(1)}, u32[]{:S(2)}, u32[]{:S(2)}) collective-permute-start(f32[24,128]{1,0:T(8,128)S(1)} %get-tuple-element.54.sent_ref), channel_id=1, source_target_pairs={{0,1},{1,0},{2,3},{3,2},{4,5},{5,4},{6,7},{7,6},{8,9},{9,8},{10,11... | collective-permute-start | bytes 36872 | tf_op jit(solution)/shard_map/ppermute | solution.py:778
  41.7 3.2 %collective-permute-start.12 = (f32[9,8,256]{2,1,0:T(8,128)S(1)}, f32[9,8,256]{2,1,0:T(8,128)S(1)}, u32[]{:S(2)}, u32[]{:S(2)}) collective-permute-start(f32[9,8,256]{2,1,0:T(8,128)S(1)} %get-tuple-element.56.refs_0_), channel_id=1, source_target_pairs={{0,6},{1,7},{2,0},{3,1},{4,2},{5,3},{6,4},{7,5},{8,14},{9,15},{10,... | collective-permute-start | bytes 221192 | tf_op jit(solution)/shard_map/ppermute | solution.py:923
  42.8 8.2 %collective-permute-start.11 = (f32[9,8,256]{2,1,0:T(8,128)S(1)}, f32[9,8,256]{2,1,0:T(8,128)S(1)}, u32[]{:S(2)}, u32[]{:S(2)}) collective-permute-start(f32[9,8,256]{2,1,0:T(8,128)S(1)} %get-tuple-element.56.refs_0_), channel_id=1, source_target_pairs={{0,4},{1,5},{2,6},{3,7},{4,0},{5,1},{6,2},{7,3},{8,12},{9,13},{10,... | collective-permute-start | bytes 221192 | tf_op jit(solution)/shard_map/ppermute | solution.py:923
  43.7 7.3 %collective-permute-start.10 = (f32[9,8,256]{2,1,0:T(8,128)S(1)}, f32[9,8,256]{2,1,0:T(8,128)S(1)}, u32[]{:S(2)}, u32[]{:S(2)}) collective-permute-start(f32[9,8,256]{2,1,0:T(8,128)S(1)} %get-tuple-element.56.refs_0_), channel_id=1, source_target_pairs={{0,2},{1,3},{2,4},{3,5},{4,6},{5,7},{6,0},{7,1},{8,10},{9,11},{10,... | collective-permute-start | bytes 221192 | tf_op jit(solution)/shard_map/ppermute | solution.py:923
  57.7 7.7 %collective-permute-start.13 = (f32[9,8,256]{2,1,0:T(8,128)S(1)}, f32[9,8,256]{2,1,0:T(8,128)S(1)}, u32[]{:S(2)}, u32[]{:S(2)}) collective-permute-start(f32[9,8,256]{2,1,0:T(8,128)S(1)} %get-tuple-element.59), channel_id=1, source_target_pairs={{0,6},{1,7},{2,0},{3,1},{4,2},{5,3},{6,4},{7,5},{8,14},{9,15},{10,... | collective-permute-start | bytes 221192 | tf_op jit(solution)/shard_map/ppermute | solution.py:923
  58.1 7.4 %collective-permute-start.14 = (f32[9,8,256]{2,1,0:T(8,128)S(1)}, f32[9,8,256]{2,1,0:T(8,128)S(1)}, u32[]{:S(2)}, u32[]{:S(2)}) collective-permute-start(f32[9,8,256]{2,1,0:T(8,128)S(1)} %get-tuple-element.60), channel_id=1, source_target_pairs={{0,4},{1,5},{2,6},{3,7},{4,0},{5,1},{6,2},{7,3},{8,12},{9,13},{10,... | collective-permute-start | bytes 221192 | tf_op jit(solution)/shard_map/ppermute | solution.py:923
  58.9 6.9 %collective-permute-start.15 = (f32[9,8,256]{2,1,0:T(8,128)S(1)}, f32[9,8,256]{2,1,0:T(8,128)S(1)}, u32[]{:S(2)}, u32[]{:S(2)}) collective-permute-start(f32[9,8,256]{2,1,0:T(8,128)S(1)} %get-tuple-element.61), channel_id=1, source_target_pairs={{0,2},{1,3},{2,4},{3,5},{4,6},{5,7},{6,0},{7,1},{8,10},{9,11},{10,... | collective-permute-start | bytes 221192 | tf_op jit(solution)/shard_map/ppermute | solution.py:923
  65.9 2.6 %collective-permute-start.16 = (f32[8,256]{1,0:T(8,128)S(1)}, f32[8,256]{1,0:T(8,128)S(1)}, u32[]{:S(2)}, u32[]{:S(2)}) collective-permute-start(f32[8,256]{1,0:T(8,128)S(1)} %get-tuple-element.63.sent_ref), channel_id=1, source_target_pairs={{0,8},{8,0},{16,24},{24,16},{1,9},{9,1},{17,25},{25,17},{2,10},{10... | collective-permute-start | bytes 24584 | tf_op jit(solution)/shard_map/ppermute | solution.py:757
  68.5 2.5 %collective-permute-start.17 = (f32[8,256]{1,0:T(8,128)S(1)}, f32[8,256]{1,0:T(8,128)S(1)}, u32[]{:S(2)}, u32[]{:S(2)}) collective-permute-start(f32[8,256]{1,0:T(8,128)S(1)} %relay.3.refs_0_), channel_id=1, source_target_pairs={{0,16},{8,24},{16,0},{24,8},{1,17},{9,25},{17,1},{25,9},{2,18},{10... | collective-permute-start | bytes 24584 | tf_op jit(solution)/shard_map/ppermute | solution.py:760
  71.1 7.7 %collective-permute-start.19 = (f32[24,128]{1,0:T(8,128)S(1)}, f32[24,128]{1,0:T(8,128)S(1)}, u32[]{:S(2)}, u32[]{:S(2)}) collective-permute-start(f32[24,128]{1,0:T(8,128)S(1)} %get-tuple-element.65.sent_ref), channel_id=1, source_target_pairs={{1,2},{2,1},{3,4},{4,3},{5,6},{6,5},{9,10},{10,9},{11,12},{12,11},... | collective-permute-start | bytes 36872 | tf_op jit(solution)/shard_map/ppermute | solution.py:777
  77.4 1.4 %collective-permute-start.18 = (f32[24,128]{1,0:T(8,128)S(1)}, f32[24,128]{1,0:T(8,128)S(1)}, u32[]{:S(2)}, u32[]{:S(2)}) collective-permute-start(f32[24,128]{1,0:T(8,128)S(1)} %get-tuple-element.65.sent_ref), channel_id=1, source_target_pairs={{0,1},{1,0},{2,3},{3,2},{4,5},{5,4},{6,7},{7,6},{8,9},{9,8},{10,11... | collective-permute-start | bytes 36872 | tf_op jit(solution)/shard_map/ppermute | solution.py:778

commit v7 on v6

--- a/solution.py
+++ b/solution.py
@@ -693,10 +693,15 @@
     )(tile, own, got, *small, *pars, *vises)
 
 
-def pack_kernel(tile_ref, seen_ref, par_ref, vis_ref, send_ref, first_ref, sems):
-    parts = sems.shape[0]
+def pack_kernel(tile_ref, seen_ref, par_ref, vis_ref, send_ref, first_ref, vis_scr, sems):
+    parts = sems.shape[0] - 2
     width = send_ref.shape[2] // parts
-    copies = []
+    copies = [
+        pltpu.make_async_copy(vis_ref, vis_scr, sems.at[parts]),
+        pltpu.make_async_copy(par_ref, first_ref.at[0:8], sems.at[parts + 1]),
+    ]
+    copies[0].start()
+    copies[1].start()
     for z in range(parts):
         start = pl.multiple_of((2 * z + 1 - lax.rem(tile_ref[0], 2)) * width, LANES)
         copies.append(
@@ -706,10 +711,10 @@
                 sems.at[z],
             )
         )
-        copies[z].start()
-    first_ref[0:8] = par_ref[...]
-    first_ref[8] = vis_ref[...].astype(f32)
-    for copy in copies:
+        copies[z + 2].start()
+    copies[0].wait()
+    first_ref[8] = vis_scr[...].astype(f32)
+    for copy in copies[1:]:
         copy.wait()
 
 
@@ -723,11 +728,11 @@
             jax.ShapeDtypeStruct((samples, rows, width // 2), observed.dtype),
             jax.ShapeDtypeStruct((9,) + params.shape[1:], f32),
         ],
-        in_specs=[smem(), far, vmem(), vmem()],
+        in_specs=[smem(), far, far, far],
         out_specs=[far, vmem()],
-        scratch_shapes=[pltpu.SemaphoreType.DMA((parts,))],
+        scratch_shapes=[pltpu.VMEM(visible.shape, jnp.int32), pltpu.SemaphoreType.DMA((parts + 2,))],
         compiler_params=params_of(),
-    )(tile, observed, params, visible)
+    )(tile, *[pltpu.with_memory_space_constraint(x, pltpu.MemorySpace.HBM) for x in (observed, params, visible)])
 
 
 def plain_call(kernel, name, shapes, scratch, tile, *args):

time: 79.8 us -> 77.8 us (0.975)
  local copies, waits for them, and re-layouts: 3.15 us -> 0.03 us
  Pallas kernels: 27 us -> 28.2 us
    unnamed x16 -> x12, local copies, waits for them, and re-layouts: 3.15 us -> 0.03 us
    pallas_call x1, Pallas kernels: 0.21 us -> 1.44 us  [pack_call(): pl.pallas_call(pack_kernel, name='pack', out_shape=[jax.ShapeDtypeStruct(...]
  transfers between devices with their start and end apart: 20 -> 20, of which waited for: 11 -> 11; matrix products, arithmetic and copies ran while one was open for 0% -> 0% of each run, Pallas kernels for 15% -> 16%
where the time goes in v7:
time: 77.8 us; the launch traced here: 77.7 us
  Pallas kernels  28.2 us (36%)
  starting transfers between devices  28.1 us (36%)
  waiting for transfers between devices  20.5 us (26%)
  between operations  0.81 us (1%)
    pallas_call x2, Pallas kernels, sample_call(): pl.pallas_call(functools.partial(sample_kernel, parts=parts, mend=mend),...  13.2 us
    ppermute x12, waiting for transfers between devices, shifted(): lax.ppermute(x, 'tile', [(2 * z + c, 2 * ((z + by) % nz) + c) for z in ra...  13.1 us
    ppermute x12, starting transfers between devices, shifted(): lax.ppermute(x, 'tile', [(2 * z + c, 2 * ((z + by) % nz) + c) for z in ra...  11.9 us
    pallas_call x2, Pallas kernels, normal_call(): pl.pallas_call(normal_kernel, name='normal_factor', out_shape=jax.ShapeDt...  10.4 us
    ppermute x1, starting transfers between devices, settle(): ends = [lax.ppermute(sent, 'tile', pairs(tiles, 1))] if closed else []  6.41 us
    ppermute x2, starting transfers between devices, settle(): near = lax.ppermute(sent, 'tile', pairs(tiles, 0))  4.68 us
    ppermute x2, waiting for transfers between devices, settle(): first = lax.ppermute(sent, 'grp', pairs(grps, 0))  2.64 us
    ppermute x2, waiting for transfers between devices, settle(): edge = lax.ppermute(relay, 'grp', [(i, i ^ 2) for i in range(grps)])  2.59 us
  transfers between devices with their start and end apart: 20, of which 11 were waited for; matrix products, arithmetic and copies ran while one was open for 0% of the time, Pallas kernels for 16%

profile of v7, /device:TPU:1, one launch (start us, length us, event | category | flops | bytes accessed | tf_op | source)
XLA Modules:
  0.0 77.7 jit_solution(9532790971752244365)
XLA Ops:
  0.7 1.4 %pack.1 = (bf16[64,8,1024]{2,1,0:T(8,128)(2,1)S(1)}, f32[9,8,256]{2,1,0:T(8,128)S(1)}) custom-call(s32[1]{0:T(128)} %bitcast.tile_ref, bf16[64,8,2048]{2,1,0:T(8,128)(2,1)} %own_ref.3, f32[8,8,256]{2,1,0:T(8,128)} %par_ref.5, s32[8,256]{1,0:T(8,128)} %vis_ref.5), custom_call_target="tpu_custom_call" | custom-call | tf_op jit(solution)/shard_map/pack/pallas_call | solution.py:724
  2.1 0.0 copy-start.1
  2.1 0.0 copy-start.2
  2.2 0.1 collective-permute-start
  2.3 4.8 %collective-permute-start.3 = (f32[9,8,256]{2,1,0:T(8,128)S(1)}, f32[9,8,256]{2,1,0:T(8,128)S(1)}, u32[]{:S(2)}, u32[]{:S(2)}) collective-permute-start(f32[9,8,256]{2,1,0:T(8,128)S(1)} %get-tuple-element.46.refs_0_.refs_4_), channel_id=1, source_target_pairs={{0,6},{1,7},{2,0},{3,1},{4,2},{5,3},{6,4},{7,5},{8,14},{9,15},{10,... | collective-permute-start | bytes 221192 | tf_op jit(solution)/shard_map/ppermute | solution.py:928
  7.0 0.5 collective-permute-start.1
  7.5 1.9 %tables.1 = (f32[8,32]{1,0:T(8,128)S(1)}, f32[8,16]{1,0:T(8,128)S(1)}, bf16[512,48]{1,0:T(8,128)(2,1)S(1)}, f32[32,512]{1,0:T(8,128)S(1)}, bf16[128,32]{1,0:T(8,...) custom-call(s32[1]{0:T(128)} %bitcast.tile_ref, ...), custom_call_target="tpu_custom_call" | custom-call | tf_op jit(solution)/shard_map/tables/pallas_call | solution.py:915
  9.4 0.0 collective-permute-done.3.refs_3_.refs_7_
  9.4 5.3 %collective-permute-done.2.refs_2_.refs_6_ = f32[9,8,256]{2,1,0:T(8,128)S(1)} collective-permute-done((f32[9,8,256]{2,1,0:T(8,128)S(1)}, f32[9,8,256]{2,1,0:T(8,128)S(1)}, u32[]{:S(2)}, u32[]{:S(2)}) %collective-permute-start.2) | collective-permute-done | bytes 73760 | tf_op jit(solution)/shard_map/ppermute | solution.py:928
  14.7 6.5 %sample_sums.2 = (f32[9,8,256]{2,1,0:T(8,128)S(1)}, f32[9,8,256]{2,1,0:T(8,128)S(1)}, f32[9,8,256]{2,1,0:T(8,128)S(1)}, f32[9,8,256]{2,1,0:T(8,128)S(1)}) custom-call(s32[1]{0:T(128)} %bitcast.tile_ref, bf16[64,8,2048]{2,1,0:T(8,128)(2,1)S(1)} %copy-done, bf16[64,8,1024]{2,1,0:T(8,128)(2,1)S(1)} %collective-permute-done.got_ref, f32[1,32]{1,0:T(1,128)S(1)} %bitcast.3, ...), custom_call_target="tpu_custom_call" | custom-call | tf_op jit(solution)/shard_map/sample_sums/pallas_call | solution.py:665
  21.2 0.2 collective-permute-start.4
  21.4 0.7 collective-permute-start.5
  22.1 1.4 %collective-permute-start.6 = (f32[9,8,256]{2,1,0:T(8,128)S(1)}, f32[9,8,256]{2,1,0:T(8,128)S(1)}, u32[]{:S(2)}, u32[]{:S(2)}) collective-permute-start(f32[9,8,256]{2,1,0:T(8,128)S(1)} %get-tuple-element.50), channel_id=1, source_target_pairs={{0,2},{1,3},{2,4},{3,5},{4,6},{5,7},{6,0},{7,1},{8,10},{9,11},{10,... | collective-permute-start | bytes 221192 | tf_op jit(solution)/shard_map/ppermute | solution.py:928
  23.5 5.2 %normal_factor.2.low_ref = f32[44,8,256]{2,1,0:T(8,128)S(1)} custom-call(f32[8,8,256]{2,1,0:T(8,128)S(1)} %copy-done.1, s32[8,256]{1,0:T(8,128)S(1)} %copy-done.2, f32[1,32]{1,0:T(1,128)S(1)} %bitcast.4, f32[8,32]{1,0:T(8,128)S(1)} %get-tuple-element.36.near_ref, f32[8,16]{1,0:T(8,128)S(1)} %get-tuple-element.37.cams_ref, ...), custom_call_target="tpu_custom_call" | custom-call | tf_op jit(solution)/shard_map/normal_factor/pallas_call | solution.py:629
  28.7 0.0 collective-permute-done.5.refs_2_
  28.8 0.2 collective-permute-done.6.refs_3_
  28.9 0.1 solve.2
  29.0 1.2 %collective-permute-start.7 = (f32[8,256]{1,0:T(8,128)S(1)}, f32[8,256]{1,0:T(8,128)S(1)}, u32[]{:S(2)}, u32[]{:S(2)}) collective-permute-start(f32[8,256]{1,0:T(8,128)S(1)} %get-tuple-element.52.sent_ref), channel_id=1, source_target_pairs={{0,8},{8,0},{16,24},{24,16},{1,9},{9,1},{17,25},{25,17},{2,10},{10... | collective-permute-start | bytes 24584 | tf_op jit(solution)/shard_map/ppermute | solution.py:762
  30.3 1.3 %collective-permute-done.7.first_ref = f32[8,256]{1,0:T(8,128)S(1)} collective-permute-done((f32[8,256]{1,0:T(8,128)S(1)}, f32[8,256]{1,0:T(8,128)S(1)}, u32[]{:S(2)}, u32[]{:S(2)}) %collective-permute-start.7) | collective-permute-done | bytes 8224 | tf_op jit(solution)/shard_map/ppermute | solution.py:762
  31.6 1.2 %collective-permute-start.8 = (f32[8,256]{1,0:T(8,128)S(1)}, f32[8,256]{1,0:T(8,128)S(1)}, u32[]{:S(2)}, u32[]{:S(2)}) collective-permute-start(f32[8,256]{1,0:T(8,128)S(1)} %relay.2.refs_0_), channel_id=1, source_target_pairs={{0,16},{8,24},{16,0},{24,8},{1,17},{9,25},{17,1},{25,9},{2,18},{10... | collective-permute-start | bytes 24584 | tf_op jit(solution)/shard_map/ppermute | solution.py:765
  32.8 1.3 %collective-permute-done.8.edge_ref.refs_1_ = f32[8,256]{1,0:T(8,128)S(1)} collective-permute-done((f32[8,256]{1,0:T(8,128)S(1)}, f32[8,256]{1,0:T(8,128)S(1)}, u32[]{:S(2)}, u32[]{:S(2)}) %collective-permute-start.8) | collective-permute-done | bytes 8224 | tf_op jit(solution)/shard_map/ppermute | solution.py:765
  34.1 0.1 rows.2
  34.2 4.6 %collective-permute-start.9 = (f32[24,128]{1,0:T(8,128)S(1)}, f32[24,128]{1,0:T(8,128)S(1)}, u32[]{:S(2)}, u32[]{:S(2)}) collective-permute-start(f32[24,128]{1,0:T(8,128)S(1)} %get-tuple-element.54.sent_ref), channel_id=1, source_target_pairs={{0,1},{1,0},{2,3},{3,2},{4,5},{5,4},{6,7},{7,6},{8,9},{9,8},{10,11... | collective-permute-start | bytes 36872 | tf_op jit(solution)/shard_map/ppermute | solution.py:783
  38.8 0.8 %collective-permute-done.9.near_ref = f32[24,128]{1,0:T(8,128)S(1)} collective-permute-done((f32[24,128]{1,0:T(8,128)S(1)}, f32[24,128]{1,0:T(8,128)S(1)}, u32[]{:S(2)}, u32[]{:S(2)}) %collective-permute-start.9) | collective-permute-done | bytes 12320 | tf_op jit(solution)/shard_map/ppermute | solution.py:783
  39.7 0.1 smooth.2
  39.8 1.2 %collective-permute-start.12 = (f32[9,8,256]{2,1,0:T(8,128)S(1)}, f32[9,8,256]{2,1,0:T(8,128)S(1)}, u32[]{:S(2)}, u32[]{:S(2)}) collective-permute-start(f32[9,8,256]{2,1,0:T(8,128)S(1)} %get-tuple-element.56.refs_0_), channel_id=1, source_target_pairs={{0,6},{1,7},{2,0},{3,1},{4,2},{5,3},{6,4},{7,5},{8,14},{9,15},{10,... | collective-permute-start | bytes 221192 | tf_op jit(solution)/shard_map/ppermute | solution.py:928
  41.0 0.8 %collective-permute-start.11 = (f32[9,8,256]{2,1,0:T(8,128)S(1)}, f32[9,8,256]{2,1,0:T(8,128)S(1)}, u32[]{:S(2)}, u32[]{:S(2)}) collective-permute-start(f32[9,8,256]{2,1,0:T(8,128)S(1)} %get-tuple-element.56.refs_0_), channel_id=1, source_target_pairs={{0,4},{1,5},{2,6},{3,7},{4,0},{5,1},{6,2},{7,3},{8,12},{9,13},{10,... | collective-permute-start | bytes 221192 | tf_op jit(solution)/shard_map/ppermute | solution.py:928
  41.8 1.2 %collective-permute-done.12.refs_3_ = f32[9,8,256]{2,1,0:T(8,128)S(1)} collective-permute-done((f32[9,8,256]{2,1,0:T(8,128)S(1)}, f32[9,8,256]{2,1,0:T(8,128)S(1)}, u32[]{:S(2)}, u32[]{:S(2)}) %collective-permute-start.12) | collective-permute-done | bytes 73760 | tf_op jit(solution)/shard_map/ppermute | solution.py:928
  43.0 6.2 %collective-permute-done.11.refs_2_ = f32[9,8,256]{2,1,0:T(8,128)S(1)} collective-permute-done((f32[9,8,256]{2,1,0:T(8,128)S(1)}, f32[9,8,256]{2,1,0:T(8,128)S(1)}, u32[]{:S(2)}, u32[]{:S(2)}) %collective-permute-start.11) | collective-permute-done | bytes 73760 | tf_op jit(solution)/shard_map/ppermute | solution.py:928
  49.2 0.0 collective-permute-done.10.refs_1_
  49.2 6.7 %sample_sums.3 = (f32[9,8,256]{2,1,0:T(8,128)S(1)}, f32[9,8,256]{2,1,0:T(8,128)S(1)}, f32[9,8,256]{2,1,0:T(8,128)S(1)}, f32[9,8,256]{2,1,0:T(8,128)S(1)}, f32[8,8,256]{2,1,0:T(8,128)S(1)}) custom-call(s32[1]{0:T(128)} %bitcast.tile_ref, bf16[64,8,2048]{2,1,0:T(8,128)(2,1)S(1)} %copy-done, bf16[64,8,1024]{2,1,0:T(8,128)(2,1)S(1)} %collective-permute-done.got_ref, ...), custom_call_target="tpu_custom_call" | custom-call | tf_op jit(solution)/shard_map/sample_sums/pallas_call | solution.py:665
  55.9 0.2 collective-permute-start.13
  56.1 0.8 %collective-permute-start.14 = (f32[9,8,256]{2,1,0:T(8,128)S(1)}, f32[9,8,256]{2,1,0:T(8,128)S(1)}, u32[]{:S(2)}, u32[]{:S(2)}) collective-permute-start(f32[9,8,256]{2,1,0:T(8,128)S(1)} %get-tuple-element.60), channel_id=1, source_target_pairs={{0,4},{1,5},{2,6},{3,7},{4,0},{5,1},{6,2},{7,3},{8,12},{9,13},{10,... | collective-permute-start | bytes 221192 | tf_op jit(solution)/shard_map/ppermute | solution.py:928
  56.9 1.4 %collective-permute-start.15 = (f32[9,8,256]{2,1,0:T(8,128)S(1)}, f32[9,8,256]{2,1,0:T(8,128)S(1)}, u32[]{:S(2)}, u32[]{:S(2)}) collective-permute-start(f32[9,8,256]{2,1,0:T(8,128)S(1)} %get-tuple-element.61), channel_id=1, source_target_pairs={{0,2},{1,3},{2,4},{3,5},{4,6},{5,7},{6,0},{7,1},{8,10},{9,11},{10,... | collective-permute-start | bytes 221192 | tf_op jit(solution)/shard_map/ppermute | solution.py:928
  58.3 5.2 %normal_factor.3.low_ref = f32[44,8,256]{2,1,0:T(8,128)S(1)} custom-call(f32[8,8,256]{2,1,0:T(8,128)S(1)} %get-tuple-element.57.par_ref, s32[8,256]{1,0:T(8,128)S(1)} %copy-done.2, f32[1,32]{1,0:T(1,128)S(1)} %get-tuple-element.55.gain_ref, f32[8,32]{1,0:T(8,128)S(1)} %get-tuple-element.36.near_ref, f32[8,16]{1,0:T(8,128)S(1)} %get-tuple-element.37.cams_ref, ...), custom_call_target="tpu_custom_call" | custom-call | tf_op jit(solution)/shard_map/normal_factor/pallas_call | solution.py:629
  63.5 0.0 collective-permute-done.13.refs_1_
  63.5 0.3 collective-permute-done.15.refs_3_
  63.8 0.1 solve.3
  63.9 1.2 %collective-permute-start.16 = (f32[8,256]{1,0:T(8,128)S(1)}, f32[8,256]{1,0:T(8,128)S(1)}, u32[]{:S(2)}, u32[]{:S(2)}) collective-permute-start(f32[8,256]{1,0:T(8,128)S(1)} %get-tuple-element.63.sent_ref), channel_id=1, source_target_pairs={{0,8},{8,0},{16,24},{24,16},{1,9},{9,1},{17,25},{25,17},{2,10},{10... | collective-permute-start | bytes 24584 | tf_op jit(solution)/shard_map/ppermute | solution.py:762
  65.2 1.3 %collective-permute-done.16.first_ref = f32[8,256]{1,0:T(8,128)S(1)} collective-permute-done((f32[8,256]{1,0:T(8,128)S(1)}, f32[8,256]{1,0:T(8,128)S(1)}, u32[]{:S(2)}, u32[]{:S(2)}) %collective-permute-start.16) | collective-permute-done | bytes 8224 | tf_op jit(solution)/shard_map/ppermute | solution.py:762
  66.5 1.2 %collective-permute-start.17 = (f32[8,256]{1,0:T(8,128)S(1)}, f32[8,256]{1,0:T(8,128)S(1)}, u32[]{:S(2)}, u32[]{:S(2)}) collective-permute-start(f32[8,256]{1,0:T(8,128)S(1)} %relay.3.refs_0_), channel_id=1, source_target_pairs={{0,16},{8,24},{16,0},{24,8},{1,17},{9,25},{17,1},{25,9},{2,18},{10... | collective-permute-start | bytes 24584 | tf_op jit(solution)/shard_map/ppermute | solution.py:765
  67.7 1.3 %collective-permute-done.17.edge_ref.refs_1_ = f32[8,256]{1,0:T(8,128)S(1)} collective-permute-done((f32[8,256]{1,0:T(8,128)S(1)}, f32[8,256]{1,0:T(8,128)S(1)}, u32[]{:S(2)}, u32[]{:S(2)}) %collective-permute-start.17) | collective-permute-done | bytes 8224 | tf_op jit(solution)/shard_map/ppermute | solution.py:765
  69.0 0.1 rows.3
  69.2 6.4 %collective-permute-start.19 = (f32[24,128]{1,0:T(8,128)S(1)}, f32[24,128]{1,0:T(8,128)S(1)}, u32[]{:S(2)}, u32[]{:S(2)}) collective-permute-start(f32[24,128]{1,0:T(8,128)S(1)} %get-tuple-element.65.sent_ref), channel_id=1, source_target_pairs={{1,2},{2,1},{3,4},{4,3},{5,6},{6,5},{9,10},{10,9},{11,12},{12,11},... | collective-permute-start | bytes 36872 | tf_op jit(solution)/shard_map/ppermute | solution.py:782
  75.6 0.1 collective-permute-start.18
  75.7 1.3 %collective-permute-done.19.refs_0_ = f32[24,128]{1,0:T(8,128)S(1)} collective-permute-done((f32[24,128]{1,0:T(8,128)S(1)}, f32[24,128]{1,0:T(8,128)S(1)}, u32[]{:S(2)}, u32[]{:S(2)}) %collective-permute-start.19) | collective-permute-done | bytes 12320 | tf_op jit(solution)/shard_map/ppermute | solution.py:782
  76.9 0.0 collective-permute-done.18.near_ref
  76.9 0.7 smooth.3
  (18 shorter events, 0.0 us)
Async XLA Ops:
  0.6 14.1 %copy-start = (bf16[64,8,2048]{2,1,0:T(8,128)(2,1)S(1)}, bf16[64,8,2048]{2,1,0:T(8,128)(2,1)}, u32[]{:S(2)}) copy-start(bf16[64,8,2048]{2,1,0:T(8,128)(2,1)} %own_ref.3) | copy-start | bytes 6291460
  0.6 6.9 %copy-start.5 = (f32[3,16]{1,0:T(4,128)S(1)}, f32[3,16]{1,0:T(4,128)}, u32[]{:S(2)}) copy-start(f32[3,16]{1,0:T(4,128)} %view_ref.1) | copy-start | bytes 580
  0.7 6.9 %copy-start.4 = (f32[3,32]{1,0:T(4,128)S(1)}, f32[3,32]{1,0:T(4,128)}, u32[]{:S(2)}) copy-start(f32[3,32]{1,0:T(4,128)} %light_ref.1) | copy-start | bytes 1156
  0.7 14.1 %copy-start.3 = (f32[32]{0:T(128)S(1)}, f32[32]{0:T(128)}, u32[]{:S(2)}) copy-start(f32[32]{0:T(128)} %param.11) | copy-start | bytes 388
  2.1 21.4 %copy-start.1 = (f32[8,8,256]{2,1,0:T(8,128)S(1)}, f32[8,8,256]{2,1,0:T(8,128)}, u32[]{:S(2)}) copy-start(f32[8,8,256]{2,1,0:T(8,128)} %par_ref.5) | copy-start | bytes 196612
  2.1 21.4 %copy-start.2 = (s32[8,256]{1,0:T(8,128)S(1)}, s32[8,256]{1,0:T(8,128)}, u32[]{:S(2)}) copy-start(s32[8,256]{1,0:T(8,128)} %vis_ref.5) | copy-start | bytes 24580
  2.2 12.6 %collective-permute-start = (bf16[64,8,1024]{2,1,0:T(8,128)(2,1)S(1)}, bf16[64,8,1024]{2,1,0:T(8,128)(2,1)S(1)}, u32[]{:S(2)}, u32[]{:S(2)}) collective-permute-start(bf16[64,8,1024]{2,1,0:T(8,128)(2,1)S(1)} %get-tuple-element.35), channel_id=1, source_target_pairs={{0,1},{1,0},{2,3},{3,2},{4,5},{5,4},{6,7},{7,6},{8,9},{9,8},{10,11... | collective-permute-start | bytes 3145736 | tf_op jit(solution)/shard_map/ppermute | solution.py:940
  2.3 7.1 %collective-permute-start.3 = (f32[9,8,256]{2,1,0:T(8,128)S(1)}, f32[9,8,256]{2,1,0:T(8,128)S(1)}, u32[]{:S(2)}, u32[]{:S(2)}) collective-permute-start(f32[9,8,256]{2,1,0:T(8,128)S(1)} %get-tuple-element.46.refs_0_.refs_4_), channel_id=1, source_target_pairs={{0,6},{1,7},{2,0},{3,1},{4,2},{5,3},{6,4},{7,5},{8,14},{9,15},{10,... | collective-permute-start | bytes 221192 | tf_op jit(solution)/shard_map/ppermute | solution.py:928
  7.0 7.7 %collective-permute-start.2 = (f32[9,8,256]{2,1,0:T(8,128)S(1)}, f32[9,8,256]{2,1,0:T(8,128)S(1)}, u32[]{:S(2)}, u32[]{:S(2)}) collective-permute-start(f32[9,8,256]{2,1,0:T(8,128)S(1)} %get-tuple-element.46.refs_0_.refs_4_), channel_id=1, source_target_pairs={{0,4},{1,5},{2,6},{3,7},{4,0},{5,1},{6,2},{7,3},{8,12},{9,13},{10,... | collective-permute-start | bytes 221192 | tf_op jit(solution)/shard_map/ppermute | solution.py:928
  7.0 7.7 %collective-permute-start.1 = (f32[9,8,256]{2,1,0:T(8,128)S(1)}, f32[9,8,256]{2,1,0:T(8,128)S(1)}, u32[]{:S(2)}, u32[]{:S(2)}) collective-permute-start(f32[9,8,256]{2,1,0:T(8,128)S(1)} %get-tuple-element.46.refs_0_.refs_4_), channel_id=1, source_target_pairs={{0,2},{1,3},{2,4},{3,5},{4,6},{5,7},{6,0},{7,1},{8,10},{9,11},{10,... | collective-permute-start | bytes 221192 | tf_op jit(solution)/shard_map/ppermute | solution.py:928
  21.2 7.5 %collective-permute-start.4 = (f32[9,8,256]{2,1,0:T(8,128)S(1)}, f32[9,8,256]{2,1,0:T(8,128)S(1)}, u32[]{:S(2)}, u32[]{:S(2)}) collective-permute-start(f32[9,8,256]{2,1,0:T(8,128)S(1)} %get-tuple-element.48), channel_id=1, source_target_pairs={{0,6},{1,7},{2,0},{3,1},{4,2},{5,3},{6,4},{7,5},{8,14},{9,15},{10,... | collective-permute-start | bytes 221192 | tf_op jit(solution)/shard_map/ppermute | solution.py:928
  21.4 7.3 %collective-permute-start.5 = (f32[9,8,256]{2,1,0:T(8,128)S(1)}, f32[9,8,256]{2,1,0:T(8,128)S(1)}, u32[]{:S(2)}, u32[]{:S(2)}) collective-permute-start(f32[9,8,256]{2,1,0:T(8,128)S(1)} %get-tuple-element.49), channel_id=1, source_target_pairs={{0,4},{1,5},{2,6},{3,7},{4,0},{5,1},{6,2},{7,3},{8,12},{9,13},{10,... | collective-permute-start | bytes 221192 | tf_op jit(solution)/shard_map/ppermute | solution.py:928
  22.1 6.8 %collective-permute-start.6 = (f32[9,8,256]{2,1,0:T(8,128)S(1)}, f32[9,8,256]{2,1,0:T(8,128)S(1)}, u32[]{:S(2)}, u32[]{:S(2)}) collective-permute-start(f32[9,8,256]{2,1,0:T(8,128)S(1)} %get-tuple-element.50), channel_id=1, source_target_pairs={{0,2},{1,3},{2,4},{3,5},{4,6},{5,7},{6,0},{7,1},{8,10},{9,11},{10,... | collective-permute-start | bytes 221192 | tf_op jit(solution)/shard_map/ppermute | solution.py:928
  29.0 2.6 %collective-permute-start.7 = (f32[8,256]{1,0:T(8,128)S(1)}, f32[8,256]{1,0:T(8,128)S(1)}, u32[]{:S(2)}, u32[]{:S(2)}) collective-permute-start(f32[8,256]{1,0:T(8,128)S(1)} %get-tuple-element.52.sent_ref), channel_id=1, source_target_pairs={{0,8},{8,0},{16,24},{24,16},{1,9},{9,1},{17,25},{25,17},{2,10},{10... | collective-permute-start | bytes 24584 | tf_op jit(solution)/shard_map/ppermute | solution.py:762
  31.6 2.5 %collective-permute-start.8 = (f32[8,256]{1,0:T(8,128)S(1)}, f32[8,256]{1,0:T(8,128)S(1)}, u32[]{:S(2)}, u32[]{:S(2)}) collective-permute-start(f32[8,256]{1,0:T(8,128)S(1)} %relay.2.refs_0_), channel_id=1, source_target_pairs={{0,16},{8,24},{16,0},{24,8},{1,17},{9,25},{17,1},{25,9},{2,18},{10... | collective-permute-start | bytes 24584 | tf_op jit(solution)/shard_map/ppermute | solution.py:765
  34.2 5.4 %collective-permute-start.9 = (f32[24,128]{1,0:T(8,128)S(1)}, f32[24,128]{1,0:T(8,128)S(1)}, u32[]{:S(2)}, u32[]{:S(2)}) collective-permute-start(f32[24,128]{1,0:T(8,128)S(1)} %get-tuple-element.54.sent_ref), channel_id=1, source_target_pairs={{0,1},{1,0},{2,3},{3,2},{4,5},{5,4},{6,7},{7,6},{8,9},{9,8},{10,11... | collective-permute-start | bytes 36872 | tf_op jit(solution)/shard_map/ppermute | solution.py:783
  39.8 3.2 %collective-permute-start.12 = (f32[9,8,256]{2,1,0:T(8,128)S(1)}, f32[9,8,256]{2,1,0:T(8,128)S(1)}, u32[]{:S(2)}, u32[]{:S(2)}) collective-permute-start(f32[9,8,256]{2,1,0:T(8,128)S(1)} %get-tuple-element.56.refs_0_), channel_id=1, source_target_pairs={{0,6},{1,7},{2,0},{3,1},{4,2},{5,3},{6,4},{7,5},{8,14},{9,15},{10,... | collective-permute-start | bytes 221192 | tf_op jit(solution)/shard_map/ppermute | solution.py:928
  41.0 8.2 %collective-permute-start.11 = (f32[9,8,256]{2,1,0:T(8,128)S(1)}, f32[9,8,256]{2,1,0:T(8,128)S(1)}, u32[]{:S(2)}, u32[]{:S(2)}) collective-permute-start(f32[9,8,256]{2,1,0:T(8,128)S(1)} %get-tuple-element.56.refs_0_), channel_id=1, source_target_pairs={{0,4},{1,5},{2,6},{3,7},{4,0},{5,1},{6,2},{7,3},{8,12},{9,13},{10,... | collective-permute-start | bytes 221192 | tf_op jit(solution)/shard_map/ppermute | solution.py:928
  41.8 7.4 %collective-permute-start.10 = (f32[9,8,256]{2,1,0:T(8,128)S(1)}, f32[9,8,256]{2,1,0:T(8,128)S(1)}, u32[]{:S(2)}, u32[]{:S(2)}) collective-permute-start(f32[9,8,256]{2,1,0:T(8,128)S(1)} %get-tuple-element.56.refs_0_), channel_id=1, source_target_pairs={{0,2},{1,3},{2,4},{3,5},{4,6},{5,7},{6,0},{7,1},{8,10},{9,11},{10,... | collective-permute-start | bytes 221192 | tf_op jit(solution)/shard_map/ppermute | solution.py:928
  55.9 7.6 %collective-permute-start.13 = (f32[9,8,256]{2,1,0:T(8,128)S(1)}, f32[9,8,256]{2,1,0:T(8,128)S(1)}, u32[]{:S(2)}, u32[]{:S(2)}) collective-permute-start(f32[9,8,256]{2,1,0:T(8,128)S(1)} %get-tuple-element.59), channel_id=1, source_target_pairs={{0,6},{1,7},{2,0},{3,1},{4,2},{5,3},{6,4},{7,5},{8,14},{9,15},{10,... | collective-permute-start | bytes 221192 | tf_op jit(solution)/shard_map/ppermute | solution.py:928
  56.1 7.4 %collective-permute-start.14 = (f32[9,8,256]{2,1,0:T(8,128)S(1)}, f32[9,8,256]{2,1,0:T(8,128)S(1)}, u32[]{:S(2)}, u32[]{:S(2)}) collective-permute-start(f32[9,8,256]{2,1,0:T(8,128)S(1)} %get-tuple-element.60), channel_id=1, source_target_pairs={{0,4},{1,5},{2,6},{3,7},{4,0},{5,1},{6,2},{7,3},{8,12},{9,13},{10,... | collective-permute-start | bytes 221192 | tf_op jit(solution)/shard_map/ppermute | solution.py:928
  56.9 6.9 %collective-permute-start.15 = (f32[9,8,256]{2,1,0:T(8,128)S(1)}, f32[9,8,256]{2,1,0:T(8,128)S(1)}, u32[]{:S(2)}, u32[]{:S(2)}) collective-permute-start(f32[9,8,256]{2,1,0:T(8,128)S(1)} %get-tuple-element.61), channel_id=1, source_target_pairs={{0,2},{1,3},{2,4},{3,5},{4,6},{5,7},{6,0},{7,1},{8,10},{9,11},{10,... | collective-permute-start | bytes 221192 | tf_op jit(solution)/shard_map/ppermute | solution.py:928
  63.9 2.6 %collective-permute-start.16 = (f32[8,256]{1,0:T(8,128)S(1)}, f32[8,256]{1,0:T(8,128)S(1)}, u32[]{:S(2)}, u32[]{:S(2)}) collective-permute-start(f32[8,256]{1,0:T(8,128)S(1)} %get-tuple-element.63.sent_ref), channel_id=1, source_target_pairs={{0,8},{8,0},{16,24},{24,16},{1,9},{9,1},{17,25},{25,17},{2,10},{10... | collective-permute-start | bytes 24584 | tf_op jit(solution)/shard_map/ppermute | solution.py:762
  66.5 2.5 %collective-permute-start.17 = (f32[8,256]{1,0:T(8,128)S(1)}, f32[8,256]{1,0:T(8,128)S(1)}, u32[]{:S(2)}, u32[]{:S(2)}) collective-permute-start(f32[8,256]{1,0:T(8,128)S(1)} %relay.3.refs_0_), channel_id=1, source_target_pairs={{0,16},{8,24},{16,0},{24,8},{1,17},{9,25},{17,1},{25,9},{2,18},{10... | collective-permute-start | bytes 24584 | tf_op jit(solution)/shard_map/ppermute | solution.py:765
  69.2 7.8 %collective-permute-start.19 = (f32[24,128]{1,0:T(8,128)S(1)}, f32[24,128]{1,0:T(8,128)S(1)}, u32[]{:S(2)}, u32[]{:S(2)}) collective-permute-start(f32[24,128]{1,0:T(8,128)S(1)} %get-tuple-element.65.sent_ref), channel_id=1, source_target_pairs={{1,2},{2,1},{3,4},{4,3},{5,6},{6,5},{9,10},{10,9},{11,12},{12,11},... | collective-permute-start | bytes 36872 | tf_op jit(solution)/shard_map/ppermute | solution.py:782
  75.6 1.4 %collective-permute-start.18 = (f32[24,128]{1,0:T(8,128)S(1)}, f32[24,128]{1,0:T(8,128)S(1)}, u32[]{:S(2)}, u32[]{:S(2)}) collective-permute-start(f32[24,128]{1,0:T(8,128)S(1)} %get-tuple-element.65.sent_ref), channel_id=1, source_target_pairs={{0,1},{1,0},{2,3},{3,2},{4,5},{5,4},{6,7},{7,6},{8,9},{9,8},{10,11... | collective-permute-start | bytes 36872 | tf_op jit(solution)/shard_map/ppermute | solution.py:783

commit v8 on v7

--- a/solution.py
+++ b/solution.py
@@ -342,7 +342,7 @@
 def sample_kernel(
     tile_ref, own_ref, got_ref, gain_ref, lobe_ref, shade_ref, plain_ref, tall_ref, slab_ref, *refs, parts, mend
 ):
-    par_refs, vis_refs = refs[:parts], refs[parts : 2 * parts]
+    par_refs, vis_refs = by_shift(refs[:parts]), by_shift(refs[parts : 2 * parts])
     out_refs = refs[2 * parts : 3 * parts]
     extra = 1 if mend else 0
     own_out_refs = refs[3 * parts : 3 * parts + extra]
@@ -690,7 +690,7 @@
             ],
         ),
         compiler_params=params_of(),
-    )(tile, own, got, *small, *pars, *vises)
+    )(tile, own, got, *small, *in_order(pars), *in_order(vises))
 
 
 def pack_kernel(tile_ref, seen_ref, par_ref, vis_ref, send_ref, first_ref, vis_scr, sems):
@@ -924,6 +924,19 @@
     return dict(zip(TABLES, outs))
 
 
+def passing_order(parts):
+    return ([1] + list(range(parts - 1, 1, -1)) if parts > 1 else []) + [0]
+
+
+def in_order(items):
+    return [items[i] for i in passing_order(len(items))]
+
+
+def by_shift(items):
+    order = passing_order(len(items))
+    return [items[order.index(i)] for i in range(len(items))]
+
+
 def shifted(x, by, nz):
     return lax.ppermute(x, "tile", [(2 * z + c, 2 * ((z + by) % nz) + c) for z in range(nz) for c in range(2)])
 

time: 77.8 us -> 77.1 us (level)
  waiting for transfers between devices: 20.5 us -> 15 us
  starting transfers between devices: 28.1 us -> 32.9 us
    ppermute x12, waiting for transfers between devices: 13.1 us -> 7.7 us  [shifted(): lax.ppermute(x, 'tile', [(2 * z + c, 2 * ((z + by) % nz) + c) for z in ra...]
    ppermute x12, starting transfers between devices: 11.9 us -> 17.1 us  [shifted(): lax.ppermute(x, 'tile', [(2 * z + c, 2 * ((z + by) % nz) + c) for z in ra...]
    ppermute x2, starting transfers between devices: 4.68 us -> 3.82 us  [settle(): near = lax.ppermute(sent, 'tile', pairs(tiles, 0))]
  transfers between devices with their start and end apart: 20 -> 20, of which waited for: 11 -> 10; matrix products, arithmetic and copies ran while one was open for 0% -> 0% of each run, Pallas kernels for 16% -> 16%
where the time goes in v8:
time: 77.1 us; the launch traced here: 77 us
  starting transfers between devices  32.9 us (43%)
  Pallas kernels  28.2 us (37%)
  waiting for transfers between devices  15 us (19%)
  between operations  0.81 us (1%)
    ppermute x12, starting transfers between devices, shifted(): lax.ppermute(x, 'tile', [(2 * z + c, 2 * ((z + by) % nz) + c) for z in ra...  17.1 us
    pallas_call x2, Pallas kernels, sample_call(): pl.pallas_call(functools.partial(sample_kernel, parts=parts, mend=mend),...  13.2 us
    pallas_call x2, Pallas kernels, normal_call(): pl.pallas_call(normal_kernel, name='normal_factor', out_shape=jax.ShapeDt...  10.4 us
    ppermute x12, waiting for transfers between devices, shifted(): lax.ppermute(x, 'tile', [(2 * z + c, 2 * ((z + by) % nz) + c) for z in ra...  7.7 us
    ppermute x1, starting transfers between devices, settle(): ends = [lax.ppermute(sent, 'tile', pairs(tiles, 1))] if closed else []  6.78 us
    ppermute x2, starting transfers between devices, settle(): near = lax.ppermute(sent, 'tile', pairs(tiles, 0))  3.82 us
    ppermute x2, waiting for transfers between devices, settle(): edge = lax.ppermute(relay, 'grp', [(i, i ^ 2) for i in range(grps)])  2.61 us
    ppermute x2, waiting for transfers between devices, settle(): first = lax.ppermute(sent, 'grp', pairs(grps, 0))  2.58 us
  transfers between devices with their start and end apart: 20, of which 10 were waited for; matrix products, arithmetic and copies ran while one was open for 0% of the time, Pallas kernels for 16%

profile of v8, /device:TPU:1, one launch (start us, length us, event | category | flops | bytes accessed | tf_op | source)
XLA Modules:
  0.0 77.0 jit_solution(2160041360584008486)
XLA Ops:
  0.7 1.4 %pack.1 = (bf16[64,8,1024]{2,1,0:T(8,128)(2,1)S(1)}, f32[9,8,256]{2,1,0:T(8,128)S(1)}) custom-call(s32[1]{0:T(128)} %bitcast.tile_ref, bf16[64,8,2048]{2,1,0:T(8,128)(2,1)} %own_ref.3, f32[8,8,256]{2,1,0:T(8,128)} %par_ref.5, s32[8,256]{1,0:T(8,128)} %vis_ref.5), custom_call_target="tpu_custom_call" | custom-call | tf_op jit(solution)/shard_map/pack/pallas_call | solution.py:724
  2.1 0.0 copy-start.1
  2.1 0.0 copy-start.2
  2.2 0.1 collective-permute-start
  2.3 3.8 %collective-permute-start.3 = (f32[9,8,256]{2,1,0:T(8,128)S(1)}, f32[9,8,256]{2,1,0:T(8,128)S(1)}, u32[]{:S(2)}, u32[]{:S(2)}) collective-permute-start(f32[9,8,256]{2,1,0:T(8,128)S(1)} %get-tuple-element.46.refs_3_.refs_7_), channel_id=1, source_target_pairs={{0,4},{1,5},{2,6},{3,7},{4,0},{5,1},{6,2},{7,3},{8,12},{9,13},{10,... | collective-permute-start | bytes 221192 | tf_op jit(solution)/shard_map/ppermute | solution.py:941
  6.0 1.1 %collective-permute-start.2 = (f32[9,8,256]{2,1,0:T(8,128)S(1)}, f32[9,8,256]{2,1,0:T(8,128)S(1)}, u32[]{:S(2)}, u32[]{:S(2)}) collective-permute-start(f32[9,8,256]{2,1,0:T(8,128)S(1)} %get-tuple-element.46.refs_3_.refs_7_), channel_id=1, source_target_pairs={{0,6},{1,7},{2,0},{3,1},{4,2},{5,3},{6,4},{7,5},{8,14},{9,15},{10,... | collective-permute-start | bytes 221192 | tf_op jit(solution)/shard_map/ppermute | solution.py:941
  7.1 0.4 collective-permute-start.1
  7.5 1.9 %tables.1 = (f32[8,32]{1,0:T(8,128)S(1)}, f32[8,16]{1,0:T(8,128)S(1)}, bf16[512,48]{1,0:T(8,128)(2,1)S(1)}, f32[32,512]{1,0:T(8,128)S(1)}, bf16[128,32]{1,0:T(8,...) custom-call(s32[1]{0:T(128)} %bitcast.tile_ref, ...), custom_call_target="tpu_custom_call" | custom-call | tf_op jit(solution)/shard_map/tables/pallas_call | solution.py:915
  9.4 0.5 collective-permute-done.3.refs_2_.refs_6_
  9.9 2.3 %collective-permute-done.1.refs_0_.refs_4_ = f32[9,8,256]{2,1,0:T(8,128)S(1)} collective-permute-done((f32[9,8,256]{2,1,0:T(8,128)S(1)}, f32[9,8,256]{2,1,0:T(8,128)S(1)}, u32[]{:S(2)}, u32[]{:S(2)}) %collective-permute-start.1) | collective-permute-done | bytes 73760 | tf_op jit(solution)/shard_map/ppermute | solution.py:941
  12.2 0.0 collective-permute-done.got_ref
  12.2 6.5 %sample_sums.2 = (f32[9,8,256]{2,1,0:T(8,128)S(1)}, f32[9,8,256]{2,1,0:T(8,128)S(1)}, f32[9,8,256]{2,1,0:T(8,128)S(1)}, f32[9,8,256]{2,1,0:T(8,128)S(1)}) custom-call(s32[1]{0:T(128)} %bitcast.tile_ref, bf16[64,8,2048]{2,1,0:T(8,128)(2,1)S(1)} %copy-done, bf16[64,8,1024]{2,1,0:T(8,128)(2,1)S(1)} %collective-permute-done.got_ref, f32[1,32]{1,0:T(1,128)S(1)} %bitcast.3, ...), custom_call_target="tpu_custom_call" | custom-call | tf_op jit(solution)/shard_map/sample_sums/pallas_call | solution.py:665
  18.7 3.1 %collective-permute-start.4 = (f32[9,8,256]{2,1,0:T(8,128)S(1)}, f32[9,8,256]{2,1,0:T(8,128)S(1)}, u32[]{:S(2)}, u32[]{:S(2)}) collective-permute-start(f32[9,8,256]{2,1,0:T(8,128)S(1)} %get-tuple-element.48), channel_id=1, source_target_pairs={{0,6},{1,7},{2,0},{3,1},{4,2},{5,3},{6,4},{7,5},{8,14},{9,15},{10,... | collective-permute-start | bytes 221192 | tf_op jit(solution)/shard_map/ppermute | solution.py:941
  21.9 0.8 collective-permute-start.5
  22.6 1.4 %collective-permute-start.6 = (f32[9,8,256]{2,1,0:T(8,128)S(1)}, f32[9,8,256]{2,1,0:T(8,128)S(1)}, u32[]{:S(2)}, u32[]{:S(2)}) collective-permute-start(f32[9,8,256]{2,1,0:T(8,128)S(1)} %get-tuple-element.50), channel_id=1, source_target_pairs={{0,2},{1,3},{2,4},{3,5},{4,6},{5,7},{6,0},{7,1},{8,10},{9,11},{10,... | collective-permute-start | bytes 221192 | tf_op jit(solution)/shard_map/ppermute | solution.py:941
  24.0 5.2 %normal_factor.2.low_ref = f32[44,8,256]{2,1,0:T(8,128)S(1)} custom-call(f32[8,8,256]{2,1,0:T(8,128)S(1)} %copy-done.1, s32[8,256]{1,0:T(8,128)S(1)} %copy-done.2, f32[1,32]{1,0:T(1,128)S(1)} %bitcast.4, f32[8,32]{1,0:T(8,128)S(1)} %get-tuple-element.36.near_ref, f32[8,16]{1,0:T(8,128)S(1)} %get-tuple-element.37.cams_ref, ...), custom_call_target="tpu_custom_call" | custom-call | tf_op jit(solution)/shard_map/normal_factor/pallas_call | solution.py:629
  29.2 0.0 collective-permute-done.4.refs_1_
  29.2 0.0 collective-permute-done.5.refs_2_
  29.3 0.1 solve.2
  29.4 1.3 %collective-permute-start.7 = (f32[8,256]{1,0:T(8,128)S(1)}, f32[8,256]{1,0:T(8,128)S(1)}, u32[]{:S(2)}, u32[]{:S(2)}) collective-permute-start(f32[8,256]{1,0:T(8,128)S(1)} %get-tuple-element.52.sent_ref), channel_id=1, source_target_pairs={{0,8},{8,0},{16,24},{24,16},{1,9},{9,1},{17,25},{25,17},{2,10},{10... | collective-permute-start | bytes 24584 | tf_op jit(solution)/shard_map/ppermute | solution.py:762
  30.6 1.3 %collective-permute-done.7.first_ref = f32[8,256]{1,0:T(8,128)S(1)} collective-permute-done((f32[8,256]{1,0:T(8,128)S(1)}, f32[8,256]{1,0:T(8,128)S(1)}, u32[]{:S(2)}, u32[]{:S(2)}) %collective-permute-start.7) | collective-permute-done | bytes 8224 | tf_op jit(solution)/shard_map/ppermute | solution.py:762
  31.9 1.2 %collective-permute-start.8 = (f32[8,256]{1,0:T(8,128)S(1)}, f32[8,256]{1,0:T(8,128)S(1)}, u32[]{:S(2)}, u32[]{:S(2)}) collective-permute-start(f32[8,256]{1,0:T(8,128)S(1)} %relay.2.refs_0_), channel_id=1, source_target_pairs={{0,16},{8,24},{16,0},{24,8},{1,17},{9,25},{17,1},{25,9},{2,18},{10... | collective-permute-start | bytes 24584 | tf_op jit(solution)/shard_map/ppermute | solution.py:765
  33.2 1.3 %collective-permute-done.8.edge_ref.refs_1_ = f32[8,256]{1,0:T(8,128)S(1)} collective-permute-done((f32[8,256]{1,0:T(8,128)S(1)}, f32[8,256]{1,0:T(8,128)S(1)}, u32[]{:S(2)}, u32[]{:S(2)}) %collective-permute-start.8) | collective-permute-done | bytes 8224 | tf_op jit(solution)/shard_map/ppermute | solution.py:765
  34.4 0.1 rows.2
  34.5 3.8 %collective-permute-start.9 = (f32[24,128]{1,0:T(8,128)S(1)}, f32[24,128]{1,0:T(8,128)S(1)}, u32[]{:S(2)}, u32[]{:S(2)}) collective-permute-start(f32[24,128]{1,0:T(8,128)S(1)} %get-tuple-element.54.sent_ref), channel_id=1, source_target_pairs={{0,1},{1,0},{2,3},{3,2},{4,5},{5,4},{6,7},{7,6},{8,9},{9,8},{10,11... | collective-permute-start | bytes 36872 | tf_op jit(solution)/shard_map/ppermute | solution.py:783
  38.3 0.8 %collective-permute-done.9.near_ref = f32[24,128]{1,0:T(8,128)S(1)} collective-permute-done((f32[24,128]{1,0:T(8,128)S(1)}, f32[24,128]{1,0:T(8,128)S(1)}, u32[]{:S(2)}, u32[]{:S(2)}) %collective-permute-start.9) | collective-permute-done | bytes 12320 | tf_op jit(solution)/shard_map/ppermute | solution.py:783
  39.1 0.1 smooth.2
  39.3 1.5 %collective-permute-start.12 = (f32[9,8,256]{2,1,0:T(8,128)S(1)}, f32[9,8,256]{2,1,0:T(8,128)S(1)}, u32[]{:S(2)}, u32[]{:S(2)}) collective-permute-start(f32[9,8,256]{2,1,0:T(8,128)S(1)} %get-tuple-element.56.refs_3_), channel_id=1, source_target_pairs={{0,4},{1,5},{2,6},{3,7},{4,0},{5,1},{6,2},{7,3},{8,12},{9,13},{10,... | collective-permute-start | bytes 221192 | tf_op jit(solution)/shard_map/ppermute | solution.py:941
  40.8 1.2 %collective-permute-start.11 = (f32[9,8,256]{2,1,0:T(8,128)S(1)}, f32[9,8,256]{2,1,0:T(8,128)S(1)}, u32[]{:S(2)}, u32[]{:S(2)}) collective-permute-start(f32[9,8,256]{2,1,0:T(8,128)S(1)} %get-tuple-element.56.refs_3_), channel_id=1, source_target_pairs={{0,6},{1,7},{2,0},{3,1},{4,2},{5,3},{6,4},{7,5},{8,14},{9,15},{10,... | collective-permute-start | bytes 221192 | tf_op jit(solution)/shard_map/ppermute | solution.py:941
  42.1 0.2 collective-permute-start.10
  42.3 3.2 %collective-permute-done.12.refs_2_ = f32[9,8,256]{2,1,0:T(8,128)S(1)} collective-permute-done((f32[9,8,256]{2,1,0:T(8,128)S(1)}, f32[9,8,256]{2,1,0:T(8,128)S(1)}, u32[]{:S(2)}, u32[]{:S(2)}) %collective-permute-start.12) | collective-permute-done | bytes 73760 | tf_op jit(solution)/shard_map/ppermute | solution.py:941
  45.5 0.0 collective-permute-done.11.refs_1_
  45.5 1.6 %collective-permute-done.10.refs_0_ = f32[9,8,256]{2,1,0:T(8,128)S(1)} collective-permute-done((f32[9,8,256]{2,1,0:T(8,128)S(1)}, f32[9,8,256]{2,1,0:T(8,128)S(1)}, u32[]{:S(2)}, u32[]{:S(2)}) %collective-permute-start.10) | collective-permute-done | bytes 73760 | tf_op jit(solution)/shard_map/ppermute | solution.py:941
  47.2 6.7 %sample_sums.3 = (f32[9,8,256]{2,1,0:T(8,128)S(1)}, f32[9,8,256]{2,1,0:T(8,128)S(1)}, f32[9,8,256]{2,1,0:T(8,128)S(1)}, f32[9,8,256]{2,1,0:T(8,128)S(1)}, f32[8,8,256]{2,1,0:T(8,128)S(1)}) custom-call(s32[1]{0:T(128)} %bitcast.tile_ref, bf16[64,8,2048]{2,1,0:T(8,128)(2,1)S(1)} %copy-done, bf16[64,8,1024]{2,1,0:T(8,128)(2,1)S(1)} %collective-permute-done.got_ref, ...), custom_call_target="tpu_custom_call" | custom-call | tf_op jit(solution)/shard_map/sample_sums/pallas_call | solution.py:665
  53.9 0.7 collective-permute-start.13
  54.6 1.6 %collective-permute-start.14 = (f32[9,8,256]{2,1,0:T(8,128)S(1)}, f32[9,8,256]{2,1,0:T(8,128)S(1)}, u32[]{:S(2)}, u32[]{:S(2)}) collective-permute-start(f32[9,8,256]{2,1,0:T(8,128)S(1)} %get-tuple-element.60), channel_id=1, source_target_pairs={{0,4},{1,5},{2,6},{3,7},{4,0},{5,1},{6,2},{7,3},{8,12},{9,13},{10,... | collective-permute-start | bytes 221192 | tf_op jit(solution)/shard_map/ppermute | solution.py:941
  56.2 1.3 %collective-permute-start.15 = (f32[9,8,256]{2,1,0:T(8,128)S(1)}, f32[9,8,256]{2,1,0:T(8,128)S(1)}, u32[]{:S(2)}, u32[]{:S(2)}) collective-permute-start(f32[9,8,256]{2,1,0:T(8,128)S(1)} %get-tuple-element.61), channel_id=1, source_target_pairs={{0,2},{1,3},{2,4},{3,5},{4,6},{5,7},{6,0},{7,1},{8,10},{9,11},{10,... | collective-permute-start | bytes 221192 | tf_op jit(solution)/shard_map/ppermute | solution.py:941
  57.5 5.2 %normal_factor.3.low_ref = f32[44,8,256]{2,1,0:T(8,128)S(1)} custom-call(f32[8,8,256]{2,1,0:T(8,128)S(1)} %get-tuple-element.57.par_ref, s32[8,256]{1,0:T(8,128)S(1)} %copy-done.2, f32[1,32]{1,0:T(1,128)S(1)} %get-tuple-element.55.gain_ref, f32[8,32]{1,0:T(8,128)S(1)} %get-tuple-element.36.near_ref, f32[8,16]{1,0:T(8,128)S(1)} %get-tuple-element.37.cams_ref, ...), custom_call_target="tpu_custom_call" | custom-call | tf_op jit(solution)/shard_map/normal_factor/pallas_call | solution.py:629
  62.7 0.1 solve.3
  62.8 1.3 %collective-permute-start.16 = (f32[8,256]{1,0:T(8,128)S(1)}, f32[8,256]{1,0:T(8,128)S(1)}, u32[]{:S(2)}, u32[]{:S(2)}) collective-permute-start(f32[8,256]{1,0:T(8,128)S(1)} %get-tuple-element.63.sent_ref), channel_id=1, source_target_pairs={{0,8},{8,0},{16,24},{24,16},{1,9},{9,1},{17,25},{25,17},{2,10},{10... | collective-permute-start | bytes 24584 | tf_op jit(solution)/shard_map/ppermute | solution.py:762
  64.1 1.3 %collective-permute-done.16.first_ref = f32[8,256]{1,0:T(8,128)S(1)} collective-permute-done((f32[8,256]{1,0:T(8,128)S(1)}, f32[8,256]{1,0:T(8,128)S(1)}, u32[]{:S(2)}, u32[]{:S(2)}) %collective-permute-start.16) | collective-permute-done | bytes 8224 | tf_op jit(solution)/shard_map/ppermute | solution.py:762
  65.4 1.2 %collective-permute-start.17 = (f32[8,256]{1,0:T(8,128)S(1)}, f32[8,256]{1,0:T(8,128)S(1)}, u32[]{:S(2)}, u32[]{:S(2)}) collective-permute-start(f32[8,256]{1,0:T(8,128)S(1)} %relay.3.refs_0_), channel_id=1, source_target_pairs={{0,16},{8,24},{16,0},{24,8},{1,17},{9,25},{17,1},{25,9},{2,18},{10... | collective-permute-start | bytes 24584 | tf_op jit(solution)/shard_map/ppermute | solution.py:765
  66.6 1.3 %collective-permute-done.17.edge_ref.refs_1_ = f32[8,256]{1,0:T(8,128)S(1)} collective-permute-done((f32[8,256]{1,0:T(8,128)S(1)}, f32[8,256]{1,0:T(8,128)S(1)}, u32[]{:S(2)}, u32[]{:S(2)}) %collective-permute-start.17) | collective-permute-done | bytes 8224 | tf_op jit(solution)/shard_map/ppermute | solution.py:765
  68.0 0.1 rows.3
  68.1 6.8 %collective-permute-start.19 = (f32[24,128]{1,0:T(8,128)S(1)}, f32[24,128]{1,0:T(8,128)S(1)}, u32[]{:S(2)}, u32[]{:S(2)}) collective-permute-start(f32[24,128]{1,0:T(8,128)S(1)} %get-tuple-element.65.sent_ref), channel_id=1, source_target_pairs={{1,2},{2,1},{3,4},{4,3},{5,6},{6,5},{9,10},{10,9},{11,12},{12,11},... | collective-permute-start | bytes 36872 | tf_op jit(solution)/shard_map/ppermute | solution.py:782
  74.9 0.1 collective-permute-start.18
  75.0 1.3 %collective-permute-done.19.refs_0_ = f32[24,128]{1,0:T(8,128)S(1)} collective-permute-done((f32[24,128]{1,0:T(8,128)S(1)}, f32[24,128]{1,0:T(8,128)S(1)}, u32[]{:S(2)}, u32[]{:S(2)}) %collective-permute-start.19) | collective-permute-done | bytes 12320 | tf_op jit(solution)/shard_map/ppermute | solution.py:782
  76.2 0.7 smooth.3
  (18 shorter events, 0.0 us)
Async XLA Ops:
  0.6 11.6 %copy-start = (bf16[64,8,2048]{2,1,0:T(8,128)(2,1)S(1)}, bf16[64,8,2048]{2,1,0:T(8,128)(2,1)}, u32[]{:S(2)}) copy-start(bf16[64,8,2048]{2,1,0:T(8,128)(2,1)} %own_ref.3) | copy-start | bytes 6291460
  0.6 6.9 %copy-start.5 = (f32[3,16]{1,0:T(4,128)S(1)}, f32[3,16]{1,0:T(4,128)}, u32[]{:S(2)}) copy-start(f32[3,16]{1,0:T(4,128)} %view_ref.1) | copy-start | bytes 580
  0.7 6.9 %copy-start.4 = (f32[3,32]{1,0:T(4,128)S(1)}, f32[3,32]{1,0:T(4,128)}, u32[]{:S(2)}) copy-start(f32[3,32]{1,0:T(4,128)} %light_ref.1) | copy-start | bytes 1156
  0.7 11.6 %copy-start.3 = (f32[32]{0:T(128)S(1)}, f32[32]{0:T(128)}, u32[]{:S(2)}) copy-start(f32[32]{0:T(128)} %param.11) | copy-start | bytes 388
  2.1 21.9 %copy-start.1 = (f32[8,8,256]{2,1,0:T(8,128)S(1)}, f32[8,8,256]{2,1,0:T(8,128)}, u32[]{:S(2)}) copy-start(f32[8,8,256]{2,1,0:T(8,128)} %par_ref.5) | copy-start | bytes 196612
  2.1 21.9 %copy-start.2 = (s32[8,256]{1,0:T(8,128)S(1)}, s32[8,256]{1,0:T(8,128)}, u32[]{:S(2)}) copy-start(s32[8,256]{1,0:T(8,128)} %vis_ref.5) | copy-start | bytes 24580
  2.2 10.1 %collective-permute-start = (bf16[64,8,1024]{2,1,0:T(8,128)(2,1)S(1)}, bf16[64,8,1024]{2,1,0:T(8,128)(2,1)S(1)}, u32[]{:S(2)}, u32[]{:S(2)}) collective-permute-start(bf16[64,8,1024]{2,1,0:T(8,128)(2,1)S(1)} %get-tuple-element.35), channel_id=1, source_target_pairs={{0,1},{1,0},{2,3},{3,2},{4,5},{5,4},{6,7},{7,6},{8,9},{9,8},{10,11... | collective-permute-start | bytes 3145736 | tf_op jit(solution)/shard_map/ppermute | solution.py:953
  2.3 7.6 %collective-permute-start.3 = (f32[9,8,256]{2,1,0:T(8,128)S(1)}, f32[9,8,256]{2,1,0:T(8,128)S(1)}, u32[]{:S(2)}, u32[]{:S(2)}) collective-permute-start(f32[9,8,256]{2,1,0:T(8,128)S(1)} %get-tuple-element.46.refs_3_.refs_7_), channel_id=1, source_target_pairs={{0,4},{1,5},{2,6},{3,7},{4,0},{5,1},{6,2},{7,3},{8,12},{9,13},{10,... | collective-permute-start | bytes 221192 | tf_op jit(solution)/shard_map/ppermute | solution.py:941
  6.0 3.9 %collective-permute-start.2 = (f32[9,8,256]{2,1,0:T(8,128)S(1)}, f32[9,8,256]{2,1,0:T(8,128)S(1)}, u32[]{:S(2)}, u32[]{:S(2)}) collective-permute-start(f32[9,8,256]{2,1,0:T(8,128)S(1)} %get-tuple-element.46.refs_3_.refs_7_), channel_id=1, source_target_pairs={{0,6},{1,7},{2,0},{3,1},{4,2},{5,3},{6,4},{7,5},{8,14},{9,15},{10,... | collective-permute-start | bytes 221192 | tf_op jit(solution)/shard_map/ppermute | solution.py:941
  7.1 5.1 %collective-permute-start.1 = (f32[9,8,256]{2,1,0:T(8,128)S(1)}, f32[9,8,256]{2,1,0:T(8,128)S(1)}, u32[]{:S(2)}, u32[]{:S(2)}) collective-permute-start(f32[9,8,256]{2,1,0:T(8,128)S(1)} %get-tuple-element.46.refs_3_.refs_7_), channel_id=1, source_target_pairs={{0,2},{1,3},{2,4},{3,5},{4,6},{5,7},{6,0},{7,1},{8,10},{9,11},{10,... | collective-permute-start | bytes 221192 | tf_op jit(solution)/shard_map/ppermute | solution.py:941
  18.7 10.5 %collective-permute-start.4 = (f32[9,8,256]{2,1,0:T(8,128)S(1)}, f32[9,8,256]{2,1,0:T(8,128)S(1)}, u32[]{:S(2)}, u32[]{:S(2)}) collective-permute-start(f32[9,8,256]{2,1,0:T(8,128)S(1)} %get-tuple-element.48), channel_id=1, source_target_pairs={{0,6},{1,7},{2,0},{3,1},{4,2},{5,3},{6,4},{7,5},{8,14},{9,15},{10,... | collective-permute-start | bytes 221192 | tf_op jit(solution)/shard_map/ppermute | solution.py:941
  21.9 7.4 %collective-permute-start.5 = (f32[9,8,256]{2,1,0:T(8,128)S(1)}, f32[9,8,256]{2,1,0:T(8,128)S(1)}, u32[]{:S(2)}, u32[]{:S(2)}) collective-permute-start(f32[9,8,256]{2,1,0:T(8,128)S(1)} %get-tuple-element.49), channel_id=1, source_target_pairs={{0,4},{1,5},{2,6},{3,7},{4,0},{5,1},{6,2},{7,3},{8,12},{9,13},{10,... | collective-permute-start | bytes 221192 | tf_op jit(solution)/shard_map/ppermute | solution.py:941
  22.6 6.6 %collective-permute-start.6 = (f32[9,8,256]{2,1,0:T(8,128)S(1)}, f32[9,8,256]{2,1,0:T(8,128)S(1)}, u32[]{:S(2)}, u32[]{:S(2)}) collective-permute-start(f32[9,8,256]{2,1,0:T(8,128)S(1)} %get-tuple-element.50), channel_id=1, source_target_pairs={{0,2},{1,3},{2,4},{3,5},{4,6},{5,7},{6,0},{7,1},{8,10},{9,11},{10,... | collective-permute-start | bytes 221192 | tf_op jit(solution)/shard_map/ppermute | solution.py:941
  29.4 2.6 %collective-permute-start.7 = (f32[8,256]{1,0:T(8,128)S(1)}, f32[8,256]{1,0:T(8,128)S(1)}, u32[]{:S(2)}, u32[]{:S(2)}) collective-permute-start(f32[8,256]{1,0:T(8,128)S(1)} %get-tuple-element.52.sent_ref), channel_id=1, source_target_pairs={{0,8},{8,0},{16,24},{24,16},{1,9},{9,1},{17,25},{25,17},{2,10},{10... | collective-permute-start | bytes 24584 | tf_op jit(solution)/shard_map/ppermute | solution.py:762
  31.9 2.5 %collective-permute-start.8 = (f32[8,256]{1,0:T(8,128)S(1)}, f32[8,256]{1,0:T(8,128)S(1)}, u32[]{:S(2)}, u32[]{:S(2)}) collective-permute-start(f32[8,256]{1,0:T(8,128)S(1)} %relay.2.refs_0_), channel_id=1, source_target_pairs={{0,16},{8,24},{16,0},{24,8},{1,17},{9,25},{17,1},{25,9},{2,18},{10... | collective-permute-start | bytes 24584 | tf_op jit(solution)/shard_map/ppermute | solution.py:765
  34.5 4.6 %collective-permute-start.9 = (f32[24,128]{1,0:T(8,128)S(1)}, f32[24,128]{1,0:T(8,128)S(1)}, u32[]{:S(2)}, u32[]{:S(2)}) collective-permute-start(f32[24,128]{1,0:T(8,128)S(1)} %get-tuple-element.54.sent_ref), channel_id=1, source_target_pairs={{0,1},{1,0},{2,3},{3,2},{4,5},{5,4},{6,7},{7,6},{8,9},{9,8},{10,11... | collective-permute-start | bytes 36872 | tf_op jit(solution)/shard_map/ppermute | solution.py:783
  39.3 6.2 %collective-permute-start.12 = (f32[9,8,256]{2,1,0:T(8,128)S(1)}, f32[9,8,256]{2,1,0:T(8,128)S(1)}, u32[]{:S(2)}, u32[]{:S(2)}) collective-permute-start(f32[9,8,256]{2,1,0:T(8,128)S(1)} %get-tuple-element.56.refs_3_), channel_id=1, source_target_pairs={{0,4},{1,5},{2,6},{3,7},{4,0},{5,1},{6,2},{7,3},{8,12},{9,13},{10,... | collective-permute-start | bytes 221192 | tf_op jit(solution)/shard_map/ppermute | solution.py:941
  40.8 4.7 %collective-permute-start.11 = (f32[9,8,256]{2,1,0:T(8,128)S(1)}, f32[9,8,256]{2,1,0:T(8,128)S(1)}, u32[]{:S(2)}, u32[]{:S(2)}) collective-permute-start(f32[9,8,256]{2,1,0:T(8,128)S(1)} %get-tuple-element.56.refs_3_), channel_id=1, source_target_pairs={{0,6},{1,7},{2,0},{3,1},{4,2},{5,3},{6,4},{7,5},{8,14},{9,15},{10,... | collective-permute-start | bytes 221192 | tf_op jit(solution)/shard_map/ppermute | solution.py:941
  42.1 5.1 %collective-permute-start.10 = (f32[9,8,256]{2,1,0:T(8,128)S(1)}, f32[9,8,256]{2,1,0:T(8,128)S(1)}, u32[]{:S(2)}, u32[]{:S(2)}) collective-permute-start(f32[9,8,256]{2,1,0:T(8,128)S(1)} %get-tuple-element.56.refs_3_), channel_id=1, source_target_pairs={{0,2},{1,3},{2,4},{3,5},{4,6},{5,7},{6,0},{7,1},{8,10},{9,11},{10,... | collective-permute-start | bytes 221192 | tf_op jit(solution)/shard_map/ppermute | solution.py:941
  53.9 8.8 %collective-permute-start.13 = (f32[9,8,256]{2,1,0:T(8,128)S(1)}, f32[9,8,256]{2,1,0:T(8,128)S(1)}, u32[]{:S(2)}, u32[]{:S(2)}) collective-permute-start(f32[9,8,256]{2,1,0:T(8,128)S(1)} %get-tuple-element.59), channel_id=1, source_target_pairs={{0,6},{1,7},{2,0},{3,1},{4,2},{5,3},{6,4},{7,5},{8,14},{9,15},{10,... | collective-permute-start | bytes 221192 | tf_op jit(solution)/shard_map/ppermute | solution.py:941
  54.6 8.1 %collective-permute-start.14 = (f32[9,8,256]{2,1,0:T(8,128)S(1)}, f32[9,8,256]{2,1,0:T(8,128)S(1)}, u32[]{:S(2)}, u32[]{:S(2)}) collective-permute-start(f32[9,8,256]{2,1,0:T(8,128)S(1)} %get-tuple-element.60), channel_id=1, source_target_pairs={{0,4},{1,5},{2,6},{3,7},{4,0},{5,1},{6,2},{7,3},{8,12},{9,13},{10,... | collective-permute-start | bytes 221192 | tf_op jit(solution)/shard_map/ppermute | solution.py:941
  56.2 6.5 %collective-permute-start.15 = (f32[9,8,256]{2,1,0:T(8,128)S(1)}, f32[9,8,256]{2,1,0:T(8,128)S(1)}, u32[]{:S(2)}, u32[]{:S(2)}) collective-permute-start(f32[9,8,256]{2,1,0:T(8,128)S(1)} %get-tuple-element.61), channel_id=1, source_target_pairs={{0,2},{1,3},{2,4},{3,5},{4,6},{5,7},{6,0},{7,1},{8,10},{9,11},{10,... | collective-permute-start | bytes 221192 | tf_op jit(solution)/shard_map/ppermute | solution.py:941
  62.8 2.6 %collective-permute-start.16 = (f32[8,256]{1,0:T(8,128)S(1)}, f32[8,256]{1,0:T(8,128)S(1)}, u32[]{:S(2)}, u32[]{:S(2)}) collective-permute-start(f32[8,256]{1,0:T(8,128)S(1)} %get-tuple-element.63.sent_ref), channel_id=1, source_target_pairs={{0,8},{8,0},{16,24},{24,16},{1,9},{9,1},{17,25},{25,17},{2,10},{10... | collective-permute-start | bytes 24584 | tf_op jit(solution)/shard_map/ppermute | solution.py:762
  65.4 2.6 %collective-permute-start.17 = (f32[8,256]{1,0:T(8,128)S(1)}, f32[8,256]{1,0:T(8,128)S(1)}, u32[]{:S(2)}, u32[]{:S(2)}) collective-permute-start(f32[8,256]{1,0:T(8,128)S(1)} %relay.3.refs_0_), channel_id=1, source_target_pairs={{0,16},{8,24},{16,0},{24,8},{1,17},{9,25},{17,1},{25,9},{2,18},{10... | collective-permute-start | bytes 24584 | tf_op jit(solution)/shard_map/ppermute | solution.py:765
  68.1 8.2 %collective-permute-start.19 = (f32[24,128]{1,0:T(8,128)S(1)}, f32[24,128]{1,0:T(8,128)S(1)}, u32[]{:S(2)}, u32[]{:S(2)}) collective-permute-start(f32[24,128]{1,0:T(8,128)S(1)} %get-tuple-element.65.sent_ref), channel_id=1, source_target_pairs={{1,2},{2,1},{3,4},{4,3},{5,6},{6,5},{9,10},{10,9},{11,12},{12,11},... | collective-permute-start | bytes 36872 | tf_op jit(solution)/shard_map/ppermute | solution.py:782
  74.9 1.4 %collective-permute-start.18 = (f32[24,128]{1,0:T(8,128)S(1)}, f32[24,128]{1,0:T(8,128)S(1)}, u32[]{:S(2)}, u32[]{:S(2)}) collective-permute-start(f32[24,128]{1,0:T(8,128)S(1)} %get-tuple-element.65.sent_ref), channel_id=1, source_target_pairs={{0,1},{1,0},{2,3},{3,2},{4,5},{5,4},{6,7},{7,6},{8,9},{9,8},{10,11... | collective-permute-start | bytes 36872 | tf_op jit(solution)/shard_map/ppermute | solution.py:783

commit v9 on v8

--- a/solution.py
+++ b/solution.py
@@ -336,7 +336,7 @@
             out_ref[where, :, at] = lower[j, i]
         return carry
 
-    lax.fori_loop(0, cols // LANES, one_part, 0)
+    lax.fori_loop(0, cols // LANES, one_part, 0, unroll=2)
 
 
 def sample_kernel(
@@ -355,8 +355,13 @@
 
         @pl.when(step == s)
         def _():
-            par_scr[...] = par_refs[s][0:8]
-            if mend:
+            if not mend:
+                par_scr[...] = par_refs[s][0:8]
+            else:
+                wide = cols // LANES
+                for i in range(8 * wide):
+                    h = i % wide
+                    par_scr[i // wide, :, h * LANES : (h + 1) * LANES] = par_refs[s][i]
                 side = column_is_odd(tile_ref)
                 chip = lax.rem(tile_of(tile_ref) // 2 + (parts - s), parts)
                 inside = jnp.where(side, chip, parts - 1 - chip) < parts - 1
@@ -364,8 +369,8 @@
                 hit = jnp.logical_and(lane == jnp.where(side, cols - 1, 0), inside)
                 lower, upper = par_refs[(s + 1) % parts], par_refs[(s - 1) % parts]
                 for k in range(2):
-                    end = jnp.where(side, upper[8, :, k : k + 1], lower[8, :, k : k + 1])
-                    par_scr[k] = par_refs[s][k] + jnp.where(hit, end, 0.0)
+                    end = jnp.where(side, upper[8 * wide, :, k : k + 1], lower[8 * wide, :, k : k + 1])
+                    par_scr[k] = par_scr[k] + jnp.where(hit, end, 0.0)
                 if s == 0:
                     own_out_refs[0][...] = par_scr[...]
             vis_scr[...] = vis_refs[s][8].astype(jnp.int32)
@@ -588,6 +593,14 @@
     side = column_is_odd(tile_ref)
     lane = iota((rows, cols), 1)
     spill = jnp.zeros((rows, cols), f32)
+
+    def give(k, value):
+        if far_refs:
+            out_ref[k] = value
+        else:
+            for h in range(cols // LANES):
+                out_ref[k * (cols // LANES) + h] = value[:, h * LANES : (h + 1) * LANES]
+
     for k in range(2):
         at = slice(k * rows, (k + 1) * rows)
         tall = tall_ref[k]
@@ -599,12 +612,12 @@
         after = jnp.where(side, far_left, near_left)
         left = jnp.where(lane == 0, before, pltpu.roll(tall, 1, 1))
         right = jnp.where(lane == cols - 1, after, pltpu.roll(tall, cols - 1, 1))
-        out_ref[k] = 0.5 * par_ref[k] + (tall + left + right) * (0.5 / 9.0)
+        give(k, 0.5 * par_ref[k] + (tall + left + right) * (0.5 / 9.0))
         spill = jnp.where(lane == k, jnp.where(side, near_left, near_right) * (0.5 / 9.0), spill)
     for k in range(2, 8):
-        out_ref[k] = par_ref[k]
+        give(k, par_ref[k])
     if not far_refs:
-        out_ref[8] = spill
+        out_ref[8 * (cols // LANES)] = spill[:, 0:LANES]
     light = sent_ref[2 * rows : 2 * rows + 2, 0:LIGHTS] + near_ref[2 * rows : 2 * rows + 2, 0:LIGHTS]
     gains = gain_ref[...]
     gain_out_ref[...] = gains + (light[0:1] - gains * light[1:2]) / (light[1:2] + 1.0)
@@ -648,7 +661,7 @@
 def sample_call(tile, own, got, gains, tables, pars, vises, mend):
     parts = len(pars)
     samples, rows, _ = own.shape
-    cols = pars[0].shape[2]
+    cols = vises[0].shape[2]
     held = 2 * samples
 
     def full(x):
@@ -781,9 +794,9 @@
     )
     ends = [lax.ppermute(sent, "tile", pairs(tiles, 1))] if closed else []
     near = lax.ppermute(sent, "tile", pairs(tiles, 0))
-    slabs = 8 if closed else 9
+    shape = params.shape if closed else (8 * (cols // LANES) + 1, rows, LANES)
     return plain_call(
-        smooth_kernel, "smooth", [(slabs, rows, cols), gains.shape], [], tile, params, tall, gains, sent, near, *ends
+        smooth_kernel, "smooth", [shape, gains.shape], [], tile, params, tall, gains, sent, near, *ends
     )
 
 

time: 77.1 us -> 76.6 us (level)
  no operation moved by 1% of the time
where the time goes in v9:
time: 76.6 us; the launch traced here: 76.4 us
  starting transfers between devices  32.7 us (43%)
  Pallas kernels  27.9 us (36%)
  waiting for transfers between devices  14.9 us (19%)
  between operations  0.81 us (1%)
    ppermute x12, starting transfers between devices, shifted(): lax.ppermute(x, 'tile', [(2 * z + c, 2 * ((z + by) % nz) + c) for z in ra...  17 us
    pallas_call x2, Pallas kernels, sample_call(): pl.pallas_call(functools.partial(sample_kernel, parts=parts, mend=mend),...  13.2 us
    pallas_call x2, Pallas kernels, normal_call(): pl.pallas_call(normal_kernel, name='normal_factor', out_shape=jax.ShapeDt...  10.1 us
    ppermute x12, waiting for transfers between devices, shifted(): lax.ppermute(x, 'tile', [(2 * z + c, 2 * ((z + by) % nz) + c) for z in ra...  7.5 us
    ppermute x1, starting transfers between devices, settle(): ends = [lax.ppermute(sent, 'tile', pairs(tiles, 1))] if closed else []  6.59 us
    ppermute x2, starting transfers between devices, settle(): near = lax.ppermute(sent, 'tile', pairs(tiles, 0))  3.98 us
    ppermute x2, waiting for transfers between devices, settle(): edge = lax.ppermute(relay, 'grp', [(i, i ^ 2) for i in range(grps)])  2.72 us
    ppermute x2, waiting for transfers between devices, settle(): first = lax.ppermute(sent, 'grp', pairs(grps, 0))  2.58 us
  transfers between devices with their start and end apart: 20, of which 10 were waited for; matrix products, arithmetic and copies ran while one was open for 0% of the time, Pallas kernels for 16%

profile of v9, /device:TPU:1, one launch (start us, length us, event | category | flops | bytes accessed | tf_op | source)
XLA Modules:
  0.0 76.4 jit_solution(6033953586876802953)
XLA Ops:
  0.7 1.4 %pack.1 = (bf16[64,8,1024]{2,1,0:T(8,128)(2,1)S(1)}, f32[9,8,256]{2,1,0:T(8,128)S(1)}) custom-call(s32[1]{0:T(128)} %bitcast.tile_ref, bf16[64,8,2048]{2,1,0:T(8,128)(2,1)} %own_ref.3, f32[8,8,256]{2,1,0:T(8,128)} %par_ref.5, s32[8,256]{1,0:T(8,128)} %vis_ref.5), custom_call_target="tpu_custom_call" | custom-call | tf_op jit(solution)/shard_map/pack/pallas_call | solution.py:737
  2.1 0.0 copy-start.1
  2.1 0.0 copy-start.2
  2.2 0.1 collective-permute-start
  2.3 3.8 %collective-permute-start.3 = (f32[9,8,256]{2,1,0:T(8,128)S(1)}, f32[9,8,256]{2,1,0:T(8,128)S(1)}, u32[]{:S(2)}, u32[]{:S(2)}) collective-permute-start(f32[9,8,256]{2,1,0:T(8,128)S(1)} %get-tuple-element.46.refs_3_.refs_7_), channel_id=1, source_target_pairs={{0,4},{1,5},{2,6},{3,7},{4,0},{5,1},{6,2},{7,3},{8,12},{9,13},{10,... | collective-permute-start | bytes 221192 | tf_op jit(solution)/shard_map/ppermute | solution.py:954
  6.0 1.1 %collective-permute-start.2 = (f32[9,8,256]{2,1,0:T(8,128)S(1)}, f32[9,8,256]{2,1,0:T(8,128)S(1)}, u32[]{:S(2)}, u32[]{:S(2)}) collective-permute-start(f32[9,8,256]{2,1,0:T(8,128)S(1)} %get-tuple-element.46.refs_3_.refs_7_), channel_id=1, source_target_pairs={{0,6},{1,7},{2,0},{3,1},{4,2},{5,3},{6,4},{7,5},{8,14},{9,15},{10,... | collective-permute-start | bytes 221192 | tf_op jit(solution)/shard_map/ppermute | solution.py:954
  7.1 0.4 collective-permute-start.1
  7.5 1.9 %tables.1 = (f32[8,32]{1,0:T(8,128)S(1)}, f32[8,16]{1,0:T(8,128)S(1)}, bf16[512,48]{1,0:T(8,128)(2,1)S(1)}, f32[32,512]{1,0:T(8,128)S(1)}, bf16[128,32]{1,0:T(8,...) custom-call(s32[1]{0:T(128)} %bitcast.tile_ref, ...), custom_call_target="tpu_custom_call" | custom-call | tf_op jit(solution)/shard_map/tables/pallas_call | solution.py:928
  9.4 0.5 collective-permute-done.3.refs_2_.refs_6_
  9.9 0.0 collective-permute-done.2.refs_1_.refs_5_
  9.9 2.3 %collective-permute-done.1.refs_0_.refs_4_ = f32[9,8,256]{2,1,0:T(8,128)S(1)} collective-permute-done((f32[9,8,256]{2,1,0:T(8,128)S(1)}, f32[9,8,256]{2,1,0:T(8,128)S(1)}, u32[]{:S(2)}, u32[]{:S(2)}) %collective-permute-start.1) | collective-permute-done | bytes 73760 | tf_op jit(solution)/shard_map/ppermute | solution.py:954
  12.2 0.0 collective-permute-done.got_ref
  12.2 6.5 %sample_sums.2 = (f32[9,8,256]{2,1,0:T(8,128)S(1)}, f32[9,8,256]{2,1,0:T(8,128)S(1)}, f32[9,8,256]{2,1,0:T(8,128)S(1)}, f32[9,8,256]{2,1,0:T(8,128)S(1)}) custom-call(s32[1]{0:T(128)} %bitcast.tile_ref, bf16[64,8,2048]{2,1,0:T(8,128)(2,1)S(1)} %copy-done, bf16[64,8,1024]{2,1,0:T(8,128)(2,1)S(1)} %collective-permute-done.got_ref, f32[1,32]{1,0:T(1,128)S(1)} %bitcast.3, ...), custom_call_target="tpu_custom_call" | custom-call | tf_op jit(solution)/shard_map/sample_sums/pallas_call | solution.py:678
  18.7 3.1 %collective-permute-start.4 = (f32[9,8,256]{2,1,0:T(8,128)S(1)}, f32[9,8,256]{2,1,0:T(8,128)S(1)}, u32[]{:S(2)}, u32[]{:S(2)}) collective-permute-start(f32[9,8,256]{2,1,0:T(8,128)S(1)} %get-tuple-element.48), channel_id=1, source_target_pairs={{0,6},{1,7},{2,0},{3,1},{4,2},{5,3},{6,4},{7,5},{8,14},{9,15},{10,... | collective-permute-start | bytes 221192 | tf_op jit(solution)/shard_map/ppermute | solution.py:954
  21.9 0.8 collective-permute-start.5
  22.6 1.4 %collective-permute-start.6 = (f32[9,8,256]{2,1,0:T(8,128)S(1)}, f32[9,8,256]{2,1,0:T(8,128)S(1)}, u32[]{:S(2)}, u32[]{:S(2)}) collective-permute-start(f32[9,8,256]{2,1,0:T(8,128)S(1)} %get-tuple-element.50), channel_id=1, source_target_pairs={{0,2},{1,3},{2,4},{3,5},{4,6},{5,7},{6,0},{7,1},{8,10},{9,11},{10,... | collective-permute-start | bytes 221192 | tf_op jit(solution)/shard_map/ppermute | solution.py:954
  24.0 5.0 %normal_factor.2.low_ref = f32[44,8,256]{2,1,0:T(8,128)S(1)} custom-call(f32[8,8,256]{2,1,0:T(8,128)S(1)} %copy-done.1, s32[8,256]{1,0:T(8,128)S(1)} %copy-done.2, f32[1,32]{1,0:T(1,128)S(1)} %bitcast.4, f32[8,32]{1,0:T(8,128)S(1)} %get-tuple-element.36.near_ref, f32[8,16]{1,0:T(8,128)S(1)} %get-tuple-element.37.cams_ref, ...), custom_call_target="tpu_custom_call" | custom-call | tf_op jit(solution)/shard_map/normal_factor/pallas_call | solution.py:642
  29.1 0.0 collective-permute-done.4.refs_1_
  29.1 0.0 collective-permute-done.5.refs_2_
  29.1 0.1 solve.2
  29.2 1.3 %collective-permute-start.7 = (f32[8,256]{1,0:T(8,128)S(1)}, f32[8,256]{1,0:T(8,128)S(1)}, u32[]{:S(2)}, u32[]{:S(2)}) collective-permute-start(f32[8,256]{1,0:T(8,128)S(1)} %get-tuple-element.52.sent_ref), channel_id=1, source_target_pairs={{0,8},{8,0},{16,24},{24,16},{1,9},{9,1},{17,25},{25,17},{2,10},{10... | collective-permute-start | bytes 24584 | tf_op jit(solution)/shard_map/ppermute | solution.py:775
  30.5 1.3 %collective-permute-done.7.first_ref = f32[8,256]{1,0:T(8,128)S(1)} collective-permute-done((f32[8,256]{1,0:T(8,128)S(1)}, f32[8,256]{1,0:T(8,128)S(1)}, u32[]{:S(2)}, u32[]{:S(2)}) %collective-permute-start.7) | collective-permute-done | bytes 8224 | tf_op jit(solution)/shard_map/ppermute | solution.py:775
  31.8 1.2 %collective-permute-start.8 = (f32[8,256]{1,0:T(8,128)S(1)}, f32[8,256]{1,0:T(8,128)S(1)}, u32[]{:S(2)}, u32[]{:S(2)}) collective-permute-start(f32[8,256]{1,0:T(8,128)S(1)} %relay.2.refs_0_), channel_id=1, source_target_pairs={{0,16},{8,24},{16,0},{24,8},{1,17},{9,25},{17,1},{25,9},{2,18},{10... | collective-permute-start | bytes 24584 | tf_op jit(solution)/shard_map/ppermute | solution.py:778
  33.0 1.3 %collective-permute-done.8.edge_ref.refs_1_ = f32[8,256]{1,0:T(8,128)S(1)} collective-permute-done((f32[8,256]{1,0:T(8,128)S(1)}, f32[8,256]{1,0:T(8,128)S(1)}, u32[]{:S(2)}, u32[]{:S(2)}) %collective-permute-start.8) | collective-permute-done | bytes 8224 | tf_op jit(solution)/shard_map/ppermute | solution.py:778
  34.3 0.1 rows.2
  34.4 3.9 %collective-permute-start.9 = (f32[24,128]{1,0:T(8,128)S(1)}, f32[24,128]{1,0:T(8,128)S(1)}, u32[]{:S(2)}, u32[]{:S(2)}) collective-permute-start(f32[24,128]{1,0:T(8,128)S(1)} %get-tuple-element.54.sent_ref), channel_id=1, source_target_pairs={{0,1},{1,0},{2,3},{3,2},{4,5},{5,4},{6,7},{7,6},{8,9},{9,8},{10,11... | collective-permute-start | bytes 36872 | tf_op jit(solution)/shard_map/ppermute | solution.py:796
  38.3 0.8 %collective-permute-done.9.near_ref = f32[24,128]{1,0:T(8,128)S(1)} collective-permute-done((f32[24,128]{1,0:T(8,128)S(1)}, f32[24,128]{1,0:T(8,128)S(1)}, u32[]{:S(2)}, u32[]{:S(2)}) %collective-permute-start.9) | collective-permute-done | bytes 12320 | tf_op jit(solution)/shard_map/ppermute | solution.py:796
  39.1 0.1 smooth.2
  39.3 1.5 %collective-permute-start.12 = (f32[17,8,128]{2,1,0:T(8,128)S(1)}, f32[17,8,128]{2,1,0:T(8,128)S(1)}, u32[]{:S(2)}, u32[]{:S(2)}) collective-permute-start(f32[17,8,128]{2,1,0:T(8,128)S(1)} %get-tuple-element.56.refs_3_), channel_id=1, source_target_pairs={{0,4},{1,5},{2,6},{3,7},{4,0},{5,1},{6,2},{7,3},{8,12},{9,13},{10,... | collective-permute-start | bytes 208904 | tf_op jit(solution)/shard_map/ppermute | solution.py:954
  40.8 1.1 %collective-permute-start.11 = (f32[17,8,128]{2,1,0:T(8,128)S(1)}, f32[17,8,128]{2,1,0:T(8,128)S(1)}, u32[]{:S(2)}, u32[]{:S(2)}) collective-permute-start(f32[17,8,128]{2,1,0:T(8,128)S(1)} %get-tuple-element.56.refs_3_), channel_id=1, source_target_pairs={{0,6},{1,7},{2,0},{3,1},{4,2},{5,3},{6,4},{7,5},{8,14},{9,15},{10,... | collective-permute-start | bytes 208904 | tf_op jit(solution)/shard_map/ppermute | solution.py:954
  41.9 0.4 collective-permute-start.10
  42.3 3.3 %collective-permute-done.12.refs_2_ = f32[17,8,128]{2,1,0:T(8,128)S(1)} collective-permute-done((f32[17,8,128]{2,1,0:T(8,128)S(1)}, f32[17,8,128]{2,1,0:T(8,128)S(1)}, u32[]{:S(2)}, u32[]{:S(2)}) %collective-permute-start.12) | collective-permute-done | bytes 69664 | tf_op jit(solution)/shard_map/ppermute | solution.py:954
  45.5 1.4 %collective-permute-done.10.refs_0_ = f32[17,8,128]{2,1,0:T(8,128)S(1)} collective-permute-done((f32[17,8,128]{2,1,0:T(8,128)S(1)}, f32[17,8,128]{2,1,0:T(8,128)S(1)}, u32[]{:S(2)}, u32[]{:S(2)}) %collective-permute-start.10) | collective-permute-done | bytes 69664 | tf_op jit(solution)/shard_map/ppermute | solution.py:954
  47.0 6.7 %sample_sums.3 = (f32[9,8,256]{2,1,0:T(8,128)S(1)}, f32[9,8,256]{2,1,0:T(8,128)S(1)}, f32[9,8,256]{2,1,0:T(8,128)S(1)}, f32[9,8,256]{2,1,0:T(8,128)S(1)}, f32[8,8,256]{2,1,0:T(8,128)S(1)}) custom-call(s32[1]{0:T(128)} %bitcast.tile_ref, bf16[64,8,2048]{2,1,0:T(8,128)(2,1)S(1)} %copy-done, bf16[64,8,1024]{2,1,0:T(8,128)(2,1)S(1)} %collective-permute-done.got_ref, ...), custom_call_target="tpu_custom_call" | custom-call | tf_op jit(solution)/shard_map/sample_sums/pallas_call | solution.py:678
  53.7 0.8 %collective-permute-start.13 = (f32[9,8,256]{2,1,0:T(8,128)S(1)}, f32[9,8,256]{2,1,0:T(8,128)S(1)}, u32[]{:S(2)}, u32[]{:S(2)}) collective-permute-start(f32[9,8,256]{2,1,0:T(8,128)S(1)} %get-tuple-element.59), channel_id=1, source_target_pairs={{0,6},{1,7},{2,0},{3,1},{4,2},{5,3},{6,4},{7,5},{8,14},{9,15},{10,... | collective-permute-start | bytes 221192 | tf_op jit(solution)/shard_map/ppermute | solution.py:954
  54.5 1.5 %collective-permute-start.14 = (f32[9,8,256]{2,1,0:T(8,128)S(1)}, f32[9,8,256]{2,1,0:T(8,128)S(1)}, u32[]{:S(2)}, u32[]{:S(2)}) collective-permute-start(f32[9,8,256]{2,1,0:T(8,128)S(1)} %get-tuple-element.60), channel_id=1, source_target_pairs={{0,4},{1,5},{2,6},{3,7},{4,0},{5,1},{6,2},{7,3},{8,12},{9,13},{10,... | collective-permute-start | bytes 221192 | tf_op jit(solution)/shard_map/ppermute | solution.py:954
  56.0 1.1 %collective-permute-start.15 = (f32[9,8,256]{2,1,0:T(8,128)S(1)}, f32[9,8,256]{2,1,0:T(8,128)S(1)}, u32[]{:S(2)}, u32[]{:S(2)}) collective-permute-start(f32[9,8,256]{2,1,0:T(8,128)S(1)} %get-tuple-element.61), channel_id=1, source_target_pairs={{0,2},{1,3},{2,4},{3,5},{4,6},{5,7},{6,0},{7,1},{8,10},{9,11},{10,... | collective-permute-start | bytes 221192 | tf_op jit(solution)/shard_map/ppermute | solution.py:954
  57.2 5.0 %normal_factor.3.low_ref = f32[44,8,256]{2,1,0:T(8,128)S(1)} custom-call(f32[8,8,256]{2,1,0:T(8,128)S(1)} %get-tuple-element.57.par_ref, s32[8,256]{1,0:T(8,128)S(1)} %copy-done.2, f32[1,32]{1,0:T(1,128)S(1)} %get-tuple-element.55.gain_ref, f32[8,32]{1,0:T(8,128)S(1)} %get-tuple-element.36.near_ref, f32[8,16]{1,0:T(8,128)S(1)} %get-tuple-element.37.cams_ref, ...), custom_call_target="tpu_custom_call" | custom-call | tf_op jit(solution)/shard_map/normal_factor/pallas_call | solution.py:642
  62.2 0.1 solve.3
  62.4 1.3 %collective-permute-start.16 = (f32[8,256]{1,0:T(8,128)S(1)}, f32[8,256]{1,0:T(8,128)S(1)}, u32[]{:S(2)}, u32[]{:S(2)}) collective-permute-start(f32[8,256]{1,0:T(8,128)S(1)} %get-tuple-element.63.sent_ref), channel_id=1, source_target_pairs={{0,8},{8,0},{16,24},{24,16},{1,9},{9,1},{17,25},{25,17},{2,10},{10... | collective-permute-start | bytes 24584 | tf_op jit(solution)/shard_map/ppermute | solution.py:775
  63.6 1.3 %collective-permute-done.16.first_ref = f32[8,256]{1,0:T(8,128)S(1)} collective-permute-done((f32[8,256]{1,0:T(8,128)S(1)}, f32[8,256]{1,0:T(8,128)S(1)}, u32[]{:S(2)}, u32[]{:S(2)}) %collective-permute-start.16) | collective-permute-done | bytes 8224 | tf_op jit(solution)/shard_map/ppermute | solution.py:775
  64.9 1.2 %collective-permute-start.17 = (f32[8,256]{1,0:T(8,128)S(1)}, f32[8,256]{1,0:T(8,128)S(1)}, u32[]{:S(2)}, u32[]{:S(2)}) collective-permute-start(f32[8,256]{1,0:T(8,128)S(1)} %relay.3.refs_0_), channel_id=1, source_target_pairs={{0,16},{8,24},{16,0},{24,8},{1,17},{9,25},{17,1},{25,9},{2,18},{10... | collective-permute-start | bytes 24584 | tf_op jit(solution)/shard_map/ppermute | solution.py:778
  66.2 1.5 %collective-permute-done.17.edge_ref.refs_1_ = f32[8,256]{1,0:T(8,128)S(1)} collective-permute-done((f32[8,256]{1,0:T(8,128)S(1)}, f32[8,256]{1,0:T(8,128)S(1)}, u32[]{:S(2)}, u32[]{:S(2)}) %collective-permute-start.17) | collective-permute-done | bytes 8224 | tf_op jit(solution)/shard_map/ppermute | solution.py:778
  67.6 0.1 rows.3
  67.7 6.6 %collective-permute-start.19 = (f32[24,128]{1,0:T(8,128)S(1)}, f32[24,128]{1,0:T(8,128)S(1)}, u32[]{:S(2)}, u32[]{:S(2)}) collective-permute-start(f32[24,128]{1,0:T(8,128)S(1)} %get-tuple-element.65.sent_ref), channel_id=1, source_target_pairs={{1,2},{2,1},{3,4},{4,3},{5,6},{6,5},{9,10},{10,9},{11,12},{12,11},... | collective-permute-start | bytes 36872 | tf_op jit(solution)/shard_map/ppermute | solution.py:795
  74.3 0.1 collective-permute-start.18
  74.4 1.3 %collective-permute-done.19.refs_0_ = f32[24,128]{1,0:T(8,128)S(1)} collective-permute-done((f32[24,128]{1,0:T(8,128)S(1)}, f32[24,128]{1,0:T(8,128)S(1)}, u32[]{:S(2)}, u32[]{:S(2)}) %collective-permute-start.19) | collective-permute-done | bytes 12320 | tf_op jit(solution)/shard_map/ppermute | solution.py:795
  75.7 0.7 smooth.3
  (18 shorter events, 0.0 us)
Async XLA Ops:
  0.6 11.6 %copy-start = (bf16[64,8,2048]{2,1,0:T(8,128)(2,1)S(1)}, bf16[64,8,2048]{2,1,0:T(8,128)(2,1)}, u32[]{:S(2)}) copy-start(bf16[64,8,2048]{2,1,0:T(8,128)(2,1)} %own_ref.3) | copy-start | bytes 6291460
  0.6 6.9 %copy-start.5 = (f32[3,16]{1,0:T(4,128)S(1)}, f32[3,16]{1,0:T(4,128)}, u32[]{:S(2)}) copy-start(f32[3,16]{1,0:T(4,128)} %view_ref.1) | copy-start | bytes 580
  0.7 6.9 %copy-start.4 = (f32[3,32]{1,0:T(4,128)S(1)}, f32[3,32]{1,0:T(4,128)}, u32[]{:S(2)}) copy-start(f32[3,32]{1,0:T(4,128)} %light_ref.1) | copy-start | bytes 1156
  0.7 11.6 %copy-start.3 = (f32[32]{0:T(128)S(1)}, f32[32]{0:T(128)}, u32[]{:S(2)}) copy-start(f32[32]{0:T(128)} %param.11) | copy-start | bytes 388
  2.1 21.9 %copy-start.1 = (f32[8,8,256]{2,1,0:T(8,128)S(1)}, f32[8,8,256]{2,1,0:T(8,128)}, u32[]{:S(2)}) copy-start(f32[8,8,256]{2,1,0:T(8,128)} %par_ref.5) | copy-start | bytes 196612
  2.1 21.9 %copy-start.2 = (s32[8,256]{1,0:T(8,128)S(1)}, s32[8,256]{1,0:T(8,128)}, u32[]{:S(2)}) copy-start(s32[8,256]{1,0:T(8,128)} %vis_ref.5) | copy-start | bytes 24580
  2.2 10.1 %collective-permute-start = (bf16[64,8,1024]{2,1,0:T(8,128)(2,1)S(1)}, bf16[64,8,1024]{2,1,0:T(8,128)(2,1)S(1)}, u32[]{:S(2)}, u32[]{:S(2)}) collective-permute-start(bf16[64,8,1024]{2,1,0:T(8,128)(2,1)S(1)} %get-tuple-element.35), channel_id=1, source_target_pairs={{0,1},{1,0},{2,3},{3,2},{4,5},{5,4},{6,7},{7,6},{8,9},{9,8},{10,11... | collective-permute-start | bytes 3145736 | tf_op jit(solution)/shard_map/ppermute | solution.py:966
  2.3 7.6 %collective-permute-start.3 = (f32[9,8,256]{2,1,0:T(8,128)S(1)}, f32[9,8,256]{2,1,0:T(8,128)S(1)}, u32[]{:S(2)}, u32[]{:S(2)}) collective-permute-start(f32[9,8,256]{2,1,0:T(8,128)S(1)} %get-tuple-element.46.refs_3_.refs_7_), channel_id=1, source_target_pairs={{0,4},{1,5},{2,6},{3,7},{4,0},{5,1},{6,2},{7,3},{8,12},{9,13},{10,... | collective-permute-start | bytes 221192 | tf_op jit(solution)/shard_map/ppermute | solution.py:954
  6.0 3.9 %collective-permute-start.2 = (f32[9,8,256]{2,1,0:T(8,128)S(1)}, f32[9,8,256]{2,1,0:T(8,128)S(1)}, u32[]{:S(2)}, u32[]{:S(2)}) collective-permute-start(f32[9,8,256]{2,1,0:T(8,128)S(1)} %get-tuple-element.46.refs_3_.refs_7_), channel_id=1, source_target_pairs={{0,6},{1,7},{2,0},{3,1},{4,2},{5,3},{6,4},{7,5},{8,14},{9,15},{10,... | collective-permute-start | bytes 221192 | tf_op jit(solution)/shard_map/ppermute | solution.py:954
  7.1 5.1 %collective-permute-start.1 = (f32[9,8,256]{2,1,0:T(8,128)S(1)}, f32[9,8,256]{2,1,0:T(8,128)S(1)}, u32[]{:S(2)}, u32[]{:S(2)}) collective-permute-start(f32[9,8,256]{2,1,0:T(8,128)S(1)} %get-tuple-element.46.refs_3_.refs_7_), channel_id=1, source_target_pairs={{0,2},{1,3},{2,4},{3,5},{4,6},{5,7},{6,0},{7,1},{8,10},{9,11},{10,... | collective-permute-start | bytes 221192 | tf_op jit(solution)/shard_map/ppermute | solution.py:954
  18.7 10.3 %collective-permute-start.4 = (f32[9,8,256]{2,1,0:T(8,128)S(1)}, f32[9,8,256]{2,1,0:T(8,128)S(1)}, u32[]{:S(2)}, u32[]{:S(2)}) collective-permute-start(f32[9,8,256]{2,1,0:T(8,128)S(1)} %get-tuple-element.48), channel_id=1, source_target_pairs={{0,6},{1,7},{2,0},{3,1},{4,2},{5,3},{6,4},{7,5},{8,14},{9,15},{10,... | collective-permute-start | bytes 221192 | tf_op jit(solution)/shard_map/ppermute | solution.py:954
  21.9 7.2 %collective-permute-start.5 = (f32[9,8,256]{2,1,0:T(8,128)S(1)}, f32[9,8,256]{2,1,0:T(8,128)S(1)}, u32[]{:S(2)}, u32[]{:S(2)}) collective-permute-start(f32[9,8,256]{2,1,0:T(8,128)S(1)} %get-tuple-element.49), channel_id=1, source_target_pairs={{0,4},{1,5},{2,6},{3,7},{4,0},{5,1},{6,2},{7,3},{8,12},{9,13},{10,... | collective-permute-start | bytes 221192 | tf_op jit(solution)/shard_map/ppermute | solution.py:954
  22.6 6.5 %collective-permute-start.6 = (f32[9,8,256]{2,1,0:T(8,128)S(1)}, f32[9,8,256]{2,1,0:T(8,128)S(1)}, u32[]{:S(2)}, u32[]{:S(2)}) collective-permute-start(f32[9,8,256]{2,1,0:T(8,128)S(1)} %get-tuple-element.50), channel_id=1, source_target_pairs={{0,2},{1,3},{2,4},{3,5},{4,6},{5,7},{6,0},{7,1},{8,10},{9,11},{10,... | collective-permute-start | bytes 221192 | tf_op jit(solution)/shard_map/ppermute | solution.py:954
  29.2 2.6 %collective-permute-start.7 = (f32[8,256]{1,0:T(8,128)S(1)}, f32[8,256]{1,0:T(8,128)S(1)}, u32[]{:S(2)}, u32[]{:S(2)}) collective-permute-start(f32[8,256]{1,0:T(8,128)S(1)} %get-tuple-element.52.sent_ref), channel_id=1, source_target_pairs={{0,8},{8,0},{16,24},{24,16},{1,9},{9,1},{17,25},{25,17},{2,10},{10... | collective-permute-start | bytes 24584 | tf_op jit(solution)/shard_map/ppermute | solution.py:775
  31.8 2.5 %collective-permute-start.8 = (f32[8,256]{1,0:T(8,128)S(1)}, f32[8,256]{1,0:T(8,128)S(1)}, u32[]{:S(2)}, u32[]{:S(2)}) collective-permute-start(f32[8,256]{1,0:T(8,128)S(1)} %relay.2.refs_0_), channel_id=1, source_target_pairs={{0,16},{8,24},{16,0},{24,8},{1,17},{9,25},{17,1},{25,9},{2,18},{10... | collective-permute-start | bytes 24584 | tf_op jit(solution)/shard_map/ppermute | solution.py:778
  34.4 4.7 %collective-permute-start.9 = (f32[24,128]{1,0:T(8,128)S(1)}, f32[24,128]{1,0:T(8,128)S(1)}, u32[]{:S(2)}, u32[]{:S(2)}) collective-permute-start(f32[24,128]{1,0:T(8,128)S(1)} %get-tuple-element.54.sent_ref), channel_id=1, source_target_pairs={{0,1},{1,0},{2,3},{3,2},{4,5},{5,4},{6,7},{7,6},{8,9},{9,8},{10,11... | collective-permute-start | bytes 36872 | tf_op jit(solution)/shard_map/ppermute | solution.py:796
  39.3 6.3 %collective-permute-start.12 = (f32[17,8,128]{2,1,0:T(8,128)S(1)}, f32[17,8,128]{2,1,0:T(8,128)S(1)}, u32[]{:S(2)}, u32[]{:S(2)}) collective-permute-start(f32[17,8,128]{2,1,0:T(8,128)S(1)} %get-tuple-element.56.refs_3_), channel_id=1, source_target_pairs={{0,4},{1,5},{2,6},{3,7},{4,0},{5,1},{6,2},{7,3},{8,12},{9,13},{10,... | collective-permute-start | bytes 208904 | tf_op jit(solution)/shard_map/ppermute | solution.py:954
  40.8 4.7 %collective-permute-start.11 = (f32[17,8,128]{2,1,0:T(8,128)S(1)}, f32[17,8,128]{2,1,0:T(8,128)S(1)}, u32[]{:S(2)}, u32[]{:S(2)}) collective-permute-start(f32[17,8,128]{2,1,0:T(8,128)S(1)} %get-tuple-element.56.refs_3_), channel_id=1, source_target_pairs={{0,6},{1,7},{2,0},{3,1},{4,2},{5,3},{6,4},{7,5},{8,14},{9,15},{10,... | collective-permute-start | bytes 208904 | tf_op jit(solution)/shard_map/ppermute | solution.py:954
  41.9 5.1 %collective-permute-start.10 = (f32[17,8,128]{2,1,0:T(8,128)S(1)}, f32[17,8,128]{2,1,0:T(8,128)S(1)}, u32[]{:S(2)}, u32[]{:S(2)}) collective-permute-start(f32[17,8,128]{2,1,0:T(8,128)S(1)} %get-tuple-element.56.refs_3_), channel_id=1, source_target_pairs={{0,2},{1,3},{2,4},{3,5},{4,6},{5,7},{6,0},{7,1},{8,10},{9,11},{10,... | collective-permute-start | bytes 208904 | tf_op jit(solution)/shard_map/ppermute | solution.py:954
  53.7 8.5 %collective-permute-start.13 = (f32[9,8,256]{2,1,0:T(8,128)S(1)}, f32[9,8,256]{2,1,0:T(8,128)S(1)}, u32[]{:S(2)}, u32[]{:S(2)}) collective-permute-start(f32[9,8,256]{2,1,0:T(8,128)S(1)} %get-tuple-element.59), channel_id=1, source_target_pairs={{0,6},{1,7},{2,0},{3,1},{4,2},{5,3},{6,4},{7,5},{8,14},{9,15},{10,... | collective-permute-start | bytes 221192 | tf_op jit(solution)/shard_map/ppermute | solution.py:954
  54.5 7.7 %collective-permute-start.14 = (f32[9,8,256]{2,1,0:T(8,128)S(1)}, f32[9,8,256]{2,1,0:T(8,128)S(1)}, u32[]{:S(2)}, u32[]{:S(2)}) collective-permute-start(f32[9,8,256]{2,1,0:T(8,128)S(1)} %get-tuple-element.60), channel_id=1, source_target_pairs={{0,4},{1,5},{2,6},{3,7},{4,0},{5,1},{6,2},{7,3},{8,12},{9,13},{10,... | collective-permute-start | bytes 221192 | tf_op jit(solution)/shard_map/ppermute | solution.py:954
  56.0 6.2 %collective-permute-start.15 = (f32[9,8,256]{2,1,0:T(8,128)S(1)}, f32[9,8,256]{2,1,0:T(8,128)S(1)}, u32[]{:S(2)}, u32[]{:S(2)}) collective-permute-start(f32[9,8,256]{2,1,0:T(8,128)S(1)} %get-tuple-element.61), channel_id=1, source_target_pairs={{0,2},{1,3},{2,4},{3,5},{4,6},{5,7},{6,0},{7,1},{8,10},{9,11},{10,... | collective-permute-start | bytes 221192 | tf_op jit(solution)/shard_map/ppermute | solution.py:954
  62.4 2.6 %collective-permute-start.16 = (f32[8,256]{1,0:T(8,128)S(1)}, f32[8,256]{1,0:T(8,128)S(1)}, u32[]{:S(2)}, u32[]{:S(2)}) collective-permute-start(f32[8,256]{1,0:T(8,128)S(1)} %get-tuple-element.63.sent_ref), channel_id=1, source_target_pairs={{0,8},{8,0},{16,24},{24,16},{1,9},{9,1},{17,25},{25,17},{2,10},{10... | collective-permute-start | bytes 24584 | tf_op jit(solution)/shard_map/ppermute | solution.py:775
  64.9 2.7 %collective-permute-start.17 = (f32[8,256]{1,0:T(8,128)S(1)}, f32[8,256]{1,0:T(8,128)S(1)}, u32[]{:S(2)}, u32[]{:S(2)}) collective-permute-start(f32[8,256]{1,0:T(8,128)S(1)} %relay.3.refs_0_), channel_id=1, source_target_pairs={{0,16},{8,24},{16,0},{24,8},{1,17},{9,25},{17,1},{25,9},{2,18},{10... | collective-permute-start | bytes 24584 | tf_op jit(solution)/shard_map/ppermute | solution.py:778
  67.7 8.0 %collective-permute-start.19 = (f32[24,128]{1,0:T(8,128)S(1)}, f32[24,128]{1,0:T(8,128)S(1)}, u32[]{:S(2)}, u32[]{:S(2)}) collective-permute-start(f32[24,128]{1,0:T(8,128)S(1)} %get-tuple-element.65.sent_ref), channel_id=1, source_target_pairs={{1,2},{2,1},{3,4},{4,3},{5,6},{6,5},{9,10},{10,9},{11,12},{12,11},... | collective-permute-start | bytes 36872 | tf_op jit(solution)/shard_map/ppermute | solution.py:795
  74.3 1.4 %collective-permute-start.18 = (f32[24,128]{1,0:T(8,128)S(1)}, f32[24,128]{1,0:T(8,128)S(1)}, u32[]{:S(2)}, u32[]{:S(2)}) collective-permute-start(f32[24,128]{1,0:T(8,128)S(1)} %get-tuple-element.65.sent_ref), channel_id=1, source_target_pairs={{0,1},{1,0},{2,3},{3,2},{4,5},{5,4},{6,7},{7,6},{8,9},{9,8},{10,11... | collective-permute-start | bytes 36872 | tf_op jit(solution)/shard_map/ppermute | solution.py:796
